TPU v7x, 32 devices: a whole 2x2x4 slice. The times are simulated.
32 devices in a mesh: ctx: 16 (over z, y, core), tp: 2 (over x).
Axes of the slice: x: 2, y: 2, z: 4, core: 2. Of those that a mesh axis runs over, the one named last changes fastest.
Arguments:
- qkv: bfloat16 [2048, 32, 3, 128], P('ctx', 'tp'), may hold values from -5 to 5
- grad_out: bfloat16 [2048, 8192], P(('ctx', 'tp')), may hold values from -6 to 6
- attn_out: bfloat16 [4096, 8192], P('tp'), may hold values from -0.09375 to 0.09375
Outputs:
- mixed_out: float32 [2048, 8192], P(('ctx', 'tp'))
- grad_qkv: float32 [2048, 32, 3, 128], P('ctx', 'tp')
All inputs are finite; a program needn't handle non-finite values.
Results may differ from a plain program's by a relative error of at most 0.0063.
Values may be sent and summed in bfloat16 or wider, within the bound.
No kernel may reach another device: no remote copies, remote signals or barrier semaphores. Data moves between devices by JAX's collectives and lax.ppermute only.
A program may use at most 192 MiB of HBM per device.

v0:
```python
import math

import jax
import jax.numpy as jnp
from jax import lax
from jax.sharding import PartitionSpec as P

HD = 128


def per_device(qkv, grad_out, attn_out):
    row_count, heads_local = (qkv.shape[0], qkv.shape[1])
    factor = 1.0 / math.sqrt(HD)
    queries = qkv[:, :, 0]
    keys_local = qkv[:, :, 1]
    values_local = qkv[:, :, 2]
    all_keys, all_values = (
        lax.all_gather(keys_local, "ctx", axis=0, tiled=True),
        lax.all_gather(values_local, "ctx", axis=0, tiled=True),
    )
    seq_len = all_keys.shape[0]
    offset = lax.axis_index("ctx") * row_count
    query_pos = offset + jnp.arange(row_count, dtype=jnp.int32)
    key_pos = jnp.arange(seq_len, dtype=jnp.int32)
    visible = key_pos[None, :] <= query_pos[:, None]
    scores = (
        jnp.einsum("rhd,shd->hrs", queries, all_keys, preferred_element_type=jnp.float32) * factor
    )
    scores = jnp.where(visible[None], scores, -jnp.inf)
    row_max = jnp.max(scores, axis=2, keepdims=True)
    log_total = row_max + jnp.log(jnp.sum(jnp.exp(scores - row_max), axis=2, keepdims=True))
    weights = jnp.exp(scores - log_total)
    weights_low = weights.astype(jnp.bfloat16)
    attended = jnp.einsum(
        "hrs,shd->rhd", weights_low, all_values, preferred_element_type=jnp.float32
    ).astype(jnp.bfloat16)
    attended_flat = attended.reshape(row_count, heads_local * HD)
    mixed_out = lax.psum_scatter(
        jnp.dot(attended_flat, attn_out, preferred_element_type=jnp.float32),
        "tp",
        scatter_dimension=0,
        tiled=True,
    )
    grad_full = jnp.einsum(
        "nm,km->nk",
        lax.all_gather(grad_out, "tp", axis=0, tiled=True),
        attn_out,
        preferred_element_type=jnp.float32,
    )
    grad_att = grad_full.astype(jnp.bfloat16).reshape(row_count, heads_local, HD)
    row_delta = jnp.einsum("rhd,rhd->rh", grad_att, attended, preferred_element_type=jnp.float32)
    grad_weights = jnp.einsum(
        "rhd,shd->hrs", grad_att, all_values, preferred_element_type=jnp.float32
    )
    grad_scores = (weights * (grad_weights - row_delta.T[:, :, None]) * factor).astype(jnp.bfloat16)
    grad_queries = jnp.einsum(
        "hrs,shd->rhd", grad_scores, all_keys, preferred_element_type=jnp.float32
    )
    lse_rows = log_total[:, :, 0].T
    row_stats = (
        lax.all_gather(lse_rows, "ctx", axis=0, tiled=True),
        lax.all_gather(row_delta, "ctx", axis=0, tiled=True),
    )
    piece_q = lax.all_gather(queries, "ctx", axis=0, tiled=True)
    piece_g = lax.all_gather(grad_att, "ctx", axis=0, tiled=True)
    piece_len = piece_q.shape[0]
    piece_lse = row_stats[0]
    piece_delta = row_stats[1]
    piece_pos = jnp.arange(piece_len, dtype=jnp.int32)
    visible_part = query_pos[None, :] <= piece_pos[:, None]
    part_scores = (
        jnp.einsum("nhd,rhd->hnr", piece_q, keys_local, preferred_element_type=jnp.float32) * factor
    )
    part_weights = jnp.where(
        visible_part[None], jnp.exp(part_scores - piece_lse.T[:, :, None]), 0.0
    )
    part_grad = jnp.einsum(
        "nhd,rhd->hnr", piece_g, values_local, preferred_element_type=jnp.float32
    )
    part_ds = (part_weights * (part_grad - piece_delta.T[:, :, None]) * factor).astype(jnp.bfloat16)
    grad_k = jnp.einsum("hnr,nhd->rhd", part_ds, piece_q, preferred_element_type=jnp.float32)
    grad_v = jnp.einsum(
        "hnr,nhd->rhd",
        part_weights.astype(jnp.bfloat16),
        piece_g,
        preferred_element_type=jnp.float32,
    )
    grad_qkv = jnp.stack([grad_queries, grad_k, grad_v], axis=2)
    return (mixed_out, grad_qkv)


def solution(mesh):
    in_specs = (P("ctx", "tp", None, None), P(("ctx", "tp"), None), P("tp", None))
    out_specs = (P(("ctx", "tp"), None), P("ctx", "tp", None, None))
    return jax.shard_map(
        per_device, mesh=mesh, in_specs=in_specs, out_specs=out_specs, check_vma=False
    )
```

profile of v0, /device:TPU:0, one launch (start us, length us, event | category | flops | bytes accessed | tf_op | source)
XLA Modules:
  0.0 417.6 jit_solution(8683926837222314162)
XLA Ops:
  7.2 0.7 all-gather.9.cloned.1.call-update
  7.9 1.7 fusion.71
  9.6 0.9 copy.20
  10.6 1.2 copy.21
  11.9 0.9 copy.19
  13.0 32.4 %all-gather.9.cloned.1.call-done = bf16[128,8192]{1,0:T(8,128)(2,1)} async-done(((bf16[64,8192]{1,0:T(8,128)(2,1)}), bf16[128,8192]{1,0:T(8,128)(2,1)}) %all-gather.9.cloned.1.call-update) | async-done | bytes 2097168 | tf_op jit(solution)/shard_map/all_gather | solution.py:46
  45.4 16.9 %fusion.56 = bf16[16,8,16,128]{3,1,2,0:T(8,128)(2,1)S(1)} fusion(bf16[128,8192]{1,0:T(8,128)(2,1)} %all-gather.9.cloned.1.call-done, bf16[2048,8192]{1,0:T(8,128)(2,1)} %param.5), kind=kOutput, calls=%fused_computation.45 | convolution fusion | flops 4295229440 | bytes 36175872 | tf_op jit(solution)/shard_map/nm,km->nk/dot_general | solution.py:44
  62.3 0.1 copy.22
  62.4 1.2 copy.8
  63.7 0.2 reduce-scatter.2.cloned.1.call-start
  63.9 0.2 iota_compare_fusion.1
  64.1 0.1 bitcast_convert_fusion
  64.2 1.4 copy.16
  65.6 56.3 %all-gather.13.cloned.1.call-done = bf16[2048,16,1,128]{3,0,1,2:T(8,128)(2,1)} async-done(((bf16[128,16,1,128]{3,0,1,2:T(8,128)(2,1)}), bf16[2048,16,1,128]{3,0,1,2:T(8,128)(2,1)}) %all-gather.13.cloned.1.call-update) | async-done | bytes 8388624 | tf_op jit(solution)/shard_map/all_gather | solution.py:18
  121.9 12.3 %fusion.2 = (f32[16,128]{1,0:T(8,128)S(1)}, f32[16,128,2048]{2,1,0:T(8,128)}) fusion(pred[128,2048]{1,0:T(8,128)(4,1)S(1)} %iota_compare_fusion.1, bf16[2048,16,1,128]{3,0,1,2:T(8,128)(2,1)} %all-gather.13.cloned.1.call-done, bf16[128,16,1,128]{3,1,2,0:T(8,128)(2,1)S(1)} %get-tuple-element.4), kind=kOutput, calls=%fused_computation.8 | convolution fusion | flops 1086322688 | bytes 25960448 | tf_op jit(solution)/shard_map/rhd,shd->hrs/dot_general | solution.py:27
  134.2 8.0 %exponential_reduce_fusion = f32[16,128]{1,0:T(8,128)S(1)} fusion(f32[16,128,2048]{2,1,0:T(8,128)} %get-tuple-element.8, f32[16,128]{1,0:T(8,128)S(1)} %get-tuple-element.7, pred[128,2048]{1,0:T(8,128)(4,1)S(1)} %iota_compare_fusion.1), kind=kLoop, calls=%fused_computation.4 | loop fusion | flops 16775168 | bytes 17055744 | tf_op jit(solution)/shard_map/reduce_sum | solution.py:31
  142.3 58.7 %all-gather.15.cloned.1.call-done = bf16[2048,16,1,128]{0,3,1,2:T(8,128)(2,1)} async-done(((bf16[128,16,1,128]{0,3,1,2:T(8,128)(2,1)}), bf16[2048,16,1,128]{0,3,1,2:T(8,128)(2,1)}) %all-gather.15.cloned.1.call-update) | async-done | bytes 8388624 | tf_op jit(solution)/shard_map/all_gather | solution.py:19
  201.0 10.7 %multiply_reduce_fusion = (f32[128,16]{0,1:T(8,128)S(1)}, bf16[16,128,128]{1,2,0:T(8,128)(2,1)S(1)}) fusion(f32[128,16,128]{0,2,1:T(8,128)S(1)} %copy-done.2, bf16[2048,16,1,128]{0,3,1,2:T(8,128)(2,1)} %all-gather.15.cloned.1.call-done, f32[16,128,2048]{2,1,0:T(8,128)} %get-tuple-element.8, f32[16,128]{1,0:T(8,128)S(1)} %log_add_fusion, ...), kind=kOutput, calls=%fused_computation.46 | convolution fusion | flops 1091565568 | bytes 27017216 | tf_op jit(solution)/shard_map/hrs,shd->rhd/dot_general | solution.py:34
  211.7 15.3 %fusion.72 = f32[128,8192]{1,0:T(8,128)} fusion(bf16[128,2048]{0,1:T(8,128)(2,1)S(1)} %bitcast.84, bf16[2048,8192]{1,0:T(8,128)(2,1)} %param.5), kind=kOutput, calls=%fused_computation.66 | convolution fusion | flops 4294967296 | bytes 38273024 | tf_op jit(solution)/shard_map/dot_general | solution.py:39
  227.0 0.2 iota_compare_fusion
  227.2 19.9 %all_gather.27 = f32[2048,16]{0,1:T(8,128)S(1)} all-gather(f32[128,16]{0,1:T(8,128)S(1)} %get-tuple-element.9), channel_id=1, replica_groups=mesh['ctx'=16,'tp'=2] {'ctx'}, dimensions={0}, use_global_device_ids=true | all-gather | bytes 139264 | tf_op jit(solution)/shard_map/all_gather | solution.py:62
  247.1 18.9 %all_gather.25 = f32[2048,16]{0,1:T(8,128)S(1)} all-gather(f32[128,16]{0,1:T(8,128)S(1)} %bitcast.88), channel_id=1, replica_groups=mesh['ctx'=16,'tp'=2] {'ctx'}, dimensions={0}, use_global_device_ids=true | all-gather | bytes 139264 | tf_op jit(solution)/shard_map/all_gather | solution.py:61
  266.0 11.0 %all-gather.17.cloned.1.call-done = bf16[2048,16,1,128]{3,0,1,2:T(8,128)(2,1)} async-done(((bf16[128,16,1,128]{3,0,1,2:T(8,128)(2,1)}), bf16[2048,16,1,128]{3,0,1,2:T(8,128)(2,1)}) %all-gather.17.cloned.1.call-update) | async-done | bytes 8388624 | tf_op jit(solution)/shard_map/all_gather | solution.py:64
  277.0 11.8 %fusion.9 = f32[16,2048,128]{2,1,0:T(8,128)} fusion(bf16[2048,16,1,128]{3,0,1,2:T(8,128)(2,1)} %all-gather.17.cloned.1.call-done, bf16[128,16,1,128]{3,1,2,0:T(8,128)(2,1)S(1)} %get-tuple-element.6), kind=kOutput, calls=%fused_computation.13 | convolution fusion | flops 1073741824 | bytes 25690112 | tf_op jit(solution)/shard_map/nhd,rhd->hnr/dot_general | solution.py:72
  288.8 15.1 %fusion.43 = f32[128,16,1,128]{3,0,1,2:T(8,128)S(1)} fusion(bf16[2048,16,1,128]{3,0,1,2:T(8,128)(2,1)} %all-gather.13.cloned.1.call-done, f32[16,128,2048]{2,1,0:T(8,128)} %get-tuple-element.8, f32[16,128]{1,0:T(8,128)S(1)} %bitcast.89, f32[16,128]{1,0:T(8,128)S(1)} %log_add_fusion, pred[128,2048]{1,0:T(8,128)(4,1)S(1)} %iota_compare_fusion.1, ...), kind=kOutput, calls=%fused_computation.42 | convolution fusion | flops 2176843776 | bytes 35405824 | tf_op jit(solution)/shard_map/hrs,shd->rhd/dot_general | solution.py:56
  303.9 51.6 %all-gather.11.cloned.1.call-done = bf16[2048,16,128]{0,2,1:T(8,128)(2,1)} async-done(((bf16[128,16,128]{0,2,1:T(8,128)(2,1)}), bf16[2048,16,128]{0,2,1:T(8,128)(2,1)}) %all-gather.11.cloned.1.call-update) | async-done | bytes 8388624 | tf_op jit(solution)/shard_map/all_gather | solution.py:65
  355.5 14.0 %multiply_convert_fusion.10 = bf16[16,2048,128]{2,1,0:T(8,128)(2,1)S(1)} fusion(f32[16,2048,128]{2,1,0:T(8,128)} %fusion.9, f32[16,2048]{1,0:T(8,128)S(1)} %bitcast.87, f32[16,2048]{1,0:T(8,128)S(1)} %bitcast.85, pred[2048,128]{1,0:T(8,128)(4,1)S(1)} %iota_compare_fusion, bf16[2048,16,128]{0,2,1:T(8,128)(2,1)} %all-gather.11.cloned.1.call-done, ...), kind=kOutput, calls=%fused_computation.clone.clone.clone.clone.1 | convolution fusion | flops 1103101952 | bytes 34603008 | tf_op jit(solution)/shard_map/nhd,rhd->hnr/dot_general | solution.py:77
  369.4 6.2 %fusion.48 = f32[128,16,1,128]{3,0,1,2:T(8,128)S(1)} fusion(bf16[2048,16,1,128]{3,0,1,2:T(8,128)(2,1)} %all-gather.17.cloned.1.call-done, bf16[16,2048,128]{2,1,0:T(8,128)(2,1)S(1)} %multiply_convert_fusion.10), kind=kOutput, calls=%fused_computation.43 | convolution fusion | flops 1073741824 | bytes 17825792 | tf_op jit(solution)/shard_map/hnr,nhd->rhd/dot_general | solution.py:81
  375.7 13.6 %fusion.40 = f32[128,16,1,128]{3,0,1,2:T(8,128)S(1)} fusion(bf16[2048,16,128]{0,2,1:T(8,128)(2,1)} %all-gather.11.cloned.1.call-done, f32[16,2048,128]{2,1,0:T(8,128)} %fusion.9, f32[16,2048]{1,0:T(8,128)S(1)} %bitcast.86, pred[2048,128]{1,0:T(8,128)(4,1)S(1)} %iota_compare_fusion), kind=kOutput, calls=%fused_computation.41 | convolution fusion | flops 1090519040 | bytes 26607616 | tf_op jit(solution)/shard_map/hnr,nhd->rhd/dot_general | solution.py:82
  389.3 0.3 pad_maximum_fusion
  389.6 3.5 copy.11
  393.1 17.7 %reduce-scatter.2.cloned.1.call-done = f32[64,8192]{1,0:T(8,128)} async-done(((f32[128,8192]{1,0:T(8,128)}), f32[64,8192]{1,0:T(8,128)}) %reduce-scatter.2.cloned.1.call-update) | async-done | bytes 2097168 | tf_op jit(solution)/shard_map/reduce_scatter | solution.py:38
  (18 shorter events, 0.3 us)
Async XLA Ops:
  7.2 38.2 %all-gather.9.cloned.1.call-start = ((), (), s32[]{:S(2)}) async-start(), calls=%async_computation.2 | async-start | bytes 3145728 | tf_op jit(solution)/shard_map/all_gather | solution.py:46
  7.9 114.0 %all-gather.13.cloned.1.call-start = ((), (), s32[]{:S(2)}) async-start(), calls=%async_computation.4 | async-start | bytes 8912896 | tf_op jit(solution)/shard_map/all_gather | solution.py:18
  10.6 190.4 %all-gather.15.cloned.1.call-start = ((), (), s32[]{:S(2)}) async-start(), calls=%async_computation.5 | async-start | bytes 8912896 | tf_op jit(solution)/shard_map/all_gather | solution.py:19
  11.9 265.1 %all-gather.17.cloned.1.call-start = ((), (), s32[]{:S(2)}) async-start(), calls=%async_computation.6 | async-start | bytes 8912896 | tf_op jit(solution)/shard_map/all_gather | solution.py:64
  12.9 342.6 %all-gather.11.cloned.1.call-start = ((), (), s32[]{:S(2)}) async-start(), calls=%async_computation.3 | async-start | bytes 8912896 | tf_op jit(solution)/shard_map/all_gather | solution.py:65
  63.7 347.1 %reduce-scatter.2.cloned.1.call-start = ((), (), s32[]{:S(2)}) async-start(), calls=%async_computation.1 | async-start | bytes 6291456 | tf_op jit(solution)/shard_map/reduce_scatter | solution.py:38
  65.6 135.3 %copy-start.2 = (f32[128,16,128]{0,2,1:T(8,128)S(1)}, f32[128,16,128]{0,2,1:T(8,128)}, u32[]{:S(2)}) copy-start(f32[128,16,128]{0,2,1:T(8,128)} %copy.16) | copy-start | bytes 3145732
  266.0 22.8 %copy-start.1 = (bf16[128,16,128]{0,2,1:T(8,128)(2,1)S(1)}, bf16[128,16,128]{0,2,1:T(8,128)(2,1)}, u32[]{:S(2)}) copy-start(bf16[128,16,128]{0,2,1:T(8,128)(2,1)} %copy.8) | copy-start | bytes 1572868
  288.8 66.7 %copy-start = (bf16[128,16,1,128]{0,3,1,2:T(8,128)(2,1)S(1)}, bf16[128,16,1,128]{0,3,1,2:T(8,128)(2,1)}, u32[]{:S(2)}) copy-start(bf16[128,16,1,128]{0,3,1,2:T(8,128)(2,1)} %copy.21) | copy-start | bytes 1572868
Sparse Core Ops, SparseCore 0:
  9.5 35.8 all-gather.8
  47.5 74.3 all-gather.12
  124.6 76.2 all-gather.14
  203.0 73.9 all-gather.16
  279.0 76.4 all-gather.10
  358.2 52.5 reduce-scatter.1
where the time goes:
time: 418 us
  waiting for transfers between devices  228 us (55%)
  matrix products  116 us (28%)
  blocking collectives  38.8 us (9%)
  between operations  14.2 us (3%)
  local copies, waits for them, and re-layouts  11 us (3%)
  other arithmetic  8.84 us (2%)
    all_gather x1, waiting for transfers between devices, per_device(): lax.all_gather(values_local, 'ctx', axis=0, tiled=True)  58.7 us
    all_gather x1, waiting for transfers between devices, per_device(): lax.all_gather(keys_local, 'ctx', axis=0, tiled=True)  56.3 us
    all_gather x1, waiting for transfers between devices, per_device(): piece_g = lax.all_gather(grad_att, 'ctx', axis=0, tiled=True)  51.6 us
    all_gather x1, waiting for transfers between devices, per_device(): lax.all_gather(grad_out, 'tp', axis=0, tiled=True)  32.4 us
    all_gather x1, blocking collectives, per_device(): lax.all_gather(row_delta, 'ctx', axis=0, tiled=True)  19.9 us
    all_gather x1, blocking collectives, per_device(): lax.all_gather(lse_rows, 'ctx', axis=0, tiled=True)  18.9 us
    reduce_scatter x1, waiting for transfers between devices, per_device(): lax.psum_scatter(jnp.dot(attended_flat, attn_out, preferred_element_type=...  17.7 us
    dot_general x1, matrix products, per_device(): jnp.einsum('nm,km->nk', lax.all_gather(grad_out, 'tp', axis=0, tiled=True...  16.9 us
  transfers between devices with their start and end apart: 6, of which 6 were waited for; matrix products, arithmetic and copies ran while one was open for 33% of the time, Pallas kernels for 0%

commit v1 on v0

--- a/solution.py
+++ b/solution.py
@@ -1,14 +1,225 @@
+import functools
 import math
 
 import jax
 import jax.numpy as jnp
 from jax import lax
+from jax.experimental import pallas as pl
+from jax.experimental.pallas import tpu as pltpu
 from jax.sharding import PartitionSpec as P
 
 HD = 128
-
-
-def per_device(qkv, grad_out, attn_out):
+LOG2E = math.log2(math.e)
+VMEM_LIMIT = 48 * 1024 * 1024
+
+
+def dot_nt(a, b):
+    return lax.dot_general(a, b, (((1,), (1,)), ((), ())), preferred_element_type=jnp.float32)
+
+
+def dot_nn(a, b):
+    return lax.dot_general(a, b, (((1,), (0,)), ((), ())), preferred_element_type=jnp.float32)
+
+
+def rows_of(ref, start, count, *which):
+    part = ref[(pl.ds(start, count), *which)]
+    return part.reshape(count * part.shape[1], part.shape[2])
+
+
+def forward_kernel(step, qkv_ref, att_ref, lse_ref, v_t, s_buf):
+    chunks, _, unit, _ = qkv_ref.shape
+    per = step // unit
+    blocks = chunks // per
+    scale = LOG2E / math.sqrt(HD)
+    for b in range(blocks):
+        v_t[b] = rows_of(qkv_ref, b * per, per, 2).T
+
+    def query_block(i, _):
+        q = rows_of(qkv_ref, i * per, per, 0)
+
+        def scores(j, top):
+            s = dot_nt(rows_of(qkv_ref, j * per, per, 1), q)
+            s_buf[j] = s
+            return jnp.maximum(top, jnp.max(s, axis=0, keepdims=True))
+
+        top = lax.fori_loop(0, i, scores, jnp.full((1, step), -jnp.inf, jnp.float32))
+        s = dot_nt(rows_of(qkv_ref, i * per, per, 1), q)
+        key = lax.broadcasted_iota(jnp.int32, s.shape, 0)
+        query = lax.broadcasted_iota(jnp.int32, s.shape, 1)
+        s = jnp.where(key <= query, s, -jnp.inf)
+        s_buf[i] = s
+        top = jnp.maximum(top, jnp.max(s, axis=0, keepdims=True))
+
+        def exps(j, total):
+            p = jnp.exp2((s_buf[j] - top) * scale)
+            s_buf[j] = p
+            return total + jnp.sum(p, axis=0, keepdims=True)
+
+        total = lax.fori_loop(0, i + 1, exps, jnp.zeros((1, step), jnp.float32))
+        inverse = 1.0 / total
+
+        def mix(j, acc):
+            return acc + dot_nn(v_t[j], (s_buf[j] * inverse).astype(jnp.bfloat16))
+
+        acc = lax.fori_loop(0, i + 1, mix, jnp.zeros((HD, step), jnp.float32))
+        att_ref[pl.ds(i * per, per)] = acc.T.astype(jnp.bfloat16).reshape(per, unit, HD)
+        lse_ref[i] = top * scale + jnp.log2(total)
+        return 0
+
+    lax.fori_loop(0, blocks, query_block, 0)
+
+
+def backward_kernel(step, qkv_ref, g_ref, att_ref, lse_ref, out_ref, k_t, dq_t, delta):
+    chunks, _, unit, _ = qkv_ref.shape
+    per = step // unit
+    blocks = chunks // per
+    factor = 1.0 / math.sqrt(HD)
+    for b in range(blocks):
+        k_t[b] = rows_of(qkv_ref, b * per, per, 1).T
+        prod = rows_of(g_ref, b * per, per).astype(jnp.float32)
+        prod = prod * rows_of(att_ref, b * per, per).astype(jnp.float32)
+        delta[b] = jnp.sum(prod.T, axis=0, keepdims=True)
+
+    def key_block(j, _):
+        k = rows_of(qkv_ref, j * per, per, 1)
+        v = rows_of(qkv_ref, j * per, per, 2)
+        kt = k_t[j]
+
+        def pair(i, diagonal):
+            q = rows_of(qkv_ref, i * per, per, 0)
+            g = rows_of(g_ref, i * per, per)
+            w = jnp.exp2(dot_nt(k, q) * (factor * LOG2E) - lse_ref[i])
+            if diagonal:
+                key = lax.broadcasted_iota(jnp.int32, w.shape, 0)
+                query = lax.broadcasted_iota(jnp.int32, w.shape, 1)
+                w = jnp.where(key <= query, w, 0.0)
+            ds = (w * (dot_nt(v, g) - delta[i]) * factor).astype(jnp.bfloat16)
+            dv = dot_nn(w.astype(jnp.bfloat16), g)
+            dk = dot_nn(ds, q)
+            return dk, dv, dot_nn(kt, ds)
+
+        dk, dv, part = pair(j, True)
+
+        @pl.when(j == 0)
+        def _():
+            dq_t[j] = part
+
+        @pl.when(j > 0)
+        def _():
+            dq_t[j] = dq_t[j] + part
+
+        def later(i, carry):
+            dk, dv, part = pair(i, False)
+
+            @pl.when(j == 0)
+            def _():
+                dq_t[i] = part
+
+            @pl.when(j > 0)
+            def _():
+                dq_t[i] = dq_t[i] + part
+
+            return carry[0] + dk, carry[1] + dv
+
+        dk, dv = lax.fori_loop(j + 1, blocks, later, (dk, dv))
+        spot = pl.ds(j * per, per)
+        out_ref[spot, 1] = dk.astype(jnp.bfloat16).reshape(per, unit, HD)
+        out_ref[spot, 2] = dv.astype(jnp.bfloat16).reshape(per, unit, HD)
+        return 0
+
+    lax.fori_loop(0, blocks, key_block, 0)
+    for b in range(blocks):
+        out_ref[pl.ds(b * per, per), 0] = dq_t[b].T.astype(jnp.bfloat16).reshape(per, unit, HD)
+
+
+def in_vmem(count):
+    return [pl.BlockSpec(memory_space=pltpu.VMEM)] * count
+
+
+def attend(qkv, step):
+    chunks, _, unit, _ = qkv.shape
+    length = chunks * unit
+    blocks = length // step
+    area = length * length // 2
+    return pl.pallas_call(
+        functools.partial(forward_kernel, step),
+        out_shape=(
+            jax.ShapeDtypeStruct((chunks, unit, HD), jnp.bfloat16),
+            jax.ShapeDtypeStruct((blocks, 1, step), jnp.float32),
+        ),
+        in_specs=in_vmem(1),
+        out_specs=tuple(in_vmem(2)),
+        scratch_shapes=[
+            pltpu.VMEM((blocks, HD, step), jnp.bfloat16),
+            pltpu.VMEM((blocks, step, step), jnp.float32),
+        ],
+        compiler_params=pltpu.CompilerParams(vmem_limit_bytes=VMEM_LIMIT),
+        cost_estimate=pl.CostEstimate(
+            flops=4 * area * HD, transcendentals=area, bytes_accessed=8 * length * HD
+        ),
+        name="attend",
+    )(qkv)
+
+
+def attend_grad(qkv, g, att, lse, step):
+    chunks, _, unit, _ = qkv.shape
+    length = chunks * unit
+    blocks = length // step
+    area = length * length // 2
+    return pl.pallas_call(
+        functools.partial(backward_kernel, step),
+        out_shape=jax.ShapeDtypeStruct((chunks, 3, unit, HD), jnp.bfloat16),
+        in_specs=in_vmem(4),
+        out_specs=in_vmem(1)[0],
+        scratch_shapes=[
+            pltpu.VMEM((blocks, HD, step), jnp.bfloat16),
+            pltpu.VMEM((blocks, HD, step), jnp.float32),
+            pltpu.VMEM((blocks, 1, step), jnp.float32),
+        ],
+        compiler_params=pltpu.CompilerParams(vmem_limit_bytes=VMEM_LIMIT),
+        cost_estimate=pl.CostEstimate(
+            flops=10 * area * HD, transcendentals=area, bytes_accessed=16 * length * HD
+        ),
+        name="attend_grad",
+    )(qkv, g, att, lse)
+
+
+def by_head(qkv, grad_out, attn_out):
+    rows, heads = qkv.shape[:2]
+    half = grad_out.shape[0]
+    width = attn_out.shape[1]
+    step = 512 if (rows * heads) % 512 == 0 else rows
+    swap = [(0, 1), (1, 0)]
+    turn = lax.axis_index("tp")
+    weights = attn_out.reshape(heads, HD, width)
+
+    def spread(x):
+        return lax.all_to_all(x, "ctx", 0, 0, tiled=True)
+
+    other_out = lax.ppermute(grad_out, "tp", swap)
+    mine = spread(jnp.transpose(qkv, (1, 2, 0, 3)))
+
+    def back(x):
+        y = jnp.einsum("nm,hdm->hnd", x, weights, preferred_element_type=jnp.float32)
+        return y.astype(jnp.bfloat16)
+
+    g_own, g_other = back(grad_out), back(other_out)
+    first = jnp.where(turn == 0, g_own, g_other)
+    second = jnp.where(turn == 0, g_other, g_own)
+    g = spread(jnp.concatenate([first, second], axis=1))
+
+    att, lse = attend(mine, step)
+    local = spread(att)
+    mixed = jnp.einsum("hrd,hdm->rm", local, weights, preferred_element_type=jnp.float32)
+    sent = lax.dynamic_slice_in_dim(mixed, (1 - turn) * half, half, 0).astype(jnp.bfloat16)
+    kept = lax.dynamic_slice_in_dim(mixed, turn * half, half, 0)
+    mixed_out = kept + lax.ppermute(sent, "tp", swap).astype(jnp.float32)
+
+    grads = spread(attend_grad(mine, g, att, lse, step))
+    return mixed_out, jnp.transpose(grads, (2, 0, 1, 3)).astype(jnp.float32)
+
+
+def by_rows(qkv, grad_out, attn_out):
     row_count, heads_local = (qkv.shape[0], qkv.shape[1])
     factor = 1.0 / math.sqrt(HD)
     queries = qkv[:, :, 0]
@@ -90,6 +301,12 @@
 
 
 def solution(mesh):
+    ctx, tp = mesh.shape["ctx"], mesh.shape["tp"]
+
+    def per_device(qkv, grad_out, attn_out):
+        path = by_head if qkv.shape[1] == ctx and tp == 2 else by_rows
+        return path(qkv, grad_out, attn_out)
+
     in_specs = (P("ctx", "tp", None, None), P(("ctx", "tp"), None), P("tp", None))
     out_specs = (P(("ctx", "tp"), None), P("ctx", "tp", None, None))
     return jax.shard_map(

time: 418 us -> 145 us (0.35)
  waiting for transfers between devices: 228 us -> 39.6 us
  matrix products: 116 us -> 45.7 us
  blocking collectives: 38.8 us -> 0 us
  starting transfers between devices: 0.42 us -> 24.6 us
  Pallas kernels: 0 us -> 20.9 us
  between operations: 14.2 us -> 0.73 us
  other arithmetic: 8.84 us -> 4.6 us
    all_gather x5 -> x0, waiting for transfers between devices: 210 us -> none  [the longest x1 58.7 us: per_device(): lax.all_gather(values_local, 'ctx', axis=0, tiled=True)]
    dot_general x9 -> x3, matrix products: 116 us -> 45.7 us  [the longest x2 32.6 us: back(): jnp.einsum('nm,hdm->hnd', x, weights, preferred_element_type=jnp.float32)]
    all_gather x2 -> x0, blocking collectives: 38.8 us -> none  [the longest x1 19.9 us: per_device(): lax.all_gather(row_delta, 'ctx', axis=0, tiled=True)]
    ppermute x0 -> x2, waiting for transfers between devices: none -> 32 us  [the longest x1 24.1 us: by_head(): mixed_out = kept + lax.ppermute(sent, 'tp', swap).astype(jnp.float32)]
    all_to_all x0 -> x4, starting transfers between devices: none -> 21.5 us  [spread(): return lax.all_to_all(x, 'ctx', 0, 0, tiled=True)]
    pallas_call x0 -> x2, Pallas kernels: none -> 20.9 us  [the longest x1 12.2 us: attend_grad(): pl.pallas_call(functools.partial(backward_kernel, step), out_shape=jax.Sh...]
    reduce_scatter x1 -> x0, waiting for transfers between devices: 17.7 us -> none  [per_device(): lax.psum_scatter(jnp.dot(attended_flat, attn_out, preferred_element_type=...]
    reduce_sum x1 -> x0, other arithmetic: 8.05 us -> none  [per_device(): jnp.sum(jnp.exp(scores - row_max), axis=2, keepdims=True)]
  transfers between devices with their start and end apart: 6 -> 6, of which waited for: 6 -> 4; matrix products, arithmetic and copies ran while one was open for 33% -> 35% of each run, Pallas kernels for 0% -> 14%
where the time goes in v1:
time: 145 us
  matrix products  45.7 us (32%)
  waiting for transfers between devices  39.6 us (27%)
  starting transfers between devices  24.6 us (17%)
  Pallas kernels  20.9 us (14%)
  local copies, waits for them, and re-layouts  8.59 us (6%)
  other arithmetic  4.6 us (3%)
    dot_general x2, matrix products, back(): jnp.einsum('nm,hdm->hnd', x, weights, preferred_element_type=jnp.float32)  32.6 us
    ppermute x1, waiting for transfers between devices, by_head(): mixed_out = kept + lax.ppermute(sent, 'tp', swap).astype(jnp.float32)  24.1 us
    all_to_all x4, starting transfers between devices, spread(): return lax.all_to_all(x, 'ctx', 0, 0, tiled=True)  21.5 us
    dot_general x1, matrix products, by_head(): jnp.einsum('hrd,hdm->rm', local, weights, preferred_element_type=jnp.floa...  13.1 us
    pallas_call x1, Pallas kernels, attend_grad(): pl.pallas_call(functools.partial(backward_kernel, step), out_shape=jax.Sh...  12.2 us
    pallas_call x1, Pallas kernels, attend(): pl.pallas_call(functools.partial(forward_kernel, step), out_shape=(jax.Sh...  8.71 us
    unnamed x6, local copies, waits for them, and re-layouts  8.48 us
    ppermute x1, waiting for transfers between devices, by_head(): other_out = lax.ppermute(grad_out, 'tp', swap)  7.88 us
  transfers between devices with their start and end apart: 6, of which 4 were waited for; matrix products, arithmetic and copies ran while one was open for 35% of the time, Pallas kernels for 14%

profile of v1, /device:TPU:0, one launch (start us, length us, event | category | flops | bytes accessed | tf_op | source)
XLA Modules:
  0.0 144.7 jit_solution(9638790416476654192)
XLA Ops:
  0.6 0.0 copy-start.1
  0.6 3.0 %copy.8 = bf16[128,16,3,128]{3,0,2,1:T(8,128)(2,1)} copy(bf16[128,16,3,128]{3,1,2,0:T(8,128)(2,1)} %param.3) | data formatting | bytes 3145728 | tf_op args[0]
  3.7 7.4 %all-to-all-start = ((bf16[16,3,128,128]{3,2,1,0:T(8,128)(2,1)}), bf16[16,3,128,128]{3,2,1,0:T(8,128)(2,1)S(1)}, u32[]{:S(2)}, u32[]{:S(2)}) async-start(bf16[16,3,128,128]{3,2,1,0:T(8,128)(2,1)} %bitcast.23), calls=%async_computation | async-start | bytes 3145728 | tf_op jit(solution)/shard_map/all_to_all | solution.py:197
  11.1 0.0 copy-done.1
  11.1 1.6 %collective-permute-start.1 = (bf16[64,8192]{1,0:T(8,128)(2,1)S(1)}, bf16[64,8192]{1,0:T(8,128)(2,1)}, u32[]{:S(2)}, u32[]{:S(2)}) collective-permute-start(bf16[64,8192]{1,0:T(8,128)(2,1)S(1)} %copy-done.1), channel_id=1, source_target_pairs={{0,1},{1,0},{2,3},{3,2},{4,5},{5,4},{6,7},{7,6},{8,9},{9,8},{10,11... | collective-permute-start | bytes 3145736 | tf_op jit(solution)/shard_map/ppermute | solution.py:199
  12.7 16.2 %convolution_convert_fusion.1 = bf16[16,128,64]{1,2,0:T(8,128)(2,1)S(1)} fusion(bf16[16,128,8192]{2,1,0:T(8,128)(2,1)} %bitcast.24, bf16[64,8192]{1,0:T(8,128)(2,1)S(1)} %copy-done.1), kind=kOutput, calls=%fused_computation.6 | convolution fusion | flops 2147614720 | bytes 34865152 | tf_op jit(solution)/shard_map/nm,hdm->hnd/dot_general | solution.py:203
  28.9 7.9 %collective-permute-done.1 = bf16[64,8192]{1,0:T(8,128)(2,1)} collective-permute-done((bf16[64,8192]{1,0:T(8,128)(2,1)S(1)}, bf16[64,8192]{1,0:T(8,128)(2,1)}, u32[]{:S(2)}, u32[]{:S(2)}) %collective-permute-start.1) | collective-permute-done | bytes 1048608 | tf_op jit(solution)/shard_map/ppermute | solution.py:199
  36.8 16.4 %select_bitcast_fusion.1 = (bf16[16,64,128]{2,1,0:T(8,128)(2,1)S(1)}, bf16[16,64,128]{2,1,0:T(8,128)(2,1)S(1)}) fusion(bf16[16,128,64]{1,2,0:T(8,128)(2,1)S(1)} %convolution_convert_fusion.1, pred[]{:T(512)S(6)} %eq.4, bf16[16,128,8192]{2,1,0:T(8,128)(2,1)} %bitcast.25, bf16[64,8192]{1,0:T(8,128)(2,1)} %collective-permute-done.1), kind=kOutput, calls=%fused_computation.11 | convolution fusion | flops 2147876864 | bytes 35389440 | tf_op jit(solution)/shard_map/nm,hdm->hnd/dot_general | solution.py:203
  53.2 0.8 pad_maximum_fusion
  54.0 0.0 all-to-all-done.qkv_ref
  54.0 5.7 %all-to-all-start.2 = ((bf16[16,128,128]{2,1,0:T(8,128)(2,1)}), bf16[16,128,128]{2,1,0:T(8,128)(2,1)S(1)}, u32[]{:S(2)}, u32[]{:S(2)}) async-start(bf16[16,128,128]{2,1,0:T(8,128)(2,1)} %pad_maximum_fusion), calls=%async_computation.2 | async-start | bytes 1048576 | tf_op jit(solution)/shard_map/all_to_all | solution.py:197
  59.7 8.7 %attend.1 = (bf16[16,128,128]{2,1,0:T(8,128)(2,1)}, f32[4,1,512]{2,1,0:T(1,128)S(1)}) custom-call(bf16[16,3,128,128]{3,2,1,0:T(8,128)(2,1)S(1)} %all-to-all-done.qkv_ref), custom_call_target="tpu_custom_call" | custom-call | flops 1073741824 | bytes 2097152 | tf_op jit(solution)/shard_map/attend/pallas_call | solution.py:144
  68.4 5.6 %all-to-all-done.2.g_ref = bf16[16,128,128]{2,1,0:T(8,128)(2,1)S(1)} async-done(((bf16[16,128,128]{2,1,0:T(8,128)(2,1)}), bf16[16,128,128]{2,1,0:T(8,128)(2,1)S(1)}, u32[]{:S(2)}, u32[]{:S(2)}) %all-to-all-start.2) | async-done | bytes 524320 | tf_op jit(solution)/shard_map/all_to_all | solution.py:197
  74.0 4.2 %all-to-all-start.1 = ((bf16[16,128,128]{2,1,0:T(8,128)(2,1)}), bf16[16,128,128]{2,1,0:T(8,128)(2,1)S(1)}, u32[]{:S(2)}, u32[]{:S(2)}) async-start(bf16[16,128,128]{2,1,0:T(8,128)(2,1)} %get-tuple-element.4.att_ref), calls=%async_computation.1 | async-start | bytes 1048576 | tf_op jit(solution)/shard_map/all_to_all | solution.py:197
  78.2 12.2 %attend_grad.1 = bf16[16,3,128,128]{3,2,1,0:T(8,128)(2,1)} custom-call(bf16[16,3,128,128]{3,2,1,0:T(8,128)(2,1)S(1)} %all-to-all-done.qkv_ref, bf16[16,128,128]{2,1,0:T(8,128)(2,1)S(1)} %all-to-all-done.2.g_ref, bf16[16,128,128]{2,1,0:T(8,128)(2,1)} %get-tuple-element.4.att_ref, f32[4,1,512]{2,1,0:T(1,128)S(1)} %get-tuple-element.5.lse_ref), custom_call_target="tpu_custom_call" | custom-call | flops 2684354560 | bytes 4194304 | tf_op jit(solution)/shard_map/attend_grad/pallas_call | solution.py:169
  90.3 2.1 %all-to-all-done.1 = bf16[16,128,128]{2,1,0:T(8,128)(2,1)S(1)} async-done(((bf16[16,128,128]{2,1,0:T(8,128)(2,1)}), bf16[16,128,128]{2,1,0:T(8,128)(2,1)S(1)}, u32[]{:S(2)}, u32[]{:S(2)}) %all-to-all-start.1) | async-done | bytes 524320 | tf_op jit(solution)/shard_map/all_to_all | solution.py:197
  92.4 4.2 %all-to-all-start.3 = ((bf16[16,3,128,128]{3,2,1,0:T(8,128)(2,1)}), bf16[16,3,128,128]{3,2,1,0:T(8,128)(2,1)S(1)}, u32[]{:S(2)}, u32[]{:S(2)}) async-start(bf16[16,3,128,128]{3,2,1,0:T(8,128)(2,1)} %attend_grad.1), calls=%async_computation.3 | async-start | bytes 3145728 | tf_op jit(solution)/shard_map/all_to_all | solution.py:197
  96.6 13.1 %convolution_bitcast_fusion = f32[128,8192]{1,0:T(8,128)S(1)} fusion(bf16[16,128,128]{2,1,0:T(8,128)(2,1)S(1)} %all-to-all-done.1, bf16[16,128,8192]{2,1,0:T(8,128)(2,1)} %bitcast.26), kind=kOutput, calls=%fused_computation | convolution fusion | flops 4294967296 | bytes 38273024 | tf_op jit(solution)/shard_map/hrd,hdm->rm/dot_general | solution.py:213
  109.7 0.0 copy-start
  109.7 1.9 %copy-done = f32[128,8192]{1,0:T(8,128)} copy-done((f32[128,8192]{1,0:T(8,128)}, f32[128,8192]{1,0:T(8,128)S(1)}, u32[]{:S(2)}) %copy-start) | copy-done | bytes 4194328
  111.7 0.1 dynamic-slice_convert_fusion
  111.8 1.6 %collective-permute-start = (bf16[64,8192]{1,0:T(8,128)(2,1)S(1)}, bf16[64,8192]{1,0:T(8,128)(2,1)}, u32[]{:S(2)}, u32[]{:S(2)}) collective-permute-start(bf16[64,8192]{1,0:T(8,128)(2,1)S(1)} %dynamic-slice_convert_fusion), channel_id=1, source_target_pairs={{0,1},{1,0},{2,3},{3,2},{4,5},{5,4},{6,7},{7,6},{8,9},{9,8},{10,11... | collective-permute-start | bytes 3145736 | tf_op jit(solution)/shard_map/ppermute | solution.py:216
  113.3 24.1 %collective-permute-done = bf16[64,8192]{1,0:T(8,128)(2,1)} collective-permute-done((bf16[64,8192]{1,0:T(8,128)(2,1)S(1)}, bf16[64,8192]{1,0:T(8,128)(2,1)}, u32[]{:S(2)}, u32[]{:S(2)}) %collective-permute-start) | collective-permute-done | bytes 1048608 | tf_op jit(solution)/shard_map/ppermute | solution.py:216
  137.4 3.4 %convert_add_fusion = f32[64,8192]{1,0:T(8,128)} fusion(bf16[64,8192]{1,0:T(8,128)(2,1)} %collective-permute-done, f32[128,8192]{1,0:T(8,128)} %copy-done, s32[]{:T(128)S(6)} %select_n.24), kind=kLoop, calls=%fused_computation.2 | loop fusion | flops 1048576 | bytes 5242884 | tf_op jit(solution)/shard_map/add | solution.py:216
  140.8 0.0 all-to-all-done.3
  140.8 0.4 convert_bitcast_fusion
  141.2 3.5 %copy.6 = f32[128,16,3,128]{3,1,2,0:T(8,128)} copy(f32[128,16,3,128]{3,0,2,1:T(8,128)S(1)} %convert_bitcast_fusion) | data formatting | bytes 6291456
Async XLA Ops:
  0.6 10.5 %copy-start.1 = (bf16[64,8192]{1,0:T(8,128)(2,1)S(1)}, bf16[64,8192]{1,0:T(8,128)(2,1)}, u32[]{:S(2)}) copy-start(bf16[64,8192]{1,0:T(8,128)(2,1)} %param.4) | copy-start | bytes 3145732
  3.7 50.3 %all-to-all-start = ((bf16[16,3,128,128]{3,2,1,0:T(8,128)(2,1)}), bf16[16,3,128,128]{3,2,1,0:T(8,128)(2,1)S(1)}, u32[]{:S(2)}, u32[]{:S(2)}) async-start(bf16[16,3,128,128]{3,2,1,0:T(8,128)(2,1)} %bitcast.23), calls=%async_computation | async-start | bytes 3145728 | tf_op jit(solution)/shard_map/all_to_all | solution.py:197
  11.1 25.6 %collective-permute-start.1 = (bf16[64,8192]{1,0:T(8,128)(2,1)S(1)}, bf16[64,8192]{1,0:T(8,128)(2,1)}, u32[]{:S(2)}, u32[]{:S(2)}) collective-permute-start(bf16[64,8192]{1,0:T(8,128)(2,1)S(1)} %copy-done.1), channel_id=1, source_target_pairs={{0,1},{1,0},{2,3},{3,2},{4,5},{5,4},{6,7},{7,6},{8,9},{9,8},{10,11... | collective-permute-start | bytes 3145736 | tf_op jit(solution)/shard_map/ppermute | solution.py:199
  54.0 20.0 %all-to-all-start.2 = ((bf16[16,128,128]{2,1,0:T(8,128)(2,1)}), bf16[16,128,128]{2,1,0:T(8,128)(2,1)S(1)}, u32[]{:S(2)}, u32[]{:S(2)}) async-start(bf16[16,128,128]{2,1,0:T(8,128)(2,1)} %pad_maximum_fusion), calls=%async_computation.2 | async-start | bytes 1048576 | tf_op jit(solution)/shard_map/all_to_all | solution.py:197
  74.0 18.4 %all-to-all-start.1 = ((bf16[16,128,128]{2,1,0:T(8,128)(2,1)}), bf16[16,128,128]{2,1,0:T(8,128)(2,1)S(1)}, u32[]{:S(2)}, u32[]{:S(2)}) async-start(bf16[16,128,128]{2,1,0:T(8,128)(2,1)} %get-tuple-element.4.att_ref), calls=%async_computation.1 | async-start | bytes 1048576 | tf_op jit(solution)/shard_map/all_to_all | solution.py:197
  92.4 48.4 %all-to-all-start.3 = ((bf16[16,3,128,128]{3,2,1,0:T(8,128)(2,1)}), bf16[16,3,128,128]{3,2,1,0:T(8,128)(2,1)S(1)}, u32[]{:S(2)}, u32[]{:S(2)}) async-start(bf16[16,3,128,128]{3,2,1,0:T(8,128)(2,1)} %attend_grad.1), calls=%async_computation.3 | async-start | bytes 3145728 | tf_op jit(solution)/shard_map/all_to_all | solution.py:197
  109.7 1.9 %copy-start = (f32[128,8192]{1,0:T(8,128)}, f32[128,8192]{1,0:T(8,128)S(1)}, u32[]{:S(2)}) copy-start(f32[128,8192]{1,0:T(8,128)S(1)} %convolution_bitcast_fusion) | copy-start | bytes 12582916
  111.8 25.6 %collective-permute-start = (bf16[64,8192]{1,0:T(8,128)(2,1)S(1)}, bf16[64,8192]{1,0:T(8,128)(2,1)}, u32[]{:S(2)}, u32[]{:S(2)}) collective-permute-start(bf16[64,8192]{1,0:T(8,128)(2,1)S(1)} %dynamic-slice_convert_fusion), channel_id=1, source_target_pairs={{0,1},{1,0},{2,3},{3,2},{4,5},{5,4},{6,7},{7,6},{8,9},{9,8},{10,11... | collective-permute-start | bytes 3145736 | tf_op jit(solution)/shard_map/ppermute | solution.py:216

commit v2 on v1

--- a/solution.py
+++ b/solution.py
@@ -8,8 +8,10 @@
 from jax.experimental.pallas import tpu as pltpu
 from jax.sharding import PartitionSpec as P
 
+
 HD = 128
 LOG2E = math.log2(math.e)
+MIX_PARTS = 2
 VMEM_LIMIT = 48 * 1024 * 1024
 
 
@@ -196,26 +198,35 @@
     def spread(x):
         return lax.all_to_all(x, "ctx", 0, 0, tiled=True)
 
-    other_out = lax.ppermute(grad_out, "tp", swap)
-    mine = spread(jnp.transpose(qkv, (1, 2, 0, 3)))
-
     def back(x):
         y = jnp.einsum("nm,hdm->hnd", x, weights, preferred_element_type=jnp.float32)
         return y.astype(jnp.bfloat16)
 
+    other_out = lax.ppermute(grad_out, "tp", swap)
+    mine = spread(jnp.transpose(qkv, (1, 2, 0, 3)))
     g_own, g_other = back(grad_out), back(other_out)
     first = jnp.where(turn == 0, g_own, g_other)
     second = jnp.where(turn == 0, g_other, g_own)
-    g = spread(jnp.concatenate([first, second], axis=1))
-
+    g_all = jnp.concatenate([first, second], axis=1)
+    g = spread(g_all)
     att, lse = attend(mine, step)
     local = spread(att)
-    mixed = jnp.einsum("hrd,hdm->rm", local, weights, preferred_element_type=jnp.float32)
-    sent = lax.dynamic_slice_in_dim(mixed, (1 - turn) * half, half, 0).astype(jnp.bfloat16)
-    kept = lax.dynamic_slice_in_dim(mixed, turn * half, half, 0)
-    mixed_out = kept + lax.ppermute(sent, "tp", swap).astype(jnp.float32)
-
-    grads = spread(attend_grad(mine, g, att, lse, step))
+    grads = attend_grad(mine, g, att, lse, step)
+    grads = spread(grads)
+    pieces = []
+    part = width // MIX_PARTS
+    for c in range(MIX_PARTS):
+        mixed = jnp.einsum(
+            "hrd,hdm->rm",
+            local,
+            weights[:, :, c * part : (c + 1) * part],
+            preferred_element_type=jnp.float32,
+        )
+        sent = lax.dynamic_slice_in_dim(mixed, (1 - turn) * half, half, 0)
+        kept = lax.dynamic_slice_in_dim(mixed, turn * half, half, 0)
+        got = lax.ppermute(sent.astype(jnp.bfloat16), "tp", swap)
+        pieces.append(kept + got.astype(jnp.float32))
+    mixed_out = jnp.concatenate(pieces, axis=1)
     return mixed_out, jnp.transpose(grads, (2, 0, 1, 3)).astype(jnp.float32)
 
 
@@ -302,13 +313,18 @@
 
 def solution(mesh):
     ctx, tp = mesh.shape["ctx"], mesh.shape["tp"]
-
-    def per_device(qkv, grad_out, attn_out):
-        path = by_head if qkv.shape[1] == ctx and tp == 2 else by_rows
-        return path(qkv, grad_out, attn_out)
-
     in_specs = (P("ctx", "tp", None, None), P(("ctx", "tp"), None), P("tp", None))
     out_specs = (P(("ctx", "tp"), None), P("ctx", "tp", None, None))
-    return jax.shard_map(
-        per_device, mesh=mesh, in_specs=in_specs, out_specs=out_specs, check_vma=False
-    )
+
+    def whole(qkv, grad_out, attn_out):
+        split = qkv.shape[1] == ctx * tp and tp == 2
+        step = jax.shard_map(
+            by_head if split else by_rows,
+            mesh=mesh,
+            in_specs=in_specs,
+            out_specs=out_specs,
+            check_vma=False,
+        )
+        return step(qkv, grad_out, attn_out)
+
+    return whole

time: 145 us -> 130 us (0.90)
  waiting for transfers between devices: 39.6 us -> 23.7 us
  starting transfers between devices: 24.6 us -> 26.9 us
  local copies, waits for them, and re-layouts: 8.59 us -> 6.58 us
  other arithmetic: 4.6 us -> 2.87 us
    ppermute x1 -> x2, waiting for transfers between devices: 24.1 us -> 16 us  [by_head(): got = lax.ppermute(sent.astype(jnp.bfloat16), 'tp', swap)]
    ppermute x1, waiting for transfers between devices: 7.88 us -> 0.01 us  [by_head(): other_out = lax.ppermute(grad_out, 'tp', swap)]
    add x1 -> x2, other arithmetic: 3.41 us -> 0.21 us  [by_head(): pieces.append(kept + got.astype(jnp.float32))]
    unnamed x6 -> x4, local copies, waits for them, and re-layouts: 8.48 us -> 6.45 us
    ppermute x1, starting transfers between devices: 1.56 us -> 3.03 us  [by_head(): other_out = lax.ppermute(grad_out, 'tp', swap)]
    concatenate x1 -> x2, other arithmetic: 0.83 us -> 2.3 us  [the longest x1 1.47 us: by_head(): mixed_out = jnp.concatenate(pieces, axis=1)]
    dot_general x1 -> x2, matrix products: 13.1 us -> 14.3 us  [by_head(): jnp.einsum('hrd,hdm->rm', local, weights[:, :, c * part:(c + 1) * part],...]
  transfers between devices with their start and end apart: 6 -> 7, of which waited for: 4 -> 4; matrix products, arithmetic and copies ran while one was open for 35% -> 41% of each run, Pallas kernels for 14% -> 16%
where the time goes in v2:
time: 130 us; the launch traced here: 129 us
  matrix products  46.9 us (36%)
  starting transfers between devices  26.9 us (21%)
  waiting for transfers between devices  23.7 us (18%)
  Pallas kernels  20.9 us (16%)
  local copies, waits for them, and re-layouts  6.58 us (5%)
  other arithmetic  2.87 us (2%)
    dot_general x2, matrix products, back(): jnp.einsum('nm,hdm->hnd', x, weights, preferred_element_type=jnp.float32)  32.6 us
    all_to_all x4, starting transfers between devices, spread(): return lax.all_to_all(x, 'ctx', 0, 0, tiled=True)  21.7 us
    ppermute x2, waiting for transfers between devices, by_head(): got = lax.ppermute(sent.astype(jnp.bfloat16), 'tp', swap)  16 us
    dot_general x2, matrix products, by_head(): jnp.einsum('hrd,hdm->rm', local, weights[:, :, c * part:(c + 1) * part],...  14.3 us
    pallas_call x1, Pallas kernels, attend_grad(): pl.pallas_call(functools.partial(backward_kernel, step), out_shape=jax.Sh...  12.2 us
    pallas_call x1, Pallas kernels, attend(): pl.pallas_call(functools.partial(forward_kernel, step), out_shape=(jax.Sh...  8.74 us
    all_to_all x4, waiting for transfers between devices, spread(): return lax.all_to_all(x, 'ctx', 0, 0, tiled=True)  7.64 us
    unnamed x4, local copies, waits for them, and re-layouts  6.45 us
  transfers between devices with their start and end apart: 7, of which 4 were waited for; matrix products, arithmetic and copies ran while one was open for 41% of the time, Pallas kernels for 16%

profile of v2, /device:TPU:0, one launch (start us, length us, event | category | flops | bytes accessed | tf_op | source)
XLA Modules:
  0.0 128.7 jit_solution(18335210280456272107)
XLA Ops:
  0.6 0.0 copy-start
  0.6 3.0 %collective-permute-start.2 = (bf16[64,8192]{1,0:T(8,128)(2,1)}, bf16[64,8192]{1,0:T(8,128)(2,1)}, u32[]{:S(2)}, u32[]{:S(2)}) collective-permute-start(bf16[64,8192]{1,0:T(8,128)(2,1)} %param.4), channel_id=1, source_target_pairs={{0,1},{1,0},{2,3},{3,2},{4,5},{5,4},{6,7},{7,6},{8,9},{9,8},{10,11... | collective-permute-start | bytes 3145736 | tf_op jit(solution)/shard_map/ppermute | solution.py:205
  3.7 3.0 %copy.8 = bf16[128,16,3,128]{3,0,2,1:T(8,128)(2,1)} copy(bf16[128,16,3,128]{3,1,2,0:T(8,128)(2,1)} %param.3) | data formatting | bytes 3145728 | tf_op args[0]
  6.6 5.9 %all-to-all-start = ((bf16[16,3,128,128]{3,2,1,0:T(8,128)(2,1)}), bf16[16,3,128,128]{3,2,1,0:T(8,128)(2,1)S(1)}, u32[]{:S(2)}, u32[]{:S(2)}) async-start(bf16[16,3,128,128]{3,2,1,0:T(8,128)(2,1)} %bitcast.25), calls=%async_computation | async-start | bytes 3145728 | tf_op jit(solution)/shard_map/all_to_all | solution.py:199
  12.6 0.0 copy-done
  12.6 16.2 %convolution_convert_fusion.1 = bf16[16,128,64]{1,2,0:T(8,128)(2,1)S(1)} fusion(bf16[16,128,8192]{2,1,0:T(8,128)(2,1)} %bitcast.26, bf16[64,8192]{1,0:T(8,128)(2,1)S(1)} %copy-done), kind=kOutput, calls=%fused_computation.10 | convolution fusion | flops 2147614720 | bytes 34865152 | tf_op jit(solution)/shard_map/nm,hdm->hnd/dot_general | solution.py:202
  28.8 0.0 collective-permute-done.2
  28.8 16.4 %select_bitcast_fusion.1 = (bf16[16,64,128]{2,1,0:T(8,128)(2,1)S(1)}, bf16[16,64,128]{2,1,0:T(8,128)(2,1)S(1)}) fusion(bf16[16,128,64]{1,2,0:T(8,128)(2,1)S(1)} %convolution_convert_fusion.1, pred[]{:T(512)S(6)} %eq.4, bf16[16,128,8192]{2,1,0:T(8,128)(2,1)} %bitcast.27, bf16[64,8192]{1,0:T(8,128)(2,1)} %collective-permute-done.2), kind=kOutput, calls=%fused_computation.19 | convolution fusion | flops 2147876864 | bytes 35389440 | tf_op jit(solution)/shard_map/nm,hdm->hnd/dot_general | solution.py:202
  45.2 0.8 pad_maximum_fusion.1
  46.1 0.0 all-to-all-done.qkv_ref
  46.1 7.5 %all-to-all-start.2 = ((bf16[16,128,128]{2,1,0:T(8,128)(2,1)}), bf16[16,128,128]{2,1,0:T(8,128)(2,1)S(1)}, u32[]{:S(2)}, u32[]{:S(2)}) async-start(bf16[16,128,128]{2,1,0:T(8,128)(2,1)} %pad_maximum_fusion.1), calls=%async_computation.2 | async-start | bytes 1048576 | tf_op jit(solution)/shard_map/all_to_all | solution.py:199
  53.5 8.7 %attend.1 = (bf16[16,128,128]{2,1,0:T(8,128)(2,1)}, f32[4,1,512]{2,1,0:T(1,128)S(1)}) custom-call(bf16[16,3,128,128]{3,2,1,0:T(8,128)(2,1)S(1)} %all-to-all-done.qkv_ref), custom_call_target="tpu_custom_call" | custom-call | flops 1073741824 | bytes 2097152 | tf_op jit(solution)/shard_map/attend/pallas_call | solution.py:146
  62.3 5.5 %all-to-all-done.2.g_ref = bf16[16,128,128]{2,1,0:T(8,128)(2,1)S(1)} async-done(((bf16[16,128,128]{2,1,0:T(8,128)(2,1)}), bf16[16,128,128]{2,1,0:T(8,128)(2,1)S(1)}, u32[]{:S(2)}, u32[]{:S(2)}) %all-to-all-start.2) | async-done | bytes 524320 | tf_op jit(solution)/shard_map/all_to_all | solution.py:199
  67.8 4.2 %all-to-all-start.1 = ((bf16[16,128,128]{2,1,0:T(8,128)(2,1)}), bf16[16,128,128]{2,1,0:T(8,128)(2,1)S(1)}, u32[]{:S(2)}, u32[]{:S(2)}) async-start(bf16[16,128,128]{2,1,0:T(8,128)(2,1)} %get-tuple-element.4.att_ref), calls=%async_computation.1 | async-start | bytes 1048576 | tf_op jit(solution)/shard_map/all_to_all | solution.py:199
  72.0 12.2 %attend_grad.1 = bf16[16,3,128,128]{3,2,1,0:T(8,128)(2,1)} custom-call(bf16[16,3,128,128]{3,2,1,0:T(8,128)(2,1)S(1)} %all-to-all-done.qkv_ref, bf16[16,128,128]{2,1,0:T(8,128)(2,1)S(1)} %all-to-all-done.2.g_ref, bf16[16,128,128]{2,1,0:T(8,128)(2,1)} %get-tuple-element.4.att_ref, f32[4,1,512]{2,1,0:T(1,128)S(1)} %get-tuple-element.5.lse_ref), custom_call_target="tpu_custom_call" | custom-call | flops 2684354560 | bytes 4194304 | tf_op jit(solution)/shard_map/attend_grad/pallas_call | solution.py:171
  84.1 2.1 %all-to-all-done.1 = bf16[16,128,128]{2,1,0:T(8,128)(2,1)S(1)} async-done(((bf16[16,128,128]{2,1,0:T(8,128)(2,1)}), bf16[16,128,128]{2,1,0:T(8,128)(2,1)S(1)}, u32[]{:S(2)}, u32[]{:S(2)}) %all-to-all-start.1) | async-done | bytes 524320 | tf_op jit(solution)/shard_map/all_to_all | solution.py:199
  86.3 4.2 %all-to-all-start.3 = ((bf16[16,3,128,128]{3,2,1,0:T(8,128)(2,1)}), bf16[16,3,128,128]{3,2,1,0:T(8,128)(2,1)S(1)}, u32[]{:S(2)}, u32[]{:S(2)}) async-start(bf16[16,3,128,128]{3,2,1,0:T(8,128)(2,1)} %attend_grad.1), calls=%async_computation.3 | async-start | bytes 3145728 | tf_op jit(solution)/shard_map/all_to_all | solution.py:199
  90.4 7.2 %fusion.7 = f32[128,4096]{1,0:T(8,128)S(1)} fusion(bf16[16,128,128]{2,1,0:T(8,128)(2,1)S(1)} %all-to-all-done.1, bf16[16,128,8192]{2,1,0:T(8,128)(2,1)} %bitcast.28), kind=kOutput, calls=%fused_computation.5 | convolution fusion | flops 2147483648 | bytes 19398656 | tf_op jit(solution)/shard_map/hrd,hdm->rm/dot_general | solution.py:219
  97.6 0.1 dynamic-slice_convert_fusion
  97.7 0.6 collective-permute-start.1
  98.3 7.1 %fusion.4 = f32[128,4096]{1,0:T(8,128)S(1)} fusion(bf16[16,128,128]{2,1,0:T(8,128)(2,1)S(1)} %all-to-all-done.1, bf16[16,128,8192]{2,1,0:T(8,128)(2,1)} %bitcast.29), kind=kOutput, calls=%fused_computation.4 | convolution fusion | flops 2147483648 | bytes 19398656 | tf_op jit(solution)/shard_map/hrd,hdm->rm/dot_general | solution.py:219
  105.4 0.1 dynamic-slice_convert_fusion.1
  105.5 1.6 %collective-permute-start = (bf16[64,4096]{1,0:T(8,128)(2,1)S(1)}, bf16[64,4096]{1,0:T(8,128)(2,1)S(1)}, u32[]{:S(2)}, u32[]{:S(2)}) collective-permute-start(bf16[64,4096]{1,0:T(8,128)(2,1)S(1)} %dynamic-slice_convert_fusion.1), channel_id=1, source_target_pairs={{0,1},{1,0},{2,3},{3,2},{4,5},{5,4},{6,7},{7,6},{8,9},{9,8},{10,11... | collective-permute-start | bytes 1572872 | tf_op jit(solution)/shard_map/ppermute | solution.py:227
  107.1 5.5 %collective-permute-done.1 = bf16[64,4096]{1,0:T(8,128)(2,1)S(1)} collective-permute-done((bf16[64,4096]{1,0:T(8,128)(2,1)S(1)}, bf16[64,4096]{1,0:T(8,128)(2,1)S(1)}, u32[]{:S(2)}, u32[]{:S(2)}) %collective-permute-start.1) | collective-permute-done | bytes 524320 | tf_op jit(solution)/shard_map/ppermute | solution.py:227
  112.5 0.1 convert_add_fusion
  112.6 10.6 %collective-permute-done = bf16[64,4096]{1,0:T(8,128)(2,1)S(1)} collective-permute-done((bf16[64,4096]{1,0:T(8,128)(2,1)S(1)}, bf16[64,4096]{1,0:T(8,128)(2,1)S(1)}, u32[]{:S(2)}, u32[]{:S(2)}) %collective-permute-start) | collective-permute-done | bytes 524320 | tf_op jit(solution)/shard_map/ppermute | solution.py:227
  123.2 0.1 convert_add_fusion.1
  123.3 1.5 %pad_maximum_fusion = f32[64,8192]{1,0:T(8,128)} fusion(f32[64,4096]{1,0:T(8,128)S(1)} %convert_add_fusion, f32[64,4096]{1,0:T(8,128)S(1)} %convert_add_fusion.1), kind=kLoop, calls=%fused_computation.7 | loop fusion | flops 524288 | bytes 4194304 | tf_op jit(solution)/shard_map/concatenate | solution.py:229
  124.8 0.0 all-to-all-done.3
  124.8 0.4 convert_bitcast_fusion
  125.2 3.5 %copy.6 = f32[128,16,3,128]{3,1,2,0:T(8,128)} copy(f32[128,16,3,128]{3,0,2,1:T(8,128)S(1)} %convert_bitcast_fusion) | data formatting | bytes 6291456
Async XLA Ops:
  0.6 12.0 %copy-start = (bf16[64,8192]{1,0:T(8,128)(2,1)S(1)}, bf16[64,8192]{1,0:T(8,128)(2,1)}, u32[]{:S(2)}) copy-start(bf16[64,8192]{1,0:T(8,128)(2,1)} %param.4) | copy-start | bytes 3145732
  0.6 28.2 %collective-permute-start.2 = (bf16[64,8192]{1,0:T(8,128)(2,1)}, bf16[64,8192]{1,0:T(8,128)(2,1)}, u32[]{:S(2)}, u32[]{:S(2)}) collective-permute-start(bf16[64,8192]{1,0:T(8,128)(2,1)} %param.4), channel_id=1, source_target_pairs={{0,1},{1,0},{2,3},{3,2},{4,5},{5,4},{6,7},{7,6},{8,9},{9,8},{10,11... | collective-permute-start | bytes 3145736 | tf_op jit(solution)/shard_map/ppermute | solution.py:205
  6.6 39.4 %all-to-all-start = ((bf16[16,3,128,128]{3,2,1,0:T(8,128)(2,1)}), bf16[16,3,128,128]{3,2,1,0:T(8,128)(2,1)S(1)}, u32[]{:S(2)}, u32[]{:S(2)}) async-start(bf16[16,3,128,128]{3,2,1,0:T(8,128)(2,1)} %bitcast.25), calls=%async_computation | async-start | bytes 3145728 | tf_op jit(solution)/shard_map/all_to_all | solution.py:199
  46.1 21.7 %all-to-all-start.2 = ((bf16[16,128,128]{2,1,0:T(8,128)(2,1)}), bf16[16,128,128]{2,1,0:T(8,128)(2,1)S(1)}, u32[]{:S(2)}, u32[]{:S(2)}) async-start(bf16[16,128,128]{2,1,0:T(8,128)(2,1)} %pad_maximum_fusion.1), calls=%async_computation.2 | async-start | bytes 1048576 | tf_op jit(solution)/shard_map/all_to_all | solution.py:199
  67.8 18.4 %all-to-all-start.1 = ((bf16[16,128,128]{2,1,0:T(8,128)(2,1)}), bf16[16,128,128]{2,1,0:T(8,128)(2,1)S(1)}, u32[]{:S(2)}, u32[]{:S(2)}) async-start(bf16[16,128,128]{2,1,0:T(8,128)(2,1)} %get-tuple-element.4.att_ref), calls=%async_computation.1 | async-start | bytes 1048576 | tf_op jit(solution)/shard_map/all_to_all | solution.py:199
  86.3 38.5 %all-to-all-start.3 = ((bf16[16,3,128,128]{3,2,1,0:T(8,128)(2,1)}), bf16[16,3,128,128]{3,2,1,0:T(8,128)(2,1)S(1)}, u32[]{:S(2)}, u32[]{:S(2)}) async-start(bf16[16,3,128,128]{3,2,1,0:T(8,128)(2,1)} %attend_grad.1), calls=%async_computation.3 | async-start | bytes 3145728 | tf_op jit(solution)/shard_map/all_to_all | solution.py:199
  97.7 14.9 %collective-permute-start.1 = (bf16[64,4096]{1,0:T(8,128)(2,1)S(1)}, bf16[64,4096]{1,0:T(8,128)(2,1)S(1)}, u32[]{:S(2)}, u32[]{:S(2)}) collective-permute-start(bf16[64,4096]{1,0:T(8,128)(2,1)S(1)} %dynamic-slice_convert_fusion), channel_id=1, source_target_pairs={{0,1},{1,0},{2,3},{3,2},{4,5},{5,4},{6,7},{7,6},{8,9},{9,8},{10,11... | collective-permute-start | bytes 1572872 | tf_op jit(solution)/shard_map/ppermute | solution.py:227
  105.5 17.7 %collective-permute-start = (bf16[64,4096]{1,0:T(8,128)(2,1)S(1)}, bf16[64,4096]{1,0:T(8,128)(2,1)S(1)}, u32[]{:S(2)}, u32[]{:S(2)}) collective-permute-start(bf16[64,4096]{1,0:T(8,128)(2,1)S(1)} %dynamic-slice_convert_fusion.1), channel_id=1, source_target_pairs={{0,1},{1,0},{2,3},{3,2},{4,5},{5,4},{6,7},{7,6},{8,9},{9,8},{10,11... | collective-permute-start | bytes 1572872 | tf_op jit(solution)/shard_map/ppermute | solution.py:227

commit v3 on v2

--- a/solution.py
+++ b/solution.py
@@ -11,7 +11,8 @@
 
 HD = 128
 LOG2E = math.log2(math.e)
-MIX_PARTS = 2
+MIX_PARTS = 4
+BACK_PARTS = (4, 2, 2)
 VMEM_LIMIT = 48 * 1024 * 1024
 
 
@@ -186,6 +187,35 @@
     )(qkv, g, att, lse)
 
 
+def staged(x):
+    count = x.shape[0]
+    me = lax.axis_index("ctx")
+    outer = count // 4
+    x = x.reshape(outer, 2, 2, *x.shape[1:])
+
+    def pair(x, axis, bit):
+        place = (me // bit) % 2
+        kept = lax.dynamic_index_in_dim(x, place, axis, keepdims=False)
+        sent = lax.dynamic_index_in_dim(x, 1 - place, axis, keepdims=False)
+        got = lax.ppermute(sent, "ctx", [(i, i ^ bit) for i in range(count)])
+        first = jnp.where(place == 0, kept, got)
+        second = jnp.where(place == 0, got, kept)
+        return jnp.stack([first, second], axis=axis)
+
+    x = pair(x, 2, 1)
+    x = pair(x, 1, 2)
+    place = me // 4
+    pieces = [lax.dynamic_index_in_dim(x, place, 0, keepdims=False)]
+    for d in range(1, outer):
+        sent = lax.dynamic_index_in_dim(x, place ^ d, 0, keepdims=False)
+        pieces.append(lax.ppermute(sent, "ctx", [(i, i ^ (4 * d)) for i in range(count)]))
+    x = jnp.stack(pieces)
+    x = jnp.concatenate(
+        [lax.dynamic_slice_in_dim(x, place ^ d, 1, axis=0) for d in range(outer)], axis=0
+    )
+    return x.reshape(count, *x.shape[3:])
+
+
 def by_head(qkv, grad_out, attn_out):
     rows, heads = qkv.shape[:2]
     half = grad_out.shape[0]
@@ -198,19 +228,30 @@
     def spread(x):
         return lax.all_to_all(x, "ctx", 0, 0, tiled=True)
 
-    def back(x):
-        y = jnp.einsum("nm,hdm->hnd", x, weights, preferred_element_type=jnp.float32)
-        return y.astype(jnp.bfloat16)
-
-    other_out = lax.ppermute(grad_out, "tp", swap)
+    y = None
+    start = 0
+    for eighths in BACK_PARTS:
+        stop = start + eighths * (width // 8)
+        part = grad_out[:, start:stop]
+        other = lax.ppermute(part, "tp", swap)
+        term = jnp.einsum(
+            "nm,hdm->hnd",
+            jnp.concatenate([part, other], axis=0),
+            weights[:, :, start:stop],
+            preferred_element_type=jnp.float32,
+        )
+        y = term if y is None else term + lax.optimization_barrier(y)
+        start = stop
     mine = spread(jnp.transpose(qkv, (1, 2, 0, 3)))
-    g_own, g_other = back(grad_out), back(other_out)
+    y = y.astype(jnp.bfloat16)
+    g_own, g_other = y[:, :half], y[:, half:]
     first = jnp.where(turn == 0, g_own, g_other)
     second = jnp.where(turn == 0, g_other, g_own)
     g_all = jnp.concatenate([first, second], axis=1)
-    g = spread(g_all)
+    g = staged(g_all)
     att, lse = attend(mine, step)
-    local = spread(att)
+    att, g = lax.optimization_barrier((att, g))
+    local = staged(att)
     grads = attend_grad(mine, g, att, lse, step)
     grads = spread(grads)
     pieces = []
@@ -317,7 +358,7 @@
     out_specs = (P(("ctx", "tp"), None), P("ctx", "tp", None, None))
 
     def whole(qkv, grad_out, attn_out):
-        split = qkv.shape[1] == ctx * tp and tp == 2
+        split = qkv.shape[1] == ctx * tp and tp == 2 and ctx % 4 == 0
         step = jax.shard_map(
             by_head if split else by_rows,
             mesh=mesh,

time: 130 us -> 159 us (1.22)
  waiting for transfers between devices: 23.7 us -> 49.4 us
  starting transfers between devices: 26.9 us -> 33.4 us
  matrix products: 46.9 us -> 43.8 us
  local copies, waits for them, and re-layouts: 6.58 us -> 8.98 us
  Pallas kernels: 20.9 us -> 19.2 us
    ppermute x1 -> x13, waiting for transfers between devices: 0.01 us -> 28.5 us  [the longest x4 17.9 us: pair(): got = lax.ppermute(sent, 'ctx', [(i, i ^ bit) for i in range(count)])]
    ppermute x1 -> x13, starting transfers between devices: 3.03 us -> 18.4 us  [the longest x6 9.44 us: staged(): lax.ppermute(sent, 'ctx', [(i, i ^ 4 * d) for i in range(count)])]
    all_to_all x4 -> x2, starting transfers between devices: 21.7 us -> 10.6 us  [spread(): return lax.all_to_all(x, 'ctx', 0, 0, tiled=True)]
    all_to_all x4 -> x2, waiting for transfers between devices: 7.64 us -> 0.01 us  [spread(): return lax.all_to_all(x, 'ctx', 0, 0, tiled=True)]
    dot_general x2 -> x3, matrix products: 32.6 us -> 25.2 us  [by_head(): jnp.einsum('nm,hdm->hnd', jnp.concatenate([part, other], axis=0), weights...]
    ppermute x2 -> x4, waiting for transfers between devices: 16 us -> 20.9 us  [by_head(): got = lax.ppermute(sent.astype(jnp.bfloat16), 'tp', swap)]
    dot_general x2 -> x4, matrix products: 14.3 us -> 18.5 us  [by_head(): jnp.einsum('hrd,hdm->rm', local, weights[:, :, c * part:(c + 1) * part],...]
    ppermute x2 -> x4, starting transfers between devices: 2.16 us -> 4.31 us  [by_head(): got = lax.ppermute(sent.astype(jnp.bfloat16), 'tp', swap)]
  transfers between devices with their start and end apart: 7 -> 19, of which waited for: 4 -> 11; matrix products, arithmetic and copies ran while one was open for 41% -> 32% of each run, Pallas kernels for 16% -> 7%
where the time goes in v3:
time: 159 us
  waiting for transfers between devices  49.4 us (31%)
  matrix products  43.8 us (28%)
  starting transfers between devices  33.4 us (21%)
  Pallas kernels  19.2 us (12%)
  local copies, waits for them, and re-layouts  8.98 us (6%)
  other arithmetic  2.77 us (2%)
    dot_general x3, matrix products, by_head(): jnp.einsum('nm,hdm->hnd', jnp.concatenate([part, other], axis=0), weights...  25.2 us
    ppermute x4, waiting for transfers between devices, by_head(): got = lax.ppermute(sent.astype(jnp.bfloat16), 'tp', swap)  20.9 us
    dot_general x4, matrix products, by_head(): jnp.einsum('hrd,hdm->rm', local, weights[:, :, c * part:(c + 1) * part],...  18.5 us
    ppermute x4, waiting for transfers between devices, pair(): got = lax.ppermute(sent, 'ctx', [(i, i ^ bit) for i in range(count)])  17.9 us
    pallas_call x1, Pallas kernels, attend_grad(): pl.pallas_call(functools.partial(backward_kernel, step), out_shape=jax.Sh...  11.2 us
    all_to_all x2, starting transfers between devices, spread(): return lax.all_to_all(x, 'ctx', 0, 0, tiled=True)  10.6 us
    ppermute x6, waiting for transfers between devices, staged(): lax.ppermute(sent, 'ctx', [(i, i ^ 4 * d) for i in range(count)])  9.9 us
    ppermute x6, starting transfers between devices, staged(): lax.ppermute(sent, 'ctx', [(i, i ^ 4 * d) for i in range(count)])  9.44 us
  transfers between devices with their start and end apart: 19, of which 11 were waited for; matrix products, arithmetic and copies ran while one was open for 32% of the time, Pallas kernels for 7%

profile of v3, /device:TPU:0, one launch (start us, length us, event | category | flops | bytes accessed | tf_op | source)
XLA Modules:
  0.0 158.6 jit_solution(17290254471456334210)
XLA Ops:
  1.7 3.0 %collective-permute-start.2 = (bf16[64,4096]{1,0:T(8,128)(2,1)S(1)}, bf16[64,4096]{1,0:T(8,128)(2,1)S(1)}, u32[]{:S(2)}, u32[]{:S(2)}) collective-permute-start(bf16[64,4096]{1,0:T(8,128)(2,1)S(1)} %slice.36), channel_id=1, source_target_pairs={{0,1},{1,0},{2,3},{3,2},{4,5},{5,4},{6,7},{7,6},{8,9},{9,8},{10,11... | collective-permute-start | bytes 1572872 | tf_op jit(solution)/shard_map/ppermute | solution.py:236
  5.9 2.0 %collective-permute-start = (bf16[64,2048]{1,0:T(8,128)(2,1)S(1)}, bf16[64,2048]{1,0:T(8,128)(2,1)S(1)}, u32[]{:S(2)}, u32[]{:S(2)}) collective-permute-start(bf16[64,2048]{1,0:T(8,128)(2,1)S(1)} %get-tuple-element.16), channel_id=1, source_target_pairs={{0,1},{1,0},{2,3},{3,2},{4,5},{5,4},{6,7},{7,6},{8,9},{9,8},{10,11... | collective-permute-start | bytes 786440 | tf_op jit(solution)/shard_map/ppermute | solution.py:236
  7.9 3.0 %copy.43 = bf16[128,16,3,128]{3,0,2,1:T(8,128)(2,1)} copy(bf16[128,16,3,128]{3,1,2,0:T(8,128)(2,1)} %param.3) | data formatting | bytes 3145728 | tf_op args[0]
  10.9 5.9 %all-to-all-start = ((bf16[16,3,128,128]{3,2,1,0:T(8,128)(2,1)}), bf16[16,3,128,128]{3,2,1,0:T(8,128)(2,1)S(1)}, u32[]{:S(2)}, u32[]{:S(2)}) async-start(bf16[16,3,128,128]{3,2,1,0:T(8,128)(2,1)} %bitcast.120), calls=%async_computation | async-start | bytes 3145728 | tf_op jit(solution)/shard_map/all_to_all | solution.py:229
  17.5 12.4 %fusion.32 = f32[16,128,128]{2,1,0:T(8,128)} fusion(bf16[16,128,8192]{2,1,0:T(8,128)(2,1)} %bitcast.140, bf16[64,4096]{1,0:T(8,128)(2,1)S(1)} %collective-permute-done.2, bf16[64,4096]{1,0:T(8,128)(2,1)S(1)} %slice.36), kind=kOutput, calls=%fused_computation.23 | convolution fusion | flops 2149580800 | bytes 18874368 | tf_op jit(solution)/shard_map/nm,hdm->hnd/dot_general | solution.py:237
  29.9 6.6 %fusion.35 = f32[16,128,128]{2,1,0:T(8,128)S(1)} fusion(f32[16,128,128]{2,1,0:T(8,128)} %fusion.32, bf16[16,128,8192]{2,1,0:T(8,128)(2,1)} %bitcast.141, bf16[64,2048]{1,0:T(8,128)(2,1)} %collective-permute-done.1, bf16[64,2048]{1,0:T(8,128)(2,1)S(1)} %get-tuple-element.17), kind=kOutput, calls=%fused_computation.24 | convolution fusion | flops 1075052544 | bytes 11010048 | tf_op jit(solution)/shard_map/nm,hdm->hnd/dot_general | solution.py:237
  36.5 6.3 %fusion.41 = bf16[16,128,128]{2,1,0:T(8,128)(2,1)S(1)} fusion(f32[16,128,128]{2,1,0:T(8,128)S(1)} %fusion.35, bf16[16,128,8192]{2,1,0:T(8,128)(2,1)} %bitcast.142, bf16[64,2048]{1,0:T(8,128)(2,1)S(1)} %collective-permute-done, bf16[64,2048]{1,0:T(8,128)(2,1)S(1)} %get-tuple-element.16), kind=kOutput, calls=%fused_computation.26 | convolution fusion | flops 1075314688 | bytes 10485760 | tf_op jit(solution)/shard_map/nm,hdm->hnd/dot_general | solution.py:237
  43.0 1.5 collective-permute-done.3
  44.6 2.1 %collective-permute-start.4 = (bf16[4,2,128,128]{3,2,1,0:T(8,128)(2,1)S(1)}, bf16[4,2,128,128]{3,2,1,0:T(8,128)(2,1)S(1)}, u32[]{:S(2)}, u32[]{:S(2)}) collective-permute-start(bf16[4,2,128,128]{3,2,1,0:T(8,128)(2,1)S(1)} %bitcast.132), channel_id=1, source_target_pairs={{0,4},{2,6},{4,0},{6,2},{8,12},{10,14},{12,8},{14,10},{16,20},{18,... | collective-permute-start | bytes 786440 | tf_op jit(solution)/shard_map/ppermute | solution.py:200
  46.8 8.1 %collective-permute-done.4 = bf16[4,2,128,128]{3,2,1,0:T(8,128)(2,1)S(1)} collective-permute-done((bf16[4,2,128,128]{3,2,1,0:T(8,128)(2,1)S(1)}, bf16[4,2,128,128]{3,2,1,0:T(8,128)(2,1)S(1)}, u32[]{:S(2)}, u32[]{:S(2)}) %collective-permute-start.4) | collective-permute-done | bytes 262176 | tf_op jit(solution)/shard_map/ppermute | solution.py:200
  55.0 2.5 %collective-permute-start.5 = (bf16[2,2,128,128]{3,2,1,0:T(8,128)(2,1)S(1)}, bf16[2,2,128,128]{3,2,1,0:T(8,128)(2,1)S(1)}, u32[]{:S(2)}, u32[]{:S(2)}) collective-permute-start(bf16[2,2,128,128]{3,2,1,0:T(8,128)(2,1)S(1)} %get-tuple-element.39), channel_id=1, source_target_pairs={{0,8},{2,10},{4,12},{6,14},{8,0},{10,2},{12,4},{14,6},{16,24},{18,... | collective-permute-start | bytes 393224 | tf_op jit(solution)/shard_map/ppermute | solution.py:211
  57.4 1.6 %collective-permute-start.6 = (bf16[2,2,128,128]{3,2,1,0:T(8,128)(2,1)S(1)}, bf16[2,2,128,128]{3,2,1,0:T(8,128)(2,1)S(1)}, u32[]{:S(2)}, u32[]{:S(2)}) collective-permute-start(bf16[2,2,128,128]{3,2,1,0:T(8,128)(2,1)S(1)} %get-tuple-element.40), channel_id=1, source_target_pairs={{0,16},{2,18},{4,20},{6,22},{8,24},{10,26},{12,28},{14,30},{16,0},... | collective-permute-start | bytes 393224 | tf_op jit(solution)/shard_map/ppermute | solution.py:211
  59.9 2.0 %collective-permute-done.5 = bf16[2,2,128,128]{3,2,1,0:T(8,128)(2,1)S(1)} collective-permute-done((bf16[2,2,128,128]{3,2,1,0:T(8,128)(2,1)S(1)}, bf16[2,2,128,128]{3,2,1,0:T(8,128)(2,1)S(1)}, u32[]{:S(2)}, u32[]{:S(2)}) %collective-permute-start.5) | collective-permute-done | bytes 131104 | tf_op jit(solution)/shard_map/ppermute | solution.py:211
  61.9 7.9 %collective-permute-done.6 = bf16[2,2,128,128]{3,2,1,0:T(8,128)(2,1)S(1)} collective-permute-done((bf16[2,2,128,128]{3,2,1,0:T(8,128)(2,1)S(1)}, bf16[2,2,128,128]{3,2,1,0:T(8,128)(2,1)S(1)}, u32[]{:S(2)}, u32[]{:S(2)}) %collective-permute-start.6) | collective-permute-done | bytes 131104 | tf_op jit(solution)/shard_map/ppermute | solution.py:211
  70.1 7.9 %attend.1 = (bf16[16,128,128]{2,1,0:T(8,128)(2,1)S(1)}, f32[4,1,512]{2,1,0:T(1,128)S(1)}) custom-call(bf16[16,3,128,128]{3,2,1,0:T(8,128)(2,1)S(1)} %all-to-all-done.qkv_ref), custom_call_target="tpu_custom_call" | custom-call | flops 1073741824 | bytes 2097152 | tf_op jit(solution)/shard_map/attend/pallas_call | solution.py:147
  78.1 1.5 collective-permute-done.8
  79.8 1.6 %collective-permute-start.9 = (bf16[4,2,128,128]{3,2,1,0:T(8,128)(2,1)S(1)}, bf16[4,2,128,128]{3,2,1,0:T(8,128)(2,1)S(1)}, u32[]{:S(2)}, u32[]{:S(2)}) collective-permute-start(bf16[4,2,128,128]{3,2,1,0:T(8,128)(2,1)S(1)} %bitcast.133), channel_id=1, source_target_pairs={{0,4},{2,6},{4,0},{6,2},{8,12},{10,14},{12,8},{14,10},{16,20},{18,... | collective-permute-start | bytes 786440 | tf_op jit(solution)/shard_map/ppermute | solution.py:200
  81.4 6.8 %collective-permute-done.9 = bf16[4,2,128,128]{3,2,1,0:T(8,128)(2,1)S(1)} collective-permute-done((bf16[4,2,128,128]{3,2,1,0:T(8,128)(2,1)S(1)}, bf16[4,2,128,128]{3,2,1,0:T(8,128)(2,1)S(1)}, u32[]{:S(2)}, u32[]{:S(2)}) %collective-permute-start.9) | collective-permute-done | bytes 262176 | tf_op jit(solution)/shard_map/ppermute | solution.py:200
  88.3 2.0 %collective-permute-start.10 = (bf16[2,2,128,128]{3,2,1,0:T(8,128)(2,1)S(1)}, bf16[2,2,128,128]{3,2,1,0:T(8,128)(2,1)S(1)}, u32[]{:S(2)}, u32[]{:S(2)}) collective-permute-start(bf16[2,2,128,128]{3,2,1,0:T(8,128)(2,1)S(1)} %get-tuple-element.27), channel_id=1, source_target_pairs={{0,8},{2,10},{4,12},{6,14},{8,0},{10,2},{12,4},{14,6},{16,24},{18,... | collective-permute-start | bytes 393224 | tf_op jit(solution)/shard_map/ppermute | solution.py:211
  92.8 11.2 %attend_grad.1 = bf16[16,3,128,128]{3,2,1,0:T(8,128)(2,1)} custom-call(bf16[16,3,128,128]{3,2,1,0:T(8,128)(2,1)S(1)} %all-to-all-done.qkv_ref, bf16[16,128,128]{2,1,0:T(8,128)(2,1)S(1)} %bitcast.125, bf16[16,128,128]{2,1,0:T(8,128)(2,1)S(1)} %get-tuple-element.7.att_ref, f32[4,1,512]{2,1,0:T(1,128)S(1)} %get-tuple-element.9.lse_ref), custom_call_target="tpu_custom_call" | custom-call | flops 2684354560 | bytes 4194304 | tf_op jit(solution)/shard_map/attend_grad/pallas_call | solution.py:172
  104.0 4.7 %all-to-all-start.1 = ((bf16[16,3,128,128]{3,2,1,0:T(8,128)(2,1)}), bf16[16,3,128,128]{3,2,1,0:T(8,128)(2,1)S(1)}, u32[]{:S(2)}, u32[]{:S(2)}) async-start(bf16[16,3,128,128]{3,2,1,0:T(8,128)(2,1)} %attend_grad.1), calls=%async_computation.1 | async-start | bytes 3145728 | tf_op jit(solution)/shard_map/all_to_all | solution.py:229
  109.0 4.6 %fusion.20 = f32[128,2048]{1,0:T(8,128)S(1)} fusion(bf16[16,128,128]{2,1,0:T(8,128)(2,1)S(1)} %bitcast.128, bf16[16,128,8192]{2,1,0:T(8,128)(2,1)} %bitcast.143), kind=kOutput, calls=%fused_computation.17 | convolution fusion | flops 1073741824 | bytes 9961472 | tf_op jit(solution)/shard_map/hrd,hdm->rm/dot_general | solution.py:260
  113.7 4.6 %fusion.23 = f32[128,2048]{1,0:T(8,128)S(1)} fusion(bf16[16,128,128]{2,1,0:T(8,128)(2,1)S(1)} %bitcast.129, bf16[16,128,8192]{2,1,0:T(8,128)(2,1)} %bitcast.144), kind=kOutput, calls=%fused_computation.18 | convolution fusion | flops 1073741824 | bytes 9961472 | tf_op jit(solution)/shard_map/hrd,hdm->rm/dot_general | solution.py:260
  118.3 4.6 %fusion.17 = f32[128,2048]{1,0:T(8,128)S(1)} fusion(bf16[16,128,128]{2,1,0:T(8,128)(2,1)S(1)} %bitcast.130, bf16[16,128,8192]{2,1,0:T(8,128)(2,1)} %bitcast.145), kind=kOutput, calls=%fused_computation.16 | convolution fusion | flops 1073741824 | bytes 9961472 | tf_op jit(solution)/shard_map/hrd,hdm->rm/dot_general | solution.py:260
  123.0 4.6 %fusion.14 = f32[128,2048]{1,0:T(8,128)S(1)} fusion(bf16[16,128,128]{2,1,0:T(8,128)(2,1)S(1)} %bitcast.131, bf16[16,128,8192]{2,1,0:T(8,128)(2,1)} %bitcast.146), kind=kOutput, calls=%fused_computation.15 | convolution fusion | flops 1073741824 | bytes 9961472 | tf_op jit(solution)/shard_map/hrd,hdm->rm/dot_general | solution.py:260
  127.7 1.6 %collective-permute-start.13 = (bf16[64,2048]{1,0:T(8,128)(2,1)S(1)}, bf16[64,2048]{1,0:T(8,128)(2,1)S(1)}, u32[]{:S(2)}, u32[]{:S(2)}) collective-permute-start(bf16[64,2048]{1,0:T(8,128)(2,1)S(1)} %dynamic-slice_convert_fusion.3), channel_id=1, source_target_pairs={{0,1},{1,0},{2,3},{3,2},{4,5},{5,4},{6,7},{7,6},{8,9},{9,8},{10,11... | collective-permute-start | bytes 786440 | tf_op jit(solution)/shard_map/ppermute | solution.py:268
  129.9 1.6 %collective-permute-start.15 = (bf16[64,2048]{1,0:T(8,128)(2,1)S(1)}, bf16[64,2048]{1,0:T(8,128)(2,1)S(1)}, u32[]{:S(2)}, u32[]{:S(2)}) collective-permute-start(bf16[64,2048]{1,0:T(8,128)(2,1)S(1)} %dynamic-slice_convert_fusion.1), channel_id=1, source_target_pairs={{0,1},{1,0},{2,3},{3,2},{4,5},{5,4},{6,7},{7,6},{8,9},{9,8},{10,11... | collective-permute-start | bytes 786440 | tf_op jit(solution)/shard_map/ppermute | solution.py:268
  132.1 4.8 %collective-permute-done.13 = bf16[64,2048]{1,0:T(8,128)(2,1)S(1)} collective-permute-done((bf16[64,2048]{1,0:T(8,128)(2,1)S(1)}, bf16[64,2048]{1,0:T(8,128)(2,1)S(1)}, u32[]{:S(2)}, u32[]{:S(2)}) %collective-permute-start.13) | collective-permute-done | bytes 262176 | tf_op jit(solution)/shard_map/ppermute | solution.py:268
  137.0 5.6 %collective-permute-done.14 = bf16[64,2048]{1,0:T(8,128)(2,1)S(1)} collective-permute-done((bf16[64,2048]{1,0:T(8,128)(2,1)S(1)}, bf16[64,2048]{1,0:T(8,128)(2,1)S(1)}, u32[]{:S(2)}, u32[]{:S(2)}) %collective-permute-start.14) | collective-permute-done | bytes 262176 | tf_op jit(solution)/shard_map/ppermute | solution.py:268
  142.6 5.6 %collective-permute-done.15 = bf16[64,2048]{1,0:T(8,128)(2,1)S(1)} collective-permute-done((bf16[64,2048]{1,0:T(8,128)(2,1)S(1)}, bf16[64,2048]{1,0:T(8,128)(2,1)S(1)}, u32[]{:S(2)}, u32[]{:S(2)}) %collective-permute-start.15) | collective-permute-done | bytes 262176 | tf_op jit(solution)/shard_map/ppermute | solution.py:268
  148.2 5.0 %collective-permute-done.16 = bf16[64,2048]{1,0:T(8,128)(2,1)S(1)} collective-permute-done((bf16[64,2048]{1,0:T(8,128)(2,1)S(1)}, bf16[64,2048]{1,0:T(8,128)(2,1)S(1)}, u32[]{:S(2)}, u32[]{:S(2)}) %collective-permute-start.16) | collective-permute-done | bytes 262176 | tf_op jit(solution)/shard_map/ppermute | solution.py:268
  155.1 3.5 %copy.31 = f32[128,16,3,128]{3,1,2,0:T(8,128)} copy(f32[128,16,3,128]{3,0,2,1:T(8,128)S(1)} %convert_bitcast_fusion) | data formatting | bytes 6291456
  (51 shorter events, 10.7 us)
Async XLA Ops:
  1.7 15.8 %collective-permute-start.2 = (bf16[64,4096]{1,0:T(8,128)(2,1)S(1)}, bf16[64,4096]{1,0:T(8,128)(2,1)S(1)}, u32[]{:S(2)}, u32[]{:S(2)}) collective-permute-start(bf16[64,4096]{1,0:T(8,128)(2,1)S(1)} %slice.36), channel_id=1, source_target_pairs={{0,1},{1,0},{2,3},{3,2},{4,5},{5,4},{6,7},{7,6},{8,9},{9,8},{10,11... | collective-permute-start | bytes 1572872 | tf_op jit(solution)/shard_map/ppermute | solution.py:236
  5.8 24.1 %collective-permute-start.1 = (bf16[64,2048]{1,0:T(8,128)(2,1)S(1)}, bf16[64,2048]{1,0:T(8,128)(2,1)}, u32[]{:S(2)}, u32[]{:S(2)}) collective-permute-start(bf16[64,2048]{1,0:T(8,128)(2,1)S(1)} %get-tuple-element.17), channel_id=1, source_target_pairs={{0,1},{1,0},{2,3},{3,2},{4,5},{5,4},{6,7},{7,6},{8,9},{9,8},{10,11... | collective-permute-start | bytes 786440 | tf_op jit(solution)/shard_map/ppermute | solution.py:236
  5.9 30.6 %collective-permute-start = (bf16[64,2048]{1,0:T(8,128)(2,1)S(1)}, bf16[64,2048]{1,0:T(8,128)(2,1)S(1)}, u32[]{:S(2)}, u32[]{:S(2)}) collective-permute-start(bf16[64,2048]{1,0:T(8,128)(2,1)S(1)} %get-tuple-element.16), channel_id=1, source_target_pairs={{0,1},{1,0},{2,3},{3,2},{4,5},{5,4},{6,7},{7,6},{8,9},{9,8},{10,11... | collective-permute-start | bytes 786440 | tf_op jit(solution)/shard_map/ppermute | solution.py:236
  10.9 59.2 %all-to-all-start = ((bf16[16,3,128,128]{3,2,1,0:T(8,128)(2,1)}), bf16[16,3,128,128]{3,2,1,0:T(8,128)(2,1)S(1)}, u32[]{:S(2)}, u32[]{:S(2)}) async-start(bf16[16,3,128,128]{3,2,1,0:T(8,128)(2,1)} %bitcast.120), calls=%async_computation | async-start | bytes 3145728 | tf_op jit(solution)/shard_map/all_to_all | solution.py:229
  42.9 1.6 %collective-permute-start.3 = (bf16[4,2,128,128]{3,2,1,0:T(8,128)(2,1)S(1)}, bf16[4,2,128,128]{3,2,1,0:T(8,128)(2,1)S(1)}, u32[]{:S(2)}, u32[]{:S(2)}) collective-permute-start(bf16[4,2,128,128]{3,2,1,0:T(8,128)(2,1)S(1)} %dynamic-slice_bitcast_fusion.1), channel_id=1, source_target_pairs={{0,2},{2,0},{4,6},{6,4},{8,10},{10,8},{12,14},{14,12},{16,18},{18,... | collective-permute-start | bytes 786440 | tf_op jit(solution)/shard_map/ppermute | solution.py:200
  44.6 10.2 %collective-permute-start.4 = (bf16[4,2,128,128]{3,2,1,0:T(8,128)(2,1)S(1)}, bf16[4,2,128,128]{3,2,1,0:T(8,128)(2,1)S(1)}, u32[]{:S(2)}, u32[]{:S(2)}) collective-permute-start(bf16[4,2,128,128]{3,2,1,0:T(8,128)(2,1)S(1)} %bitcast.132), channel_id=1, source_target_pairs={{0,4},{2,6},{4,0},{6,2},{8,12},{10,14},{12,8},{14,10},{16,20},{18,... | collective-permute-start | bytes 786440 | tf_op jit(solution)/shard_map/ppermute | solution.py:200
  55.0 6.9 %collective-permute-start.5 = (bf16[2,2,128,128]{3,2,1,0:T(8,128)(2,1)S(1)}, bf16[2,2,128,128]{3,2,1,0:T(8,128)(2,1)S(1)}, u32[]{:S(2)}, u32[]{:S(2)}) collective-permute-start(bf16[2,2,128,128]{3,2,1,0:T(8,128)(2,1)S(1)} %get-tuple-element.39), channel_id=1, source_target_pairs={{0,8},{2,10},{4,12},{6,14},{8,0},{10,2},{12,4},{14,6},{16,24},{18,... | collective-permute-start | bytes 393224 | tf_op jit(solution)/shard_map/ppermute | solution.py:211
  57.4 12.4 %collective-permute-start.6 = (bf16[2,2,128,128]{3,2,1,0:T(8,128)(2,1)S(1)}, bf16[2,2,128,128]{3,2,1,0:T(8,128)(2,1)S(1)}, u32[]{:S(2)}, u32[]{:S(2)}) collective-permute-start(bf16[2,2,128,128]{3,2,1,0:T(8,128)(2,1)S(1)} %get-tuple-element.40), channel_id=1, source_target_pairs={{0,16},{2,18},{4,20},{6,22},{8,24},{10,26},{12,28},{14,30},{16,0},... | collective-permute-start | bytes 393224 | tf_op jit(solution)/shard_map/ppermute | solution.py:211
  59.1 10.7 %collective-permute-start.7 = (bf16[2,2,128,128]{3,2,1,0:T(8,128)(2,1)S(1)}, bf16[2,2,128,128]{3,2,1,0:T(8,128)(2,1)S(1)}, u32[]{:S(2)}, u32[]{:S(2)}) collective-permute-start(bf16[2,2,128,128]{3,2,1,0:T(8,128)(2,1)S(1)} %get-tuple-element.41), channel_id=1, source_target_pairs={{0,24},{2,26},{4,28},{6,30},{8,16},{10,18},{12,20},{14,22},{16,8},... | collective-permute-start | bytes 393224 | tf_op jit(solution)/shard_map/ppermute | solution.py:211
  78.0 1.6 %collective-permute-start.8 = (bf16[4,2,128,128]{3,2,1,0:T(8,128)(2,1)S(1)}, bf16[4,2,128,128]{3,2,1,0:T(8,128)(2,1)S(1)}, u32[]{:S(2)}, u32[]{:S(2)}) collective-permute-start(bf16[4,2,128,128]{3,2,1,0:T(8,128)(2,1)S(1)} %dynamic-slice_bitcast_fusion), channel_id=1, source_target_pairs={{0,2},{2,0},{4,6},{6,4},{8,10},{10,8},{12,14},{14,12},{16,18},{18,... | collective-permute-start | bytes 786440 | tf_op jit(solution)/shard_map/ppermute | solution.py:200
  79.8 8.4 %collective-permute-start.9 = (bf16[4,2,128,128]{3,2,1,0:T(8,128)(2,1)S(1)}, bf16[4,2,128,128]{3,2,1,0:T(8,128)(2,1)S(1)}, u32[]{:S(2)}, u32[]{:S(2)}) collective-permute-start(bf16[4,2,128,128]{3,2,1,0:T(8,128)(2,1)S(1)} %bitcast.133), channel_id=1, source_target_pairs={{0,4},{2,6},{4,0},{6,2},{8,12},{10,14},{12,8},{14,10},{16,20},{18,... | collective-permute-start | bytes 786440 | tf_op jit(solution)/shard_map/ppermute | solution.py:200
  88.3 20.5 %collective-permute-start.10 = (bf16[2,2,128,128]{3,2,1,0:T(8,128)(2,1)S(1)}, bf16[2,2,128,128]{3,2,1,0:T(8,128)(2,1)S(1)}, u32[]{:S(2)}, u32[]{:S(2)}) collective-permute-start(bf16[2,2,128,128]{3,2,1,0:T(8,128)(2,1)S(1)} %get-tuple-element.27), channel_id=1, source_target_pairs={{0,8},{2,10},{4,12},{6,14},{8,0},{10,2},{12,4},{14,6},{16,24},{18,... | collective-permute-start | bytes 393224 | tf_op jit(solution)/shard_map/ppermute | solution.py:211
  90.3 18.4 %collective-permute-start.11 = (bf16[2,2,128,128]{3,2,1,0:T(8,128)(2,1)S(1)}, bf16[2,2,128,128]{3,2,1,0:T(8,128)(2,1)S(1)}, u32[]{:S(2)}, u32[]{:S(2)}) collective-permute-start(bf16[2,2,128,128]{3,2,1,0:T(8,128)(2,1)S(1)} %get-tuple-element.28), channel_id=1, source_target_pairs={{0,16},{2,18},{4,20},{6,22},{8,24},{10,26},{12,28},{14,30},{16,0},... | collective-permute-start | bytes 393224 | tf_op jit(solution)/shard_map/ppermute | solution.py:211
  91.4 17.4 %collective-permute-start.12 = (bf16[2,2,128,128]{3,2,1,0:T(8,128)(2,1)S(1)}, bf16[2,2,128,128]{3,2,1,0:T(8,128)(2,1)S(1)}, u32[]{:S(2)}, u32[]{:S(2)}) collective-permute-start(bf16[2,2,128,128]{3,2,1,0:T(8,128)(2,1)S(1)} %get-tuple-element.29), channel_id=1, source_target_pairs={{0,24},{2,26},{4,28},{6,30},{8,16},{10,18},{12,20},{14,22},{16,8},... | collective-permute-start | bytes 393224 | tf_op jit(solution)/shard_map/ppermute | solution.py:211
  104.0 50.7 %all-to-all-start.1 = ((bf16[16,3,128,128]{3,2,1,0:T(8,128)(2,1)}), bf16[16,3,128,128]{3,2,1,0:T(8,128)(2,1)S(1)}, u32[]{:S(2)}, u32[]{:S(2)}) async-start(bf16[16,3,128,128]{3,2,1,0:T(8,128)(2,1)} %attend_grad.1), calls=%async_computation.1 | async-start | bytes 3145728 | tf_op jit(solution)/shard_map/all_to_all | solution.py:229
  127.7 9.2 %collective-permute-start.13 = (bf16[64,2048]{1,0:T(8,128)(2,1)S(1)}, bf16[64,2048]{1,0:T(8,128)(2,1)S(1)}, u32[]{:S(2)}, u32[]{:S(2)}) collective-permute-start(bf16[64,2048]{1,0:T(8,128)(2,1)S(1)} %dynamic-slice_convert_fusion.3), channel_id=1, source_target_pairs={{0,1},{1,0},{2,3},{3,2},{4,5},{5,4},{6,7},{7,6},{8,9},{9,8},{10,11... | collective-permute-start | bytes 786440 | tf_op jit(solution)/shard_map/ppermute | solution.py:268
  129.3 13.2 %collective-permute-start.14 = (bf16[64,2048]{1,0:T(8,128)(2,1)S(1)}, bf16[64,2048]{1,0:T(8,128)(2,1)S(1)}, u32[]{:S(2)}, u32[]{:S(2)}) collective-permute-start(bf16[64,2048]{1,0:T(8,128)(2,1)S(1)} %dynamic-slice_convert_fusion.2), channel_id=1, source_target_pairs={{0,1},{1,0},{2,3},{3,2},{4,5},{5,4},{6,7},{7,6},{8,9},{9,8},{10,11... | collective-permute-start | bytes 786440 | tf_op jit(solution)/shard_map/ppermute | solution.py:268
  129.9 18.3 %collective-permute-start.15 = (bf16[64,2048]{1,0:T(8,128)(2,1)S(1)}, bf16[64,2048]{1,0:T(8,128)(2,1)S(1)}, u32[]{:S(2)}, u32[]{:S(2)}) collective-permute-start(bf16[64,2048]{1,0:T(8,128)(2,1)S(1)} %dynamic-slice_convert_fusion.1), channel_id=1, source_target_pairs={{0,1},{1,0},{2,3},{3,2},{4,5},{5,4},{6,7},{7,6},{8,9},{9,8},{10,11... | collective-permute-start | bytes 786440 | tf_op jit(solution)/shard_map/ppermute | solution.py:268
  131.5 21.7 %collective-permute-start.16 = (bf16[64,2048]{1,0:T(8,128)(2,1)S(1)}, bf16[64,2048]{1,0:T(8,128)(2,1)S(1)}, u32[]{:S(2)}, u32[]{:S(2)}) collective-permute-start(bf16[64,2048]{1,0:T(8,128)(2,1)S(1)} %dynamic-slice_convert_fusion), channel_id=1, source_target_pairs={{0,1},{1,0},{2,3},{3,2},{4,5},{5,4},{6,7},{7,6},{8,9},{9,8},{10,11... | collective-permute-start | bytes 786440 | tf_op jit(solution)/shard_map/ppermute | solution.py:268

commit v4 on v2

--- a/solution.py
+++ b/solution.py
@@ -12,7 +12,7 @@
 HD = 128
 LOG2E = math.log2(math.e)
 MIX_PARTS = 2
-VMEM_LIMIT = 48 * 1024 * 1024
+VMEM_LIMIT = 20 * 1024 * 1024
 
 
 def dot_nt(a, b):
@@ -28,7 +28,51 @@
     return part.reshape(count * part.shape[1], part.shape[2])
 
 
-def forward_kernel(step, qkv_ref, att_ref, lse_ref, v_t, s_buf):
+def swap_matrix(heads, chunk, me):
+    size = heads * chunk
+    row = lax.broadcasted_iota(jnp.int32, (size, size), 0)
+    col = lax.broadcasted_iota(jnp.int32, (size, size), 1)
+    want = (row % chunk) * heads + ((row // chunk) ^ me)
+    return jnp.where(col == want, 1.0, 0.0).astype(jnp.bfloat16)
+
+
+def split_kernel(me_ref, x_ref, *out_refs):
+    rows, three, heads, _ = x_ref.shape
+    chunk = 16
+    order = swap_matrix(heads, chunk, me_ref[0])
+    for b in range(rows // chunk):
+        span = slice(b * chunk, (b + 1) * chunk)
+        for c in range(three):
+            y = dot_nn(order, x_ref[span, c].reshape(chunk * heads, HD)).astype(jnp.bfloat16)
+            y = y.reshape(heads, chunk, HD)
+            for k in range(heads):
+                out_refs[k][c, span] = y[k]
+
+
+def join_kernel(x_ref, out_ref):
+    heads, three, _, _ = x_ref.shape
+    chunk = out_ref.shape[0]
+    order = swap_matrix(chunk, heads, 0)
+    span = pl.ds(pl.program_id(0) * chunk, chunk)
+    for c in range(three):
+        x = x_ref[:, c, span].reshape(chunk * heads, HD)
+        out_ref[:, c] = dot_nn(order, x).reshape(chunk, heads, HD)
+
+
+def back_kernel(turn_ref, own_ref, other_ref, w_ref, out_ref):
+    half = own_ref.shape[0]
+    turn = turn_ref[0]
+    for x_ref, place in ((own_ref, turn), (other_ref, 1 - turn)):
+        y = dot_nt(x_ref[...], w_ref[...]).astype(jnp.bfloat16)
+        for h in range(out_ref.shape[0]):
+            out_ref[h, pl.ds(pl.multiple_of(place * half, half), half)] = y[:, h * HD : (h + 1) * HD]
+
+
+def forward_kernel(step, me_ref, *refs):
+    *parts, qkv_ref, att_ref, lse_ref, v_t, s_buf = refs
+    me = me_ref[0]
+    for k, part in enumerate(parts):
+        qkv_ref[me ^ k] = part[...]
     chunks, _, unit, _ = qkv_ref.shape
     per = step // unit
     blocks = chunks // per
@@ -138,19 +182,76 @@
     return [pl.BlockSpec(memory_space=pltpu.VMEM)] * count
 
 
-def attend(qkv, step):
-    chunks, _, unit, _ = qkv.shape
+def in_smem():
+    return pl.BlockSpec(memory_space=pltpu.SMEM)
+
+
+def split_heads(me, qkv):
+    rows, heads = qkv.shape[:2]
+    return pl.pallas_call(
+        split_kernel,
+        out_shape=[jax.ShapeDtypeStruct((3, rows, HD), jnp.bfloat16)] * heads,
+        in_specs=[in_smem(), *in_vmem(1)],
+        out_specs=in_vmem(heads),
+        compiler_params=pltpu.CompilerParams(vmem_limit_bytes=VMEM_LIMIT),
+        name="split_heads",
+    )(me, jnp.transpose(qkv, (0, 2, 1, 3)))
+
+
+def join_heads(grads):
+    heads, three, rows, _ = grads.shape
+    chunk = 16
+    out = pl.pallas_call(
+        join_kernel,
+        grid=(rows // chunk,),
+        out_shape=jax.ShapeDtypeStruct((rows, three, heads, HD), jnp.float32),
+        in_specs=in_vmem(1),
+        out_specs=pl.BlockSpec((chunk, three, heads, HD), lambda b: (b, 0, 0, 0)),
+        compiler_params=pltpu.CompilerParams(vmem_limit_bytes=VMEM_LIMIT),
+        name="join_heads",
+    )(grads)
+    return jnp.transpose(out, (0, 2, 1, 3))
+
+
+def project_back(turn, own, other, weights):
+    half, width = own.shape
+    heads = weights.shape[0] // HD
+    group = 2
+    return pl.pallas_call(
+        back_kernel,
+        grid=(heads // group,),
+        out_shape=jax.ShapeDtypeStruct((heads, 2 * half, HD), jnp.bfloat16),
+        in_specs=[
+            in_smem(),
+            *in_vmem(2),
+            pl.BlockSpec((group * HD, width), lambda b: (b, 0)),
+        ],
+        out_specs=pl.BlockSpec((group, 2 * half, HD), lambda b: (b, 0, 0)),
+        compiler_params=pltpu.CompilerParams(vmem_limit_bytes=VMEM_LIMIT),
+        cost_estimate=pl.CostEstimate(
+            flops=4 * half * width * heads * HD,
+            transcendentals=0,
+            bytes_accessed=2 * width * heads * HD,
+        ),
+        name="project_back",
+    )(turn, own, other, weights)
+
+
+def attend(me, parts, step):
+    chunks = len(parts)
+    unit = parts[0].shape[1]
     length = chunks * unit
     blocks = length // step
     area = length * length // 2
     return pl.pallas_call(
         functools.partial(forward_kernel, step),
         out_shape=(
+            jax.ShapeDtypeStruct((chunks, 3, unit, HD), jnp.bfloat16),
             jax.ShapeDtypeStruct((chunks, unit, HD), jnp.bfloat16),
             jax.ShapeDtypeStruct((blocks, 1, step), jnp.float32),
         ),
-        in_specs=in_vmem(1),
-        out_specs=tuple(in_vmem(2)),
+        in_specs=[in_smem(), *in_vmem(chunks)],
+        out_specs=tuple(in_vmem(3)),
         scratch_shapes=[
             pltpu.VMEM((blocks, HD, step), jnp.bfloat16),
             pltpu.VMEM((blocks, step, step), jnp.float32),
@@ -160,7 +261,7 @@
             flops=4 * area * HD, transcendentals=area, bytes_accessed=8 * length * HD
         ),
         name="attend",
-    )(qkv)
+    )(me, *parts)
 
 
 def attend_grad(qkv, g, att, lse, step):
@@ -193,23 +294,19 @@
     step = 512 if (rows * heads) % 512 == 0 else rows
     swap = [(0, 1), (1, 0)]
     turn = lax.axis_index("tp")
+    me = lax.axis_index("ctx").reshape(1)
     weights = attn_out.reshape(heads, HD, width)
 
     def spread(x):
         return lax.all_to_all(x, "ctx", 0, 0, tiled=True)
 
-    def back(x):
-        y = jnp.einsum("nm,hdm->hnd", x, weights, preferred_element_type=jnp.float32)
-        return y.astype(jnp.bfloat16)
-
     other_out = lax.ppermute(grad_out, "tp", swap)
-    mine = spread(jnp.transpose(qkv, (1, 2, 0, 3)))
-    g_own, g_other = back(grad_out), back(other_out)
-    first = jnp.where(turn == 0, g_own, g_other)
-    second = jnp.where(turn == 0, g_other, g_own)
-    g_all = jnp.concatenate([first, second], axis=1)
-    g = spread(g_all)
-    att, lse = attend(mine, step)
+    parts = list(split_heads(me, qkv))
+    for k in range(1, heads):
+        parts[k] = lax.ppermute(parts[k], "ctx", [(i, i ^ k) for i in range(heads)])
+    g = project_back(turn.reshape(1), grad_out, other_out, attn_out)
+    g = spread(g)
+    mine, att, lse = attend(me, parts, step)
     local = spread(att)
     grads = attend_grad(mine, g, att, lse, step)
     grads = spread(grads)
@@ -227,7 +324,7 @@
         got = lax.ppermute(sent.astype(jnp.bfloat16), "tp", swap)
         pieces.append(kept + got.astype(jnp.float32))
     mixed_out = jnp.concatenate(pieces, axis=1)
-    return mixed_out, jnp.transpose(grads, (2, 0, 1, 3)).astype(jnp.float32)
+    return mixed_out, join_heads(grads)
 
 
 def by_rows(qkv, grad_out, attn_out):
@@ -317,7 +414,7 @@
     out_specs = (P(("ctx", "tp"), None), P("ctx", "tp", None, None))
 
     def whole(qkv, grad_out, attn_out):
-        split = qkv.shape[1] == ctx * tp and tp == 2
+        split = qkv.shape[1] == ctx * tp and tp == 2 and ctx & (ctx - 1) == 0
         step = jax.shard_map(
             by_head if split else by_rows,
             mesh=mesh,

time: 130 us -> 173 us (1.33)
  the two profiles are of different devices: /device:TPU:0 before, /device:TPU:13 now
where the time goes in v4:
time: 173 us; the launch traced here: 172 us
  waiting for transfers between devices  52.9 us (31%)
  Pallas kernels  50.2 us (29%)
  starting transfers between devices  43.8 us (25%)
  matrix products  16.8 us (10%)
  local copies, waits for them, and re-layouts  5 us (3%)
  other arithmetic  3.03 us (2%)
    pallas_call x1, Pallas kernels, project_back(): pl.pallas_call(back_kernel, grid=(heads // group,), out_shape=jax.ShapeDt...  23.9 us
    ppermute x15, starting transfers between devices, by_head(): parts[k] = lax.ppermute(parts[k], 'ctx', [(i, i ^ k) for i in range(heads)])  23.7 us
    ppermute x15, waiting for transfers between devices, by_head(): parts[k] = lax.ppermute(parts[k], 'ctx', [(i, i ^ k) for i in range(heads)])  21.5 us
    all_to_all x3, waiting for transfers between devices, spread(): return lax.all_to_all(x, 'ctx', 0, 0, tiled=True)  20 us
    all_to_all x3, starting transfers between devices, spread(): return lax.all_to_all(x, 'ctx', 0, 0, tiled=True)  17 us
    dot_general x2, matrix products, by_head(): jnp.einsum('hrd,hdm->rm', local, weights[:, :, c * part:(c + 1) * part],...  16.8 us
    pallas_call x1, Pallas kernels, attend_grad(): pl.pallas_call(functools.partial(backward_kernel, step), out_shape=jax.Sh...  12.2 us
    ppermute x2, waiting for transfers between devices, by_head(): got = lax.ppermute(sent.astype(jnp.bfloat16), 'tp', swap)  11.4 us
  transfers between devices with their start and end apart: 21, of which 10 were waited for; matrix products, arithmetic and copies ran while one was open for 13% of the time, Pallas kernels for 26%

profile of v4, /device:TPU:13, one launch (start us, length us, event | category | flops | bytes accessed | tf_op | source)
XLA Modules:
  0.0 172.5 jit_solution(10152806609280400420)
XLA Ops:
  0.6 1.4 copy-done
  4.0 1.5 collective-permute-start.2
  6.9 1.9 %collective-permute-start.4 = (bf16[3,128,128]{2,1,0:T(8,128)(2,1)S(1)}, bf16[3,128,128]{2,1,0:T(8,128)(2,1)S(1)}, u32[]{:S(2)}, u32[]{:S(2)}) collective-permute-start(bf16[3,128,128]{2,1,0:T(8,128)(2,1)S(1)} %get-tuple-element.26), channel_id=1, source_target_pairs={{0,10},{2,8},{4,14},{6,12},{8,2},{10,0},{12,6},{14,4},{16,26},{18,... | collective-permute-start | bytes 294920 | tf_op jit(solution)/shard_map/ppermute | solution.py:306
  8.9 1.8 %collective-permute-done.2.refs_3_ = bf16[3,128,128]{2,1,0:T(8,128)(2,1)S(1)} collective-permute-done((bf16[3,128,128]{2,1,0:T(8,128)(2,1)S(1)}, bf16[3,128,128]{2,1,0:T(8,128)(2,1)S(1)}, u32[]{:S(2)}, u32[]{:S(2)}) %collective-permute-start.2) | collective-permute-done | bytes 98336 | tf_op jit(solution)/shard_map/ppermute | solution.py:306
  10.7 1.4 collective-permute-start.6
  12.0 2.3 %collective-permute-start.7 = (bf16[3,128,128]{2,1,0:T(8,128)(2,1)S(1)}, bf16[3,128,128]{2,1,0:T(8,128)(2,1)S(1)}, u32[]{:S(2)}, u32[]{:S(2)}) collective-permute-start(bf16[3,128,128]{2,1,0:T(8,128)(2,1)S(1)} %get-tuple-element.29), channel_id=1, source_target_pairs={{0,16},{2,18},{4,20},{6,22},{8,24},{10,26},{12,28},{14,30},{16,0},... | collective-permute-start | bytes 294920 | tf_op jit(solution)/shard_map/ppermute | solution.py:306
  15.3 2.7 %collective-permute-start.9 = (bf16[3,128,128]{2,1,0:T(8,128)(2,1)S(1)}, bf16[3,128,128]{2,1,0:T(8,128)(2,1)S(1)}, u32[]{:S(2)}, u32[]{:S(2)}) collective-permute-start(bf16[3,128,128]{2,1,0:T(8,128)(2,1)S(1)} %get-tuple-element.31), channel_id=1, source_target_pairs={{0,20},{2,22},{4,16},{6,18},{8,28},{10,30},{12,24},{14,26},{16,4},... | collective-permute-start | bytes 294920 | tf_op jit(solution)/shard_map/ppermute | solution.py:306
  19.2 3.2 %collective-permute-start.10 = (bf16[3,128,128]{2,1,0:T(8,128)(2,1)S(1)}, bf16[3,128,128]{2,1,0:T(8,128)(2,1)S(1)}, u32[]{:S(2)}, u32[]{:S(2)}) collective-permute-start(bf16[3,128,128]{2,1,0:T(8,128)(2,1)S(1)} %get-tuple-element.32), channel_id=1, source_target_pairs={{0,22},{2,20},{4,18},{6,16},{8,30},{10,28},{12,26},{14,24},{16,6},... | collective-permute-start | bytes 294920 | tf_op jit(solution)/shard_map/ppermute | solution.py:306
  22.4 1.3 collective-permute-start.11
  23.7 3.6 %collective-permute-done.8.refs_9_ = bf16[3,128,128]{2,1,0:T(8,128)(2,1)S(1)} collective-permute-done((bf16[3,128,128]{2,1,0:T(8,128)(2,1)S(1)}, bf16[3,128,128]{2,1,0:T(8,128)(2,1)S(1)}, u32[]{:S(2)}, u32[]{:S(2)}) %collective-permute-start.8) | collective-permute-done | bytes 98336 | tf_op jit(solution)/shard_map/ppermute | solution.py:306
  27.4 2.2 %collective-permute-start.12 = (bf16[3,128,128]{2,1,0:T(8,128)(2,1)S(1)}, bf16[3,128,128]{2,1,0:T(8,128)(2,1)S(1)}, u32[]{:S(2)}, u32[]{:S(2)}) collective-permute-start(bf16[3,128,128]{2,1,0:T(8,128)(2,1)S(1)} %get-tuple-element.34), channel_id=1, source_target_pairs={{0,26},{2,24},{4,30},{6,28},{8,18},{10,16},{12,22},{14,20},{16,10}... | collective-permute-start | bytes 294920 | tf_op jit(solution)/shard_map/ppermute | solution.py:306
  29.6 2.6 %collective-permute-start.13 = (bf16[3,128,128]{2,1,0:T(8,128)(2,1)S(1)}, bf16[3,128,128]{2,1,0:T(8,128)(2,1)S(1)}, u32[]{:S(2)}, u32[]{:S(2)}) collective-permute-start(bf16[3,128,128]{2,1,0:T(8,128)(2,1)S(1)} %get-tuple-element.35), channel_id=1, source_target_pairs={{0,28},{2,30},{4,24},{6,26},{8,20},{10,22},{12,16},{14,18},{16,12}... | collective-permute-start | bytes 294920 | tf_op jit(solution)/shard_map/ppermute | solution.py:306
  32.2 2.5 %collective-permute-start.14 = (bf16[3,128,128]{2,1,0:T(8,128)(2,1)S(1)}, bf16[3,128,128]{2,1,0:T(8,128)(2,1)S(1)}, u32[]{:S(2)}, u32[]{:S(2)}) collective-permute-start(bf16[3,128,128]{2,1,0:T(8,128)(2,1)S(1)} %get-tuple-element.36), channel_id=1, source_target_pairs={{0,30},{2,28},{4,26},{6,24},{8,22},{10,20},{12,18},{14,16},{16,14}... | collective-permute-start | bytes 294920 | tf_op jit(solution)/shard_map/ppermute | solution.py:306
  34.7 5.8 %collective-permute-done.11.refs_12_ = bf16[3,128,128]{2,1,0:T(8,128)(2,1)S(1)} collective-permute-done((bf16[3,128,128]{2,1,0:T(8,128)(2,1)S(1)}, bf16[3,128,128]{2,1,0:T(8,128)(2,1)S(1)}, u32[]{:S(2)}, u32[]{:S(2)}) %collective-permute-start.11) | collective-permute-done | bytes 98336 | tf_op jit(solution)/shard_map/ppermute | solution.py:306
  40.5 4.2 %collective-permute-done.12.refs_13_ = bf16[3,128,128]{2,1,0:T(8,128)(2,1)S(1)} collective-permute-done((bf16[3,128,128]{2,1,0:T(8,128)(2,1)S(1)}, bf16[3,128,128]{2,1,0:T(8,128)(2,1)S(1)}, u32[]{:S(2)}, u32[]{:S(2)}) %collective-permute-start.12) | collective-permute-done | bytes 98336 | tf_op jit(solution)/shard_map/ppermute | solution.py:306
  44.7 2.9 %collective-permute-done.13.refs_14_ = bf16[3,128,128]{2,1,0:T(8,128)(2,1)S(1)} collective-permute-done((bf16[3,128,128]{2,1,0:T(8,128)(2,1)S(1)}, bf16[3,128,128]{2,1,0:T(8,128)(2,1)S(1)}, u32[]{:S(2)}, u32[]{:S(2)}) %collective-permute-start.13) | collective-permute-done | bytes 98336 | tf_op jit(solution)/shard_map/ppermute | solution.py:306
  47.5 1.9 %collective-permute-done.14.refs_15_ = bf16[3,128,128]{2,1,0:T(8,128)(2,1)S(1)} collective-permute-done((bf16[3,128,128]{2,1,0:T(8,128)(2,1)S(1)}, bf16[3,128,128]{2,1,0:T(8,128)(2,1)S(1)}, u32[]{:S(2)}, u32[]{:S(2)}) %collective-permute-start.14) | collective-permute-done | bytes 98336 | tf_op jit(solution)/shard_map/ppermute | solution.py:306
  49.5 8.9 %attend.1 = (bf16[16,3,128,128]{3,2,1,0:T(8,128)(2,1)S(1)}, bf16[16,128,128]{2,1,0:T(8,128)(2,1)}, f32[4,1,512]{2,1,0:T(1,128)S(1)}) custom-call(s32[1]{0:T(128)} %bitcast.me_ref, bf16[3,128,128]{2,1,0:T(8,128)(2,1)S(1)} %get-tuple-element.21.refs_0_, bf16[3,128,128]{2,1,0:T(8,128)(2,1)S(1)} %collective-permute-done.refs_1_, ...), custom_call_target="tpu_custom_call" | custom-call | flops 1073741824 | bytes 2097152 | tf_op jit(solution)/shard_map/attend/pallas_call | solution.py:246
  59.5 4.7 %all-to-all-start = ((bf16[16,128,128]{2,1,0:T(8,128)(2,1)}), bf16[16,128,128]{2,1,0:T(8,128)(2,1)S(1)}, u32[]{:S(2)}, u32[]{:S(2)}) async-start(bf16[16,128,128]{2,1,0:T(8,128)(2,1)} %get-tuple-element.37.att_ref), calls=%async_computation | async-start | bytes 1048576 | tf_op jit(solution)/shard_map/all_to_all | solution.py:301
  64.2 23.9 %project_back.1 = bf16[16,128,128]{2,1,0:T(8,128)(2,1)} custom-call(s32[1]{0:T(128)} %bitcast.5.turn_ref, bf16[64,8192]{1,0:T(8,128)(2,1)S(1)} %copy-done.1, bf16[64,8192]{1,0:T(8,128)(2,1)S(1)} %collective-permute-done.17.other_ref, bf16[2048,8192]{1,0:T(8,128)(2,1)} %w_ref.1), custom_call_target="tpu_custom_call" | custom-call | flops 4294967296 | bytes 33554432 | tf_op jit(solution)/shard_map/project_back/pallas_call | solution.py:220
  88.2 6.0 %all-to-all-start.1 = ((bf16[16,128,128]{2,1,0:T(8,128)(2,1)}), bf16[16,128,128]{2,1,0:T(8,128)(2,1)S(1)}, u32[]{:S(2)}, u32[]{:S(2)}) async-start(bf16[16,128,128]{2,1,0:T(8,128)(2,1)} %project_back.1), calls=%async_computation.1 | async-start | bytes 1048576 | tf_op jit(solution)/shard_map/all_to_all | solution.py:301
  94.2 7.2 %fusion.7 = f32[128,4096]{1,0:T(8,128)S(1)} fusion(bf16[16,128,128]{2,1,0:T(8,128)(2,1)S(1)} %all-to-all-done, bf16[16,128,8192]{2,1,0:T(8,128)(2,1)} %bitcast.12), kind=kOutput, calls=%fused_computation.5 | convolution fusion | flops 2147483648 | bytes 19398656 | tf_op jit(solution)/shard_map/hrd,hdm->rm/dot_general | solution.py:316
  102.3 1.6 collective-permute-start.16
  103.9 9.6 %fusion.4 = f32[128,4096]{1,0:T(8,128)} fusion(bf16[16,128,128]{2,1,0:T(8,128)(2,1)S(1)} %all-to-all-done, bf16[16,128,8192]{2,1,0:T(8,128)(2,1)} %bitcast.13), kind=kOutput, calls=%fused_computation.4 | convolution fusion | flops 2147483648 | bytes 19398656 | tf_op jit(solution)/shard_map/hrd,hdm->rm/dot_general | solution.py:316
  113.5 12.2 %attend_grad.1 = bf16[16,3,128,128]{3,2,1,0:T(8,128)(2,1)} custom-call(bf16[16,3,128,128]{3,2,1,0:T(8,128)(2,1)S(1)} %copy-done.3, bf16[16,128,128]{2,1,0:T(8,128)(2,1)S(1)} %all-to-all-done.1.g_ref, bf16[16,128,128]{2,1,0:T(8,128)(2,1)} %get-tuple-element.37.att_ref, f32[4,1,512]{2,1,0:T(1,128)S(1)} %get-tuple-element.39.lse_ref), custom_call_target="tpu_custom_call" | custom-call | flops 2684354560 | bytes 4194304 | tf_op jit(solution)/shard_map/attend_grad/pallas_call | solution.py:272
  125.8 6.3 %all-to-all-start.2 = ((bf16[16,3,128,128]{3,2,1,0:T(8,128)(2,1)}), bf16[16,3,128,128]{3,2,1,0:T(8,128)(2,1)S(1)}, u32[]{:S(2)}, u32[]{:S(2)}) async-start(bf16[16,3,128,128]{3,2,1,0:T(8,128)(2,1)} %attend_grad.1), calls=%async_computation.2 | async-start | bytes 3145728 | tf_op jit(solution)/shard_map/all_to_all | solution.py:301
  132.1 1.4 dynamic-slice_convert_fusion.1
  133.8 1.5 convert_add_fusion
  135.3 11.4 %collective-permute-done.15 = bf16[64,4096]{1,0:T(8,128)(2,1)S(1)} collective-permute-done((bf16[64,4096]{1,0:T(8,128)(2,1)S(1)}, bf16[64,4096]{1,0:T(8,128)(2,1)S(1)}, u32[]{:S(2)}, u32[]{:S(2)}) %collective-permute-start.15) | collective-permute-done | bytes 524320 | tf_op jit(solution)/shard_map/ppermute | solution.py:324
  146.7 1.5 pad_maximum_fusion
  148.2 20.0 %all-to-all-done.2.x_ref = bf16[16,3,128,128]{3,2,1,0:T(8,128)(2,1)S(1)} async-done(((bf16[16,3,128,128]{3,2,1,0:T(8,128)(2,1)}), bf16[16,3,128,128]{3,2,1,0:T(8,128)(2,1)S(1)}, u32[]{:S(2)}, u32[]{:S(2)}) %all-to-all-start.2) | async-done | bytes 1572896 | tf_op jit(solution)/shard_map/all_to_all | solution.py:301
  168.2 4.2 %join_heads.1 = f32[128,3,16,128]{3,2,1,0:T(8,128)} custom-call(bf16[16,3,128,128]{3,2,1,0:T(8,128)(2,1)S(1)} %all-to-all-done.2.x_ref), custom_call_target="tpu_custom_call" | custom-call | tf_op jit(solution)/shard_map/join_heads/pallas_call | solution.py:204
  (34 shorter events, 8.2 us)
Async XLA Ops:
  0.6 1.4 copy-start
  3.0 3.8 %collective-permute-start = (bf16[3,128,128]{2,1,0:T(8,128)(2,1)S(1)}, bf16[3,128,128]{2,1,0:T(8,128)(2,1)S(1)}, u32[]{:S(2)}, u32[]{:S(2)}) collective-permute-start(bf16[3,128,128]{2,1,0:T(8,128)(2,1)S(1)} %get-tuple-element.22), channel_id=1, source_target_pairs={{0,2},{2,0},{4,6},{6,4},{8,10},{10,8},{12,14},{14,12},{16,18},{18,... | collective-permute-start | bytes 294920 | tf_op jit(solution)/shard_map/ppermute | solution.py:306
  3.8 5.0 %collective-permute-start.1 = (bf16[3,128,128]{2,1,0:T(8,128)(2,1)S(1)}, bf16[3,128,128]{2,1,0:T(8,128)(2,1)S(1)}, u32[]{:S(2)}, u32[]{:S(2)}) collective-permute-start(bf16[3,128,128]{2,1,0:T(8,128)(2,1)S(1)} %get-tuple-element.23), channel_id=1, source_target_pairs={{0,4},{2,6},{4,0},{6,2},{8,12},{10,14},{12,8},{14,10},{16,20},{18,... | collective-permute-start | bytes 294920 | tf_op jit(solution)/shard_map/ppermute | solution.py:306
  4.0 6.7 %collective-permute-start.2 = (bf16[3,128,128]{2,1,0:T(8,128)(2,1)S(1)}, bf16[3,128,128]{2,1,0:T(8,128)(2,1)S(1)}, u32[]{:S(2)}, u32[]{:S(2)}) collective-permute-start(bf16[3,128,128]{2,1,0:T(8,128)(2,1)S(1)} %get-tuple-element.24), channel_id=1, source_target_pairs={{0,6},{2,4},{4,2},{6,0},{8,14},{10,12},{12,10},{14,8},{16,22},{18,... | collective-permute-start | bytes 294920 | tf_op jit(solution)/shard_map/ppermute | solution.py:306
  5.5 58.8 %collective-permute-start.17 = (bf16[64,8192]{1,0:T(8,128)(2,1)}, bf16[64,8192]{1,0:T(8,128)(2,1)S(1)}, u32[]{:S(2)}, u32[]{:S(2)}) collective-permute-start(bf16[64,8192]{1,0:T(8,128)(2,1)} %own_ref.1), channel_id=1, source_target_pairs={{0,1},{1,0},{2,3},{3,2},{4,5},{5,4},{6,7},{7,6},{8,9},{9,8},{10,11... | collective-permute-start | bytes 3145736 | tf_op jit(solution)/shard_map/ppermute | solution.py:303
  6.7 5.4 %collective-permute-start.3 = (bf16[3,128,128]{2,1,0:T(8,128)(2,1)S(1)}, bf16[3,128,128]{2,1,0:T(8,128)(2,1)S(1)}, u32[]{:S(2)}, u32[]{:S(2)}) collective-permute-start(bf16[3,128,128]{2,1,0:T(8,128)(2,1)S(1)} %get-tuple-element.25), channel_id=1, source_target_pairs={{0,8},{2,10},{4,12},{6,14},{8,0},{10,2},{12,4},{14,6},{16,24},{18,... | collective-permute-start | bytes 294920 | tf_op jit(solution)/shard_map/ppermute | solution.py:306
  6.9 7.6 %collective-permute-start.4 = (bf16[3,128,128]{2,1,0:T(8,128)(2,1)S(1)}, bf16[3,128,128]{2,1,0:T(8,128)(2,1)S(1)}, u32[]{:S(2)}, u32[]{:S(2)}) collective-permute-start(bf16[3,128,128]{2,1,0:T(8,128)(2,1)S(1)} %get-tuple-element.26), channel_id=1, source_target_pairs={{0,10},{2,8},{4,14},{6,12},{8,2},{10,0},{12,6},{14,4},{16,26},{18,... | collective-permute-start | bytes 294920 | tf_op jit(solution)/shard_map/ppermute | solution.py:306
  8.8 6.6 %collective-permute-start.5 = (bf16[3,128,128]{2,1,0:T(8,128)(2,1)S(1)}, bf16[3,128,128]{2,1,0:T(8,128)(2,1)S(1)}, u32[]{:S(2)}, u32[]{:S(2)}) collective-permute-start(bf16[3,128,128]{2,1,0:T(8,128)(2,1)S(1)} %get-tuple-element.27), channel_id=1, source_target_pairs={{0,12},{2,14},{4,8},{6,10},{8,4},{10,6},{12,0},{14,2},{16,28},{18,... | collective-permute-start | bytes 294920 | tf_op jit(solution)/shard_map/ppermute | solution.py:306
  10.7 8.5 %collective-permute-start.6 = (bf16[3,128,128]{2,1,0:T(8,128)(2,1)S(1)}, bf16[3,128,128]{2,1,0:T(8,128)(2,1)S(1)}, u32[]{:S(2)}, u32[]{:S(2)}) collective-permute-start(bf16[3,128,128]{2,1,0:T(8,128)(2,1)S(1)} %get-tuple-element.28), channel_id=1, source_target_pairs={{0,14},{2,12},{4,10},{6,8},{8,6},{10,4},{12,2},{14,0},{16,30},{18,... | collective-permute-start | bytes 294920 | tf_op jit(solution)/shard_map/ppermute | solution.py:306
  12.0 10.4 %collective-permute-start.7 = (bf16[3,128,128]{2,1,0:T(8,128)(2,1)S(1)}, bf16[3,128,128]{2,1,0:T(8,128)(2,1)S(1)}, u32[]{:S(2)}, u32[]{:S(2)}) collective-permute-start(bf16[3,128,128]{2,1,0:T(8,128)(2,1)S(1)} %get-tuple-element.29), channel_id=1, source_target_pairs={{0,16},{2,18},{4,20},{6,22},{8,24},{10,26},{12,28},{14,30},{16,0},... | collective-permute-start | bytes 294920 | tf_op jit(solution)/shard_map/ppermute | solution.py:306
  14.5 12.9 %collective-permute-start.8 = (bf16[3,128,128]{2,1,0:T(8,128)(2,1)S(1)}, bf16[3,128,128]{2,1,0:T(8,128)(2,1)S(1)}, u32[]{:S(2)}, u32[]{:S(2)}) collective-permute-start(bf16[3,128,128]{2,1,0:T(8,128)(2,1)S(1)} %get-tuple-element.30), channel_id=1, source_target_pairs={{0,18},{2,16},{4,22},{6,20},{8,26},{10,24},{12,30},{14,28},{16,2},... | collective-permute-start | bytes 294920 | tf_op jit(solution)/shard_map/ppermute | solution.py:306
  15.3 14.3 %collective-permute-start.9 = (bf16[3,128,128]{2,1,0:T(8,128)(2,1)S(1)}, bf16[3,128,128]{2,1,0:T(8,128)(2,1)S(1)}, u32[]{:S(2)}, u32[]{:S(2)}) collective-permute-start(bf16[3,128,128]{2,1,0:T(8,128)(2,1)S(1)} %get-tuple-element.31), channel_id=1, source_target_pairs={{0,20},{2,22},{4,16},{6,18},{8,28},{10,30},{12,24},{14,26},{16,4},... | collective-permute-start | bytes 294920 | tf_op jit(solution)/shard_map/ppermute | solution.py:306
  19.2 13.0 %collective-permute-start.10 = (bf16[3,128,128]{2,1,0:T(8,128)(2,1)S(1)}, bf16[3,128,128]{2,1,0:T(8,128)(2,1)S(1)}, u32[]{:S(2)}, u32[]{:S(2)}) collective-permute-start(bf16[3,128,128]{2,1,0:T(8,128)(2,1)S(1)} %get-tuple-element.32), channel_id=1, source_target_pairs={{0,22},{2,20},{4,18},{6,16},{8,30},{10,28},{12,26},{14,24},{16,6},... | collective-permute-start | bytes 294920 | tf_op jit(solution)/shard_map/ppermute | solution.py:306
  22.4 18.1 %collective-permute-start.11 = (bf16[3,128,128]{2,1,0:T(8,128)(2,1)S(1)}, bf16[3,128,128]{2,1,0:T(8,128)(2,1)S(1)}, u32[]{:S(2)}, u32[]{:S(2)}) collective-permute-start(bf16[3,128,128]{2,1,0:T(8,128)(2,1)S(1)} %get-tuple-element.33), channel_id=1, source_target_pairs={{0,24},{2,26},{4,28},{6,30},{8,16},{10,18},{12,20},{14,22},{16,8},... | collective-permute-start | bytes 294920 | tf_op jit(solution)/shard_map/ppermute | solution.py:306
  27.4 17.3 %collective-permute-start.12 = (bf16[3,128,128]{2,1,0:T(8,128)(2,1)S(1)}, bf16[3,128,128]{2,1,0:T(8,128)(2,1)S(1)}, u32[]{:S(2)}, u32[]{:S(2)}) collective-permute-start(bf16[3,128,128]{2,1,0:T(8,128)(2,1)S(1)} %get-tuple-element.34), channel_id=1, source_target_pairs={{0,26},{2,24},{4,30},{6,28},{8,18},{10,16},{12,22},{14,20},{16,10}... | collective-permute-start | bytes 294920 | tf_op jit(solution)/shard_map/ppermute | solution.py:306
  29.6 17.9 %collective-permute-start.13 = (bf16[3,128,128]{2,1,0:T(8,128)(2,1)S(1)}, bf16[3,128,128]{2,1,0:T(8,128)(2,1)S(1)}, u32[]{:S(2)}, u32[]{:S(2)}) collective-permute-start(bf16[3,128,128]{2,1,0:T(8,128)(2,1)S(1)} %get-tuple-element.35), channel_id=1, source_target_pairs={{0,28},{2,30},{4,24},{6,26},{8,20},{10,22},{12,16},{14,18},{16,12}... | collective-permute-start | bytes 294920 | tf_op jit(solution)/shard_map/ppermute | solution.py:306
  32.2 17.2 %collective-permute-start.14 = (bf16[3,128,128]{2,1,0:T(8,128)(2,1)S(1)}, bf16[3,128,128]{2,1,0:T(8,128)(2,1)S(1)}, u32[]{:S(2)}, u32[]{:S(2)}) collective-permute-start(bf16[3,128,128]{2,1,0:T(8,128)(2,1)S(1)} %get-tuple-element.36), channel_id=1, source_target_pairs={{0,30},{2,28},{4,26},{6,24},{8,22},{10,20},{12,18},{14,16},{16,14}... | collective-permute-start | bytes 294920 | tf_op jit(solution)/shard_map/ppermute | solution.py:306
  49.4 14.8 %copy-start.1 = (bf16[64,8192]{1,0:T(8,128)(2,1)S(1)}, bf16[64,8192]{1,0:T(8,128)(2,1)}, u32[]{:S(2)}) copy-start(bf16[64,8192]{1,0:T(8,128)(2,1)} %own_ref.1) | copy-start | bytes 3145732
  58.3 1.2 copy-start.2
  59.5 28.7 %all-to-all-start = ((bf16[16,128,128]{2,1,0:T(8,128)(2,1)}), bf16[16,128,128]{2,1,0:T(8,128)(2,1)S(1)}, u32[]{:S(2)}, u32[]{:S(2)}) async-start(bf16[16,128,128]{2,1,0:T(8,128)(2,1)} %get-tuple-element.37.att_ref), calls=%async_computation | async-start | bytes 1048576 | tf_op jit(solution)/shard_map/all_to_all | solution.py:301
  88.2 25.3 %all-to-all-start.1 = ((bf16[16,128,128]{2,1,0:T(8,128)(2,1)}), bf16[16,128,128]{2,1,0:T(8,128)(2,1)S(1)}, u32[]{:S(2)}, u32[]{:S(2)}) async-start(bf16[16,128,128]{2,1,0:T(8,128)(2,1)} %project_back.1), calls=%async_computation.1 | async-start | bytes 1048576 | tf_op jit(solution)/shard_map/all_to_all | solution.py:301
  101.3 2.5 %copy-start.5 = (f32[128,4096]{1,0:T(8,128)}, f32[128,4096]{1,0:T(8,128)S(1)}, u32[]{:S(2)}) copy-start(f32[128,4096]{1,0:T(8,128)S(1)} %fusion.7) | copy-start | bytes 6291460
  102.3 11.2 %copy-start.3 = (bf16[16,3,128,128]{3,2,1,0:T(8,128)(2,1)S(1)}, bf16[16,3,128,128]{3,2,1,0:T(8,128)(2,1)}, u32[]{:S(2)}) copy-start(bf16[16,3,128,128]{3,2,1,0:T(8,128)(2,1)} %copy-done.2) | copy-start | bytes 4718596
  102.3 31.5 %collective-permute-start.16 = (bf16[64,4096]{1,0:T(8,128)(2,1)}, bf16[64,4096]{1,0:T(8,128)(2,1)}, u32[]{:S(2)}, u32[]{:S(2)}) collective-permute-start(bf16[64,4096]{1,0:T(8,128)(2,1)} %dynamic-slice_convert_fusion), channel_id=1, source_target_pairs={{0,1},{1,0},{2,3},{3,2},{4,5},{5,4},{6,7},{7,6},{8,9},{9,8},{10,11... | collective-permute-start | bytes 1572872 | tf_op jit(solution)/shard_map/ppermute | solution.py:324
  125.8 42.5 %all-to-all-start.2 = ((bf16[16,3,128,128]{3,2,1,0:T(8,128)(2,1)}), bf16[16,3,128,128]{3,2,1,0:T(8,128)(2,1)S(1)}, u32[]{:S(2)}, u32[]{:S(2)}) async-start(bf16[16,3,128,128]{3,2,1,0:T(8,128)(2,1)} %attend_grad.1), calls=%async_computation.2 | async-start | bytes 3145728 | tf_op jit(solution)/shard_map/all_to_all | solution.py:301
  132.0 14.6 %copy-start.4 = (f32[128,4096]{1,0:T(8,128)S(1)}, f32[128,4096]{1,0:T(8,128)}, u32[]{:S(2)}) copy-start(f32[128,4096]{1,0:T(8,128)} %fusion.4) | copy-start | bytes 6291460
  133.5 13.2 %collective-permute-start.15 = (bf16[64,4096]{1,0:T(8,128)(2,1)S(1)}, bf16[64,4096]{1,0:T(8,128)(2,1)S(1)}, u32[]{:S(2)}, u32[]{:S(2)}) collective-permute-start(bf16[64,4096]{1,0:T(8,128)(2,1)S(1)} %dynamic-slice_convert_fusion.1), channel_id=1, source_target_pairs={{0,1},{1,0},{2,3},{3,2},{4,5},{5,4},{6,7},{7,6},{8,9},{9,8},{10,11... | collective-permute-start | bytes 1572872 | tf_op jit(solution)/shard_map/ppermute | solution.py:324

commit v5 on v4

--- a/solution.py
+++ b/solution.py
@@ -28,44 +28,68 @@
     return part.reshape(count * part.shape[1], part.shape[2])
 
 
+CHUNK = 16
+
+
+def py_loop(lo, hi, body, carry):
+    for i in range(lo, hi):
+        carry = body(i, carry)
+    return carry
+
+
 def swap_matrix(heads, chunk, me):
     size = heads * chunk
     row = lax.broadcasted_iota(jnp.int32, (size, size), 0)
     col = lax.broadcasted_iota(jnp.int32, (size, size), 1)
-    want = (row % chunk) * heads + ((row // chunk) ^ me)
+    want = lax.rem(row, chunk) * heads + (lax.div(row, chunk) ^ me)
     return jnp.where(col == want, 1.0, 0.0).astype(jnp.bfloat16)
 
 
-def split_kernel(me_ref, x_ref, *out_refs):
+def split_kernel(me_ref, x_ref, *refs):
+    *out_refs, order = refs
     rows, three, heads, _ = x_ref.shape
-    chunk = 16
-    order = swap_matrix(heads, chunk, me_ref[0])
-    for b in range(rows // chunk):
-        span = slice(b * chunk, (b + 1) * chunk)
+    step = pl.program_id(0)
+
+    @pl.when(step == 0)
+    def _():
+        order[...] = swap_matrix(heads, CHUNK, me_ref[0])
+
+    for b in range(rows // CHUNK):
+        span = pl.ds(pl.multiple_of(step * rows + b * CHUNK, CHUNK), CHUNK)
         for c in range(three):
-            y = dot_nn(order, x_ref[span, c].reshape(chunk * heads, HD)).astype(jnp.bfloat16)
-            y = y.reshape(heads, chunk, HD)
+            x = x_ref[b * CHUNK : (b + 1) * CHUNK, c].reshape(CHUNK * heads, HD)
+            y = dot_nn(order[...], x).astype(jnp.bfloat16).reshape(heads, CHUNK, HD)
             for k in range(heads):
                 out_refs[k][c, span] = y[k]
 
 
-def join_kernel(x_ref, out_ref):
+def join_kernel(x_ref, out_ref, order):
     heads, three, _, _ = x_ref.shape
-    chunk = out_ref.shape[0]
-    order = swap_matrix(chunk, heads, 0)
-    span = pl.ds(pl.program_id(0) * chunk, chunk)
-    for c in range(three):
-        x = x_ref[:, c, span].reshape(chunk * heads, HD)
-        out_ref[:, c] = dot_nn(order, x).reshape(chunk, heads, HD)
-
-
-def back_kernel(turn_ref, own_ref, other_ref, w_ref, out_ref):
+    rows = out_ref.shape[0]
+    step = pl.program_id(0)
+
+    @pl.when(step == 0)
+    def _():
+        order[...] = swap_matrix(CHUNK, heads, 0)
+
+    for b in range(rows // CHUNK):
+        span = pl.ds(pl.multiple_of(step * rows + b * CHUNK, CHUNK), CHUNK)
+        for c in range(three):
+            x = x_ref[:, c, span].reshape(CHUNK * heads, HD)
+            out_ref[b * CHUNK : (b + 1) * CHUNK, c] = dot_nn(order[...], x).reshape(CHUNK, heads, HD)
+
+
+def back_kernel(turn_ref, own_ref, other_ref, w_ref, out_ref, x_buf):
     half = own_ref.shape[0]
-    turn = turn_ref[0]
-    for x_ref, place in ((own_ref, turn), (other_ref, 1 - turn)):
-        y = dot_nt(x_ref[...], w_ref[...]).astype(jnp.bfloat16)
-        for h in range(out_ref.shape[0]):
-            out_ref[h, pl.ds(pl.multiple_of(place * half, half), half)] = y[:, h * HD : (h + 1) * HD]
+
+    @pl.when(pl.program_id(0) == 0)
+    def _():
+        for x_ref, place in ((own_ref, turn_ref[0]), (other_ref, 1 - turn_ref[0])):
+            x_buf[pl.ds(pl.multiple_of(place * half, half), half)] = x_ref[...]
+
+    y = dot_nt(x_buf[...], w_ref[...]).astype(jnp.bfloat16)
+    for h in range(out_ref.shape[0]):
+        out_ref[h] = y[:, h * HD : (h + 1) * HD]
 
 
 def forward_kernel(step, me_ref, *refs):
@@ -79,101 +103,84 @@
     scale = LOG2E / math.sqrt(HD)
     for b in range(blocks):
         v_t[b] = rows_of(qkv_ref, b * per, per, 2).T
-
-    def query_block(i, _):
+    for i in range(blocks):
         q = rows_of(qkv_ref, i * per, per, 0)
-
-        def scores(j, top):
+        top = None
+        for j in range(i + 1):
             s = dot_nt(rows_of(qkv_ref, j * per, per, 1), q)
-            s_buf[j] = s
-            return jnp.maximum(top, jnp.max(s, axis=0, keepdims=True))
-
-        top = lax.fori_loop(0, i, scores, jnp.full((1, step), -jnp.inf, jnp.float32))
-        s = dot_nt(rows_of(qkv_ref, i * per, per, 1), q)
-        key = lax.broadcasted_iota(jnp.int32, s.shape, 0)
-        query = lax.broadcasted_iota(jnp.int32, s.shape, 1)
-        s = jnp.where(key <= query, s, -jnp.inf)
-        s_buf[i] = s
-        top = jnp.maximum(top, jnp.max(s, axis=0, keepdims=True))
-
-        def exps(j, total):
-            p = jnp.exp2((s_buf[j] - top) * scale)
-            s_buf[j] = p
-            return total + jnp.sum(p, axis=0, keepdims=True)
-
-        total = lax.fori_loop(0, i + 1, exps, jnp.zeros((1, step), jnp.float32))
+            if j == i:
+                key = lax.broadcasted_iota(jnp.int32, s.shape, 0)
+                query = lax.broadcasted_iota(jnp.int32, s.shape, 1)
+                s = jnp.where(key <= query, s, -jnp.inf)
+            s_buf[i % 2, j] = s
+            peak = jnp.max(s, axis=0, keepdims=True)
+            top = peak if top is None else jnp.maximum(top, peak)
+        total = jnp.zeros((1, step), jnp.float32)
+        for j in range(i + 1):
+            p = jnp.exp2((s_buf[i % 2, j] - top) * scale)
+            s_buf[i % 2, j] = p
+            total = total + jnp.sum(p, axis=0, keepdims=True)
         inverse = 1.0 / total
-
-        def mix(j, acc):
-            return acc + dot_nn(v_t[j], (s_buf[j] * inverse).astype(jnp.bfloat16))
-
-        acc = lax.fori_loop(0, i + 1, mix, jnp.zeros((HD, step), jnp.float32))
-        att_ref[pl.ds(i * per, per)] = acc.T.astype(jnp.bfloat16).reshape(per, unit, HD)
+        acc = jnp.zeros((HD, step), jnp.float32)
+        for j in range(i + 1):
+            acc = acc + dot_nn(v_t[j], (s_buf[i % 2, j] * inverse).astype(jnp.bfloat16))
+        att_ref[i * per : (i + 1) * per] = acc.T.astype(jnp.bfloat16).reshape(per, unit, HD)
         lse_ref[i] = top * scale + jnp.log2(total)
-        return 0
-
-    lax.fori_loop(0, blocks, query_block, 0)
 
 
 def backward_kernel(step, qkv_ref, g_ref, att_ref, lse_ref, out_ref, k_t, dq_t, delta):
     chunks, _, unit, _ = qkv_ref.shape
     per = step // unit
     blocks = chunks // per
+    half = step // 2
     factor = 1.0 / math.sqrt(HD)
     for b in range(blocks):
         k_t[b] = rows_of(qkv_ref, b * per, per, 1).T
         prod = rows_of(g_ref, b * per, per).astype(jnp.float32)
         prod = prod * rows_of(att_ref, b * per, per).astype(jnp.float32)
         delta[b] = jnp.sum(prod.T, axis=0, keepdims=True)
+        dq_t[b] = jnp.zeros((HD, step), jnp.float32)
+
+    def pair(k, v, kt, q, g, lse, dlt, masked):
+        w = jnp.exp2(dot_nt(k, q) * (factor * LOG2E) - lse)
+        if masked:
+            key = lax.broadcasted_iota(jnp.int32, w.shape, 0)
+            query = lax.broadcasted_iota(jnp.int32, w.shape, 1)
+            w = jnp.where(key <= query, w, 0.0)
+        ds = (w * (dot_nt(v, g) - dlt) * factor).astype(jnp.bfloat16)
+        dv = dot_nn(w.astype(jnp.bfloat16), g)
+        return dot_nn(ds, q), dv, dot_nn(kt, ds)
 
     def key_block(j, _):
         k = rows_of(qkv_ref, j * per, per, 1)
         v = rows_of(qkv_ref, j * per, per, 2)
         kt = k_t[j]
-
-        def pair(i, diagonal):
-            q = rows_of(qkv_ref, i * per, per, 0)
-            g = rows_of(g_ref, i * per, per)
-            w = jnp.exp2(dot_nt(k, q) * (factor * LOG2E) - lse_ref[i])
-            if diagonal:
-                key = lax.broadcasted_iota(jnp.int32, w.shape, 0)
-                query = lax.broadcasted_iota(jnp.int32, w.shape, 1)
-                w = jnp.where(key <= query, w, 0.0)
-            ds = (w * (dot_nt(v, g) - delta[i]) * factor).astype(jnp.bfloat16)
-            dv = dot_nn(w.astype(jnp.bfloat16), g)
-            dk = dot_nn(ds, q)
-            return dk, dv, dot_nn(kt, ds)
-
-        dk, dv, part = pair(j, True)
-
-        @pl.when(j == 0)
-        def _():
-            dq_t[j] = part
-
-        @pl.when(j > 0)
-        def _():
-            dq_t[j] = dq_t[j] + part
+        q = rows_of(qkv_ref, j * per, per, 0)
+        g = rows_of(g_ref, j * per, per)
+        lse, dlt = lse_ref[j], delta[j]
+        dk0, dv0, part0 = pair(k[:half], v[:half], kt[:, :half], q, g, lse, dlt, True)
+        dk1, dv1, part1 = pair(
+            k[half:], v[half:], kt[:, half:], q[half:], g[half:], lse[:, half:], dlt[:, half:], True
+        )
+        dq_t[j, :, :half] += part0[:, :half]
+        dq_t[j, :, half:] += part0[:, half:] + part1
 
         def later(i, carry):
-            dk, dv, part = pair(i, False)
-
-            @pl.when(j == 0)
-            def _():
-                dq_t[i] = part
-
-            @pl.when(j > 0)
-            def _():
-                dq_t[i] = dq_t[i] + part
-
+            dk, dv, part = pair(
+                k, v, kt, rows_of(qkv_ref, i * per, per, 0), rows_of(g_ref, i * per, per),
+                lse_ref[i], delta[i], False,
+            )
+            dq_t[i] += part
             return carry[0] + dk, carry[1] + dv
 
-        dk, dv = lax.fori_loop(j + 1, blocks, later, (dk, dv))
+        start = jnp.concatenate([dk0, dk1]), jnp.concatenate([dv0, dv1])
+        dk, dv = py_loop(j + 1, blocks, later, start)
         spot = pl.ds(j * per, per)
         out_ref[spot, 1] = dk.astype(jnp.bfloat16).reshape(per, unit, HD)
         out_ref[spot, 2] = dv.astype(jnp.bfloat16).reshape(per, unit, HD)
         return 0
 
-    lax.fori_loop(0, blocks, key_block, 0)
+    py_loop(0, blocks, key_block, 0)
     for b in range(blocks):
         out_ref[pl.ds(b * per, per), 0] = dq_t[b].T.astype(jnp.bfloat16).reshape(per, unit, HD)
 
@@ -188,11 +195,14 @@
 
 def split_heads(me, qkv):
     rows, heads = qkv.shape[:2]
+    part = 4 * CHUNK
     return pl.pallas_call(
         split_kernel,
+        grid=(rows // part,),
         out_shape=[jax.ShapeDtypeStruct((3, rows, HD), jnp.bfloat16)] * heads,
-        in_specs=[in_smem(), *in_vmem(1)],
+        in_specs=[in_smem(), pl.BlockSpec((part, 3, heads, HD), lambda b: (b, 0, 0, 0))],
         out_specs=in_vmem(heads),
+        scratch_shapes=[pltpu.VMEM((CHUNK * heads, CHUNK * heads), jnp.bfloat16)],
         compiler_params=pltpu.CompilerParams(vmem_limit_bytes=VMEM_LIMIT),
         name="split_heads",
     )(me, jnp.transpose(qkv, (0, 2, 1, 3)))
@@ -200,13 +210,14 @@
 
 def join_heads(grads):
     heads, three, rows, _ = grads.shape
-    chunk = 16
+    part = 2 * CHUNK
     out = pl.pallas_call(
         join_kernel,
-        grid=(rows // chunk,),
+        grid=(rows // part,),
         out_shape=jax.ShapeDtypeStruct((rows, three, heads, HD), jnp.float32),
         in_specs=in_vmem(1),
-        out_specs=pl.BlockSpec((chunk, three, heads, HD), lambda b: (b, 0, 0, 0)),
+        out_specs=pl.BlockSpec((part, three, heads, HD), lambda b: (b, 0, 0, 0)),
+        scratch_shapes=[pltpu.VMEM((CHUNK * heads, CHUNK * heads), jnp.bfloat16)],
         compiler_params=pltpu.CompilerParams(vmem_limit_bytes=VMEM_LIMIT),
         name="join_heads",
     )(grads)
@@ -227,6 +238,7 @@
             pl.BlockSpec((group * HD, width), lambda b: (b, 0)),
         ],
         out_specs=pl.BlockSpec((group, 2 * half, HD), lambda b: (b, 0, 0)),
+        scratch_shapes=[pltpu.VMEM((2 * half, width), jnp.bfloat16)],
         compiler_params=pltpu.CompilerParams(vmem_limit_bytes=VMEM_LIMIT),
         cost_estimate=pl.CostEstimate(
             flops=4 * half * width * heads * HD,
@@ -254,7 +266,7 @@
         out_specs=tuple(in_vmem(3)),
         scratch_shapes=[
             pltpu.VMEM((blocks, HD, step), jnp.bfloat16),
-            pltpu.VMEM((blocks, step, step), jnp.float32),
+            pltpu.VMEM((2, blocks, step, step), jnp.float32),
         ],
         compiler_params=pltpu.CompilerParams(vmem_limit_bytes=VMEM_LIMIT),
         cost_estimate=pl.CostEstimate(

time: 173 us -> 158 us (0.913)
  Pallas kernels: 50.2 us -> 35.4 us
    pallas_call x1, Pallas kernels: 23.9 us -> 17.6 us  [project_back(): pl.pallas_call(back_kernel, grid=(heads // group,), out_shape=jax.ShapeDt...]
    pallas_call x1, Pallas kernels: 8.85 us -> 5.04 us  [attend(): pl.pallas_call(functools.partial(forward_kernel, step), out_shape=(jax.Sh...]
    pallas_call x1, Pallas kernels: 12.2 us -> 8.72 us  [attend_grad(): pl.pallas_call(functools.partial(backward_kernel, step), out_shape=jax.Sh...]
  transfers between devices with their start and end apart: 21 -> 21, of which waited for: 10 -> 10; matrix products, arithmetic and copies ran while one was open for 13% -> 14% of each run, Pallas kernels for 26% -> 20%
where the time goes in v5:
time: 158 us
  waiting for transfers between devices  52.9 us (33%)
  starting transfers between devices  43.8 us (28%)
  Pallas kernels  35.4 us (22%)
  matrix products  16.8 us (11%)
  local copies, waits for them, and re-layouts  5 us (3%)
  other arithmetic  3.03 us (2%)
    ppermute x15, starting transfers between devices, by_head(): parts[k] = lax.ppermute(parts[k], 'ctx', [(i, i ^ k) for i in range(heads)])  23.7 us
    ppermute x15, waiting for transfers between devices, by_head(): parts[k] = lax.ppermute(parts[k], 'ctx', [(i, i ^ k) for i in range(heads)])  21.5 us
    all_to_all x3, waiting for transfers between devices, spread(): return lax.all_to_all(x, 'ctx', 0, 0, tiled=True)  20 us
    pallas_call x1, Pallas kernels, project_back(): pl.pallas_call(back_kernel, grid=(heads // group,), out_shape=jax.ShapeDt...  17.6 us
    all_to_all x3, starting transfers between devices, spread(): return lax.all_to_all(x, 'ctx', 0, 0, tiled=True)  17 us
    dot_general x2, matrix products, by_head(): jnp.einsum('hrd,hdm->rm', local, weights[:, :, c * part:(c + 1) * part],...  16.8 us
    ppermute x2, waiting for transfers between devices, by_head(): got = lax.ppermute(sent.astype(jnp.bfloat16), 'tp', swap)  11.4 us
    pallas_call x1, Pallas kernels, attend_grad(): pl.pallas_call(functools.partial(backward_kernel, step), out_shape=jax.Sh...  8.72 us
  transfers between devices with their start and end apart: 21, of which 10 were waited for; matrix products, arithmetic and copies ran while one was open for 14% of the time, Pallas kernels for 20%

profile of v5, /device:TPU:13, one launch (start us, length us, event | category | flops | bytes accessed | tf_op | source)
XLA Modules:
  0.0 157.7 jit_solution(5386886187782008580)
XLA Ops:
  0.6 1.4 copy-done
  4.2 1.5 collective-permute-start.2
  7.1 1.9 %collective-permute-start.4 = (bf16[3,128,128]{2,1,0:T(8,128)(2,1)S(1)}, bf16[3,128,128]{2,1,0:T(8,128)(2,1)S(1)}, u32[]{:S(2)}, u32[]{:S(2)}) collective-permute-start(bf16[3,128,128]{2,1,0:T(8,128)(2,1)S(1)} %get-tuple-element.26), channel_id=1, source_target_pairs={{0,10},{2,8},{4,14},{6,12},{8,2},{10,0},{12,6},{14,4},{16,26},{18,... | collective-permute-start | bytes 294920 | tf_op jit(solution)/shard_map/ppermute | solution.py:318
  9.1 1.8 %collective-permute-done.2.refs_3_ = bf16[3,128,128]{2,1,0:T(8,128)(2,1)S(1)} collective-permute-done((bf16[3,128,128]{2,1,0:T(8,128)(2,1)S(1)}, bf16[3,128,128]{2,1,0:T(8,128)(2,1)S(1)}, u32[]{:S(2)}, u32[]{:S(2)}) %collective-permute-start.2) | collective-permute-done | bytes 98336 | tf_op jit(solution)/shard_map/ppermute | solution.py:318
  10.9 1.4 collective-permute-start.6
  12.3 2.3 %collective-permute-start.7 = (bf16[3,128,128]{2,1,0:T(8,128)(2,1)S(1)}, bf16[3,128,128]{2,1,0:T(8,128)(2,1)S(1)}, u32[]{:S(2)}, u32[]{:S(2)}) collective-permute-start(bf16[3,128,128]{2,1,0:T(8,128)(2,1)S(1)} %get-tuple-element.29), channel_id=1, source_target_pairs={{0,16},{2,18},{4,20},{6,22},{8,24},{10,26},{12,28},{14,30},{16,0},... | collective-permute-start | bytes 294920 | tf_op jit(solution)/shard_map/ppermute | solution.py:318
  15.5 2.7 %collective-permute-start.9 = (bf16[3,128,128]{2,1,0:T(8,128)(2,1)S(1)}, bf16[3,128,128]{2,1,0:T(8,128)(2,1)S(1)}, u32[]{:S(2)}, u32[]{:S(2)}) collective-permute-start(bf16[3,128,128]{2,1,0:T(8,128)(2,1)S(1)} %get-tuple-element.31), channel_id=1, source_target_pairs={{0,20},{2,22},{4,16},{6,18},{8,28},{10,30},{12,24},{14,26},{16,4},... | collective-permute-start | bytes 294920 | tf_op jit(solution)/shard_map/ppermute | solution.py:318
  19.4 3.2 %collective-permute-start.10 = (bf16[3,128,128]{2,1,0:T(8,128)(2,1)S(1)}, bf16[3,128,128]{2,1,0:T(8,128)(2,1)S(1)}, u32[]{:S(2)}, u32[]{:S(2)}) collective-permute-start(bf16[3,128,128]{2,1,0:T(8,128)(2,1)S(1)} %get-tuple-element.32), channel_id=1, source_target_pairs={{0,22},{2,20},{4,18},{6,16},{8,30},{10,28},{12,26},{14,24},{16,6},... | collective-permute-start | bytes 294920 | tf_op jit(solution)/shard_map/ppermute | solution.py:318
  22.6 1.3 collective-permute-start.11
  24.0 3.6 %collective-permute-done.8.refs_9_ = bf16[3,128,128]{2,1,0:T(8,128)(2,1)S(1)} collective-permute-done((bf16[3,128,128]{2,1,0:T(8,128)(2,1)S(1)}, bf16[3,128,128]{2,1,0:T(8,128)(2,1)S(1)}, u32[]{:S(2)}, u32[]{:S(2)}) %collective-permute-start.8) | collective-permute-done | bytes 98336 | tf_op jit(solution)/shard_map/ppermute | solution.py:318
  27.6 2.2 %collective-permute-start.12 = (bf16[3,128,128]{2,1,0:T(8,128)(2,1)S(1)}, bf16[3,128,128]{2,1,0:T(8,128)(2,1)S(1)}, u32[]{:S(2)}, u32[]{:S(2)}) collective-permute-start(bf16[3,128,128]{2,1,0:T(8,128)(2,1)S(1)} %get-tuple-element.34), channel_id=1, source_target_pairs={{0,26},{2,24},{4,30},{6,28},{8,18},{10,16},{12,22},{14,20},{16,10}... | collective-permute-start | bytes 294920 | tf_op jit(solution)/shard_map/ppermute | solution.py:318
  29.8 2.6 %collective-permute-start.13 = (bf16[3,128,128]{2,1,0:T(8,128)(2,1)S(1)}, bf16[3,128,128]{2,1,0:T(8,128)(2,1)S(1)}, u32[]{:S(2)}, u32[]{:S(2)}) collective-permute-start(bf16[3,128,128]{2,1,0:T(8,128)(2,1)S(1)} %get-tuple-element.35), channel_id=1, source_target_pairs={{0,28},{2,30},{4,24},{6,26},{8,20},{10,22},{12,16},{14,18},{16,12}... | collective-permute-start | bytes 294920 | tf_op jit(solution)/shard_map/ppermute | solution.py:318
  32.4 2.5 %collective-permute-start.14 = (bf16[3,128,128]{2,1,0:T(8,128)(2,1)S(1)}, bf16[3,128,128]{2,1,0:T(8,128)(2,1)S(1)}, u32[]{:S(2)}, u32[]{:S(2)}) collective-permute-start(bf16[3,128,128]{2,1,0:T(8,128)(2,1)S(1)} %get-tuple-element.36), channel_id=1, source_target_pairs={{0,30},{2,28},{4,26},{6,24},{8,22},{10,20},{12,18},{14,16},{16,14}... | collective-permute-start | bytes 294920 | tf_op jit(solution)/shard_map/ppermute | solution.py:318
  34.9 5.8 %collective-permute-done.11.refs_12_ = bf16[3,128,128]{2,1,0:T(8,128)(2,1)S(1)} collective-permute-done((bf16[3,128,128]{2,1,0:T(8,128)(2,1)S(1)}, bf16[3,128,128]{2,1,0:T(8,128)(2,1)S(1)}, u32[]{:S(2)}, u32[]{:S(2)}) %collective-permute-start.11) | collective-permute-done | bytes 98336 | tf_op jit(solution)/shard_map/ppermute | solution.py:318
  40.7 4.2 %collective-permute-done.12.refs_13_ = bf16[3,128,128]{2,1,0:T(8,128)(2,1)S(1)} collective-permute-done((bf16[3,128,128]{2,1,0:T(8,128)(2,1)S(1)}, bf16[3,128,128]{2,1,0:T(8,128)(2,1)S(1)}, u32[]{:S(2)}, u32[]{:S(2)}) %collective-permute-start.12) | collective-permute-done | bytes 98336 | tf_op jit(solution)/shard_map/ppermute | solution.py:318
  44.9 2.9 %collective-permute-done.13.refs_14_ = bf16[3,128,128]{2,1,0:T(8,128)(2,1)S(1)} collective-permute-done((bf16[3,128,128]{2,1,0:T(8,128)(2,1)S(1)}, bf16[3,128,128]{2,1,0:T(8,128)(2,1)S(1)}, u32[]{:S(2)}, u32[]{:S(2)}) %collective-permute-start.13) | collective-permute-done | bytes 98336 | tf_op jit(solution)/shard_map/ppermute | solution.py:318
  47.8 1.9 %collective-permute-done.14.refs_15_ = bf16[3,128,128]{2,1,0:T(8,128)(2,1)S(1)} collective-permute-done((bf16[3,128,128]{2,1,0:T(8,128)(2,1)S(1)}, bf16[3,128,128]{2,1,0:T(8,128)(2,1)S(1)}, u32[]{:S(2)}, u32[]{:S(2)}) %collective-permute-start.14) | collective-permute-done | bytes 98336 | tf_op jit(solution)/shard_map/ppermute | solution.py:318
  49.7 5.0 %attend.1 = (bf16[16,3,128,128]{3,2,1,0:T(8,128)(2,1)S(1)}, bf16[16,128,128]{2,1,0:T(8,128)(2,1)}, f32[4,1,512]{2,1,0:T(1,128)S(1)}) custom-call(s32[1]{0:T(128)} %bitcast.me_ref, bf16[3,128,128]{2,1,0:T(8,128)(2,1)S(1)} %get-tuple-element.21.refs_0_, bf16[3,128,128]{2,1,0:T(8,128)(2,1)S(1)} %collective-permute-done.refs_1_, ...), custom_call_target="tpu_custom_call" | custom-call | flops 1073741824 | bytes 2097152 | tf_op jit(solution)/shard_map/attend/pallas_call | solution.py:258
  55.9 4.7 %all-to-all-start = ((bf16[16,128,128]{2,1,0:T(8,128)(2,1)}), bf16[16,128,128]{2,1,0:T(8,128)(2,1)S(1)}, u32[]{:S(2)}, u32[]{:S(2)}) async-start(bf16[16,128,128]{2,1,0:T(8,128)(2,1)} %get-tuple-element.37.att_ref), calls=%async_computation | async-start | bytes 1048576 | tf_op jit(solution)/shard_map/all_to_all | solution.py:313
  60.6 17.6 %project_back.1 = bf16[16,128,128]{2,1,0:T(8,128)(2,1)} custom-call(s32[1]{0:T(128)} %bitcast.5.turn_ref, bf16[64,8192]{1,0:T(8,128)(2,1)S(1)} %copy-done.1, bf16[64,8192]{1,0:T(8,128)(2,1)S(1)} %collective-permute-done.17.other_ref, bf16[2048,8192]{1,0:T(8,128)(2,1)} %w_ref.1), custom_call_target="tpu_custom_call" | custom-call | flops 4294967296 | bytes 33554432 | tf_op jit(solution)/shard_map/project_back/pallas_call | solution.py:231
  78.2 6.0 %all-to-all-start.1 = ((bf16[16,128,128]{2,1,0:T(8,128)(2,1)}), bf16[16,128,128]{2,1,0:T(8,128)(2,1)S(1)}, u32[]{:S(2)}, u32[]{:S(2)}) async-start(bf16[16,128,128]{2,1,0:T(8,128)(2,1)} %project_back.1), calls=%async_computation.1 | async-start | bytes 1048576 | tf_op jit(solution)/shard_map/all_to_all | solution.py:313
  84.3 7.2 %fusion.7 = f32[128,4096]{1,0:T(8,128)S(1)} fusion(bf16[16,128,128]{2,1,0:T(8,128)(2,1)S(1)} %all-to-all-done, bf16[16,128,8192]{2,1,0:T(8,128)(2,1)} %bitcast.12), kind=kOutput, calls=%fused_computation.5 | convolution fusion | flops 2147483648 | bytes 19398656 | tf_op jit(solution)/shard_map/hrd,hdm->rm/dot_general | solution.py:328
  92.4 1.6 collective-permute-start.16
  94.0 9.6 %fusion.4 = f32[128,4096]{1,0:T(8,128)} fusion(bf16[16,128,128]{2,1,0:T(8,128)(2,1)S(1)} %all-to-all-done, bf16[16,128,8192]{2,1,0:T(8,128)(2,1)} %bitcast.13), kind=kOutput, calls=%fused_computation.4 | convolution fusion | flops 2147483648 | bytes 19398656 | tf_op jit(solution)/shard_map/hrd,hdm->rm/dot_general | solution.py:328
  103.6 8.7 %attend_grad.1 = bf16[16,3,128,128]{3,2,1,0:T(8,128)(2,1)} custom-call(bf16[16,3,128,128]{3,2,1,0:T(8,128)(2,1)S(1)} %copy-done.3, bf16[16,128,128]{2,1,0:T(8,128)(2,1)S(1)} %all-to-all-done.1.g_ref, bf16[16,128,128]{2,1,0:T(8,128)(2,1)} %get-tuple-element.37.att_ref, f32[4,1,512]{2,1,0:T(1,128)S(1)} %get-tuple-element.39.lse_ref), custom_call_target="tpu_custom_call" | custom-call | flops 2684354560 | bytes 4194304 | tf_op jit(solution)/shard_map/attend_grad/pallas_call | solution.py:284
  112.3 6.3 %all-to-all-start.2 = ((bf16[16,3,128,128]{3,2,1,0:T(8,128)(2,1)}), bf16[16,3,128,128]{3,2,1,0:T(8,128)(2,1)S(1)}, u32[]{:S(2)}, u32[]{:S(2)}) async-start(bf16[16,3,128,128]{3,2,1,0:T(8,128)(2,1)} %attend_grad.1), calls=%async_computation.2 | async-start | bytes 3145728 | tf_op jit(solution)/shard_map/all_to_all | solution.py:313
  118.6 1.4 dynamic-slice_convert_fusion.1
  120.4 1.5 convert_add_fusion
  121.8 11.4 %collective-permute-done.15 = bf16[64,4096]{1,0:T(8,128)(2,1)S(1)} collective-permute-done((bf16[64,4096]{1,0:T(8,128)(2,1)S(1)}, bf16[64,4096]{1,0:T(8,128)(2,1)S(1)}, u32[]{:S(2)}, u32[]{:S(2)}) %collective-permute-start.15) | collective-permute-done | bytes 524320 | tf_op jit(solution)/shard_map/ppermute | solution.py:336
  133.3 1.5 pad_maximum_fusion
  134.8 20.0 %all-to-all-done.2.x_ref = bf16[16,3,128,128]{3,2,1,0:T(8,128)(2,1)S(1)} async-done(((bf16[16,3,128,128]{3,2,1,0:T(8,128)(2,1)}), bf16[16,3,128,128]{3,2,1,0:T(8,128)(2,1)S(1)}, u32[]{:S(2)}, u32[]{:S(2)}) %all-to-all-start.2) | async-done | bytes 1572896 | tf_op jit(solution)/shard_map/all_to_all | solution.py:313
  154.8 2.9 %join_heads.1 = f32[128,3,16,128]{3,2,1,0:T(8,128)} custom-call(bf16[16,3,128,128]{3,2,1,0:T(8,128)(2,1)S(1)} %all-to-all-done.2.x_ref), custom_call_target="tpu_custom_call" | custom-call | tf_op jit(solution)/shard_map/join_heads/pallas_call | solution.py:214
  (34 shorter events, 8.4 us)
Async XLA Ops:
  0.6 1.4 copy-start
  3.2 3.8 %collective-permute-start = (bf16[3,128,128]{2,1,0:T(8,128)(2,1)S(1)}, bf16[3,128,128]{2,1,0:T(8,128)(2,1)S(1)}, u32[]{:S(2)}, u32[]{:S(2)}) collective-permute-start(bf16[3,128,128]{2,1,0:T(8,128)(2,1)S(1)} %get-tuple-element.22), channel_id=1, source_target_pairs={{0,2},{2,0},{4,6},{6,4},{8,10},{10,8},{12,14},{14,12},{16,18},{18,... | collective-permute-start | bytes 294920 | tf_op jit(solution)/shard_map/ppermute | solution.py:318
  4.0 5.0 %collective-permute-start.1 = (bf16[3,128,128]{2,1,0:T(8,128)(2,1)S(1)}, bf16[3,128,128]{2,1,0:T(8,128)(2,1)S(1)}, u32[]{:S(2)}, u32[]{:S(2)}) collective-permute-start(bf16[3,128,128]{2,1,0:T(8,128)(2,1)S(1)} %get-tuple-element.23), channel_id=1, source_target_pairs={{0,4},{2,6},{4,0},{6,2},{8,12},{10,14},{12,8},{14,10},{16,20},{18,... | collective-permute-start | bytes 294920 | tf_op jit(solution)/shard_map/ppermute | solution.py:318
  4.2 6.7 %collective-permute-start.2 = (bf16[3,128,128]{2,1,0:T(8,128)(2,1)S(1)}, bf16[3,128,128]{2,1,0:T(8,128)(2,1)S(1)}, u32[]{:S(2)}, u32[]{:S(2)}) collective-permute-start(bf16[3,128,128]{2,1,0:T(8,128)(2,1)S(1)} %get-tuple-element.24), channel_id=1, source_target_pairs={{0,6},{2,4},{4,2},{6,0},{8,14},{10,12},{12,10},{14,8},{16,22},{18,... | collective-permute-start | bytes 294920 | tf_op jit(solution)/shard_map/ppermute | solution.py:318
  5.7 54.9 %collective-permute-start.17 = (bf16[64,8192]{1,0:T(8,128)(2,1)}, bf16[64,8192]{1,0:T(8,128)(2,1)S(1)}, u32[]{:S(2)}, u32[]{:S(2)}) collective-permute-start(bf16[64,8192]{1,0:T(8,128)(2,1)} %own_ref.1), channel_id=1, source_target_pairs={{0,1},{1,0},{2,3},{3,2},{4,5},{5,4},{6,7},{7,6},{8,9},{9,8},{10,11... | collective-permute-start | bytes 3145736 | tf_op jit(solution)/shard_map/ppermute | solution.py:315
  6.9 5.4 %collective-permute-start.3 = (bf16[3,128,128]{2,1,0:T(8,128)(2,1)S(1)}, bf16[3,128,128]{2,1,0:T(8,128)(2,1)S(1)}, u32[]{:S(2)}, u32[]{:S(2)}) collective-permute-start(bf16[3,128,128]{2,1,0:T(8,128)(2,1)S(1)} %get-tuple-element.25), channel_id=1, source_target_pairs={{0,8},{2,10},{4,12},{6,14},{8,0},{10,2},{12,4},{14,6},{16,24},{18,... | collective-permute-start | bytes 294920 | tf_op jit(solution)/shard_map/ppermute | solution.py:318
  7.1 7.6 %collective-permute-start.4 = (bf16[3,128,128]{2,1,0:T(8,128)(2,1)S(1)}, bf16[3,128,128]{2,1,0:T(8,128)(2,1)S(1)}, u32[]{:S(2)}, u32[]{:S(2)}) collective-permute-start(bf16[3,128,128]{2,1,0:T(8,128)(2,1)S(1)} %get-tuple-element.26), channel_id=1, source_target_pairs={{0,10},{2,8},{4,14},{6,12},{8,2},{10,0},{12,6},{14,4},{16,26},{18,... | collective-permute-start | bytes 294920 | tf_op jit(solution)/shard_map/ppermute | solution.py:318
  9.0 6.6 %collective-permute-start.5 = (bf16[3,128,128]{2,1,0:T(8,128)(2,1)S(1)}, bf16[3,128,128]{2,1,0:T(8,128)(2,1)S(1)}, u32[]{:S(2)}, u32[]{:S(2)}) collective-permute-start(bf16[3,128,128]{2,1,0:T(8,128)(2,1)S(1)} %get-tuple-element.27), channel_id=1, source_target_pairs={{0,12},{2,14},{4,8},{6,10},{8,4},{10,6},{12,0},{14,2},{16,28},{18,... | collective-permute-start | bytes 294920 | tf_op jit(solution)/shard_map/ppermute | solution.py:318
  10.9 8.5 %collective-permute-start.6 = (bf16[3,128,128]{2,1,0:T(8,128)(2,1)S(1)}, bf16[3,128,128]{2,1,0:T(8,128)(2,1)S(1)}, u32[]{:S(2)}, u32[]{:S(2)}) collective-permute-start(bf16[3,128,128]{2,1,0:T(8,128)(2,1)S(1)} %get-tuple-element.28), channel_id=1, source_target_pairs={{0,14},{2,12},{4,10},{6,8},{8,6},{10,4},{12,2},{14,0},{16,30},{18,... | collective-permute-start | bytes 294920 | tf_op jit(solution)/shard_map/ppermute | solution.py:318
  12.3 10.4 %collective-permute-start.7 = (bf16[3,128,128]{2,1,0:T(8,128)(2,1)S(1)}, bf16[3,128,128]{2,1,0:T(8,128)(2,1)S(1)}, u32[]{:S(2)}, u32[]{:S(2)}) collective-permute-start(bf16[3,128,128]{2,1,0:T(8,128)(2,1)S(1)} %get-tuple-element.29), channel_id=1, source_target_pairs={{0,16},{2,18},{4,20},{6,22},{8,24},{10,26},{12,28},{14,30},{16,0},... | collective-permute-start | bytes 294920 | tf_op jit(solution)/shard_map/ppermute | solution.py:318
  14.7 12.9 %collective-permute-start.8 = (bf16[3,128,128]{2,1,0:T(8,128)(2,1)S(1)}, bf16[3,128,128]{2,1,0:T(8,128)(2,1)S(1)}, u32[]{:S(2)}, u32[]{:S(2)}) collective-permute-start(bf16[3,128,128]{2,1,0:T(8,128)(2,1)S(1)} %get-tuple-element.30), channel_id=1, source_target_pairs={{0,18},{2,16},{4,22},{6,20},{8,26},{10,24},{12,30},{14,28},{16,2},... | collective-permute-start | bytes 294920 | tf_op jit(solution)/shard_map/ppermute | solution.py:318
  15.5 14.3 %collective-permute-start.9 = (bf16[3,128,128]{2,1,0:T(8,128)(2,1)S(1)}, bf16[3,128,128]{2,1,0:T(8,128)(2,1)S(1)}, u32[]{:S(2)}, u32[]{:S(2)}) collective-permute-start(bf16[3,128,128]{2,1,0:T(8,128)(2,1)S(1)} %get-tuple-element.31), channel_id=1, source_target_pairs={{0,20},{2,22},{4,16},{6,18},{8,28},{10,30},{12,24},{14,26},{16,4},... | collective-permute-start | bytes 294920 | tf_op jit(solution)/shard_map/ppermute | solution.py:318
  19.4 13.0 %collective-permute-start.10 = (bf16[3,128,128]{2,1,0:T(8,128)(2,1)S(1)}, bf16[3,128,128]{2,1,0:T(8,128)(2,1)S(1)}, u32[]{:S(2)}, u32[]{:S(2)}) collective-permute-start(bf16[3,128,128]{2,1,0:T(8,128)(2,1)S(1)} %get-tuple-element.32), channel_id=1, source_target_pairs={{0,22},{2,20},{4,18},{6,16},{8,30},{10,28},{12,26},{14,24},{16,6},... | collective-permute-start | bytes 294920 | tf_op jit(solution)/shard_map/ppermute | solution.py:318
  22.6 18.1 %collective-permute-start.11 = (bf16[3,128,128]{2,1,0:T(8,128)(2,1)S(1)}, bf16[3,128,128]{2,1,0:T(8,128)(2,1)S(1)}, u32[]{:S(2)}, u32[]{:S(2)}) collective-permute-start(bf16[3,128,128]{2,1,0:T(8,128)(2,1)S(1)} %get-tuple-element.33), channel_id=1, source_target_pairs={{0,24},{2,26},{4,28},{6,30},{8,16},{10,18},{12,20},{14,22},{16,8},... | collective-permute-start | bytes 294920 | tf_op jit(solution)/shard_map/ppermute | solution.py:318
  27.6 17.3 %collective-permute-start.12 = (bf16[3,128,128]{2,1,0:T(8,128)(2,1)S(1)}, bf16[3,128,128]{2,1,0:T(8,128)(2,1)S(1)}, u32[]{:S(2)}, u32[]{:S(2)}) collective-permute-start(bf16[3,128,128]{2,1,0:T(8,128)(2,1)S(1)} %get-tuple-element.34), channel_id=1, source_target_pairs={{0,26},{2,24},{4,30},{6,28},{8,18},{10,16},{12,22},{14,20},{16,10}... | collective-permute-start | bytes 294920 | tf_op jit(solution)/shard_map/ppermute | solution.py:318
  29.8 17.9 %collective-permute-start.13 = (bf16[3,128,128]{2,1,0:T(8,128)(2,1)S(1)}, bf16[3,128,128]{2,1,0:T(8,128)(2,1)S(1)}, u32[]{:S(2)}, u32[]{:S(2)}) collective-permute-start(bf16[3,128,128]{2,1,0:T(8,128)(2,1)S(1)} %get-tuple-element.35), channel_id=1, source_target_pairs={{0,28},{2,30},{4,24},{6,26},{8,20},{10,22},{12,16},{14,18},{16,12}... | collective-permute-start | bytes 294920 | tf_op jit(solution)/shard_map/ppermute | solution.py:318
  32.4 17.2 %collective-permute-start.14 = (bf16[3,128,128]{2,1,0:T(8,128)(2,1)S(1)}, bf16[3,128,128]{2,1,0:T(8,128)(2,1)S(1)}, u32[]{:S(2)}, u32[]{:S(2)}) collective-permute-start(bf16[3,128,128]{2,1,0:T(8,128)(2,1)S(1)} %get-tuple-element.36), channel_id=1, source_target_pairs={{0,30},{2,28},{4,26},{6,24},{8,22},{10,20},{12,18},{14,16},{16,14}... | collective-permute-start | bytes 294920 | tf_op jit(solution)/shard_map/ppermute | solution.py:318
  49.7 11.0 %copy-start.1 = (bf16[64,8192]{1,0:T(8,128)(2,1)S(1)}, bf16[64,8192]{1,0:T(8,128)(2,1)}, u32[]{:S(2)}) copy-start(bf16[64,8192]{1,0:T(8,128)(2,1)} %own_ref.1) | copy-start | bytes 3145732
  54.7 1.2 copy-start.2
  55.9 22.3 %all-to-all-start = ((bf16[16,128,128]{2,1,0:T(8,128)(2,1)}), bf16[16,128,128]{2,1,0:T(8,128)(2,1)S(1)}, u32[]{:S(2)}, u32[]{:S(2)}) async-start(bf16[16,128,128]{2,1,0:T(8,128)(2,1)} %get-tuple-element.37.att_ref), calls=%async_computation | async-start | bytes 1048576 | tf_op jit(solution)/shard_map/all_to_all | solution.py:313
  78.2 25.3 %all-to-all-start.1 = ((bf16[16,128,128]{2,1,0:T(8,128)(2,1)}), bf16[16,128,128]{2,1,0:T(8,128)(2,1)S(1)}, u32[]{:S(2)}, u32[]{:S(2)}) async-start(bf16[16,128,128]{2,1,0:T(8,128)(2,1)} %project_back.1), calls=%async_computation.1 | async-start | bytes 1048576 | tf_op jit(solution)/shard_map/all_to_all | solution.py:313
  91.4 2.5 %copy-start.5 = (f32[128,4096]{1,0:T(8,128)}, f32[128,4096]{1,0:T(8,128)S(1)}, u32[]{:S(2)}) copy-start(f32[128,4096]{1,0:T(8,128)S(1)} %fusion.7) | copy-start | bytes 6291460
  92.4 11.2 %copy-start.3 = (bf16[16,3,128,128]{3,2,1,0:T(8,128)(2,1)S(1)}, bf16[16,3,128,128]{3,2,1,0:T(8,128)(2,1)}, u32[]{:S(2)}) copy-start(bf16[16,3,128,128]{3,2,1,0:T(8,128)(2,1)} %copy-done.2) | copy-start | bytes 4718596
  92.4 28.0 %collective-permute-start.16 = (bf16[64,4096]{1,0:T(8,128)(2,1)}, bf16[64,4096]{1,0:T(8,128)(2,1)}, u32[]{:S(2)}, u32[]{:S(2)}) collective-permute-start(bf16[64,4096]{1,0:T(8,128)(2,1)} %dynamic-slice_convert_fusion), channel_id=1, source_target_pairs={{0,1},{1,0},{2,3},{3,2},{4,5},{5,4},{6,7},{7,6},{8,9},{9,8},{10,11... | collective-permute-start | bytes 1572872 | tf_op jit(solution)/shard_map/ppermute | solution.py:336
  112.3 42.5 %all-to-all-start.2 = ((bf16[16,3,128,128]{3,2,1,0:T(8,128)(2,1)}), bf16[16,3,128,128]{3,2,1,0:T(8,128)(2,1)S(1)}, u32[]{:S(2)}, u32[]{:S(2)}) async-start(bf16[16,3,128,128]{3,2,1,0:T(8,128)(2,1)} %attend_grad.1), calls=%async_computation.2 | async-start | bytes 3145728 | tf_op jit(solution)/shard_map/all_to_all | solution.py:313
  118.6 14.6 %copy-start.4 = (f32[128,4096]{1,0:T(8,128)S(1)}, f32[128,4096]{1,0:T(8,128)}, u32[]{:S(2)}) copy-start(f32[128,4096]{1,0:T(8,128)} %fusion.4) | copy-start | bytes 6291460
  120.0 13.2 %collective-permute-start.15 = (bf16[64,4096]{1,0:T(8,128)(2,1)S(1)}, bf16[64,4096]{1,0:T(8,128)(2,1)S(1)}, u32[]{:S(2)}, u32[]{:S(2)}) collective-permute-start(bf16[64,4096]{1,0:T(8,128)(2,1)S(1)} %dynamic-slice_convert_fusion.1), channel_id=1, source_target_pairs={{0,1},{1,0},{2,3},{3,2},{4,5},{5,4},{6,7},{7,6},{8,9},{9,8},{10,11... | collective-permute-start | bytes 1572872 | tf_op jit(solution)/shard_map/ppermute | solution.py:336

commit v6 on v5

--- a/solution.py
+++ b/solution.py
@@ -11,7 +11,7 @@
 
 HD = 128
 LOG2E = math.log2(math.e)
-MIX_PARTS = 2
+MIX_PARTS = 4
 VMEM_LIMIT = 20 * 1024 * 1024
 
 
@@ -29,6 +29,7 @@
 
 
 CHUNK = 16
+PLANE = 4
 
 
 def py_loop(lo, hi, body, carry):
@@ -87,13 +88,14 @@
         for x_ref, place in ((own_ref, turn_ref[0]), (other_ref, 1 - turn_ref[0])):
             x_buf[pl.ds(pl.multiple_of(place * half, half), half)] = x_ref[...]
 
-    y = dot_nt(x_buf[...], w_ref[...]).astype(jnp.bfloat16)
+    y = dot_nt(w_ref[...], x_buf[...])
     for h in range(out_ref.shape[0]):
-        out_ref[h] = y[:, h * HD : (h + 1) * HD]
-
-
-def forward_kernel(step, me_ref, *refs):
-    *parts, qkv_ref, att_ref, lse_ref, v_t, s_buf = refs
+        out_ref[h] = y[h * HD : (h + 1) * HD].T.astype(jnp.bfloat16)
+
+
+def forward_kernel(step, outer, me_ref, *refs):
+    parts, rest = refs[:-5 - outer], refs[-5 - outer :]
+    qkv_ref, att_ref, lse_ref, *sent, v_t, s_buf = rest
     me = me_ref[0]
     for k, part in enumerate(parts):
         qkv_ref[me ^ k] = part[...]
@@ -126,6 +128,18 @@
             acc = acc + dot_nn(v_t[j], (s_buf[i % 2, j] * inverse).astype(jnp.bfloat16))
         att_ref[i * per : (i + 1) * per] = acc.T.astype(jnp.bfloat16).reshape(per, unit, HD)
         lse_ref[i] = top * scale + jnp.log2(total)
+    for d, ref in enumerate(sent):
+        for e in range(PLANE):
+            ref[e] = att_ref[me ^ (PLANE * d + e)]
+
+
+def gather_kernel(me_ref, *refs):
+    *parts, out_ref = refs
+    own, others = parts[: len(parts) - PLANE + 1], parts[len(parts) - PLANE + 1 :]
+    for d, ref in enumerate(own):
+        out_ref[me_ref[0] ^ (PLANE * d)] = ref[0]
+        for e in range(1, PLANE):
+            out_ref[me_ref[0] ^ (PLANE * d + e)] = others[e - 1][d]
 
 
 def backward_kernel(step, qkv_ref, g_ref, att_ref, lse_ref, out_ref, k_t, dq_t, delta):
@@ -205,7 +219,7 @@
         scratch_shapes=[pltpu.VMEM((CHUNK * heads, CHUNK * heads), jnp.bfloat16)],
         compiler_params=pltpu.CompilerParams(vmem_limit_bytes=VMEM_LIMIT),
         name="split_heads",
-    )(me, jnp.transpose(qkv, (0, 2, 1, 3)))
+    )(me, pltpu.with_memory_space_constraint(jnp.transpose(qkv, (0, 2, 1, 3)), pltpu.HBM))
 
 
 def join_heads(grads):
@@ -227,7 +241,7 @@
 def project_back(turn, own, other, weights):
     half, width = own.shape
     heads = weights.shape[0] // HD
-    group = 2
+    group = 4
     return pl.pallas_call(
         back_kernel,
         grid=(heads // group,),
@@ -239,7 +253,7 @@
         ],
         out_specs=pl.BlockSpec((group, 2 * half, HD), lambda b: (b, 0, 0)),
         scratch_shapes=[pltpu.VMEM((2 * half, width), jnp.bfloat16)],
-        compiler_params=pltpu.CompilerParams(vmem_limit_bytes=VMEM_LIMIT),
+        compiler_params=pltpu.CompilerParams(vmem_limit_bytes=32 * 1024 * 1024),
         cost_estimate=pl.CostEstimate(
             flops=4 * half * width * heads * HD,
             transcendentals=0,
@@ -251,19 +265,21 @@
 
 def attend(me, parts, step):
     chunks = len(parts)
+    outer = chunks // PLANE
     unit = parts[0].shape[1]
     length = chunks * unit
     blocks = length // step
     area = length * length // 2
     return pl.pallas_call(
-        functools.partial(forward_kernel, step),
+        functools.partial(forward_kernel, step, outer),
         out_shape=(
             jax.ShapeDtypeStruct((chunks, 3, unit, HD), jnp.bfloat16),
             jax.ShapeDtypeStruct((chunks, unit, HD), jnp.bfloat16),
             jax.ShapeDtypeStruct((blocks, 1, step), jnp.float32),
+            *[jax.ShapeDtypeStruct((PLANE, unit, HD), jnp.bfloat16)] * outer,
         ),
         in_specs=[in_smem(), *in_vmem(chunks)],
-        out_specs=tuple(in_vmem(3)),
+        out_specs=tuple(in_vmem(3 + outer)),
         scratch_shapes=[
             pltpu.VMEM((blocks, HD, step), jnp.bfloat16),
             pltpu.VMEM((2, blocks, step, step), jnp.float32),
@@ -274,6 +290,19 @@
         ),
         name="attend",
     )(me, *parts)
+
+
+def gather_heads(me, own, others):
+    chunks = PLANE * len(own)
+    shape = (chunks, *own[0].shape[1:])
+    return pl.pallas_call(
+        gather_kernel,
+        out_shape=jax.ShapeDtypeStruct(shape, jnp.bfloat16),
+        in_specs=[in_smem(), *in_vmem(len(own) + PLANE - 1)],
+        out_specs=in_vmem(1)[0],
+        compiler_params=pltpu.CompilerParams(vmem_limit_bytes=VMEM_LIMIT),
+        name="gather_heads",
+    )(me, *own, *others)
 
 
 def attend_grad(qkv, g, att, lse, step):
@@ -318,10 +347,16 @@
         parts[k] = lax.ppermute(parts[k], "ctx", [(i, i ^ k) for i in range(heads)])
     g = project_back(turn.reshape(1), grad_out, other_out, attn_out)
     g = spread(g)
-    mine, att, lse = attend(me, parts, step)
-    local = spread(att)
+    mine, att, lse, *own = attend(me, parts, step)
+    for d in range(1, len(own)):
+        own[d] = lax.ppermute(own[d], "ctx", [(i, i ^ (PLANE * d)) for i in range(heads)])
     grads = attend_grad(mine, g, att, lse, step)
+    others = []
+    for e in range(1, PLANE):
+        sent = jnp.stack([x[e] for x in own])
+        others.append(lax.ppermute(sent, "ctx", [(i, i ^ e) for i in range(heads)]))
     grads = spread(grads)
+    local = gather_heads(me, own, others)
     pieces = []
     part = width // MIX_PARTS
     for c in range(MIX_PARTS):
@@ -426,7 +461,7 @@
     out_specs = (P(("ctx", "tp"), None), P("ctx", "tp", None, None))
 
     def whole(qkv, grad_out, attn_out):
-        split = qkv.shape[1] == ctx * tp and tp == 2 and ctx & (ctx - 1) == 0
+        split = qkv.shape[1] == ctx * tp and tp == 2 and ctx >= 2 * PLANE and ctx & (ctx - 1) == 0
         step = jax.shard_map(
             by_head if split else by_rows,
             mesh=mesh,

time: 158 us -> 183 us (1.16)
  waiting for transfers between devices: 52.9 us -> 72.3 us
  matrix products: 16.8 us -> 22 us
  other arithmetic: 3.03 us -> 6.08 us
  Pallas kernels: 35.4 us -> 32.5 us
    ppermute x0 -> x6, waiting for transfers between devices: none -> 16.5 us  [the longest x3 11.1 us: by_head(): lax.ppermute(own[d], 'ctx', [(i, i ^ PLANE * d) for i in range(heads)])]
    ppermute x2 -> x4, waiting for transfers between devices: 11.4 us -> 2.77 us  [by_head(): got = lax.ppermute(sent.astype(jnp.bfloat16), 'tp', swap)]
    all_to_all x3 -> x2, waiting for transfers between devices: 20 us -> 28.1 us  [spread(): return lax.all_to_all(x, 'ctx', 0, 0, tiled=True)]
    ppermute x0 -> x6, starting transfers between devices: none -> 6.28 us  [the longest x3 3.15 us: by_head(): lax.ppermute(own[d], 'ctx', [(i, i ^ PLANE * d) for i in range(heads)])]
    all_to_all x3 -> x2, starting transfers between devices: 17 us -> 11.6 us  [spread(): return lax.all_to_all(x, 'ctx', 0, 0, tiled=True)]
    dot_general x2 -> x4, matrix products: 16.8 us -> 22 us  [by_head(): jnp.einsum('hrd,hdm->rm', local, weights[:, :, c * part:(c + 1) * part],...]
    ppermute x15, starting transfers between devices: 23.7 us -> 19.2 us  [by_head(): parts[k] = lax.ppermute(parts[k], 'ctx', [(i, i ^ k) for i in range(heads)])]
    ppermute x15, waiting for transfers between devices: 21.5 us -> 24.9 us  [by_head(): parts[k] = lax.ppermute(parts[k], 'ctx', [(i, i ^ k) for i in range(heads)])]
  transfers between devices with their start and end apart: 21 -> 28, of which waited for: 10 -> 15; matrix products, arithmetic and copies ran while one was open for 14% -> 18% of each run, Pallas kernels for 20% -> 13%
where the time goes in v6:
time: 183 us; the launch traced here: 182 us
  waiting for transfers between devices  72.3 us (40%)
  starting transfers between devices  42.2 us (23%)
  Pallas kernels  32.5 us (18%)
  matrix products  22 us (12%)
  local copies, waits for them, and re-layouts  6.25 us (3%)
  other arithmetic  6.08 us (3%)
    all_to_all x2, waiting for transfers between devices, spread(): return lax.all_to_all(x, 'ctx', 0, 0, tiled=True)  28.1 us
    ppermute x15, waiting for transfers between devices, by_head(): parts[k] = lax.ppermute(parts[k], 'ctx', [(i, i ^ k) for i in range(heads)])  24.9 us
    dot_general x4, matrix products, by_head(): jnp.einsum('hrd,hdm->rm', local, weights[:, :, c * part:(c + 1) * part],...  22 us
    ppermute x15, starting transfers between devices, by_head(): parts[k] = lax.ppermute(parts[k], 'ctx', [(i, i ^ k) for i in range(heads)])  19.2 us
    pallas_call x1, Pallas kernels, project_back(): pl.pallas_call(back_kernel, grid=(heads // group,), out_shape=jax.ShapeDt...  15.3 us
    all_to_all x2, starting transfers between devices, spread(): return lax.all_to_all(x, 'ctx', 0, 0, tiled=True)  11.6 us
    ppermute x3, waiting for transfers between devices, by_head(): lax.ppermute(own[d], 'ctx', [(i, i ^ PLANE * d) for i in range(heads)])  11.1 us
    pallas_call x1, Pallas kernels, attend_grad(): pl.pallas_call(functools.partial(backward_kernel, step), out_shape=jax.Sh...  7.63 us
  transfers between devices with their start and end apart: 28, of which 15 were waited for; matrix products, arithmetic and copies ran while one was open for 18% of the time, Pallas kernels for 13%

profile of v6, /device:TPU:13, one launch (start us, length us, event | category | flops | bytes accessed | tf_op | source)
XLA Modules:
  0.0 182.1 jit_solution(3264614968232882658)
XLA Ops:
  0.6 2.4 %split_heads.1 = (bf16[3,128,128]{2,1,0:T(8,128)(2,1)S(1)}, bf16[3,128,128]{2,1,0:T(8,128)(2,1)S(1)}, bf16[3,128,128]{2,1,0:T(8,128)(2,1)S(1)}, bf16[3,128,128]{...) custom-call(s32[1]{0:T(128)} %bitcast.me_ref, ...), custom_call_target="tpu_custom_call" | custom-call | tf_op jit(solution)/shard_map/split_heads/pallas_call | solution.py:213
  5.6 1.6 collective-permute-start.4
  8.0 1.8 %collective-permute-start.6 = (bf16[3,128,128]{2,1,0:T(8,128)(2,1)S(1)}, bf16[3,128,128]{2,1,0:T(8,128)(2,1)S(1)}, u32[]{:S(2)}, u32[]{:S(2)}) collective-permute-start(bf16[3,128,128]{2,1,0:T(8,128)(2,1)S(1)} %get-tuple-element.32), channel_id=1, source_target_pairs={{0,14},{2,12},{4,10},{6,8},{8,6},{10,4},{12,2},{14,0},{16,30},{18,... | collective-permute-start | bytes 294920 | tf_op jit(solution)/shard_map/ppermute | solution.py:347
  10.7 2.3 %collective-permute-start.7 = (bf16[3,128,128]{2,1,0:T(8,128)(2,1)S(1)}, bf16[3,128,128]{2,1,0:T(8,128)(2,1)S(1)}, u32[]{:S(2)}, u32[]{:S(2)}) collective-permute-start(bf16[3,128,128]{2,1,0:T(8,128)(2,1)S(1)} %get-tuple-element.33), channel_id=1, source_target_pairs={{0,16},{2,18},{4,20},{6,22},{8,24},{10,26},{12,28},{14,30},{16,0},... | collective-permute-start | bytes 294920 | tf_op jit(solution)/shard_map/ppermute | solution.py:347
  13.5 1.8 %collective-permute-start.9 = (bf16[3,128,128]{2,1,0:T(8,128)(2,1)S(1)}, bf16[3,128,128]{2,1,0:T(8,128)(2,1)S(1)}, u32[]{:S(2)}, u32[]{:S(2)}) collective-permute-start(bf16[3,128,128]{2,1,0:T(8,128)(2,1)S(1)} %get-tuple-element.35), channel_id=1, source_target_pairs={{0,20},{2,22},{4,16},{6,18},{8,28},{10,30},{12,24},{14,26},{16,4},... | collective-permute-start | bytes 294920 | tf_op jit(solution)/shard_map/ppermute | solution.py:347
  15.3 5.4 %collective-permute-start.10 = (bf16[3,128,128]{2,1,0:T(8,128)(2,1)S(1)}, bf16[3,128,128]{2,1,0:T(8,128)(2,1)S(1)}, u32[]{:S(2)}, u32[]{:S(2)}) collective-permute-start(bf16[3,128,128]{2,1,0:T(8,128)(2,1)S(1)} %get-tuple-element.36), channel_id=1, source_target_pairs={{0,22},{2,20},{4,18},{6,16},{8,30},{10,28},{12,26},{14,24},{16,6},... | collective-permute-start | bytes 294920 | tf_op jit(solution)/shard_map/ppermute | solution.py:347
  21.6 7.4 %collective-permute-done.8.refs_9_ = bf16[3,128,128]{2,1,0:T(8,128)(2,1)S(1)} collective-permute-done((bf16[3,128,128]{2,1,0:T(8,128)(2,1)S(1)}, bf16[3,128,128]{2,1,0:T(8,128)(2,1)S(1)}, u32[]{:S(2)}, u32[]{:S(2)}) %collective-permute-start.8) | collective-permute-done | bytes 98336 | tf_op jit(solution)/shard_map/ppermute | solution.py:347
  29.0 2.1 %collective-permute-done.9.refs_10_ = bf16[3,128,128]{2,1,0:T(8,128)(2,1)S(1)} collective-permute-done((bf16[3,128,128]{2,1,0:T(8,128)(2,1)S(1)}, bf16[3,128,128]{2,1,0:T(8,128)(2,1)S(1)}, u32[]{:S(2)}, u32[]{:S(2)}) %collective-permute-start.9) | collective-permute-done | bytes 98336 | tf_op jit(solution)/shard_map/ppermute | solution.py:347
  31.1 2.2 %collective-permute-start.14 = (bf16[3,128,128]{2,1,0:T(8,128)(2,1)S(1)}, bf16[3,128,128]{2,1,0:T(8,128)(2,1)S(1)}, u32[]{:S(2)}, u32[]{:S(2)}) collective-permute-start(bf16[3,128,128]{2,1,0:T(8,128)(2,1)S(1)} %get-tuple-element.40), channel_id=1, source_target_pairs={{0,30},{2,28},{4,26},{6,24},{8,22},{10,20},{12,18},{14,16},{16,14}... | collective-permute-start | bytes 294920 | tf_op jit(solution)/shard_map/ppermute | solution.py:347
  33.3 2.9 %collective-permute-done.10.refs_11_ = bf16[3,128,128]{2,1,0:T(8,128)(2,1)S(1)} collective-permute-done((bf16[3,128,128]{2,1,0:T(8,128)(2,1)S(1)}, bf16[3,128,128]{2,1,0:T(8,128)(2,1)S(1)}, u32[]{:S(2)}, u32[]{:S(2)}) %collective-permute-start.10) | collective-permute-done | bytes 98336 | tf_op jit(solution)/shard_map/ppermute | solution.py:347
  36.2 4.4 %collective-permute-done.11.refs_12_ = bf16[3,128,128]{2,1,0:T(8,128)(2,1)S(1)} collective-permute-done((bf16[3,128,128]{2,1,0:T(8,128)(2,1)S(1)}, bf16[3,128,128]{2,1,0:T(8,128)(2,1)S(1)}, u32[]{:S(2)}, u32[]{:S(2)}) %collective-permute-start.11) | collective-permute-done | bytes 98336 | tf_op jit(solution)/shard_map/ppermute | solution.py:347
  40.6 2.6 %collective-permute-done.12.refs_13_ = bf16[3,128,128]{2,1,0:T(8,128)(2,1)S(1)} collective-permute-done((bf16[3,128,128]{2,1,0:T(8,128)(2,1)S(1)}, bf16[3,128,128]{2,1,0:T(8,128)(2,1)S(1)}, u32[]{:S(2)}, u32[]{:S(2)}) %collective-permute-start.12) | collective-permute-done | bytes 98336 | tf_op jit(solution)/shard_map/ppermute | solution.py:347
  44.8 2.3 %collective-permute-done.14.refs_15_ = bf16[3,128,128]{2,1,0:T(8,128)(2,1)S(1)} collective-permute-done((bf16[3,128,128]{2,1,0:T(8,128)(2,1)S(1)}, bf16[3,128,128]{2,1,0:T(8,128)(2,1)S(1)}, u32[]{:S(2)}, u32[]{:S(2)}) %collective-permute-start.14) | collective-permute-done | bytes 98336 | tf_op jit(solution)/shard_map/ppermute | solution.py:347
  47.1 4.3 %attend.1 = (bf16[16,3,128,128]{3,2,1,0:T(8,128)(2,1)S(1)}, bf16[16,128,128]{2,1,0:T(8,128)(2,1)S(1)}, f32[4,1,512]{2,1,0:T(1,128)S(1)}, bf16[4,128,128]{2,1,0:T...) custom-call(s32[1]{0:T(128)} %bitcast.me_ref, ...), custom_call_target="tpu_custom_call" | custom-call | flops 1073741824 | bytes 2097152 | tf_op jit(solution)/shard_map/attend/pallas_call | solution.py:273
  52.2 3.1 %collective-permute-start.16 = (bf16[4,128,128]{2,1,0:T(8,128)(2,1)S(1)}, bf16[4,128,128]{2,1,0:T(8,128)(2,1)S(1)}, u32[]{:S(2)}, u32[]{:S(2)}) collective-permute-start(bf16[4,128,128]{2,1,0:T(8,128)(2,1)S(1)} %get-tuple-element.43), channel_id=1, source_target_pairs={{0,16},{2,18},{4,20},{6,22},{8,24},{10,26},{12,28},{14,30},{16,0},... | collective-permute-start | bytes 393224 | tf_op jit(solution)/shard_map/ppermute | solution.py:352
  55.4 11.1 %collective-permute-done.17.refs_3_ = bf16[4,128,128]{2,1,0:T(8,128)(2,1)S(1)} collective-permute-done((bf16[4,128,128]{2,1,0:T(8,128)(2,1)S(1)}, bf16[4,128,128]{2,1,0:T(8,128)(2,1)S(1)}, u32[]{:S(2)}, u32[]{:S(2)}) %collective-permute-start.17) | collective-permute-done | bytes 131104 | tf_op jit(solution)/shard_map/ppermute | solution.py:352
  71.0 2.1 %collective-permute-done.19.refs_5_ = bf16[4,128,128]{2,1,0:T(8,128)(2,1)S(1)} collective-permute-done((bf16[4,128,128]{2,1,0:T(8,128)(2,1)S(1)}, bf16[4,128,128]{2,1,0:T(8,128)(2,1)S(1)}, u32[]{:S(2)}, u32[]{:S(2)}) %collective-permute-start.19) | collective-permute-done | bytes 131104 | tf_op jit(solution)/shard_map/ppermute | solution.py:357
  73.1 3.3 %collective-permute-done.20.refs_6_ = bf16[4,128,128]{2,1,0:T(8,128)(2,1)S(1)} collective-permute-done((bf16[4,128,128]{2,1,0:T(8,128)(2,1)S(1)}, bf16[4,128,128]{2,1,0:T(8,128)(2,1)S(1)}, u32[]{:S(2)}, u32[]{:S(2)}) %collective-permute-start.20) | collective-permute-done | bytes 131104 | tf_op jit(solution)/shard_map/ppermute | solution.py:357
  76.4 4.7 %fusion.17 = f32[128,2048]{1,0:T(8,128)S(1)} fusion(bf16[16,128,128]{2,1,0:T(8,128)(2,1)S(1)} %gather_heads.1, bf16[16,128,8192]{2,1,0:T(8,128)(2,1)} %bitcast.17), kind=kOutput, calls=%fused_computation.11 | convolution fusion | flops 1073741824 | bytes 9961472 | tf_op jit(solution)/shard_map/hrd,hdm->rm/dot_general | solution.py:363
  83.1 5.7 %fusion.14 = f32[128,2048]{1,0:T(8,128)} fusion(bf16[16,128,128]{2,1,0:T(8,128)(2,1)S(1)} %gather_heads.1, bf16[16,128,8192]{2,1,0:T(8,128)(2,1)} %bitcast.18), kind=kOutput, calls=%fused_computation.10 | convolution fusion | flops 1073741824 | bytes 9961472 | tf_op jit(solution)/shard_map/hrd,hdm->rm/dot_general | solution.py:363
  88.9 5.8 %fusion.11 = f32[128,2048]{1,0:T(8,128)} fusion(bf16[16,128,128]{2,1,0:T(8,128)(2,1)S(1)} %gather_heads.1, bf16[16,128,8192]{2,1,0:T(8,128)(2,1)} %bitcast.19), kind=kOutput, calls=%fused_computation.9 | convolution fusion | flops 1073741824 | bytes 9961472 | tf_op jit(solution)/shard_map/hrd,hdm->rm/dot_general | solution.py:363
  94.7 15.3 %project_back.1 = bf16[16,128,128]{2,1,0:T(8,128)(2,1)} custom-call(s32[1]{0:T(128)} %bitcast.7.turn_ref, bf16[64,8192]{1,0:T(8,128)(2,1)S(1)} %copy-done, bf16[64,8192]{1,0:T(8,128)(2,1)S(1)} %collective-permute-done.25.other_ref, bf16[2048,8192]{1,0:T(8,128)(2,1)} %w_ref.1), custom_call_target="tpu_custom_call" | custom-call | flops 4294967296 | bytes 33554432 | tf_op jit(solution)/shard_map/project_back/pallas_call | solution.py:245
  110.0 7.0 %all-to-all-start = ((bf16[16,128,128]{2,1,0:T(8,128)(2,1)}), bf16[16,128,128]{2,1,0:T(8,128)(2,1)S(1)}, u32[]{:S(2)}, u32[]{:S(2)}) async-start(bf16[16,128,128]{2,1,0:T(8,128)(2,1)} %project_back.1), calls=%async_computation | async-start | bytes 1048576 | tf_op jit(solution)/shard_map/all_to_all | solution.py:342
  117.0 1.8 dynamic-slice_convert_fusion.1
  119.9 1.8 dynamic-slice_convert_fusion.2
  122.0 5.7 %fusion.8 = f32[128,2048]{1,0:T(8,128)} fusion(bf16[16,128,128]{2,1,0:T(8,128)(2,1)S(1)} %gather_heads.1, bf16[16,128,8192]{2,1,0:T(8,128)(2,1)} %bitcast.20), kind=kOutput, calls=%fused_computation.8 | convolution fusion | flops 1073741824 | bytes 9961472 | tf_op jit(solution)/shard_map/hrd,hdm->rm/dot_general | solution.py:363
  127.7 3.1 %all-to-all-done.g_ref = bf16[16,128,128]{2,1,0:T(8,128)(2,1)S(1)} async-done(((bf16[16,128,128]{2,1,0:T(8,128)(2,1)}), bf16[16,128,128]{2,1,0:T(8,128)(2,1)S(1)}, u32[]{:S(2)}, u32[]{:S(2)}) %all-to-all-start) | async-done | bytes 524320 | tf_op jit(solution)/shard_map/all_to_all | solution.py:342
  130.8 7.6 %attend_grad.1 = bf16[16,3,128,128]{3,2,1,0:T(8,128)(2,1)} custom-call(bf16[16,3,128,128]{3,2,1,0:T(8,128)(2,1)S(1)} %copy-done.2, bf16[16,128,128]{2,1,0:T(8,128)(2,1)S(1)} %all-to-all-done.g_ref, bf16[16,128,128]{2,1,0:T(8,128)(2,1)S(1)} %copy-done.4, f32[4,1,512]{2,1,0:T(1,128)S(1)} %get-tuple-element.47.lse_ref), custom_call_target="tpu_custom_call" | custom-call | flops 2684354560 | bytes 4194304 | tf_op jit(solution)/shard_map/attend_grad/pallas_call | solution.py:313
  138.5 4.6 %all-to-all-start.1 = ((bf16[16,3,128,128]{3,2,1,0:T(8,128)(2,1)}), bf16[16,3,128,128]{3,2,1,0:T(8,128)(2,1)S(1)}, u32[]{:S(2)}, u32[]{:S(2)}) async-start(bf16[16,3,128,128]{3,2,1,0:T(8,128)(2,1)} %attend_grad.1), calls=%async_computation.1 | async-start | bytes 3145728 | tf_op jit(solution)/shard_map/all_to_all | solution.py:342
  148.9 2.8 %collective-permute-done.21 = bf16[64,2048]{1,0:T(8,128)(2,1)S(1)} collective-permute-done((bf16[64,2048]{1,0:T(8,128)(2,1)S(1)}, bf16[64,2048]{1,0:T(8,128)(2,1)S(1)}, u32[]{:S(2)}, u32[]{:S(2)}) %collective-permute-start.21) | collective-permute-done | bytes 262176 | tf_op jit(solution)/shard_map/ppermute | solution.py:371
  154.2 25.0 %all-to-all-done.1.x_ref = bf16[16,3,128,128]{3,2,1,0:T(8,128)(2,1)S(1)} async-done(((bf16[16,3,128,128]{3,2,1,0:T(8,128)(2,1)}), bf16[16,3,128,128]{3,2,1,0:T(8,128)(2,1)S(1)}, u32[]{:S(2)}, u32[]{:S(2)}) %all-to-all-start.1) | async-done | bytes 1572896 | tf_op jit(solution)/shard_map/all_to_all | solution.py:342
  179.2 2.9 %join_heads.1 = f32[128,3,16,128]{3,2,1,0:T(8,128)} custom-call(bf16[16,3,128,128]{3,2,1,0:T(8,128)(2,1)S(1)} %all-to-all-done.1.x_ref), custom_call_target="tpu_custom_call" | custom-call | tf_op jit(solution)/shard_map/join_heads/pallas_call | solution.py:228
  (62 shorter events, 24.3 us)
Async XLA Ops:
  3.0 4.2 %collective-permute-start = (bf16[3,128,128]{2,1,0:T(8,128)(2,1)S(1)}, bf16[3,128,128]{2,1,0:T(8,128)(2,1)S(1)}, u32[]{:S(2)}, u32[]{:S(2)}) collective-permute-start(bf16[3,128,128]{2,1,0:T(8,128)(2,1)S(1)} %get-tuple-element.26), channel_id=1, source_target_pairs={{0,2},{2,0},{4,6},{6,4},{8,10},{10,8},{12,14},{14,12},{16,18},{18,... | collective-permute-start | bytes 294920 | tf_op jit(solution)/shard_map/ppermute | solution.py:347
  3.7 4.3 %collective-permute-start.1 = (bf16[3,128,128]{2,1,0:T(8,128)(2,1)S(1)}, bf16[3,128,128]{2,1,0:T(8,128)(2,1)S(1)}, u32[]{:S(2)}, u32[]{:S(2)}) collective-permute-start(bf16[3,128,128]{2,1,0:T(8,128)(2,1)S(1)} %get-tuple-element.27), channel_id=1, source_target_pairs={{0,4},{2,6},{4,0},{6,2},{8,12},{10,14},{12,8},{14,10},{16,20},{18,... | collective-permute-start | bytes 294920 | tf_op jit(solution)/shard_map/ppermute | solution.py:347
  4.0 6.7 %collective-permute-start.2 = (bf16[3,128,128]{2,1,0:T(8,128)(2,1)S(1)}, bf16[3,128,128]{2,1,0:T(8,128)(2,1)S(1)}, u32[]{:S(2)}, u32[]{:S(2)}) collective-permute-start(bf16[3,128,128]{2,1,0:T(8,128)(2,1)S(1)} %get-tuple-element.28), channel_id=1, source_target_pairs={{0,6},{2,4},{4,2},{6,0},{8,14},{10,12},{12,10},{14,8},{16,22},{18,... | collective-permute-start | bytes 294920 | tf_op jit(solution)/shard_map/ppermute | solution.py:347
  5.4 7.5 %collective-permute-start.3 = (bf16[3,128,128]{2,1,0:T(8,128)(2,1)S(1)}, bf16[3,128,128]{2,1,0:T(8,128)(2,1)S(1)}, u32[]{:S(2)}, u32[]{:S(2)}) collective-permute-start(bf16[3,128,128]{2,1,0:T(8,128)(2,1)S(1)} %get-tuple-element.29), channel_id=1, source_target_pairs={{0,8},{2,10},{4,12},{6,14},{8,0},{10,2},{12,4},{14,6},{16,24},{18,... | collective-permute-start | bytes 294920 | tf_op jit(solution)/shard_map/ppermute | solution.py:347
  5.6 7.8 %collective-permute-start.4 = (bf16[3,128,128]{2,1,0:T(8,128)(2,1)S(1)}, bf16[3,128,128]{2,1,0:T(8,128)(2,1)S(1)}, u32[]{:S(2)}, u32[]{:S(2)}) collective-permute-start(bf16[3,128,128]{2,1,0:T(8,128)(2,1)S(1)} %get-tuple-element.30), channel_id=1, source_target_pairs={{0,10},{2,8},{4,14},{6,12},{8,2},{10,0},{12,6},{14,4},{16,26},{18,... | collective-permute-start | bytes 294920 | tf_op jit(solution)/shard_map/ppermute | solution.py:347
  7.2 8.1 %collective-permute-start.5 = (bf16[3,128,128]{2,1,0:T(8,128)(2,1)S(1)}, bf16[3,128,128]{2,1,0:T(8,128)(2,1)S(1)}, u32[]{:S(2)}, u32[]{:S(2)}) collective-permute-start(bf16[3,128,128]{2,1,0:T(8,128)(2,1)S(1)} %get-tuple-element.31), channel_id=1, source_target_pairs={{0,12},{2,14},{4,8},{6,10},{8,4},{10,6},{12,0},{14,2},{16,28},{18,... | collective-permute-start | bytes 294920 | tf_op jit(solution)/shard_map/ppermute | solution.py:347
  8.0 12.7 %collective-permute-start.6 = (bf16[3,128,128]{2,1,0:T(8,128)(2,1)S(1)}, bf16[3,128,128]{2,1,0:T(8,128)(2,1)S(1)}, u32[]{:S(2)}, u32[]{:S(2)}) collective-permute-start(bf16[3,128,128]{2,1,0:T(8,128)(2,1)S(1)} %get-tuple-element.32), channel_id=1, source_target_pairs={{0,14},{2,12},{4,10},{6,8},{8,6},{10,4},{12,2},{14,0},{16,30},{18,... | collective-permute-start | bytes 294920 | tf_op jit(solution)/shard_map/ppermute | solution.py:347
  10.7 10.9 %collective-permute-start.7 = (bf16[3,128,128]{2,1,0:T(8,128)(2,1)S(1)}, bf16[3,128,128]{2,1,0:T(8,128)(2,1)S(1)}, u32[]{:S(2)}, u32[]{:S(2)}) collective-permute-start(bf16[3,128,128]{2,1,0:T(8,128)(2,1)S(1)} %get-tuple-element.33), channel_id=1, source_target_pairs={{0,16},{2,18},{4,20},{6,22},{8,24},{10,26},{12,28},{14,30},{16,0},... | collective-permute-start | bytes 294920 | tf_op jit(solution)/shard_map/ppermute | solution.py:347
  13.0 16.0 %collective-permute-start.8 = (bf16[3,128,128]{2,1,0:T(8,128)(2,1)S(1)}, bf16[3,128,128]{2,1,0:T(8,128)(2,1)S(1)}, u32[]{:S(2)}, u32[]{:S(2)}) collective-permute-start(bf16[3,128,128]{2,1,0:T(8,128)(2,1)S(1)} %get-tuple-element.34), channel_id=1, source_target_pairs={{0,18},{2,16},{4,22},{6,20},{8,26},{10,24},{12,30},{14,28},{16,2},... | collective-permute-start | bytes 294920 | tf_op jit(solution)/shard_map/ppermute | solution.py:347
  13.5 17.6 %collective-permute-start.9 = (bf16[3,128,128]{2,1,0:T(8,128)(2,1)S(1)}, bf16[3,128,128]{2,1,0:T(8,128)(2,1)S(1)}, u32[]{:S(2)}, u32[]{:S(2)}) collective-permute-start(bf16[3,128,128]{2,1,0:T(8,128)(2,1)S(1)} %get-tuple-element.35), channel_id=1, source_target_pairs={{0,20},{2,22},{4,16},{6,18},{8,28},{10,30},{12,24},{14,26},{16,4},... | collective-permute-start | bytes 294920 | tf_op jit(solution)/shard_map/ppermute | solution.py:347
  15.3 20.9 %collective-permute-start.10 = (bf16[3,128,128]{2,1,0:T(8,128)(2,1)S(1)}, bf16[3,128,128]{2,1,0:T(8,128)(2,1)S(1)}, u32[]{:S(2)}, u32[]{:S(2)}) collective-permute-start(bf16[3,128,128]{2,1,0:T(8,128)(2,1)S(1)} %get-tuple-element.36), channel_id=1, source_target_pairs={{0,22},{2,20},{4,18},{6,16},{8,30},{10,28},{12,26},{14,24},{16,6},... | collective-permute-start | bytes 294920 | tf_op jit(solution)/shard_map/ppermute | solution.py:347
  20.7 19.9 %collective-permute-start.11 = (bf16[3,128,128]{2,1,0:T(8,128)(2,1)S(1)}, bf16[3,128,128]{2,1,0:T(8,128)(2,1)S(1)}, u32[]{:S(2)}, u32[]{:S(2)}) collective-permute-start(bf16[3,128,128]{2,1,0:T(8,128)(2,1)S(1)} %get-tuple-element.37), channel_id=1, source_target_pairs={{0,24},{2,26},{4,28},{6,30},{8,16},{10,18},{12,20},{14,22},{16,8},... | collective-permute-start | bytes 294920 | tf_op jit(solution)/shard_map/ppermute | solution.py:347
  21.6 21.6 %collective-permute-start.12 = (bf16[3,128,128]{2,1,0:T(8,128)(2,1)S(1)}, bf16[3,128,128]{2,1,0:T(8,128)(2,1)S(1)}, u32[]{:S(2)}, u32[]{:S(2)}) collective-permute-start(bf16[3,128,128]{2,1,0:T(8,128)(2,1)S(1)} %get-tuple-element.38), channel_id=1, source_target_pairs={{0,26},{2,24},{4,30},{6,28},{8,18},{10,16},{12,22},{14,20},{16,10}... | collective-permute-start | bytes 294920 | tf_op jit(solution)/shard_map/ppermute | solution.py:347
  29.0 15.8 %collective-permute-start.13 = (bf16[3,128,128]{2,1,0:T(8,128)(2,1)S(1)}, bf16[3,128,128]{2,1,0:T(8,128)(2,1)S(1)}, u32[]{:S(2)}, u32[]{:S(2)}) collective-permute-start(bf16[3,128,128]{2,1,0:T(8,128)(2,1)S(1)} %get-tuple-element.39), channel_id=1, source_target_pairs={{0,28},{2,30},{4,24},{6,26},{8,20},{10,22},{12,16},{14,18},{16,12}... | collective-permute-start | bytes 294920 | tf_op jit(solution)/shard_map/ppermute | solution.py:347
  31.1 16.0 %collective-permute-start.14 = (bf16[3,128,128]{2,1,0:T(8,128)(2,1)S(1)}, bf16[3,128,128]{2,1,0:T(8,128)(2,1)S(1)}, u32[]{:S(2)}, u32[]{:S(2)}) collective-permute-start(bf16[3,128,128]{2,1,0:T(8,128)(2,1)S(1)} %get-tuple-element.40), channel_id=1, source_target_pairs={{0,30},{2,28},{4,26},{6,24},{8,22},{10,20},{12,18},{14,16},{16,14}... | collective-permute-start | bytes 294920 | tf_op jit(solution)/shard_map/ppermute | solution.py:347
  52.2 16.8 %copy-start.1 = (bf16[16,3,128,128]{3,2,1,0:T(8,128)(2,1)}, bf16[16,3,128,128]{3,2,1,0:T(8,128)(2,1)S(1)}, u32[]{:S(2)}) copy-start(bf16[16,3,128,128]{3,2,1,0:T(8,128)(2,1)S(1)} %get-tuple-element.45.qkv_ref) | copy-start | bytes 4718596
  52.2 14.3 %collective-permute-start.15 = (bf16[4,128,128]{2,1,0:T(8,128)(2,1)S(1)}, bf16[4,128,128]{2,1,0:T(8,128)(2,1)S(1)}, u32[]{:S(2)}, u32[]{:S(2)}) collective-permute-start(bf16[4,128,128]{2,1,0:T(8,128)(2,1)S(1)} %get-tuple-element.42), channel_id=1, source_target_pairs={{0,8},{2,10},{4,12},{6,14},{8,0},{10,2},{12,4},{14,6},{16,24},{18,... | collective-permute-start | bytes 393224 | tf_op jit(solution)/shard_map/ppermute | solution.py:352
  52.2 14.3 %collective-permute-start.16 = (bf16[4,128,128]{2,1,0:T(8,128)(2,1)S(1)}, bf16[4,128,128]{2,1,0:T(8,128)(2,1)S(1)}, u32[]{:S(2)}, u32[]{:S(2)}) collective-permute-start(bf16[4,128,128]{2,1,0:T(8,128)(2,1)S(1)} %get-tuple-element.43), channel_id=1, source_target_pairs={{0,16},{2,18},{4,20},{6,22},{8,24},{10,26},{12,28},{14,30},{16,0},... | collective-permute-start | bytes 393224 | tf_op jit(solution)/shard_map/ppermute | solution.py:352
  55.3 11.1 %collective-permute-start.17 = (bf16[4,128,128]{2,1,0:T(8,128)(2,1)S(1)}, bf16[4,128,128]{2,1,0:T(8,128)(2,1)S(1)}, u32[]{:S(2)}, u32[]{:S(2)}) collective-permute-start(bf16[4,128,128]{2,1,0:T(8,128)(2,1)S(1)} %get-tuple-element.44), channel_id=1, source_target_pairs={{0,24},{2,26},{4,28},{6,30},{8,16},{10,18},{12,20},{14,22},{16,8},... | collective-permute-start | bytes 393224 | tf_op jit(solution)/shard_map/ppermute | solution.py:352
  66.6 4.4 %collective-permute-start.18 = (bf16[4,128,128]{2,1,0:T(8,128)(2,1)S(1)}, bf16[4,128,128]{2,1,0:T(8,128)(2,1)S(1)}, u32[]{:S(2)}, u32[]{:S(2)}) collective-permute-start(bf16[4,128,128]{2,1,0:T(8,128)(2,1)S(1)} %pad_maximum_fusion.1), channel_id=1, source_target_pairs={{0,2},{2,0},{4,6},{6,4},{8,10},{10,8},{12,14},{14,12},{16,18},{18,... | collective-permute-start | bytes 393224 | tf_op jit(solution)/shard_map/ppermute | solution.py:357
  68.0 5.1 %collective-permute-start.19 = (bf16[4,128,128]{2,1,0:T(8,128)(2,1)S(1)}, bf16[4,128,128]{2,1,0:T(8,128)(2,1)S(1)}, u32[]{:S(2)}, u32[]{:S(2)}) collective-permute-start(bf16[4,128,128]{2,1,0:T(8,128)(2,1)S(1)} %pad_maximum_fusion.2), channel_id=1, source_target_pairs={{0,4},{2,6},{4,0},{6,2},{8,12},{10,14},{12,8},{14,10},{16,20},{18,... | collective-permute-start | bytes 393224 | tf_op jit(solution)/shard_map/ppermute | solution.py:357
  69.0 7.3 %collective-permute-start.20 = (bf16[4,128,128]{2,1,0:T(8,128)(2,1)S(1)}, bf16[4,128,128]{2,1,0:T(8,128)(2,1)S(1)}, u32[]{:S(2)}, u32[]{:S(2)}) collective-permute-start(bf16[4,128,128]{2,1,0:T(8,128)(2,1)S(1)} %pad_maximum_fusion.3), channel_id=1, source_target_pairs={{0,6},{2,4},{4,2},{6,0},{8,14},{10,12},{12,10},{14,8},{16,22},{18,... | collective-permute-start | bytes 393224 | tf_op jit(solution)/shard_map/ppermute | solution.py:357
  69.8 24.9 %collective-permute-start.25 = (bf16[64,8192]{1,0:T(8,128)(2,1)}, bf16[64,8192]{1,0:T(8,128)(2,1)S(1)}, u32[]{:S(2)}, u32[]{:S(2)}) collective-permute-start(bf16[64,8192]{1,0:T(8,128)(2,1)} %own_ref.1), channel_id=1, source_target_pairs={{0,1},{1,0},{2,3},{3,2},{4,5},{5,4},{6,7},{7,6},{8,9},{9,8},{10,11... | collective-permute-start | bytes 3145736 | tf_op jit(solution)/shard_map/ppermute | solution.py:344
  81.1 13.6 %copy-start.5 = (f32[128,2048]{1,0:T(8,128)}, f32[128,2048]{1,0:T(8,128)S(1)}, u32[]{:S(2)}) copy-start(f32[128,2048]{1,0:T(8,128)S(1)} %fusion.17) | copy-start | bytes 3145732
  81.9 63.5 %collective-permute-start.24 = (bf16[64,2048]{1,0:T(8,128)(2,1)}, bf16[64,2048]{1,0:T(8,128)(2,1)}, u32[]{:S(2)}, u32[]{:S(2)}) collective-permute-start(bf16[64,2048]{1,0:T(8,128)(2,1)} %dynamic-slice_convert_fusion), channel_id=1, source_target_pairs={{0,1},{1,0},{2,3},{3,2},{4,5},{5,4},{6,7},{7,6},{8,9},{9,8},{10,11... | collective-permute-start | bytes 786440 | tf_op jit(solution)/shard_map/ppermute | solution.py:371
  110.0 20.9 %copy-start.2 = (bf16[16,3,128,128]{3,2,1,0:T(8,128)(2,1)S(1)}, bf16[16,3,128,128]{3,2,1,0:T(8,128)(2,1)}, u32[]{:S(2)}) copy-start(bf16[16,3,128,128]{3,2,1,0:T(8,128)(2,1)} %copy-done.1) | copy-start | bytes 4718596
  110.0 20.9 %copy-start.4 = (bf16[16,128,128]{2,1,0:T(8,128)(2,1)S(1)}, bf16[16,128,128]{2,1,0:T(8,128)(2,1)}, u32[]{:S(2)}) copy-start(bf16[16,128,128]{2,1,0:T(8,128)(2,1)} %copy-done.3) | copy-start | bytes 1572868
  110.0 20.8 %all-to-all-start = ((bf16[16,128,128]{2,1,0:T(8,128)(2,1)}), bf16[16,128,128]{2,1,0:T(8,128)(2,1)S(1)}, u32[]{:S(2)}, u32[]{:S(2)}) async-start(bf16[16,128,128]{2,1,0:T(8,128)(2,1)} %project_back.1), calls=%async_computation | async-start | bytes 1048576 | tf_op jit(solution)/shard_map/all_to_all | solution.py:342
  118.7 27.8 %collective-permute-start.23 = (bf16[64,2048]{1,0:T(8,128)(2,1)}, bf16[64,2048]{1,0:T(8,128)(2,1)}, u32[]{:S(2)}, u32[]{:S(2)}) collective-permute-start(bf16[64,2048]{1,0:T(8,128)(2,1)} %dynamic-slice_convert_fusion.1), channel_id=1, source_target_pairs={{0,1},{1,0},{2,3},{3,2},{4,5},{5,4},{6,7},{7,6},{8,9},{9,8},{10,11... | collective-permute-start | bytes 786440 | tf_op jit(solution)/shard_map/ppermute | solution.py:371
  121.7 26.1 %collective-permute-start.22 = (bf16[64,2048]{1,0:T(8,128)(2,1)}, bf16[64,2048]{1,0:T(8,128)(2,1)S(1)}, u32[]{:S(2)}, u32[]{:S(2)}) collective-permute-start(bf16[64,2048]{1,0:T(8,128)(2,1)} %dynamic-slice_convert_fusion.2), channel_id=1, source_target_pairs={{0,1},{1,0},{2,3},{3,2},{4,5},{5,4},{6,7},{7,6},{8,9},{9,8},{10,11... | collective-permute-start | bytes 786440 | tf_op jit(solution)/shard_map/ppermute | solution.py:371
  138.5 40.8 %all-to-all-start.1 = ((bf16[16,3,128,128]{3,2,1,0:T(8,128)(2,1)}), bf16[16,3,128,128]{3,2,1,0:T(8,128)(2,1)S(1)}, u32[]{:S(2)}, u32[]{:S(2)}) async-start(bf16[16,3,128,128]{3,2,1,0:T(8,128)(2,1)} %attend_grad.1), calls=%async_computation.1 | async-start | bytes 3145728 | tf_op jit(solution)/shard_map/all_to_all | solution.py:342
  144.1 7.5 %collective-permute-start.21 = (bf16[64,2048]{1,0:T(8,128)(2,1)S(1)}, bf16[64,2048]{1,0:T(8,128)(2,1)S(1)}, u32[]{:S(2)}, u32[]{:S(2)}) collective-permute-start(bf16[64,2048]{1,0:T(8,128)(2,1)S(1)} %dynamic-slice_convert_fusion.3), channel_id=1, source_target_pairs={{0,1},{1,0},{2,3},{3,2},{4,5},{5,4},{6,7},{7,6},{8,9},{9,8},{10,11... | collective-permute-start | bytes 786440 | tf_op jit(solution)/shard_map/ppermute | solution.py:371
  (2 other events, 6.6 us)

commit v7 on v6

--- a/solution.py
+++ b/solution.py
@@ -11,8 +11,8 @@
 
 HD = 128
 LOG2E = math.log2(math.e)
-MIX_PARTS = 4
-VMEM_LIMIT = 20 * 1024 * 1024
+MIX_PARTS = (1, 1, 2, 2, 2)
+MIB = 1024 * 1024
 
 
 def dot_nt(a, b):
@@ -94,8 +94,8 @@
 
 
 def forward_kernel(step, outer, me_ref, *refs):
-    parts, rest = refs[:-5 - outer], refs[-5 - outer :]
-    qkv_ref, att_ref, lse_ref, *sent, v_t, s_buf = rest
+    parts, rest = refs[: -5 - outer], refs[-5 - outer :]
+    lse_ref, *sent, qkv_ref, att_ref, v_t, s_buf = rest
     me = me_ref[0]
     for k, part in enumerate(parts):
         qkv_ref[me ^ k] = part[...]
@@ -142,7 +142,24 @@
             out_ref[me_ref[0] ^ (PLANE * d + e)] = others[e - 1][d]
 
 
-def backward_kernel(step, qkv_ref, g_ref, att_ref, lse_ref, out_ref, k_t, dq_t, delta):
+def finish_kernel(turn_ref, *refs):
+    *parts, out_ref = refs
+    half = out_ref.shape[0]
+    start = 0
+    for mixed_ref, got_ref in zip(parts[::2], parts[1::2]):
+        stop = start + mixed_ref.shape[1]
+        kept = mixed_ref[pl.ds(pl.multiple_of(turn_ref[0] * half, half), half)]
+        out_ref[:, start:stop] = kept + got_ref[...].astype(jnp.float32)
+        start = stop
+
+
+def backward_kernel(step, chunks, me_ref, g_ref, lse_ref, *refs):
+    parts, own, rest = refs[:chunks], refs[chunks:-6], refs[-6:]
+    out_ref, qkv_ref, att_ref, k_t, dq_t, delta = rest
+    me = me_ref[0]
+    for k, part in enumerate(parts):
+        qkv_ref[me ^ k] = part[...]
+        att_ref[me ^ k] = own[k // PLANE][k % PLANE]
     chunks, _, unit, _ = qkv_ref.shape
     per = step // unit
     blocks = chunks // per
@@ -217,7 +234,7 @@
         in_specs=[in_smem(), pl.BlockSpec((part, 3, heads, HD), lambda b: (b, 0, 0, 0))],
         out_specs=in_vmem(heads),
         scratch_shapes=[pltpu.VMEM((CHUNK * heads, CHUNK * heads), jnp.bfloat16)],
-        compiler_params=pltpu.CompilerParams(vmem_limit_bytes=VMEM_LIMIT),
+        compiler_params=pltpu.CompilerParams(vmem_limit_bytes=6 * MIB),
         name="split_heads",
     )(me, pltpu.with_memory_space_constraint(jnp.transpose(qkv, (0, 2, 1, 3)), pltpu.HBM))
 
@@ -232,7 +249,7 @@
         in_specs=in_vmem(1),
         out_specs=pl.BlockSpec((part, three, heads, HD), lambda b: (b, 0, 0, 0)),
         scratch_shapes=[pltpu.VMEM((CHUNK * heads, CHUNK * heads), jnp.bfloat16)],
-        compiler_params=pltpu.CompilerParams(vmem_limit_bytes=VMEM_LIMIT),
+        compiler_params=pltpu.CompilerParams(vmem_limit_bytes=8 * MIB),
         name="join_heads",
     )(grads)
     return jnp.transpose(out, (0, 2, 1, 3))
@@ -248,12 +265,13 @@
         out_shape=jax.ShapeDtypeStruct((heads, 2 * half, HD), jnp.bfloat16),
         in_specs=[
             in_smem(),
-            *in_vmem(2),
+            pl.BlockSpec((half, width), lambda b: (0, 0)),
+            *in_vmem(1),
             pl.BlockSpec((group * HD, width), lambda b: (b, 0)),
         ],
         out_specs=pl.BlockSpec((group, 2 * half, HD), lambda b: (b, 0, 0)),
         scratch_shapes=[pltpu.VMEM((2 * half, width), jnp.bfloat16)],
-        compiler_params=pltpu.CompilerParams(vmem_limit_bytes=32 * 1024 * 1024),
+        compiler_params=pltpu.CompilerParams(vmem_limit_bytes=26 * MIB),
         cost_estimate=pl.CostEstimate(
             flops=4 * half * width * heads * HD,
             transcendentals=0,
@@ -273,18 +291,18 @@
     return pl.pallas_call(
         functools.partial(forward_kernel, step, outer),
         out_shape=(
-            jax.ShapeDtypeStruct((chunks, 3, unit, HD), jnp.bfloat16),
-            jax.ShapeDtypeStruct((chunks, unit, HD), jnp.bfloat16),
             jax.ShapeDtypeStruct((blocks, 1, step), jnp.float32),
             *[jax.ShapeDtypeStruct((PLANE, unit, HD), jnp.bfloat16)] * outer,
         ),
         in_specs=[in_smem(), *in_vmem(chunks)],
-        out_specs=tuple(in_vmem(3 + outer)),
+        out_specs=tuple(in_vmem(1 + outer)),
         scratch_shapes=[
+            pltpu.VMEM((chunks, 3, unit, HD), jnp.bfloat16),
+            pltpu.VMEM((chunks, unit, HD), jnp.bfloat16),
             pltpu.VMEM((blocks, HD, step), jnp.bfloat16),
             pltpu.VMEM((2, blocks, step, step), jnp.float32),
         ],
-        compiler_params=pltpu.CompilerParams(vmem_limit_bytes=VMEM_LIMIT),
+        compiler_params=pltpu.CompilerParams(vmem_limit_bytes=16 * MIB),
         cost_estimate=pl.CostEstimate(
             flops=4 * area * HD, transcendentals=area, bytes_accessed=8 * length * HD
         ),
@@ -300,32 +318,49 @@
         out_shape=jax.ShapeDtypeStruct(shape, jnp.bfloat16),
         in_specs=[in_smem(), *in_vmem(len(own) + PLANE - 1)],
         out_specs=in_vmem(1)[0],
-        compiler_params=pltpu.CompilerParams(vmem_limit_bytes=VMEM_LIMIT),
+        compiler_params=pltpu.CompilerParams(vmem_limit_bytes=2 * MIB),
         name="gather_heads",
     )(me, *own, *others)
 
 
-def attend_grad(qkv, g, att, lse, step):
-    chunks, _, unit, _ = qkv.shape
+def finish(turn, parts):
+    half = parts[0][1].shape[0]
+    width = sum(mixed.shape[1] for mixed, _ in parts)
+    flat = [x for pair in parts for x in pair]
+    return pl.pallas_call(
+        finish_kernel,
+        out_shape=jax.ShapeDtypeStruct((half, width), jnp.float32),
+        in_specs=[in_smem(), *in_vmem(len(flat))],
+        out_specs=in_vmem(1)[0],
+        compiler_params=pltpu.CompilerParams(vmem_limit_bytes=4 * MIB),
+        name="finish",
+    )(turn, *flat)
+
+
+def attend_grad(me, g, lse, parts, own, step):
+    chunks = len(parts)
+    unit = parts[0].shape[1]
     length = chunks * unit
     blocks = length // step
     area = length * length // 2
     return pl.pallas_call(
-        functools.partial(backward_kernel, step),
+        functools.partial(backward_kernel, step, chunks),
         out_shape=jax.ShapeDtypeStruct((chunks, 3, unit, HD), jnp.bfloat16),
-        in_specs=in_vmem(4),
+        in_specs=[in_smem(), *in_vmem(2 + chunks + len(own))],
         out_specs=in_vmem(1)[0],
         scratch_shapes=[
+            pltpu.VMEM((chunks, 3, unit, HD), jnp.bfloat16),
+            pltpu.VMEM((chunks, unit, HD), jnp.bfloat16),
             pltpu.VMEM((blocks, HD, step), jnp.bfloat16),
             pltpu.VMEM((blocks, HD, step), jnp.float32),
             pltpu.VMEM((blocks, 1, step), jnp.float32),
         ],
-        compiler_params=pltpu.CompilerParams(vmem_limit_bytes=VMEM_LIMIT),
+        compiler_params=pltpu.CompilerParams(vmem_limit_bytes=16 * MIB),
         cost_estimate=pl.CostEstimate(
             flops=10 * area * HD, transcendentals=area, bytes_accessed=16 * length * HD
         ),
         name="attend_grad",
-    )(qkv, g, att, lse)
+    )(me, g, lse, *parts, *own)
 
 
 def by_head(qkv, grad_out, attn_out):
@@ -347,30 +382,31 @@
         parts[k] = lax.ppermute(parts[k], "ctx", [(i, i ^ k) for i in range(heads)])
     g = project_back(turn.reshape(1), grad_out, other_out, attn_out)
     g = spread(g)
-    mine, att, lse, *own = attend(me, parts, step)
+    lse, *own = attend(me, parts, step)
+    mixed_own = list(own)
     for d in range(1, len(own)):
-        own[d] = lax.ppermute(own[d], "ctx", [(i, i ^ (PLANE * d)) for i in range(heads)])
-    grads = attend_grad(mine, g, att, lse, step)
+        mixed_own[d] = lax.ppermute(own[d], "ctx", [(i, i ^ (PLANE * d)) for i in range(heads)])
+    grads = attend_grad(me, g, lse, parts, own, step)
     others = []
     for e in range(1, PLANE):
-        sent = jnp.stack([x[e] for x in own])
+        sent = jnp.stack([x[e] for x in mixed_own])
         others.append(lax.ppermute(sent, "ctx", [(i, i ^ e) for i in range(heads)]))
     grads = spread(grads)
-    local = gather_heads(me, own, others)
+    local = gather_heads(me, mixed_own, others)
     pieces = []
-    part = width // MIX_PARTS
-    for c in range(MIX_PARTS):
+    start = 0
+    for eighths in MIX_PARTS:
+        stop = start + eighths * (width // 8)
         mixed = jnp.einsum(
             "hrd,hdm->rm",
             local,
-            weights[:, :, c * part : (c + 1) * part],
+            weights[:, :, start:stop],
             preferred_element_type=jnp.float32,
         )
         sent = lax.dynamic_slice_in_dim(mixed, (1 - turn) * half, half, 0)
-        kept = lax.dynamic_slice_in_dim(mixed, turn * half, half, 0)
-        got = lax.ppermute(sent.astype(jnp.bfloat16), "tp", swap)
-        pieces.append(kept + got.astype(jnp.float32))
-    mixed_out = jnp.concatenate(pieces, axis=1)
+        pieces.append((mixed, lax.ppermute(sent.astype(jnp.bfloat16), "tp", swap)))
+        start = stop
+    mixed_out = finish(turn.reshape(1), pieces)
     return mixed_out, join_heads(grads)
 
 

time: 183 us -> 169 us (0.923)
  the two profiles are of different devices: /device:TPU:13 before, /device:TPU:15 now
where the time goes in v7:
time: 169 us; the launch traced here: 168 us
  waiting for transfers between devices  61.3 us (36%)
  starting transfers between devices  41.9 us (25%)
  Pallas kernels  32.7 us (19%)
  matrix products  19.8 us (12%)
  local copies, waits for them, and re-layouts  11.5 us (7%)
    ppermute x15, waiting for transfers between devices, by_head(): parts[k] = lax.ppermute(parts[k], 'ctx', [(i, i ^ k) for i in range(heads)])  24.5 us
    dot_general x5, matrix products, by_head(): jnp.einsum('hrd,hdm->rm', local, weights[:, :, start:stop], preferred_ele...  19.8 us
    ppermute x15, starting transfers between devices, by_head(): parts[k] = lax.ppermute(parts[k], 'ctx', [(i, i ^ k) for i in range(heads)])  19.3 us
    pallas_call x1, Pallas kernels, project_back(): pl.pallas_call(back_kernel, grid=(heads // group,), out_shape=jax.ShapeDt...  15.1 us
    all_to_all x2, starting transfers between devices, spread(): return lax.all_to_all(x, 'ctx', 0, 0, tiled=True)  12.2 us
    unnamed x64, local copies, waits for them, and re-layouts  11.4 us
    ppermute x3, waiting for transfers between devices, by_head(): lax.ppermute(own[d], 'ctx', [(i, i ^ PLANE * d) for i in range(heads)])  11.1 us
    all_to_all x2, waiting for transfers between devices, spread(): return lax.all_to_all(x, 'ctx', 0, 0, tiled=True)  10.8 us
  transfers between devices with their start and end apart: 29, of which 17 were waited for; matrix products, arithmetic and copies ran while one was open for 12% of the time, Pallas kernels for 12%

profile of v7, /device:TPU:15, one launch (start us, length us, event | category | flops | bytes accessed | tf_op | source)
XLA Modules:
  0.0 168.3 jit_solution(14726235109739514231)
XLA Ops:
  0.6 2.4 %split_heads.1 = (bf16[3,128,128]{2,1,0:T(8,128)(2,1)S(1)}, bf16[3,128,128]{2,1,0:T(8,128)(2,1)S(1)}, bf16[3,128,128]{2,1,0:T(8,128)(2,1)S(1)}, bf16[3,128,128]{...) custom-call(s32[1]{0:T(128)} %bitcast.1.me_ref, ...), custom_call_target="tpu_custom_call" | custom-call | tf_op jit(solution)/shard_map/split_heads/pallas_call | solution.py:230
  8.0 1.8 %collective-permute-start.6 = (bf16[3,128,128]{2,1,0:T(8,128)(2,1)S(1)}, bf16[3,128,128]{2,1,0:T(8,128)(2,1)S(1)}, u32[]{:S(2)}, u32[]{:S(2)}) collective-permute-start(bf16[3,128,128]{2,1,0:T(8,128)(2,1)S(1)} %get-tuple-element.30), channel_id=1, source_target_pairs={{0,14},{2,12},{4,10},{6,8},{8,6},{10,4},{12,2},{14,0},{16,30},{18,... | collective-permute-start | bytes 294920 | tf_op jit(solution)/shard_map/ppermute | solution.py:382
  10.7 2.3 %collective-permute-start.7 = (bf16[3,128,128]{2,1,0:T(8,128)(2,1)S(1)}, bf16[3,128,128]{2,1,0:T(8,128)(2,1)S(1)}, u32[]{:S(2)}, u32[]{:S(2)}) collective-permute-start(bf16[3,128,128]{2,1,0:T(8,128)(2,1)S(1)} %get-tuple-element.31), channel_id=1, source_target_pairs={{0,16},{2,18},{4,20},{6,22},{8,24},{10,26},{12,28},{14,30},{16,0},... | collective-permute-start | bytes 294920 | tf_op jit(solution)/shard_map/ppermute | solution.py:382
  13.5 1.8 %collective-permute-start.9 = (bf16[3,128,128]{2,1,0:T(8,128)(2,1)S(1)}, bf16[3,128,128]{2,1,0:T(8,128)(2,1)S(1)}, u32[]{:S(2)}, u32[]{:S(2)}) collective-permute-start(bf16[3,128,128]{2,1,0:T(8,128)(2,1)S(1)} %get-tuple-element.33), channel_id=1, source_target_pairs={{0,20},{2,22},{4,16},{6,18},{8,28},{10,30},{12,24},{14,26},{16,4},... | collective-permute-start | bytes 294920 | tf_op jit(solution)/shard_map/ppermute | solution.py:382
  15.3 5.4 %collective-permute-start.10 = (bf16[3,128,128]{2,1,0:T(8,128)(2,1)S(1)}, bf16[3,128,128]{2,1,0:T(8,128)(2,1)S(1)}, u32[]{:S(2)}, u32[]{:S(2)}) collective-permute-start(bf16[3,128,128]{2,1,0:T(8,128)(2,1)S(1)} %get-tuple-element.34), channel_id=1, source_target_pairs={{0,22},{2,20},{4,18},{6,16},{8,30},{10,28},{12,26},{14,24},{16,6},... | collective-permute-start | bytes 294920 | tf_op jit(solution)/shard_map/ppermute | solution.py:382
  21.6 7.4 %collective-permute-done.8.refs_9_ = bf16[3,128,128]{2,1,0:T(8,128)(2,1)S(1)} collective-permute-done((bf16[3,128,128]{2,1,0:T(8,128)(2,1)S(1)}, bf16[3,128,128]{2,1,0:T(8,128)(2,1)S(1)}, u32[]{:S(2)}, u32[]{:S(2)}) %collective-permute-start.8) | collective-permute-done | bytes 98336 | tf_op jit(solution)/shard_map/ppermute | solution.py:382
  29.0 2.1 %collective-permute-done.9.refs_10_ = bf16[3,128,128]{2,1,0:T(8,128)(2,1)S(1)} collective-permute-done((bf16[3,128,128]{2,1,0:T(8,128)(2,1)S(1)}, bf16[3,128,128]{2,1,0:T(8,128)(2,1)S(1)}, u32[]{:S(2)}, u32[]{:S(2)}) %collective-permute-start.9) | collective-permute-done | bytes 98336 | tf_op jit(solution)/shard_map/ppermute | solution.py:382
  31.1 2.2 %collective-permute-start.14 = (bf16[3,128,128]{2,1,0:T(8,128)(2,1)S(1)}, bf16[3,128,128]{2,1,0:T(8,128)(2,1)S(1)}, u32[]{:S(2)}, u32[]{:S(2)}) collective-permute-start(bf16[3,128,128]{2,1,0:T(8,128)(2,1)S(1)} %get-tuple-element.38), channel_id=1, source_target_pairs={{0,30},{2,28},{4,26},{6,24},{8,22},{10,20},{12,18},{14,16},{16,14}... | collective-permute-start | bytes 294920 | tf_op jit(solution)/shard_map/ppermute | solution.py:382
  33.3 2.9 %collective-permute-done.10.refs_11_ = bf16[3,128,128]{2,1,0:T(8,128)(2,1)S(1)} collective-permute-done((bf16[3,128,128]{2,1,0:T(8,128)(2,1)S(1)}, bf16[3,128,128]{2,1,0:T(8,128)(2,1)S(1)}, u32[]{:S(2)}, u32[]{:S(2)}) %collective-permute-start.10) | collective-permute-done | bytes 98336 | tf_op jit(solution)/shard_map/ppermute | solution.py:382
  36.5 4.1 %collective-permute-done.11.refs_12_ = bf16[3,128,128]{2,1,0:T(8,128)(2,1)S(1)} collective-permute-done((bf16[3,128,128]{2,1,0:T(8,128)(2,1)S(1)}, bf16[3,128,128]{2,1,0:T(8,128)(2,1)S(1)}, u32[]{:S(2)}, u32[]{:S(2)}) %collective-permute-start.11) | collective-permute-done | bytes 98336 | tf_op jit(solution)/shard_map/ppermute | solution.py:382
  40.6 2.9 %collective-permute-done.12.refs_13_ = bf16[3,128,128]{2,1,0:T(8,128)(2,1)S(1)} collective-permute-done((bf16[3,128,128]{2,1,0:T(8,128)(2,1)S(1)}, bf16[3,128,128]{2,1,0:T(8,128)(2,1)S(1)}, u32[]{:S(2)}, u32[]{:S(2)}) %collective-permute-start.12) | collective-permute-done | bytes 98336 | tf_op jit(solution)/shard_map/ppermute | solution.py:382
  44.8 2.3 %collective-permute-done.14.refs_15_ = bf16[3,128,128]{2,1,0:T(8,128)(2,1)S(1)} collective-permute-done((bf16[3,128,128]{2,1,0:T(8,128)(2,1)S(1)}, bf16[3,128,128]{2,1,0:T(8,128)(2,1)S(1)}, u32[]{:S(2)}, u32[]{:S(2)}) %collective-permute-start.14) | collective-permute-done | bytes 98336 | tf_op jit(solution)/shard_map/ppermute | solution.py:382
  47.1 4.3 %attend.1 = (f32[4,1,512]{2,1,0:T(1,128)S(1)}, bf16[4,128,128]{2,1,0:T(8,128)(2,1)S(1)}, bf16[4,128,128]{2,1,0:T(8,128)(2,1)S(1)}, bf16[4,128,128]{2,1,0:T(8,128)(2,1)S(1)}, bf16[4,128,128]{2,1,0:T(8,128)(2,1)S(1)}) custom-call(s32[1]{0:T(128)} %bitcast.1.me_ref, bf16[3,128,128]{2,1,0:T(8,128)(2,1)S(1)} %get-tuple-element.23.refs_0_, ...), custom_call_target="tpu_custom_call" | custom-call | flops 1073741824 | bytes 2097152 | tf_op jit(solution)/shard_map/attend/pallas_call | solution.py:291
  51.5 3.1 %collective-permute-start.16 = (bf16[4,128,128]{2,1,0:T(8,128)(2,1)S(1)}, bf16[4,128,128]{2,1,0:T(8,128)(2,1)S(1)}, u32[]{:S(2)}, u32[]{:S(2)}) collective-permute-start(bf16[4,128,128]{2,1,0:T(8,128)(2,1)S(1)} %get-tuple-element.41.refs_18_), channel_id=1, source_target_pairs={{0,16},{2,18},{4,20},{6,22},{8,24},{10,26},{12,28},{14,30},{16,0},... | collective-permute-start | bytes 393224 | tf_op jit(solution)/shard_map/ppermute | solution.py:388
  56.1 6.9 %collective-permute-done.16.refs_2_ = bf16[4,128,128]{2,1,0:T(8,128)(2,1)S(1)} collective-permute-done((bf16[4,128,128]{2,1,0:T(8,128)(2,1)S(1)}, bf16[4,128,128]{2,1,0:T(8,128)(2,1)S(1)}, u32[]{:S(2)}, u32[]{:S(2)}) %collective-permute-start.16) | collective-permute-done | bytes 131104 | tf_op jit(solution)/shard_map/ppermute | solution.py:388
  63.0 2.8 %collective-permute-done.17.refs_3_ = bf16[4,128,128]{2,1,0:T(8,128)(2,1)S(1)} collective-permute-done((bf16[4,128,128]{2,1,0:T(8,128)(2,1)S(1)}, bf16[4,128,128]{2,1,0:T(8,128)(2,1)S(1)}, u32[]{:S(2)}, u32[]{:S(2)}) %collective-permute-start.17) | collective-permute-done | bytes 131104 | tf_op jit(solution)/shard_map/ppermute | solution.py:388
  68.4 15.1 %project_back.1 = bf16[16,128,128]{2,1,0:T(8,128)(2,1)} custom-call(s32[1]{0:T(128)} %bitcast.turn_ref, bf16[64,8192]{1,0:T(8,128)(2,1)S(1)} %copy-done.1, bf16[64,8192]{1,0:T(8,128)(2,1)S(1)} %collective-permute-done.26.other_ref, bf16[2048,8192]{1,0:T(8,128)(2,1)} %w_ref.1), custom_call_target="tpu_custom_call" | custom-call | flops 4294967296 | bytes 33554432 | tf_op jit(solution)/shard_map/project_back/pallas_call | solution.py:262
  83.6 5.6 %all-to-all-start = ((bf16[16,128,128]{2,1,0:T(8,128)(2,1)}), bf16[16,128,128]{2,1,0:T(8,128)(2,1)S(1)}, u32[]{:S(2)}, u32[]{:S(2)}) async-start(bf16[16,128,128]{2,1,0:T(8,128)(2,1)} %project_back.1), calls=%async_computation | async-start | bytes 1048576 | tf_op jit(solution)/shard_map/all_to_all | solution.py:377
  89.6 1.8 %collective-permute-start.20 = (bf16[4,128,128]{2,1,0:T(8,128)(2,1)S(1)}, bf16[4,128,128]{2,1,0:T(8,128)(2,1)S(1)}, u32[]{:S(2)}, u32[]{:S(2)}) collective-permute-start(bf16[4,128,128]{2,1,0:T(8,128)(2,1)S(1)} %pad_maximum_fusion.2), channel_id=1, source_target_pairs={{0,6},{2,4},{4,2},{6,0},{8,14},{10,12},{12,10},{14,8},{16,22},{18,... | collective-permute-start | bytes 393224 | tf_op jit(solution)/shard_map/ppermute | solution.py:393
  91.4 5.7 %collective-permute-done.19.refs_5_ = bf16[4,128,128]{2,1,0:T(8,128)(2,1)S(1)} collective-permute-done((bf16[4,128,128]{2,1,0:T(8,128)(2,1)S(1)}, bf16[4,128,128]{2,1,0:T(8,128)(2,1)S(1)}, u32[]{:S(2)}, u32[]{:S(2)}) %collective-permute-start.19) | collective-permute-done | bytes 131104 | tf_op jit(solution)/shard_map/ppermute | solution.py:393
  97.1 4.1 %collective-permute-done.20.refs_6_ = bf16[4,128,128]{2,1,0:T(8,128)(2,1)S(1)} collective-permute-done((bf16[4,128,128]{2,1,0:T(8,128)(2,1)S(1)}, bf16[4,128,128]{2,1,0:T(8,128)(2,1)S(1)}, u32[]{:S(2)}, u32[]{:S(2)}) %collective-permute-start.20) | collective-permute-done | bytes 131104 | tf_op jit(solution)/shard_map/ppermute | solution.py:393
  101.3 4.7 %fusion.16.refs_8_ = f32[128,2048]{1,0:T(8,128)S(1)} fusion(bf16[16,128,128]{2,1,0:T(8,128)(2,1)S(1)} %gather_heads.1, bf16[16,128,8192]{2,1,0:T(8,128)(2,1)} %bitcast.20), kind=kOutput, calls=%fused_computation.12 | convolution fusion | flops 1073741824 | bytes 9961472 | tf_op jit(solution)/shard_map/hrd,hdm->rm/dot_general | solution.py:400
  115.0 6.5 %attend_grad.1 = bf16[16,3,128,128]{3,2,1,0:T(8,128)(2,1)S(1)} custom-call(s32[1]{0:T(128)} %bitcast.1.me_ref, bf16[16,128,128]{2,1,0:T(8,128)(2,1)S(1)} %all-to-all-done.g_ref, f32[4,1,512]{2,1,0:T(1,128)S(1)} %get-tuple-element.43.lse_ref, bf16[3,128,128]{2,1,0:T(8,128)(2,1)S(1)} %get-tuple-element.23.refs_0_, bf16[3,128,128]{2,1,0:T(8,128)(2,1)S(1)} %copy-done.3, ...), custom_call_target="tpu_custom_call" | custom-call | flops 2684354560 | bytes 4194304 | tf_op jit(solution)/shard_map/attend_grad/pallas_call | solution.py:346
  122.7 6.6 %all-to-all-start.1 = ((bf16[16,3,128,128]{3,2,1,0:T(8,128)(2,1)}), bf16[16,3,128,128]{3,2,1,0:T(8,128)(2,1)S(1)}, u32[]{:S(2)}, u32[]{:S(2)}) async-start(bf16[16,3,128,128]{3,2,1,0:T(8,128)(2,1)} %copy-done), calls=%async_computation.1 | async-start | bytes 3145728 | tf_op jit(solution)/shard_map/all_to_all | solution.py:377
  129.6 4.6 %fusion.13.refs_6_ = f32[128,2048]{1,0:T(8,128)S(1)} fusion(bf16[16,128,128]{2,1,0:T(8,128)(2,1)S(1)} %gather_heads.1, bf16[16,128,8192]{2,1,0:T(8,128)(2,1)} %bitcast.21), kind=kOutput, calls=%fused_computation.11 | convolution fusion | flops 1073741824 | bytes 9961472 | tf_op jit(solution)/shard_map/hrd,hdm->rm/dot_general | solution.py:400
  135.6 4.6 %fusion.10.refs_4_ = f32[128,2048]{1,0:T(8,128)S(1)} fusion(bf16[16,128,128]{2,1,0:T(8,128)(2,1)S(1)} %gather_heads.1, bf16[16,128,8192]{2,1,0:T(8,128)(2,1)} %bitcast.22), kind=kOutput, calls=%fused_computation.10 | convolution fusion | flops 1073741824 | bytes 9961472 | tf_op jit(solution)/shard_map/hrd,hdm->rm/dot_general | solution.py:400
  140.6 2.9 %fusion.22.refs_2_ = f32[128,1024]{1,0:T(8,128)S(1)} fusion(bf16[16,128,128]{2,1,0:T(8,128)(2,1)S(1)} %gather_heads.1, bf16[16,128,8192]{2,1,0:T(8,128)(2,1)} %bitcast.23), kind=kOutput, calls=%fused_computation.14 | convolution fusion | flops 536870912 | bytes 5242880 | tf_op jit(solution)/shard_map/hrd,hdm->rm/dot_general | solution.py:400
  143.5 2.9 %fusion.19.refs_0_ = f32[128,1024]{1,0:T(8,128)S(1)} fusion(bf16[16,128,128]{2,1,0:T(8,128)(2,1)S(1)} %gather_heads.1, bf16[16,128,8192]{2,1,0:T(8,128)(2,1)} %bitcast.24), kind=kOutput, calls=%fused_computation.13 | convolution fusion | flops 536870912 | bytes 5242880 | tf_op jit(solution)/shard_map/hrd,hdm->rm/dot_general | solution.py:400
  148.0 2.6 %collective-permute-done.22.refs_3_ = bf16[64,1024]{1,0:T(8,128)(2,1)S(1)} collective-permute-done((bf16[64,1024]{1,0:T(8,128)(2,1)S(1)}, bf16[64,1024]{1,0:T(8,128)(2,1)S(1)}, u32[]{:S(2)}, u32[]{:S(2)}) %collective-permute-start.22) | collective-permute-done | bytes 131104 | tf_op jit(solution)/shard_map/ppermute | solution.py:407
  150.6 2.5 %collective-permute-done.21.refs_1_ = bf16[64,1024]{1,0:T(8,128)(2,1)S(1)} collective-permute-done((bf16[64,1024]{1,0:T(8,128)(2,1)S(1)}, bf16[64,1024]{1,0:T(8,128)(2,1)S(1)}, u32[]{:S(2)}, u32[]{:S(2)}) %collective-permute-start.21) | collective-permute-done | bytes 131104 | tf_op jit(solution)/shard_map/ppermute | solution.py:407
  154.6 10.8 %all-to-all-done.1.x_ref = bf16[16,3,128,128]{3,2,1,0:T(8,128)(2,1)S(1)} async-done(((bf16[16,3,128,128]{3,2,1,0:T(8,128)(2,1)}), bf16[16,3,128,128]{3,2,1,0:T(8,128)(2,1)S(1)}, u32[]{:S(2)}, u32[]{:S(2)}) %all-to-all-start.1) | async-done | bytes 1572896 | tf_op jit(solution)/shard_map/all_to_all | solution.py:377
  165.4 2.9 %join_heads.1 = f32[128,3,16,128]{3,2,1,0:T(8,128)} custom-call(bf16[16,3,128,128]{3,2,1,0:T(8,128)(2,1)S(1)} %all-to-all-done.1.x_ref), custom_call_target="tpu_custom_call" | custom-call | tf_op jit(solution)/shard_map/join_heads/pallas_call | solution.py:245
  (114 shorter events, 28.6 us)
Async XLA Ops:
  3.0 4.2 %collective-permute-start = (bf16[3,128,128]{2,1,0:T(8,128)(2,1)S(1)}, bf16[3,128,128]{2,1,0:T(8,128)(2,1)S(1)}, u32[]{:S(2)}, u32[]{:S(2)}) collective-permute-start(bf16[3,128,128]{2,1,0:T(8,128)(2,1)S(1)} %get-tuple-element.24), channel_id=1, source_target_pairs={{0,2},{2,0},{4,6},{6,4},{8,10},{10,8},{12,14},{14,12},{16,18},{18,... | collective-permute-start | bytes 294920 | tf_op jit(solution)/shard_map/ppermute | solution.py:382
  3.7 4.3 %collective-permute-start.1 = (bf16[3,128,128]{2,1,0:T(8,128)(2,1)S(1)}, bf16[3,128,128]{2,1,0:T(8,128)(2,1)S(1)}, u32[]{:S(2)}, u32[]{:S(2)}) collective-permute-start(bf16[3,128,128]{2,1,0:T(8,128)(2,1)S(1)} %get-tuple-element.25), channel_id=1, source_target_pairs={{0,4},{2,6},{4,0},{6,2},{8,12},{10,14},{12,8},{14,10},{16,20},{18,... | collective-permute-start | bytes 294920 | tf_op jit(solution)/shard_map/ppermute | solution.py:382
  4.0 6.7 %collective-permute-start.2 = (bf16[3,128,128]{2,1,0:T(8,128)(2,1)S(1)}, bf16[3,128,128]{2,1,0:T(8,128)(2,1)S(1)}, u32[]{:S(2)}, u32[]{:S(2)}) collective-permute-start(bf16[3,128,128]{2,1,0:T(8,128)(2,1)S(1)} %get-tuple-element.26), channel_id=1, source_target_pairs={{0,6},{2,4},{4,2},{6,0},{8,14},{10,12},{12,10},{14,8},{16,22},{18,... | collective-permute-start | bytes 294920 | tf_op jit(solution)/shard_map/ppermute | solution.py:382
  5.5 7.5 %collective-permute-start.3 = (bf16[3,128,128]{2,1,0:T(8,128)(2,1)S(1)}, bf16[3,128,128]{2,1,0:T(8,128)(2,1)S(1)}, u32[]{:S(2)}, u32[]{:S(2)}) collective-permute-start(bf16[3,128,128]{2,1,0:T(8,128)(2,1)S(1)} %get-tuple-element.27), channel_id=1, source_target_pairs={{0,8},{2,10},{4,12},{6,14},{8,0},{10,2},{12,4},{14,6},{16,24},{18,... | collective-permute-start | bytes 294920 | tf_op jit(solution)/shard_map/ppermute | solution.py:382
  5.6 7.8 %collective-permute-start.4 = (bf16[3,128,128]{2,1,0:T(8,128)(2,1)S(1)}, bf16[3,128,128]{2,1,0:T(8,128)(2,1)S(1)}, u32[]{:S(2)}, u32[]{:S(2)}) collective-permute-start(bf16[3,128,128]{2,1,0:T(8,128)(2,1)S(1)} %get-tuple-element.28), channel_id=1, source_target_pairs={{0,10},{2,8},{4,14},{6,12},{8,2},{10,0},{12,6},{14,4},{16,26},{18,... | collective-permute-start | bytes 294920 | tf_op jit(solution)/shard_map/ppermute | solution.py:382
  7.2 76.3 %copy-start.2 = (bf16[3,128,128]{2,1,0:T(8,128)(2,1)}, bf16[3,128,128]{2,1,0:T(8,128)(2,1)S(1)}, u32[]{:S(2)}) copy-start(bf16[3,128,128]{2,1,0:T(8,128)(2,1)S(1)} %collective-permute-done.refs_1_) | copy-start | bytes 294916
  7.2 8.1 %collective-permute-start.5 = (bf16[3,128,128]{2,1,0:T(8,128)(2,1)S(1)}, bf16[3,128,128]{2,1,0:T(8,128)(2,1)S(1)}, u32[]{:S(2)}, u32[]{:S(2)}) collective-permute-start(bf16[3,128,128]{2,1,0:T(8,128)(2,1)S(1)} %get-tuple-element.29), channel_id=1, source_target_pairs={{0,12},{2,14},{4,8},{6,10},{8,4},{10,6},{12,0},{14,2},{16,28},{18,... | collective-permute-start | bytes 294920 | tf_op jit(solution)/shard_map/ppermute | solution.py:382
  8.0 75.5 %copy-start.4 = (bf16[3,128,128]{2,1,0:T(8,128)(2,1)}, bf16[3,128,128]{2,1,0:T(8,128)(2,1)S(1)}, u32[]{:S(2)}) copy-start(bf16[3,128,128]{2,1,0:T(8,128)(2,1)S(1)} %collective-permute-done.1.refs_2_) | copy-start | bytes 294916
  8.0 12.7 %collective-permute-start.6 = (bf16[3,128,128]{2,1,0:T(8,128)(2,1)S(1)}, bf16[3,128,128]{2,1,0:T(8,128)(2,1)S(1)}, u32[]{:S(2)}, u32[]{:S(2)}) collective-permute-start(bf16[3,128,128]{2,1,0:T(8,128)(2,1)S(1)} %get-tuple-element.30), channel_id=1, source_target_pairs={{0,14},{2,12},{4,10},{6,8},{8,6},{10,4},{12,2},{14,0},{16,30},{18,... | collective-permute-start | bytes 294920 | tf_op jit(solution)/shard_map/ppermute | solution.py:382
  10.7 72.9 %copy-start.6 = (bf16[3,128,128]{2,1,0:T(8,128)(2,1)}, bf16[3,128,128]{2,1,0:T(8,128)(2,1)S(1)}, u32[]{:S(2)}) copy-start(bf16[3,128,128]{2,1,0:T(8,128)(2,1)S(1)} %collective-permute-done.2.refs_3_) | copy-start | bytes 294916
  10.7 10.9 %collective-permute-start.7 = (bf16[3,128,128]{2,1,0:T(8,128)(2,1)S(1)}, bf16[3,128,128]{2,1,0:T(8,128)(2,1)S(1)}, u32[]{:S(2)}, u32[]{:S(2)}) collective-permute-start(bf16[3,128,128]{2,1,0:T(8,128)(2,1)S(1)} %get-tuple-element.31), channel_id=1, source_target_pairs={{0,16},{2,18},{4,20},{6,22},{8,24},{10,26},{12,28},{14,30},{16,0},... | collective-permute-start | bytes 294920 | tf_op jit(solution)/shard_map/ppermute | solution.py:382
  13.0 16.0 %collective-permute-start.8 = (bf16[3,128,128]{2,1,0:T(8,128)(2,1)S(1)}, bf16[3,128,128]{2,1,0:T(8,128)(2,1)S(1)}, u32[]{:S(2)}, u32[]{:S(2)}) collective-permute-start(bf16[3,128,128]{2,1,0:T(8,128)(2,1)S(1)} %get-tuple-element.32), channel_id=1, source_target_pairs={{0,18},{2,16},{4,22},{6,20},{8,26},{10,24},{12,30},{14,28},{16,2},... | collective-permute-start | bytes 294920 | tf_op jit(solution)/shard_map/ppermute | solution.py:382
  13.5 17.7 %collective-permute-start.9 = (bf16[3,128,128]{2,1,0:T(8,128)(2,1)S(1)}, bf16[3,128,128]{2,1,0:T(8,128)(2,1)S(1)}, u32[]{:S(2)}, u32[]{:S(2)}) collective-permute-start(bf16[3,128,128]{2,1,0:T(8,128)(2,1)S(1)} %get-tuple-element.33), channel_id=1, source_target_pairs={{0,20},{2,22},{4,16},{6,18},{8,28},{10,30},{12,24},{14,26},{16,4},... | collective-permute-start | bytes 294920 | tf_op jit(solution)/shard_map/ppermute | solution.py:382
  15.3 20.9 %collective-permute-start.10 = (bf16[3,128,128]{2,1,0:T(8,128)(2,1)S(1)}, bf16[3,128,128]{2,1,0:T(8,128)(2,1)S(1)}, u32[]{:S(2)}, u32[]{:S(2)}) collective-permute-start(bf16[3,128,128]{2,1,0:T(8,128)(2,1)S(1)} %get-tuple-element.34), channel_id=1, source_target_pairs={{0,22},{2,20},{4,18},{6,16},{8,30},{10,28},{12,26},{14,24},{16,6},... | collective-permute-start | bytes 294920 | tf_op jit(solution)/shard_map/ppermute | solution.py:382
  20.7 19.9 %collective-permute-start.11 = (bf16[3,128,128]{2,1,0:T(8,128)(2,1)S(1)}, bf16[3,128,128]{2,1,0:T(8,128)(2,1)S(1)}, u32[]{:S(2)}, u32[]{:S(2)}) collective-permute-start(bf16[3,128,128]{2,1,0:T(8,128)(2,1)S(1)} %get-tuple-element.35), channel_id=1, source_target_pairs={{0,24},{2,26},{4,28},{6,30},{8,16},{10,18},{12,20},{14,22},{16,8},... | collective-permute-start | bytes 294920 | tf_op jit(solution)/shard_map/ppermute | solution.py:382
  21.6 21.9 %collective-permute-start.12 = (bf16[3,128,128]{2,1,0:T(8,128)(2,1)S(1)}, bf16[3,128,128]{2,1,0:T(8,128)(2,1)S(1)}, u32[]{:S(2)}, u32[]{:S(2)}) collective-permute-start(bf16[3,128,128]{2,1,0:T(8,128)(2,1)S(1)} %get-tuple-element.36), channel_id=1, source_target_pairs={{0,26},{2,24},{4,30},{6,28},{8,18},{10,16},{12,22},{14,20},{16,10}... | collective-permute-start | bytes 294920 | tf_op jit(solution)/shard_map/ppermute | solution.py:382
  29.0 15.8 %collective-permute-start.13 = (bf16[3,128,128]{2,1,0:T(8,128)(2,1)S(1)}, bf16[3,128,128]{2,1,0:T(8,128)(2,1)S(1)}, u32[]{:S(2)}, u32[]{:S(2)}) collective-permute-start(bf16[3,128,128]{2,1,0:T(8,128)(2,1)S(1)} %get-tuple-element.37), channel_id=1, source_target_pairs={{0,28},{2,30},{4,24},{6,26},{8,20},{10,22},{12,16},{14,18},{16,12}... | collective-permute-start | bytes 294920 | tf_op jit(solution)/shard_map/ppermute | solution.py:382
  31.1 16.0 %collective-permute-start.14 = (bf16[3,128,128]{2,1,0:T(8,128)(2,1)S(1)}, bf16[3,128,128]{2,1,0:T(8,128)(2,1)S(1)}, u32[]{:S(2)}, u32[]{:S(2)}) collective-permute-start(bf16[3,128,128]{2,1,0:T(8,128)(2,1)S(1)} %get-tuple-element.38), channel_id=1, source_target_pairs={{0,30},{2,28},{4,26},{6,24},{8,22},{10,20},{12,18},{14,16},{16,14}... | collective-permute-start | bytes 294920 | tf_op jit(solution)/shard_map/ppermute | solution.py:382
  36.2 30.9 %collective-permute-start.26 = (bf16[64,8192]{1,0:T(8,128)(2,1)}, bf16[64,8192]{1,0:T(8,128)(2,1)S(1)}, u32[]{:S(2)}, u32[]{:S(2)}) collective-permute-start(bf16[64,8192]{1,0:T(8,128)(2,1)} %own_ref.1), channel_id=1, source_target_pairs={{0,1},{1,0},{2,3},{3,2},{4,5},{5,4},{6,7},{7,6},{8,9},{9,8},{10,11... | collective-permute-start | bytes 3145736 | tf_op jit(solution)/shard_map/ppermute | solution.py:379
  51.4 4.6 %collective-permute-start.15 = (bf16[4,128,128]{2,1,0:T(8,128)(2,1)S(1)}, bf16[4,128,128]{2,1,0:T(8,128)(2,1)S(1)}, u32[]{:S(2)}, u32[]{:S(2)}) collective-permute-start(bf16[4,128,128]{2,1,0:T(8,128)(2,1)S(1)} %get-tuple-element.40.refs_17_), channel_id=1, source_target_pairs={{0,8},{2,10},{4,12},{6,14},{8,0},{10,2},{12,4},{14,6},{16,24},{18,... | collective-permute-start | bytes 393224 | tf_op jit(solution)/shard_map/ppermute | solution.py:388
  51.5 11.4 %collective-permute-start.16 = (bf16[4,128,128]{2,1,0:T(8,128)(2,1)S(1)}, bf16[4,128,128]{2,1,0:T(8,128)(2,1)S(1)}, u32[]{:S(2)}, u32[]{:S(2)}) collective-permute-start(bf16[4,128,128]{2,1,0:T(8,128)(2,1)S(1)} %get-tuple-element.41.refs_18_), channel_id=1, source_target_pairs={{0,16},{2,18},{4,20},{6,22},{8,24},{10,26},{12,28},{14,30},{16,0},... | collective-permute-start | bytes 393224 | tf_op jit(solution)/shard_map/ppermute | solution.py:388
  54.6 11.1 %collective-permute-start.17 = (bf16[4,128,128]{2,1,0:T(8,128)(2,1)S(1)}, bf16[4,128,128]{2,1,0:T(8,128)(2,1)S(1)}, u32[]{:S(2)}, u32[]{:S(2)}) collective-permute-start(bf16[4,128,128]{2,1,0:T(8,128)(2,1)S(1)} %get-tuple-element.42.refs_19_), channel_id=1, source_target_pairs={{0,24},{2,26},{4,28},{6,30},{8,16},{10,18},{12,20},{14,22},{16,8},... | collective-permute-start | bytes 393224 | tf_op jit(solution)/shard_map/ppermute | solution.py:388
  65.8 25.6 %collective-permute-start.18 = (bf16[4,128,128]{2,1,0:T(8,128)(2,1)S(1)}, bf16[4,128,128]{2,1,0:T(8,128)(2,1)S(1)}, u32[]{:S(2)}, u32[]{:S(2)}) collective-permute-start(bf16[4,128,128]{2,1,0:T(8,128)(2,1)S(1)} %pad_maximum_fusion), channel_id=1, source_target_pairs={{0,2},{2,0},{4,6},{6,4},{8,10},{10,8},{12,14},{14,12},{16,18},{18,... | collective-permute-start | bytes 393224 | tf_op jit(solution)/shard_map/ppermute | solution.py:393
  83.6 22.4 %all-to-all-start = ((bf16[16,128,128]{2,1,0:T(8,128)(2,1)}), bf16[16,128,128]{2,1,0:T(8,128)(2,1)S(1)}, u32[]{:S(2)}, u32[]{:S(2)}) async-start(bf16[16,128,128]{2,1,0:T(8,128)(2,1)} %project_back.1), calls=%async_computation | async-start | bytes 1048576 | tf_op jit(solution)/shard_map/all_to_all | solution.py:377
  89.2 7.9 %collective-permute-start.19 = (bf16[4,128,128]{2,1,0:T(8,128)(2,1)S(1)}, bf16[4,128,128]{2,1,0:T(8,128)(2,1)S(1)}, u32[]{:S(2)}, u32[]{:S(2)}) collective-permute-start(bf16[4,128,128]{2,1,0:T(8,128)(2,1)S(1)} %pad_maximum_fusion.1), channel_id=1, source_target_pairs={{0,4},{2,6},{4,0},{6,2},{8,12},{10,14},{12,8},{14,10},{16,20},{18,... | collective-permute-start | bytes 393224 | tf_op jit(solution)/shard_map/ppermute | solution.py:393
  89.6 11.6 %collective-permute-start.20 = (bf16[4,128,128]{2,1,0:T(8,128)(2,1)S(1)}, bf16[4,128,128]{2,1,0:T(8,128)(2,1)S(1)}, u32[]{:S(2)}, u32[]{:S(2)}) collective-permute-start(bf16[4,128,128]{2,1,0:T(8,128)(2,1)S(1)} %pad_maximum_fusion.2), channel_id=1, source_target_pairs={{0,6},{2,4},{4,2},{6,0},{8,14},{10,12},{12,10},{14,8},{16,22},{18,... | collective-permute-start | bytes 393224 | tf_op jit(solution)/shard_map/ppermute | solution.py:393
  122.7 42.7 %all-to-all-start.1 = ((bf16[16,3,128,128]{3,2,1,0:T(8,128)(2,1)}), bf16[16,3,128,128]{3,2,1,0:T(8,128)(2,1)S(1)}, u32[]{:S(2)}, u32[]{:S(2)}) async-start(bf16[16,3,128,128]{3,2,1,0:T(8,128)(2,1)} %copy-done), calls=%async_computation.1 | async-start | bytes 3145728 | tf_op jit(solution)/shard_map/all_to_all | solution.py:377
  129.3 23.8 %collective-permute-start.25 = (bf16[64,2048]{1,0:T(8,128)(2,1)S(1)}, bf16[64,2048]{1,0:T(8,128)(2,1)S(1)}, u32[]{:S(2)}, u32[]{:S(2)}) collective-permute-start(bf16[64,2048]{1,0:T(8,128)(2,1)S(1)} %dynamic-slice_convert_fusion), channel_id=1, source_target_pairs={{0,1},{1,0},{2,3},{3,2},{4,5},{5,4},{6,7},{7,6},{8,9},{9,8},{10,11... | collective-permute-start | bytes 786440 | tf_op jit(solution)/shard_map/ppermute | solution.py:407
  134.3 18.8 %collective-permute-start.24 = (bf16[64,2048]{1,0:T(8,128)(2,1)S(1)}, bf16[64,2048]{1,0:T(8,128)(2,1)S(1)}, u32[]{:S(2)}, u32[]{:S(2)}) collective-permute-start(bf16[64,2048]{1,0:T(8,128)(2,1)S(1)} %dynamic-slice_convert_fusion.1), channel_id=1, source_target_pairs={{0,1},{1,0},{2,3},{3,2},{4,5},{5,4},{6,7},{7,6},{8,9},{9,8},{10,11... | collective-permute-start | bytes 786440 | tf_op jit(solution)/shard_map/ppermute | solution.py:407
  140.2 12.9 %collective-permute-start.23 = (bf16[64,2048]{1,0:T(8,128)(2,1)S(1)}, bf16[64,2048]{1,0:T(8,128)(2,1)S(1)}, u32[]{:S(2)}, u32[]{:S(2)}) collective-permute-start(bf16[64,2048]{1,0:T(8,128)(2,1)S(1)} %dynamic-slice_convert_fusion.2), channel_id=1, source_target_pairs={{0,1},{1,0},{2,3},{3,2},{4,5},{5,4},{6,7},{7,6},{8,9},{9,8},{10,11... | collective-permute-start | bytes 786440 | tf_op jit(solution)/shard_map/ppermute | solution.py:407
  146.4 4.2 %collective-permute-start.22 = (bf16[64,1024]{1,0:T(8,128)(2,1)S(1)}, bf16[64,1024]{1,0:T(8,128)(2,1)S(1)}, u32[]{:S(2)}, u32[]{:S(2)}) collective-permute-start(bf16[64,1024]{1,0:T(8,128)(2,1)S(1)} %dynamic-slice_convert_fusion.3), channel_id=1, source_target_pairs={{0,1},{1,0},{2,3},{3,2},{4,5},{5,4},{6,7},{7,6},{8,9},{9,8},{10,11... | collective-permute-start | bytes 393224 | tf_op jit(solution)/shard_map/ppermute | solution.py:407
  147.7 5.4 %collective-permute-start.21 = (bf16[64,1024]{1,0:T(8,128)(2,1)S(1)}, bf16[64,1024]{1,0:T(8,128)(2,1)S(1)}, u32[]{:S(2)}, u32[]{:S(2)}) collective-permute-start(bf16[64,1024]{1,0:T(8,128)(2,1)S(1)} %dynamic-slice_convert_fusion.4), channel_id=1, source_target_pairs={{0,1},{1,0},{2,3},{3,2},{4,5},{5,4},{6,7},{7,6},{8,9},{9,8},{10,11... | collective-permute-start | bytes 393224 | tf_op jit(solution)/shard_map/ppermute | solution.py:407
  (29 other events, 520.6 us)

commit v8 on v7

--- a/solution.py
+++ b/solution.py
@@ -93,8 +93,8 @@
         out_ref[h] = y[h * HD : (h + 1) * HD].T.astype(jnp.bfloat16)
 
 
-def forward_kernel(step, outer, me_ref, *refs):
-    parts, rest = refs[: -5 - outer], refs[-5 - outer :]
+def forward_kernel(step, me_ref, *refs):
+    parts, rest = refs[: -5 - PLANE], refs[-5 - PLANE :]
     lse_ref, *sent, qkv_ref, att_ref, v_t, s_buf = rest
     me = me_ref[0]
     for k, part in enumerate(parts):
@@ -128,18 +128,18 @@
             acc = acc + dot_nn(v_t[j], (s_buf[i % 2, j] * inverse).astype(jnp.bfloat16))
         att_ref[i * per : (i + 1) * per] = acc.T.astype(jnp.bfloat16).reshape(per, unit, HD)
         lse_ref[i] = top * scale + jnp.log2(total)
-    for d, ref in enumerate(sent):
-        for e in range(PLANE):
-            ref[e] = att_ref[me ^ (PLANE * d + e)]
+    for e, ref in enumerate(sent):
+        for d in range(chunks // PLANE):
+            ref[d] = att_ref[me ^ (PLANE * d + e)]
 
 
 def gather_kernel(me_ref, *refs):
     *parts, out_ref = refs
-    own, others = parts[: len(parts) - PLANE + 1], parts[len(parts) - PLANE + 1 :]
-    for d, ref in enumerate(own):
-        out_ref[me_ref[0] ^ (PLANE * d)] = ref[0]
-        for e in range(1, PLANE):
-            out_ref[me_ref[0] ^ (PLANE * d + e)] = others[e - 1][d]
+    plane, others = parts[:PLANE], parts[PLANE:]
+    for e, ref in enumerate(plane):
+        out_ref[me_ref[0] ^ e] = ref[0]
+        for d, other in enumerate(others, 1):
+            out_ref[me_ref[0] ^ (PLANE * d + e)] = other[e]
 
 
 def finish_kernel(turn_ref, *refs):
@@ -159,7 +159,7 @@
     me = me_ref[0]
     for k, part in enumerate(parts):
         qkv_ref[me ^ k] = part[...]
-        att_ref[me ^ k] = own[k // PLANE][k % PLANE]
+        att_ref[me ^ k] = own[k % PLANE][k // PLANE]
     chunks, _, unit, _ = qkv_ref.shape
     per = step // unit
     blocks = chunks // per
@@ -289,13 +289,13 @@
     blocks = length // step
     area = length * length // 2
     return pl.pallas_call(
-        functools.partial(forward_kernel, step, outer),
+        functools.partial(forward_kernel, step),
         out_shape=(
             jax.ShapeDtypeStruct((blocks, 1, step), jnp.float32),
-            *[jax.ShapeDtypeStruct((PLANE, unit, HD), jnp.bfloat16)] * outer,
+            *[jax.ShapeDtypeStruct((outer, unit, HD), jnp.bfloat16)] * PLANE,
         ),
         in_specs=[in_smem(), *in_vmem(chunks)],
-        out_specs=tuple(in_vmem(1 + outer)),
+        out_specs=tuple(in_vmem(1 + PLANE)),
         scratch_shapes=[
             pltpu.VMEM((chunks, 3, unit, HD), jnp.bfloat16),
             pltpu.VMEM((chunks, unit, HD), jnp.bfloat16),
@@ -310,17 +310,16 @@
     )(me, *parts)
 
 
-def gather_heads(me, own, others):
-    chunks = PLANE * len(own)
-    shape = (chunks, *own[0].shape[1:])
+def gather_heads(me, plane, others):
+    shape = (PLANE * (len(others) + 1), *plane[0].shape[1:])
     return pl.pallas_call(
         gather_kernel,
         out_shape=jax.ShapeDtypeStruct(shape, jnp.bfloat16),
-        in_specs=[in_smem(), *in_vmem(len(own) + PLANE - 1)],
+        in_specs=[in_smem(), *in_vmem(PLANE + len(others))],
         out_specs=in_vmem(1)[0],
         compiler_params=pltpu.CompilerParams(vmem_limit_bytes=2 * MIB),
         name="gather_heads",
-    )(me, *own, *others)
+    )(me, *plane, *others)
 
 
 def finish(turn, parts):
@@ -383,16 +382,17 @@
     g = project_back(turn.reshape(1), grad_out, other_out, attn_out)
     g = spread(g)
     lse, *own = attend(me, parts, step)
-    mixed_own = list(own)
-    for d in range(1, len(own)):
-        mixed_own[d] = lax.ppermute(own[d], "ctx", [(i, i ^ (PLANE * d)) for i in range(heads)])
+    plane = list(own)
+    for e in range(1, PLANE):
+        plane[e] = lax.ppermute(own[e], "ctx", [(i, i ^ e) for i in range(heads)])
+    others = []
+    for d in range(1, heads // PLANE):
+        sent = jnp.stack([x[d] for x in plane])
+        pairs = [(i, i ^ (PLANE * d)) for i in range(heads)]
+        others.append(lax.ppermute(sent, "ctx", pairs))
     grads = attend_grad(me, g, lse, parts, own, step)
-    others = []
-    for e in range(1, PLANE):
-        sent = jnp.stack([x[e] for x in mixed_own])
-        others.append(lax.ppermute(sent, "ctx", [(i, i ^ e) for i in range(heads)]))
     grads = spread(grads)
-    local = gather_heads(me, mixed_own, others)
+    local = gather_heads(me, plane, others)
     pieces = []
     start = 0
     for eighths in MIX_PARTS:

time: 169 us -> 176 us (1.041)
  the two profiles are of different devices: /device:TPU:15 before, /device:TPU:13 now
where the time goes in v8:
time: 176 us; the launch traced here: 175 us
  waiting for transfers between devices  67.4 us (38%)
  starting transfers between devices  42.9 us (24%)
  Pallas kernels  32.7 us (19%)
  matrix products  19.8 us (11%)
  local copies, waits for them, and re-layouts  11.5 us (7%)
    ppermute x15, waiting for transfers between devices, by_head(): parts[k] = lax.ppermute(parts[k], 'ctx', [(i, i ^ k) for i in range(heads)])  23.7 us
    ppermute x3, waiting for transfers between devices, by_head(): others.append(lax.ppermute(sent, 'ctx', pairs))  22.2 us
    dot_general x5, matrix products, by_head(): jnp.einsum('hrd,hdm->rm', local, weights[:, :, start:stop], preferred_ele...  19.8 us
    ppermute x15, starting transfers between devices, by_head(): parts[k] = lax.ppermute(parts[k], 'ctx', [(i, i ^ k) for i in range(heads)])  19.2 us
    pallas_call x1, Pallas kernels, project_back(): pl.pallas_call(back_kernel, grid=(heads // group,), out_shape=jax.ShapeDt...  15.1 us
    all_to_all x2, starting transfers between devices, spread(): return lax.all_to_all(x, 'ctx', 0, 0, tiled=True)  13.5 us
    unnamed x64, local copies, waits for them, and re-layouts  11.4 us
    all_to_all x2, waiting for transfers between devices, spread(): return lax.all_to_all(x, 'ctx', 0, 0, tiled=True)  9.84 us
  transfers between devices with their start and end apart: 29, of which 16 were waited for; matrix products, arithmetic and copies ran while one was open for 11% of the time, Pallas kernels for 12%

profile of v8, /device:TPU:13, one launch (start us, length us, event | category | flops | bytes accessed | tf_op | source)
XLA Modules:
  0.0 175.4 jit_solution(13618234519535778089)
XLA Ops:
  0.6 2.4 %split_heads.1 = (bf16[3,128,128]{2,1,0:T(8,128)(2,1)S(1)}, bf16[3,128,128]{2,1,0:T(8,128)(2,1)S(1)}, bf16[3,128,128]{2,1,0:T(8,128)(2,1)S(1)}, bf16[3,128,128]{...) custom-call(s32[1]{0:T(128)} %bitcast.1.me_ref, ...), custom_call_target="tpu_custom_call" | custom-call | tf_op jit(solution)/shard_map/split_heads/pallas_call | solution.py:230
  5.6 1.6 collective-permute-start.4
  8.0 1.8 %collective-permute-start.6 = (bf16[3,128,128]{2,1,0:T(8,128)(2,1)S(1)}, bf16[3,128,128]{2,1,0:T(8,128)(2,1)S(1)}, u32[]{:S(2)}, u32[]{:S(2)}) collective-permute-start(bf16[3,128,128]{2,1,0:T(8,128)(2,1)S(1)} %get-tuple-element.30), channel_id=1, source_target_pairs={{0,14},{2,12},{4,10},{6,8},{8,6},{10,4},{12,2},{14,0},{16,30},{18,... | collective-permute-start | bytes 294920 | tf_op jit(solution)/shard_map/ppermute | solution.py:381
  10.7 2.3 %collective-permute-start.7 = (bf16[3,128,128]{2,1,0:T(8,128)(2,1)S(1)}, bf16[3,128,128]{2,1,0:T(8,128)(2,1)S(1)}, u32[]{:S(2)}, u32[]{:S(2)}) collective-permute-start(bf16[3,128,128]{2,1,0:T(8,128)(2,1)S(1)} %get-tuple-element.31), channel_id=1, source_target_pairs={{0,16},{2,18},{4,20},{6,22},{8,24},{10,26},{12,28},{14,30},{16,0},... | collective-permute-start | bytes 294920 | tf_op jit(solution)/shard_map/ppermute | solution.py:381
  13.5 1.8 %collective-permute-start.9 = (bf16[3,128,128]{2,1,0:T(8,128)(2,1)S(1)}, bf16[3,128,128]{2,1,0:T(8,128)(2,1)S(1)}, u32[]{:S(2)}, u32[]{:S(2)}) collective-permute-start(bf16[3,128,128]{2,1,0:T(8,128)(2,1)S(1)} %get-tuple-element.33), channel_id=1, source_target_pairs={{0,20},{2,22},{4,16},{6,18},{8,28},{10,30},{12,24},{14,26},{16,4},... | collective-permute-start | bytes 294920 | tf_op jit(solution)/shard_map/ppermute | solution.py:381
  15.3 5.4 %collective-permute-start.10 = (bf16[3,128,128]{2,1,0:T(8,128)(2,1)S(1)}, bf16[3,128,128]{2,1,0:T(8,128)(2,1)S(1)}, u32[]{:S(2)}, u32[]{:S(2)}) collective-permute-start(bf16[3,128,128]{2,1,0:T(8,128)(2,1)S(1)} %get-tuple-element.34), channel_id=1, source_target_pairs={{0,22},{2,20},{4,18},{6,16},{8,30},{10,28},{12,26},{14,24},{16,6},... | collective-permute-start | bytes 294920 | tf_op jit(solution)/shard_map/ppermute | solution.py:381
  21.6 7.4 %collective-permute-done.8.refs_9_ = bf16[3,128,128]{2,1,0:T(8,128)(2,1)S(1)} collective-permute-done((bf16[3,128,128]{2,1,0:T(8,128)(2,1)S(1)}, bf16[3,128,128]{2,1,0:T(8,128)(2,1)S(1)}, u32[]{:S(2)}, u32[]{:S(2)}) %collective-permute-start.8) | collective-permute-done | bytes 98336 | tf_op jit(solution)/shard_map/ppermute | solution.py:381
  29.0 2.1 %collective-permute-done.9.refs_10_ = bf16[3,128,128]{2,1,0:T(8,128)(2,1)S(1)} collective-permute-done((bf16[3,128,128]{2,1,0:T(8,128)(2,1)S(1)}, bf16[3,128,128]{2,1,0:T(8,128)(2,1)S(1)}, u32[]{:S(2)}, u32[]{:S(2)}) %collective-permute-start.9) | collective-permute-done | bytes 98336 | tf_op jit(solution)/shard_map/ppermute | solution.py:381
  31.1 2.2 %collective-permute-start.14 = (bf16[3,128,128]{2,1,0:T(8,128)(2,1)S(1)}, bf16[3,128,128]{2,1,0:T(8,128)(2,1)S(1)}, u32[]{:S(2)}, u32[]{:S(2)}) collective-permute-start(bf16[3,128,128]{2,1,0:T(8,128)(2,1)S(1)} %get-tuple-element.38), channel_id=1, source_target_pairs={{0,30},{2,28},{4,26},{6,24},{8,22},{10,20},{12,18},{14,16},{16,14}... | collective-permute-start | bytes 294920 | tf_op jit(solution)/shard_map/ppermute | solution.py:381
  33.3 2.9 %collective-permute-done.10.refs_11_ = bf16[3,128,128]{2,1,0:T(8,128)(2,1)S(1)} collective-permute-done((bf16[3,128,128]{2,1,0:T(8,128)(2,1)S(1)}, bf16[3,128,128]{2,1,0:T(8,128)(2,1)S(1)}, u32[]{:S(2)}, u32[]{:S(2)}) %collective-permute-start.10) | collective-permute-done | bytes 98336 | tf_op jit(solution)/shard_map/ppermute | solution.py:381
  37.5 3.1 %collective-permute-done.11.refs_12_ = bf16[3,128,128]{2,1,0:T(8,128)(2,1)S(1)} collective-permute-done((bf16[3,128,128]{2,1,0:T(8,128)(2,1)S(1)}, bf16[3,128,128]{2,1,0:T(8,128)(2,1)S(1)}, u32[]{:S(2)}, u32[]{:S(2)}) %collective-permute-start.11) | collective-permute-done | bytes 98336 | tf_op jit(solution)/shard_map/ppermute | solution.py:381
  40.6 2.9 %collective-permute-done.12.refs_13_ = bf16[3,128,128]{2,1,0:T(8,128)(2,1)S(1)} collective-permute-done((bf16[3,128,128]{2,1,0:T(8,128)(2,1)S(1)}, bf16[3,128,128]{2,1,0:T(8,128)(2,1)S(1)}, u32[]{:S(2)}, u32[]{:S(2)}) %collective-permute-start.12) | collective-permute-done | bytes 98336 | tf_op jit(solution)/shard_map/ppermute | solution.py:381
  44.8 2.3 %collective-permute-done.14.refs_15_ = bf16[3,128,128]{2,1,0:T(8,128)(2,1)S(1)} collective-permute-done((bf16[3,128,128]{2,1,0:T(8,128)(2,1)S(1)}, bf16[3,128,128]{2,1,0:T(8,128)(2,1)S(1)}, u32[]{:S(2)}, u32[]{:S(2)}) %collective-permute-start.14) | collective-permute-done | bytes 98336 | tf_op jit(solution)/shard_map/ppermute | solution.py:381
  47.1 4.3 %attend.1 = (f32[4,1,512]{2,1,0:T(1,128)S(1)}, bf16[4,128,128]{2,1,0:T(8,128)(2,1)S(1)}, bf16[4,128,128]{2,1,0:T(8,128)(2,1)S(1)}, bf16[4,128,128]{2,1,0:T(8,128)(2,1)S(1)}, bf16[4,128,128]{2,1,0:T(8,128)(2,1)S(1)}) custom-call(s32[1]{0:T(128)} %bitcast.1.me_ref, bf16[3,128,128]{2,1,0:T(8,128)(2,1)S(1)} %get-tuple-element.23.refs_0_, ...), custom_call_target="tpu_custom_call" | custom-call | flops 1073741824 | bytes 2097152 | tf_op jit(solution)/shard_map/attend/pallas_call | solution.py:291
  53.8 3.2 %collective-permute-done.16.refs_2_ = bf16[4,128,128]{2,1,0:T(8,128)(2,1)S(1)} collective-permute-done((bf16[4,128,128]{2,1,0:T(8,128)(2,1)S(1)}, bf16[4,128,128]{2,1,0:T(8,128)(2,1)S(1)}, u32[]{:S(2)}, u32[]{:S(2)}) %collective-permute-start.16) | collective-permute-done | bytes 131104 | tf_op jit(solution)/shard_map/ppermute | solution.py:387
  57.0 3.3 %collective-permute-done.17.refs_3_ = bf16[4,128,128]{2,1,0:T(8,128)(2,1)S(1)} collective-permute-done((bf16[4,128,128]{2,1,0:T(8,128)(2,1)S(1)}, bf16[4,128,128]{2,1,0:T(8,128)(2,1)S(1)}, u32[]{:S(2)}, u32[]{:S(2)}) %collective-permute-start.17) | collective-permute-done | bytes 131104 | tf_op jit(solution)/shard_map/ppermute | solution.py:387
  61.7 15.1 %project_back.1 = bf16[16,128,128]{2,1,0:T(8,128)(2,1)} custom-call(s32[1]{0:T(128)} %bitcast.turn_ref, bf16[64,8192]{1,0:T(8,128)(2,1)S(1)} %copy-done.1, bf16[64,8192]{1,0:T(8,128)(2,1)S(1)} %collective-permute-done.26.other_ref, bf16[2048,8192]{1,0:T(8,128)(2,1)} %w_ref.1), custom_call_target="tpu_custom_call" | custom-call | flops 4294967296 | bytes 33554432 | tf_op jit(solution)/shard_map/project_back/pallas_call | solution.py:262
  76.9 8.7 %all-to-all-start = ((bf16[16,128,128]{2,1,0:T(8,128)(2,1)}), bf16[16,128,128]{2,1,0:T(8,128)(2,1)S(1)}, u32[]{:S(2)}, u32[]{:S(2)}) async-start(bf16[16,128,128]{2,1,0:T(8,128)(2,1)} %project_back.1), calls=%async_computation | async-start | bytes 1048576 | tf_op jit(solution)/shard_map/all_to_all | solution.py:376
  85.6 2.2 %collective-permute-start.19 = (bf16[4,128,128]{2,1,0:T(8,128)(2,1)S(1)}, bf16[4,128,128]{2,1,0:T(8,128)(2,1)S(1)}, u32[]{:S(2)}, u32[]{:S(2)}) collective-permute-start(bf16[4,128,128]{2,1,0:T(8,128)(2,1)S(1)} %pad_maximum_fusion.1), channel_id=1, source_target_pairs={{0,16},{2,18},{4,20},{6,22},{8,24},{10,26},{12,28},{14,30},{16,0},... | collective-permute-start | bytes 393224 | tf_op jit(solution)/shard_map/ppermute | solution.py:392
  87.8 17.6 %collective-permute-done.19.refs_5_ = bf16[4,128,128]{2,1,0:T(8,128)(2,1)S(1)} collective-permute-done((bf16[4,128,128]{2,1,0:T(8,128)(2,1)S(1)}, bf16[4,128,128]{2,1,0:T(8,128)(2,1)S(1)}, u32[]{:S(2)}, u32[]{:S(2)}) %collective-permute-start.19) | collective-permute-done | bytes 131104 | tf_op jit(solution)/shard_map/ppermute | solution.py:392
  105.5 4.6 %collective-permute-done.20.refs_6_ = bf16[4,128,128]{2,1,0:T(8,128)(2,1)S(1)} collective-permute-done((bf16[4,128,128]{2,1,0:T(8,128)(2,1)S(1)}, bf16[4,128,128]{2,1,0:T(8,128)(2,1)S(1)}, u32[]{:S(2)}, u32[]{:S(2)}) %collective-permute-start.20) | collective-permute-done | bytes 131104 | tf_op jit(solution)/shard_map/ppermute | solution.py:392
  110.2 4.7 %fusion.16.refs_8_ = f32[128,2048]{1,0:T(8,128)S(1)} fusion(bf16[16,128,128]{2,1,0:T(8,128)(2,1)S(1)} %gather_heads.1, bf16[16,128,8192]{2,1,0:T(8,128)(2,1)} %bitcast.20), kind=kOutput, calls=%fused_computation.12 | convolution fusion | flops 1073741824 | bytes 9961472 | tf_op jit(solution)/shard_map/hrd,hdm->rm/dot_general | solution.py:400
  123.9 6.5 %attend_grad.1 = bf16[16,3,128,128]{3,2,1,0:T(8,128)(2,1)S(1)} custom-call(s32[1]{0:T(128)} %bitcast.1.me_ref, bf16[16,128,128]{2,1,0:T(8,128)(2,1)S(1)} %all-to-all-done.g_ref, f32[4,1,512]{2,1,0:T(1,128)S(1)} %get-tuple-element.43.lse_ref, bf16[3,128,128]{2,1,0:T(8,128)(2,1)S(1)} %get-tuple-element.23.refs_0_, bf16[3,128,128]{2,1,0:T(8,128)(2,1)S(1)} %copy-done.3, ...), custom_call_target="tpu_custom_call" | custom-call | flops 2684354560 | bytes 4194304 | tf_op jit(solution)/shard_map/attend_grad/pallas_call | solution.py:345
  131.6 4.8 %all-to-all-start.1 = ((bf16[16,3,128,128]{3,2,1,0:T(8,128)(2,1)}), bf16[16,3,128,128]{3,2,1,0:T(8,128)(2,1)S(1)}, u32[]{:S(2)}, u32[]{:S(2)}) async-start(bf16[16,3,128,128]{3,2,1,0:T(8,128)(2,1)} %copy-done), calls=%async_computation.1 | async-start | bytes 3145728 | tf_op jit(solution)/shard_map/all_to_all | solution.py:376
  137.7 4.6 %fusion.13.refs_6_ = f32[128,2048]{1,0:T(8,128)S(1)} fusion(bf16[16,128,128]{2,1,0:T(8,128)(2,1)S(1)} %gather_heads.1, bf16[16,128,8192]{2,1,0:T(8,128)(2,1)} %bitcast.21), kind=kOutput, calls=%fused_computation.11 | convolution fusion | flops 1073741824 | bytes 9961472 | tf_op jit(solution)/shard_map/hrd,hdm->rm/dot_general | solution.py:400
  142.7 4.6 %fusion.10.refs_4_ = f32[128,2048]{1,0:T(8,128)S(1)} fusion(bf16[16,128,128]{2,1,0:T(8,128)(2,1)S(1)} %gather_heads.1, bf16[16,128,8192]{2,1,0:T(8,128)(2,1)} %bitcast.22), kind=kOutput, calls=%fused_computation.10 | convolution fusion | flops 1073741824 | bytes 9961472 | tf_op jit(solution)/shard_map/hrd,hdm->rm/dot_general | solution.py:400
  148.6 2.9 %fusion.22.refs_2_ = f32[128,1024]{1,0:T(8,128)S(1)} fusion(bf16[16,128,128]{2,1,0:T(8,128)(2,1)S(1)} %gather_heads.1, bf16[16,128,8192]{2,1,0:T(8,128)(2,1)} %bitcast.23), kind=kOutput, calls=%fused_computation.14 | convolution fusion | flops 536870912 | bytes 5242880 | tf_op jit(solution)/shard_map/hrd,hdm->rm/dot_general | solution.py:400
  151.5 2.9 %fusion.19.refs_0_ = f32[128,1024]{1,0:T(8,128)S(1)} fusion(bf16[16,128,128]{2,1,0:T(8,128)(2,1)S(1)} %gather_heads.1, bf16[16,128,8192]{2,1,0:T(8,128)(2,1)} %bitcast.24), kind=kOutput, calls=%fused_computation.13 | convolution fusion | flops 536870912 | bytes 5242880 | tf_op jit(solution)/shard_map/hrd,hdm->rm/dot_general | solution.py:400
  156.1 2.6 %collective-permute-done.22.refs_3_ = bf16[64,1024]{1,0:T(8,128)(2,1)S(1)} collective-permute-done((bf16[64,1024]{1,0:T(8,128)(2,1)S(1)}, bf16[64,1024]{1,0:T(8,128)(2,1)S(1)}, u32[]{:S(2)}, u32[]{:S(2)}) %collective-permute-start.22) | collective-permute-done | bytes 131104 | tf_op jit(solution)/shard_map/ppermute | solution.py:407
  158.7 2.5 %collective-permute-done.21.refs_1_ = bf16[64,1024]{1,0:T(8,128)(2,1)S(1)} collective-permute-done((bf16[64,1024]{1,0:T(8,128)(2,1)S(1)}, bf16[64,1024]{1,0:T(8,128)(2,1)S(1)}, u32[]{:S(2)}, u32[]{:S(2)}) %collective-permute-start.21) | collective-permute-done | bytes 131104 | tf_op jit(solution)/shard_map/ppermute | solution.py:407
  162.7 9.8 %all-to-all-done.1.x_ref = bf16[16,3,128,128]{3,2,1,0:T(8,128)(2,1)S(1)} async-done(((bf16[16,3,128,128]{3,2,1,0:T(8,128)(2,1)}), bf16[16,3,128,128]{3,2,1,0:T(8,128)(2,1)S(1)}, u32[]{:S(2)}, u32[]{:S(2)}) %all-to-all-start.1) | async-done | bytes 1572896 | tf_op jit(solution)/shard_map/all_to_all | solution.py:376
  172.5 2.9 %join_heads.1 = f32[128,3,16,128]{3,2,1,0:T(8,128)} custom-call(bf16[16,3,128,128]{3,2,1,0:T(8,128)(2,1)S(1)} %all-to-all-done.1.x_ref), custom_call_target="tpu_custom_call" | custom-call | tf_op jit(solution)/shard_map/join_heads/pallas_call | solution.py:245
  (114 shorter events, 28.1 us)
Async XLA Ops:
  3.0 4.2 %collective-permute-start = (bf16[3,128,128]{2,1,0:T(8,128)(2,1)S(1)}, bf16[3,128,128]{2,1,0:T(8,128)(2,1)S(1)}, u32[]{:S(2)}, u32[]{:S(2)}) collective-permute-start(bf16[3,128,128]{2,1,0:T(8,128)(2,1)S(1)} %get-tuple-element.24), channel_id=1, source_target_pairs={{0,2},{2,0},{4,6},{6,4},{8,10},{10,8},{12,14},{14,12},{16,18},{18,... | collective-permute-start | bytes 294920 | tf_op jit(solution)/shard_map/ppermute | solution.py:381
  3.7 4.3 %collective-permute-start.1 = (bf16[3,128,128]{2,1,0:T(8,128)(2,1)S(1)}, bf16[3,128,128]{2,1,0:T(8,128)(2,1)S(1)}, u32[]{:S(2)}, u32[]{:S(2)}) collective-permute-start(bf16[3,128,128]{2,1,0:T(8,128)(2,1)S(1)} %get-tuple-element.25), channel_id=1, source_target_pairs={{0,4},{2,6},{4,0},{6,2},{8,12},{10,14},{12,8},{14,10},{16,20},{18,... | collective-permute-start | bytes 294920 | tf_op jit(solution)/shard_map/ppermute | solution.py:381
  4.0 6.7 %collective-permute-start.2 = (bf16[3,128,128]{2,1,0:T(8,128)(2,1)S(1)}, bf16[3,128,128]{2,1,0:T(8,128)(2,1)S(1)}, u32[]{:S(2)}, u32[]{:S(2)}) collective-permute-start(bf16[3,128,128]{2,1,0:T(8,128)(2,1)S(1)} %get-tuple-element.26), channel_id=1, source_target_pairs={{0,6},{2,4},{4,2},{6,0},{8,14},{10,12},{12,10},{14,8},{16,22},{18,... | collective-permute-start | bytes 294920 | tf_op jit(solution)/shard_map/ppermute | solution.py:381
  5.4 7.5 %collective-permute-start.3 = (bf16[3,128,128]{2,1,0:T(8,128)(2,1)S(1)}, bf16[3,128,128]{2,1,0:T(8,128)(2,1)S(1)}, u32[]{:S(2)}, u32[]{:S(2)}) collective-permute-start(bf16[3,128,128]{2,1,0:T(8,128)(2,1)S(1)} %get-tuple-element.27), channel_id=1, source_target_pairs={{0,8},{2,10},{4,12},{6,14},{8,0},{10,2},{12,4},{14,6},{16,24},{18,... | collective-permute-start | bytes 294920 | tf_op jit(solution)/shard_map/ppermute | solution.py:381
  5.6 7.9 %collective-permute-start.4 = (bf16[3,128,128]{2,1,0:T(8,128)(2,1)S(1)}, bf16[3,128,128]{2,1,0:T(8,128)(2,1)S(1)}, u32[]{:S(2)}, u32[]{:S(2)}) collective-permute-start(bf16[3,128,128]{2,1,0:T(8,128)(2,1)S(1)} %get-tuple-element.28), channel_id=1, source_target_pairs={{0,10},{2,8},{4,14},{6,12},{8,2},{10,0},{12,6},{14,4},{16,26},{18,... | collective-permute-start | bytes 294920 | tf_op jit(solution)/shard_map/ppermute | solution.py:381
  7.2 69.6 %copy-start.2 = (bf16[3,128,128]{2,1,0:T(8,128)(2,1)}, bf16[3,128,128]{2,1,0:T(8,128)(2,1)S(1)}, u32[]{:S(2)}) copy-start(bf16[3,128,128]{2,1,0:T(8,128)(2,1)S(1)} %collective-permute-done.refs_1_) | copy-start | bytes 294916
  7.2 8.1 %collective-permute-start.5 = (bf16[3,128,128]{2,1,0:T(8,128)(2,1)S(1)}, bf16[3,128,128]{2,1,0:T(8,128)(2,1)S(1)}, u32[]{:S(2)}, u32[]{:S(2)}) collective-permute-start(bf16[3,128,128]{2,1,0:T(8,128)(2,1)S(1)} %get-tuple-element.29), channel_id=1, source_target_pairs={{0,12},{2,14},{4,8},{6,10},{8,4},{10,6},{12,0},{14,2},{16,28},{18,... | collective-permute-start | bytes 294920 | tf_op jit(solution)/shard_map/ppermute | solution.py:381
  8.0 68.8 %copy-start.4 = (bf16[3,128,128]{2,1,0:T(8,128)(2,1)}, bf16[3,128,128]{2,1,0:T(8,128)(2,1)S(1)}, u32[]{:S(2)}) copy-start(bf16[3,128,128]{2,1,0:T(8,128)(2,1)S(1)} %collective-permute-done.1.refs_2_) | copy-start | bytes 294916
  8.0 12.7 %collective-permute-start.6 = (bf16[3,128,128]{2,1,0:T(8,128)(2,1)S(1)}, bf16[3,128,128]{2,1,0:T(8,128)(2,1)S(1)}, u32[]{:S(2)}, u32[]{:S(2)}) collective-permute-start(bf16[3,128,128]{2,1,0:T(8,128)(2,1)S(1)} %get-tuple-element.30), channel_id=1, source_target_pairs={{0,14},{2,12},{4,10},{6,8},{8,6},{10,4},{12,2},{14,0},{16,30},{18,... | collective-permute-start | bytes 294920 | tf_op jit(solution)/shard_map/ppermute | solution.py:381
  10.7 66.1 %copy-start.6 = (bf16[3,128,128]{2,1,0:T(8,128)(2,1)}, bf16[3,128,128]{2,1,0:T(8,128)(2,1)S(1)}, u32[]{:S(2)}) copy-start(bf16[3,128,128]{2,1,0:T(8,128)(2,1)S(1)} %collective-permute-done.2.refs_3_) | copy-start | bytes 294916
  10.7 10.9 %collective-permute-start.7 = (bf16[3,128,128]{2,1,0:T(8,128)(2,1)S(1)}, bf16[3,128,128]{2,1,0:T(8,128)(2,1)S(1)}, u32[]{:S(2)}, u32[]{:S(2)}) collective-permute-start(bf16[3,128,128]{2,1,0:T(8,128)(2,1)S(1)} %get-tuple-element.31), channel_id=1, source_target_pairs={{0,16},{2,18},{4,20},{6,22},{8,24},{10,26},{12,28},{14,30},{16,0},... | collective-permute-start | bytes 294920 | tf_op jit(solution)/shard_map/ppermute | solution.py:381
  13.0 16.0 %collective-permute-start.8 = (bf16[3,128,128]{2,1,0:T(8,128)(2,1)S(1)}, bf16[3,128,128]{2,1,0:T(8,128)(2,1)S(1)}, u32[]{:S(2)}, u32[]{:S(2)}) collective-permute-start(bf16[3,128,128]{2,1,0:T(8,128)(2,1)S(1)} %get-tuple-element.32), channel_id=1, source_target_pairs={{0,18},{2,16},{4,22},{6,20},{8,26},{10,24},{12,30},{14,28},{16,2},... | collective-permute-start | bytes 294920 | tf_op jit(solution)/shard_map/ppermute | solution.py:381
  13.5 17.7 %collective-permute-start.9 = (bf16[3,128,128]{2,1,0:T(8,128)(2,1)S(1)}, bf16[3,128,128]{2,1,0:T(8,128)(2,1)S(1)}, u32[]{:S(2)}, u32[]{:S(2)}) collective-permute-start(bf16[3,128,128]{2,1,0:T(8,128)(2,1)S(1)} %get-tuple-element.33), channel_id=1, source_target_pairs={{0,20},{2,22},{4,16},{6,18},{8,28},{10,30},{12,24},{14,26},{16,4},... | collective-permute-start | bytes 294920 | tf_op jit(solution)/shard_map/ppermute | solution.py:381
  15.3 20.9 %collective-permute-start.10 = (bf16[3,128,128]{2,1,0:T(8,128)(2,1)S(1)}, bf16[3,128,128]{2,1,0:T(8,128)(2,1)S(1)}, u32[]{:S(2)}, u32[]{:S(2)}) collective-permute-start(bf16[3,128,128]{2,1,0:T(8,128)(2,1)S(1)} %get-tuple-element.34), channel_id=1, source_target_pairs={{0,22},{2,20},{4,18},{6,16},{8,30},{10,28},{12,26},{14,24},{16,6},... | collective-permute-start | bytes 294920 | tf_op jit(solution)/shard_map/ppermute | solution.py:381
  20.7 19.9 %collective-permute-start.11 = (bf16[3,128,128]{2,1,0:T(8,128)(2,1)S(1)}, bf16[3,128,128]{2,1,0:T(8,128)(2,1)S(1)}, u32[]{:S(2)}, u32[]{:S(2)}) collective-permute-start(bf16[3,128,128]{2,1,0:T(8,128)(2,1)S(1)} %get-tuple-element.35), channel_id=1, source_target_pairs={{0,24},{2,26},{4,28},{6,30},{8,16},{10,18},{12,20},{14,22},{16,8},... | collective-permute-start | bytes 294920 | tf_op jit(solution)/shard_map/ppermute | solution.py:381
  21.6 21.9 %collective-permute-start.12 = (bf16[3,128,128]{2,1,0:T(8,128)(2,1)S(1)}, bf16[3,128,128]{2,1,0:T(8,128)(2,1)S(1)}, u32[]{:S(2)}, u32[]{:S(2)}) collective-permute-start(bf16[3,128,128]{2,1,0:T(8,128)(2,1)S(1)} %get-tuple-element.36), channel_id=1, source_target_pairs={{0,26},{2,24},{4,30},{6,28},{8,18},{10,16},{12,22},{14,20},{16,10}... | collective-permute-start | bytes 294920 | tf_op jit(solution)/shard_map/ppermute | solution.py:381
  29.0 15.8 %collective-permute-start.13 = (bf16[3,128,128]{2,1,0:T(8,128)(2,1)S(1)}, bf16[3,128,128]{2,1,0:T(8,128)(2,1)S(1)}, u32[]{:S(2)}, u32[]{:S(2)}) collective-permute-start(bf16[3,128,128]{2,1,0:T(8,128)(2,1)S(1)} %get-tuple-element.37), channel_id=1, source_target_pairs={{0,28},{2,30},{4,24},{6,26},{8,20},{10,22},{12,16},{14,18},{16,12}... | collective-permute-start | bytes 294920 | tf_op jit(solution)/shard_map/ppermute | solution.py:381
  31.1 16.0 %collective-permute-start.14 = (bf16[3,128,128]{2,1,0:T(8,128)(2,1)S(1)}, bf16[3,128,128]{2,1,0:T(8,128)(2,1)S(1)}, u32[]{:S(2)}, u32[]{:S(2)}) collective-permute-start(bf16[3,128,128]{2,1,0:T(8,128)(2,1)S(1)} %get-tuple-element.38), channel_id=1, source_target_pairs={{0,30},{2,28},{4,26},{6,24},{8,22},{10,20},{12,18},{14,16},{16,14}... | collective-permute-start | bytes 294920 | tf_op jit(solution)/shard_map/ppermute | solution.py:381
  36.2 24.2 %collective-permute-start.26 = (bf16[64,8192]{1,0:T(8,128)(2,1)}, bf16[64,8192]{1,0:T(8,128)(2,1)S(1)}, u32[]{:S(2)}, u32[]{:S(2)}) collective-permute-start(bf16[64,8192]{1,0:T(8,128)(2,1)} %own_ref.1), channel_id=1, source_target_pairs={{0,1},{1,0},{2,3},{3,2},{4,5},{5,4},{6,7},{7,6},{8,9},{9,8},{10,11... | collective-permute-start | bytes 3145736 | tf_op jit(solution)/shard_map/ppermute | solution.py:378
  51.4 2.3 %collective-permute-start.15 = (bf16[4,128,128]{2,1,0:T(8,128)(2,1)S(1)}, bf16[4,128,128]{2,1,0:T(8,128)(2,1)S(1)}, u32[]{:S(2)}, u32[]{:S(2)}) collective-permute-start(bf16[4,128,128]{2,1,0:T(8,128)(2,1)S(1)} %get-tuple-element.40.refs_17_), channel_id=1, source_target_pairs={{0,2},{2,0},{4,6},{6,4},{8,10},{10,8},{12,14},{14,12},{16,18},{18,... | collective-permute-start | bytes 393224 | tf_op jit(solution)/shard_map/ppermute | solution.py:387
  52.0 5.0 %collective-permute-start.16 = (bf16[4,128,128]{2,1,0:T(8,128)(2,1)S(1)}, bf16[4,128,128]{2,1,0:T(8,128)(2,1)S(1)}, u32[]{:S(2)}, u32[]{:S(2)}) collective-permute-start(bf16[4,128,128]{2,1,0:T(8,128)(2,1)S(1)} %get-tuple-element.41.refs_18_), channel_id=1, source_target_pairs={{0,4},{2,6},{4,0},{6,2},{8,12},{10,14},{12,8},{14,10},{16,20},{18,... | collective-permute-start | bytes 393224 | tf_op jit(solution)/shard_map/ppermute | solution.py:387
  52.6 7.7 %collective-permute-start.17 = (bf16[4,128,128]{2,1,0:T(8,128)(2,1)S(1)}, bf16[4,128,128]{2,1,0:T(8,128)(2,1)S(1)}, u32[]{:S(2)}, u32[]{:S(2)}) collective-permute-start(bf16[4,128,128]{2,1,0:T(8,128)(2,1)S(1)} %get-tuple-element.42.refs_19_), channel_id=1, source_target_pairs={{0,6},{2,4},{4,2},{6,0},{8,14},{10,12},{12,10},{14,8},{16,22},{18,... | collective-permute-start | bytes 393224 | tf_op jit(solution)/shard_map/ppermute | solution.py:387
  60.4 27.4 %collective-permute-start.18 = (bf16[4,128,128]{2,1,0:T(8,128)(2,1)S(1)}, bf16[4,128,128]{2,1,0:T(8,128)(2,1)S(1)}, u32[]{:S(2)}, u32[]{:S(2)}) collective-permute-start(bf16[4,128,128]{2,1,0:T(8,128)(2,1)S(1)} %pad_maximum_fusion), channel_id=1, source_target_pairs={{0,8},{2,10},{4,12},{6,14},{8,0},{10,2},{12,4},{14,6},{16,24},{18,... | collective-permute-start | bytes 393224 | tf_op jit(solution)/shard_map/ppermute | solution.py:392
  76.9 38.0 %all-to-all-start = ((bf16[16,128,128]{2,1,0:T(8,128)(2,1)}), bf16[16,128,128]{2,1,0:T(8,128)(2,1)S(1)}, u32[]{:S(2)}, u32[]{:S(2)}) async-start(bf16[16,128,128]{2,1,0:T(8,128)(2,1)} %project_back.1), calls=%async_computation | async-start | bytes 1048576 | tf_op jit(solution)/shard_map/all_to_all | solution.py:376
  85.6 19.9 %collective-permute-start.19 = (bf16[4,128,128]{2,1,0:T(8,128)(2,1)S(1)}, bf16[4,128,128]{2,1,0:T(8,128)(2,1)S(1)}, u32[]{:S(2)}, u32[]{:S(2)}) collective-permute-start(bf16[4,128,128]{2,1,0:T(8,128)(2,1)S(1)} %pad_maximum_fusion.1), channel_id=1, source_target_pairs={{0,16},{2,18},{4,20},{6,22},{8,24},{10,26},{12,28},{14,30},{16,0},... | collective-permute-start | bytes 393224 | tf_op jit(solution)/shard_map/ppermute | solution.py:392
  87.7 22.3 %collective-permute-start.20 = (bf16[4,128,128]{2,1,0:T(8,128)(2,1)S(1)}, bf16[4,128,128]{2,1,0:T(8,128)(2,1)S(1)}, u32[]{:S(2)}, u32[]{:S(2)}) collective-permute-start(bf16[4,128,128]{2,1,0:T(8,128)(2,1)S(1)} %pad_maximum_fusion.2), channel_id=1, source_target_pairs={{0,24},{2,26},{4,28},{6,30},{8,16},{10,18},{12,20},{14,22},{16,8},... | collective-permute-start | bytes 393224 | tf_op jit(solution)/shard_map/ppermute | solution.py:392
  131.6 41.0 %all-to-all-start.1 = ((bf16[16,3,128,128]{3,2,1,0:T(8,128)(2,1)}), bf16[16,3,128,128]{3,2,1,0:T(8,128)(2,1)S(1)}, u32[]{:S(2)}, u32[]{:S(2)}) async-start(bf16[16,3,128,128]{3,2,1,0:T(8,128)(2,1)} %copy-done), calls=%async_computation.1 | async-start | bytes 3145728 | tf_op jit(solution)/shard_map/all_to_all | solution.py:376
  136.4 24.8 %collective-permute-start.25 = (bf16[64,2048]{1,0:T(8,128)(2,1)S(1)}, bf16[64,2048]{1,0:T(8,128)(2,1)S(1)}, u32[]{:S(2)}, u32[]{:S(2)}) collective-permute-start(bf16[64,2048]{1,0:T(8,128)(2,1)S(1)} %dynamic-slice_convert_fusion), channel_id=1, source_target_pairs={{0,1},{1,0},{2,3},{3,2},{4,5},{5,4},{6,7},{7,6},{8,9},{9,8},{10,11... | collective-permute-start | bytes 786440 | tf_op jit(solution)/shard_map/ppermute | solution.py:407
  142.4 18.8 %collective-permute-start.24 = (bf16[64,2048]{1,0:T(8,128)(2,1)S(1)}, bf16[64,2048]{1,0:T(8,128)(2,1)S(1)}, u32[]{:S(2)}, u32[]{:S(2)}) collective-permute-start(bf16[64,2048]{1,0:T(8,128)(2,1)S(1)} %dynamic-slice_convert_fusion.1), channel_id=1, source_target_pairs={{0,1},{1,0},{2,3},{3,2},{4,5},{5,4},{6,7},{7,6},{8,9},{9,8},{10,11... | collective-permute-start | bytes 786440 | tf_op jit(solution)/shard_map/ppermute | solution.py:407
  147.4 13.8 %collective-permute-start.23 = (bf16[64,2048]{1,0:T(8,128)(2,1)S(1)}, bf16[64,2048]{1,0:T(8,128)(2,1)S(1)}, u32[]{:S(2)}, u32[]{:S(2)}) collective-permute-start(bf16[64,2048]{1,0:T(8,128)(2,1)S(1)} %dynamic-slice_convert_fusion.2), channel_id=1, source_target_pairs={{0,1},{1,0},{2,3},{3,2},{4,5},{5,4},{6,7},{7,6},{8,9},{9,8},{10,11... | collective-permute-start | bytes 786440 | tf_op jit(solution)/shard_map/ppermute | solution.py:407
  154.5 4.2 %collective-permute-start.22 = (bf16[64,1024]{1,0:T(8,128)(2,1)S(1)}, bf16[64,1024]{1,0:T(8,128)(2,1)S(1)}, u32[]{:S(2)}, u32[]{:S(2)}) collective-permute-start(bf16[64,1024]{1,0:T(8,128)(2,1)S(1)} %dynamic-slice_convert_fusion.3), channel_id=1, source_target_pairs={{0,1},{1,0},{2,3},{3,2},{4,5},{5,4},{6,7},{7,6},{8,9},{9,8},{10,11... | collective-permute-start | bytes 393224 | tf_op jit(solution)/shard_map/ppermute | solution.py:407
  154.8 6.3 %collective-permute-start.21 = (bf16[64,1024]{1,0:T(8,128)(2,1)S(1)}, bf16[64,1024]{1,0:T(8,128)(2,1)S(1)}, u32[]{:S(2)}, u32[]{:S(2)}) collective-permute-start(bf16[64,1024]{1,0:T(8,128)(2,1)S(1)} %dynamic-slice_convert_fusion.4), channel_id=1, source_target_pairs={{0,1},{1,0},{2,3},{3,2},{4,5},{5,4},{6,7},{7,6},{8,9},{9,8},{10,11... | collective-permute-start | bytes 393224 | tf_op jit(solution)/shard_map/ppermute | solution.py:407
  (29 other events, 467.8 us)

commit v9 on v8

--- a/solution.py
+++ b/solution.py
@@ -46,24 +46,6 @@
     return jnp.where(col == want, 1.0, 0.0).astype(jnp.bfloat16)
 
 
-def split_kernel(me_ref, x_ref, *refs):
-    *out_refs, order = refs
-    rows, three, heads, _ = x_ref.shape
-    step = pl.program_id(0)
-
-    @pl.when(step == 0)
-    def _():
-        order[...] = swap_matrix(heads, CHUNK, me_ref[0])
-
-    for b in range(rows // CHUNK):
-        span = pl.ds(pl.multiple_of(step * rows + b * CHUNK, CHUNK), CHUNK)
-        for c in range(three):
-            x = x_ref[b * CHUNK : (b + 1) * CHUNK, c].reshape(CHUNK * heads, HD)
-            y = dot_nn(order[...], x).astype(jnp.bfloat16).reshape(heads, CHUNK, HD)
-            for k in range(heads):
-                out_refs[k][c, span] = y[k]
-
-
 def join_kernel(x_ref, out_ref, order):
     heads, three, _, _ = x_ref.shape
     rows = out_ref.shape[0]
@@ -80,25 +62,42 @@
             out_ref[b * CHUNK : (b + 1) * CHUNK, c] = dot_nn(order[...], x).reshape(CHUNK, heads, HD)
 
 
-def back_kernel(turn_ref, own_ref, other_ref, w_ref, out_ref, x_buf):
+def stack_rows(turn_ref, own_ref, other_ref, x_buf):
     half = own_ref.shape[0]
-
+    for x_ref, place in ((own_ref, turn_ref[0]), (other_ref, 1 - turn_ref[0])):
+        x_buf[pl.ds(pl.multiple_of(place * half, half), half)] = x_ref[...]
+
+
+def back_first_kernel(turn_ref, own_ref, other_ref, w_ref, out_ref, x_buf):
     @pl.when(pl.program_id(0) == 0)
     def _():
-        for x_ref, place in ((own_ref, turn_ref[0]), (other_ref, 1 - turn_ref[0])):
-            x_buf[pl.ds(pl.multiple_of(place * half, half), half)] = x_ref[...]
-
-    y = dot_nt(w_ref[...], x_buf[...])
-    for h in range(out_ref.shape[0]):
-        out_ref[h] = y[h * HD : (h + 1) * HD].T.astype(jnp.bfloat16)
-
-
-def forward_kernel(step, me_ref, *refs):
-    parts, rest = refs[: -5 - PLANE], refs[-5 - PLANE :]
-    lse_ref, *sent, qkv_ref, att_ref, v_t, s_buf = rest
-    me = me_ref[0]
-    for k, part in enumerate(parts):
-        qkv_ref[me ^ k] = part[...]
+        stack_rows(turn_ref, own_ref, other_ref, x_buf)
+
+    out_ref[...] = dot_nt(w_ref[...], x_buf[...])
+
+
+def back_last_kernel(turn_ref, me_ref, own_ref, other_ref, w_ref, y_ref, *refs):
+    *out_refs, x_buf, chunks = refs
+    step = pl.program_id(0)
+    group = w_ref.shape[0] // HD
+
+    @pl.when(step == 0)
+    def _():
+        stack_rows(turn_ref, own_ref, other_ref, x_buf)
+
+    y = y_ref[...] + dot_nt(w_ref[...], x_buf[...])
+    for h in range(group):
+        head = (step * group + h) ^ me_ref[0]
+        chunks[head] = y[h * HD : (h + 1) * HD].T.astype(jnp.bfloat16)
+
+    @pl.when(step == pl.num_programs(0) - 1)
+    def _():
+        for e, ref in enumerate(out_refs):
+            for d in range(ref.shape[0]):
+                ref[d] = chunks[PLANE * d + e]
+
+
+def forward_kernel(step, qkv_ref, att_ref, lse_ref, v_t, s_buf):
     chunks, _, unit, _ = qkv_ref.shape
     per = step // unit
     blocks = chunks // per
@@ -128,18 +127,6 @@
             acc = acc + dot_nn(v_t[j], (s_buf[i % 2, j] * inverse).astype(jnp.bfloat16))
         att_ref[i * per : (i + 1) * per] = acc.T.astype(jnp.bfloat16).reshape(per, unit, HD)
         lse_ref[i] = top * scale + jnp.log2(total)
-    for e, ref in enumerate(sent):
-        for d in range(chunks // PLANE):
-            ref[d] = att_ref[me ^ (PLANE * d + e)]
-
-
-def gather_kernel(me_ref, *refs):
-    *parts, out_ref = refs
-    plane, others = parts[:PLANE], parts[PLANE:]
-    for e, ref in enumerate(plane):
-        out_ref[me_ref[0] ^ e] = ref[0]
-        for d, other in enumerate(others, 1):
-            out_ref[me_ref[0] ^ (PLANE * d + e)] = other[e]
 
 
 def finish_kernel(turn_ref, *refs):
@@ -153,13 +140,14 @@
         start = stop
 
 
-def backward_kernel(step, chunks, me_ref, g_ref, lse_ref, *refs):
-    parts, own, rest = refs[:chunks], refs[chunks:-6], refs[-6:]
-    out_ref, qkv_ref, att_ref, k_t, dq_t, delta = rest
-    me = me_ref[0]
-    for k, part in enumerate(parts):
-        qkv_ref[me ^ k] = part[...]
-        att_ref[me ^ k] = own[k % PLANE][k // PLANE]
+def backward_kernel(step, me_ref, qkv_ref, att_ref, lse_ref, *refs):
+    parts, rest = refs[:-5], refs[-5:]
+    out_ref, g_ref, k_t, dq_t, delta = rest
+    plane, others = parts[:PLANE], parts[PLANE:]
+    for e, ref in enumerate(plane):
+        g_ref[me_ref[0] ^ e] = ref[0]
+        for d, other in enumerate(others, 1):
+            g_ref[me_ref[0] ^ (PLANE * d + e)] = other[e]
     chunks, _, unit, _ = qkv_ref.shape
     per = step // unit
     blocks = chunks // per
@@ -222,21 +210,6 @@
 
 def in_smem():
     return pl.BlockSpec(memory_space=pltpu.SMEM)
-
-
-def split_heads(me, qkv):
-    rows, heads = qkv.shape[:2]
-    part = 4 * CHUNK
-    return pl.pallas_call(
-        split_kernel,
-        grid=(rows // part,),
-        out_shape=[jax.ShapeDtypeStruct((3, rows, HD), jnp.bfloat16)] * heads,
-        in_specs=[in_smem(), pl.BlockSpec((part, 3, heads, HD), lambda b: (b, 0, 0, 0))],
-        out_specs=in_vmem(heads),
-        scratch_shapes=[pltpu.VMEM((CHUNK * heads, CHUNK * heads), jnp.bfloat16)],
-        compiler_params=pltpu.CompilerParams(vmem_limit_bytes=6 * MIB),
-        name="split_heads",
-    )(me, pltpu.with_memory_space_constraint(jnp.transpose(qkv, (0, 2, 1, 3)), pltpu.HBM))
 
 
 def join_heads(grads):
@@ -255,50 +228,63 @@
     return jnp.transpose(out, (0, 2, 1, 3))
 
 
-def project_back(turn, own, other, weights):
+def project_back(turn, me, own, other, weights):
     half, width = own.shape
-    heads = weights.shape[0] // HD
-    group = 4
+    deep = weights.shape[0]
+    group = 4 * HD
+    part = width // 2
+    cost = pl.CostEstimate(
+        flops=2 * half * width * deep, transcendentals=0, bytes_accessed=width * deep
+    )
+    params = pltpu.CompilerParams(vmem_limit_bytes=22 * MIB)
+
+    def rows(c):
+        return pl.BlockSpec((half, part), lambda b: (0, c))
+
+    def block(c):
+        return pl.BlockSpec((group, part), lambda b: (b, c))
+
+    partial = pl.BlockSpec((group, 2 * half), lambda b: (b, 0))
+    x_buf = pltpu.VMEM((2 * half, part), jnp.bfloat16)
+    y = pl.pallas_call(
+        back_first_kernel,
+        grid=(deep // group,),
+        out_shape=jax.ShapeDtypeStruct((deep, 2 * half), jnp.float32),
+        in_specs=[in_smem(), rows(0), *in_vmem(1), block(0)],
+        out_specs=partial,
+        scratch_shapes=[x_buf],
+        compiler_params=params,
+        cost_estimate=cost,
+        name="back_first",
+    )(turn, own, other[0], weights)
+    heads = deep // HD
     return pl.pallas_call(
-        back_kernel,
-        grid=(heads // group,),
-        out_shape=jax.ShapeDtypeStruct((heads, 2 * half, HD), jnp.bfloat16),
-        in_specs=[
-            in_smem(),
-            pl.BlockSpec((half, width), lambda b: (0, 0)),
-            *in_vmem(1),
-            pl.BlockSpec((group * HD, width), lambda b: (b, 0)),
-        ],
-        out_specs=pl.BlockSpec((group, 2 * half, HD), lambda b: (b, 0, 0)),
-        scratch_shapes=[pltpu.VMEM((2 * half, width), jnp.bfloat16)],
-        compiler_params=pltpu.CompilerParams(vmem_limit_bytes=26 * MIB),
-        cost_estimate=pl.CostEstimate(
-            flops=4 * half * width * heads * HD,
-            transcendentals=0,
-            bytes_accessed=2 * width * heads * HD,
-        ),
-        name="project_back",
-    )(turn, own, other, weights)
-
-
-def attend(me, parts, step):
-    chunks = len(parts)
-    outer = chunks // PLANE
-    unit = parts[0].shape[1]
+        back_last_kernel,
+        grid=(deep // group,),
+        out_shape=[jax.ShapeDtypeStruct((heads // PLANE, 2 * half, HD), jnp.bfloat16)] * PLANE,
+        in_specs=[in_smem(), in_smem(), rows(1), *in_vmem(1), block(1), partial],
+        out_specs=in_vmem(PLANE),
+        scratch_shapes=[x_buf, pltpu.VMEM((heads, 2 * half, HD), jnp.bfloat16)],
+        compiler_params=params,
+        cost_estimate=cost,
+        name="back_last",
+    )(turn, me, own, other[1], weights, y)
+
+
+def attend(qkv, step):
+    chunks, _, unit, _ = qkv.shape
     length = chunks * unit
     blocks = length // step
     area = length * length // 2
     return pl.pallas_call(
         functools.partial(forward_kernel, step),
         out_shape=(
+            jax.ShapeDtypeStruct((chunks, unit, HD), jnp.bfloat16),
             jax.ShapeDtypeStruct((blocks, 1, step), jnp.float32),
-            *[jax.ShapeDtypeStruct((outer, unit, HD), jnp.bfloat16)] * PLANE,
         ),
-        in_specs=[in_smem(), *in_vmem(chunks)],
-        out_specs=tuple(in_vmem(1 + PLANE)),
+        in_specs=in_vmem(1),
+        out_specs=tuple(in_vmem(2)),
         scratch_shapes=[
-            pltpu.VMEM((chunks, 3, unit, HD), jnp.bfloat16),
-            pltpu.VMEM((chunks, unit, HD), jnp.bfloat16),
             pltpu.VMEM((blocks, HD, step), jnp.bfloat16),
             pltpu.VMEM((2, blocks, step, step), jnp.float32),
         ],
@@ -307,19 +293,7 @@
             flops=4 * area * HD, transcendentals=area, bytes_accessed=8 * length * HD
         ),
         name="attend",
-    )(me, *parts)
-
-
-def gather_heads(me, plane, others):
-    shape = (PLANE * (len(others) + 1), *plane[0].shape[1:])
-    return pl.pallas_call(
-        gather_kernel,
-        out_shape=jax.ShapeDtypeStruct(shape, jnp.bfloat16),
-        in_specs=[in_smem(), *in_vmem(PLANE + len(others))],
-        out_specs=in_vmem(1)[0],
-        compiler_params=pltpu.CompilerParams(vmem_limit_bytes=2 * MIB),
-        name="gather_heads",
-    )(me, *plane, *others)
+    )(qkv)
 
 
 def finish(turn, parts):
@@ -336,19 +310,17 @@
     )(turn, *flat)
 
 
-def attend_grad(me, g, lse, parts, own, step):
-    chunks = len(parts)
-    unit = parts[0].shape[1]
+def attend_grad(me, qkv, att, lse, plane, others, step):
+    chunks, _, unit, _ = qkv.shape
     length = chunks * unit
     blocks = length // step
     area = length * length // 2
     return pl.pallas_call(
-        functools.partial(backward_kernel, step, chunks),
+        functools.partial(backward_kernel, step),
         out_shape=jax.ShapeDtypeStruct((chunks, 3, unit, HD), jnp.bfloat16),
-        in_specs=[in_smem(), *in_vmem(2 + chunks + len(own))],
+        in_specs=[in_smem(), *in_vmem(3 + len(plane) + len(others))],
         out_specs=in_vmem(1)[0],
         scratch_shapes=[
-            pltpu.VMEM((chunks, 3, unit, HD), jnp.bfloat16),
             pltpu.VMEM((chunks, unit, HD), jnp.bfloat16),
             pltpu.VMEM((blocks, HD, step), jnp.bfloat16),
             pltpu.VMEM((blocks, HD, step), jnp.float32),
@@ -359,7 +331,7 @@
             flops=10 * area * HD, transcendentals=area, bytes_accessed=16 * length * HD
         ),
         name="attend_grad",
-    )(me, g, lse, *parts, *own)
+    )(me, qkv, att, lse, *plane, *others)
 
 
 def by_head(qkv, grad_out, attn_out):
@@ -375,24 +347,23 @@
     def spread(x):
         return lax.all_to_all(x, "ctx", 0, 0, tiled=True)
 
-    other_out = lax.ppermute(grad_out, "tp", swap)
-    parts = list(split_heads(me, qkv))
-    for k in range(1, heads):
-        parts[k] = lax.ppermute(parts[k], "ctx", [(i, i ^ k) for i in range(heads)])
-    g = project_back(turn.reshape(1), grad_out, other_out, attn_out)
-    g = spread(g)
-    lse, *own = attend(me, parts, step)
-    plane = list(own)
+    other = []
+    for c in range(2):
+        cut = grad_out[:, c * (width // 2) : (c + 1) * (width // 2)]
+        other.append(lax.ppermute(cut, "tp", swap))
+    mine = spread(jnp.transpose(qkv, (1, 2, 0, 3)))
+    plane = list(project_back(turn.reshape(1), me, grad_out, other, attn_out))
     for e in range(1, PLANE):
-        plane[e] = lax.ppermute(own[e], "ctx", [(i, i ^ e) for i in range(heads)])
+        plane[e] = lax.ppermute(plane[e], "ctx", [(i, i ^ e) for i in range(heads)])
     others = []
     for d in range(1, heads // PLANE):
         sent = jnp.stack([x[d] for x in plane])
         pairs = [(i, i ^ (PLANE * d)) for i in range(heads)]
         others.append(lax.ppermute(sent, "ctx", pairs))
-    grads = attend_grad(me, g, lse, parts, own, step)
+    att, lse = attend(mine, step)
+    local = spread(att)
+    grads = attend_grad(me, mine, att, lse, plane, others, step)
     grads = spread(grads)
-    local = gather_heads(me, plane, others)
     pieces = []
     start = 0
     for eighths in MIX_PARTS:

time: 176 us -> 138 us (0.78)
  waiting for transfers between devices: 67.4 us -> 46.5 us
  starting transfers between devices: 42.9 us -> 28.9 us
  local copies, waits for them, and re-layouts: 11.5 us -> 5.51 us
  Pallas kernels: 32.7 us -> 35.3 us
    ppermute x19 -> x5, starting transfers between devices: 22.7 us -> 4.5 us  [the longest x3 3.03 us: by_head(): plane[e] = lax.ppermute(plane[e], 'ctx', [(i, i ^ e) for i in range(heads)])]
    ppermute x19 -> x5, waiting for transfers between devices: 30.3 us -> 14.7 us  [the longest x2 14.7 us: by_head(): other.append(lax.ppermute(cut, 'tp', swap))]
    unnamed x64 -> x3, local copies, waits for them, and re-layouts: 11.4 us -> 3.05 us
    all_to_all x2 -> x3, waiting for transfers between devices: 9.84 us -> 4.76 us  [spread(): return lax.all_to_all(x, 'ctx', 0, 0, tiled=True)]
    all_to_all x2 -> x3, starting transfers between devices: 13.5 us -> 17.1 us  [spread(): return lax.all_to_all(x, 'ctx', 0, 0, tiled=True)]
    slice x0 -> x1, local copies, waits for them, and re-layouts: none -> 2.26 us  [by_head(): cut = grad_out[:, c * (width // 2):(c + 1) * (width // 2)]]
    pallas_call x4 -> x3, Pallas kernels: 24 us -> 25.9 us  [the longest x1 8.86 us: project_back(): pl.pallas_call(back_last_kernel, grid=(deep // group,), out_shape=[jax.Sh...]
  transfers between devices with their start and end apart: 29 -> 16, of which waited for: 16 -> 7; matrix products, arithmetic and copies ran while one was open for 11% -> 16% of each run, Pallas kernels for 12% -> 24%
where the time goes in v9:
time: 138 us; the launch traced here: 137 us
  waiting for transfers between devices  46.5 us (34%)
  Pallas kernels  35.3 us (26%)
  starting transfers between devices  28.9 us (21%)
  matrix products  19.7 us (14%)
  local copies, waits for them, and re-layouts  5.51 us (4%)
    ppermute x3, waiting for transfers between devices, by_head(): others.append(lax.ppermute(sent, 'ctx', pairs))  21.6 us
    dot_general x5, matrix products, by_head(): jnp.einsum('hrd,hdm->rm', local, weights[:, :, start:stop], preferred_ele...  19.7 us
    all_to_all x3, starting transfers between devices, spread(): return lax.all_to_all(x, 'ctx', 0, 0, tiled=True)  17.1 us
    ppermute x2, waiting for transfers between devices, by_head(): other.append(lax.ppermute(cut, 'tp', swap))  14.7 us
    pallas_call x1, Pallas kernels, project_back(): pl.pallas_call(back_last_kernel, grid=(deep // group,), out_shape=[jax.Sh...  8.86 us
    pallas_call x1, Pallas kernels, attend_grad(): pl.pallas_call(functools.partial(backward_kernel, step), out_shape=jax.Sh...  8.6 us
    pallas_call x1, Pallas kernels, project_back(): pl.pallas_call(back_first_kernel, grid=(deep // group,), out_shape=jax.Sh...  8.48 us
    ppermute x5, waiting for transfers between devices, by_head(): pieces.append((mixed, lax.ppermute(sent.astype(jnp.bfloat16), 'tp', swap)))  5.51 us
  transfers between devices with their start and end apart: 16, of which 7 were waited for; matrix products, arithmetic and copies ran while one was open for 16% of the time, Pallas kernels for 24%

profile of v9, /device:TPU:13, one launch (start us, length us, event | category | flops | bytes accessed | tf_op | source)
XLA Modules:
  0.0 136.8 jit_solution(5124537768432804356)
XLA Ops:
  0.6 3.0 %copy.7 = bf16[128,16,3,128]{3,0,2,1:T(8,128)(2,1)} copy(bf16[128,16,3,128]{3,1,2,0:T(8,128)(2,1)} %param.3) | data formatting | bytes 3145728 | tf_op args[0]
  3.7 6.5 %all-to-all-start = ((bf16[16,3,128,128]{3,2,1,0:T(8,128)(2,1)}), bf16[16,3,128,128]{3,2,1,0:T(8,128)(2,1)S(1)}, u32[]{:S(2)}, u32[]{:S(2)}) async-start(bf16[16,3,128,128]{3,2,1,0:T(8,128)(2,1)} %bitcast.27), calls=%async_computation | async-start | bytes 3145728 | tf_op jit(solution)/shard_map/all_to_all | solution.py:348
  10.2 2.3 %fusion.25 = (bf16[64,4096]{1,0:T(8,128)(2,1)}, bf16[64,4096]{1,0:T(8,128)(2,1)}) fusion(bf16[64,8192]{1,0:T(8,128)(2,1)} %own_ref.3), kind=kLoop, calls=%fused_computation.24 | loop fusion | bytes 2097152 | tf_op jit(solution)/shard_map/slice | solution.py:352
  12.5 1.2 collective-permute-start.6
  13.9 11.8 %collective-permute-done.6.other_ref = bf16[64,4096]{1,0:T(8,128)(2,1)S(1)} collective-permute-done((bf16[64,4096]{1,0:T(8,128)(2,1)}, bf16[64,4096]{1,0:T(8,128)(2,1)S(1)}, u32[]{:S(2)}, u32[]{:S(2)}) %collective-permute-start.6) | collective-permute-done | bytes 524320 | tf_op jit(solution)/shard_map/ppermute | solution.py:353
  25.8 8.5 %back_first.1.y_ref = f32[2048,128]{1,0:T(8,128)S(1)} custom-call(s32[1]{0:T(128)} %bitcast.turn_ref, bf16[64,8192]{1,0:T(8,128)(2,1)S(1)} %copy-done, bf16[64,4096]{1,0:T(8,128)(2,1)S(1)} %collective-permute-done.6.other_ref, bf16[2048,8192]{1,0:T(8,128)(2,1)} %w_ref.3), custom_call_target="tpu_custom_call" | custom-call | flops 2147483648 | bytes 16777216 | tf_op jit(solution)/shard_map/back_first/pallas_call | solution.py:249
  34.3 2.8 %collective-permute-done.5.other_ref = bf16[64,4096]{1,0:T(8,128)(2,1)} collective-permute-done((bf16[64,4096]{1,0:T(8,128)(2,1)}, bf16[64,4096]{1,0:T(8,128)(2,1)}, u32[]{:S(2)}, u32[]{:S(2)}) %collective-permute-start.5) | collective-permute-done | bytes 524320 | tf_op jit(solution)/shard_map/ppermute | solution.py:353
  37.1 8.9 %back_last.1 = (bf16[4,128,128]{2,1,0:T(8,128)(2,1)S(1)}, bf16[4,128,128]{2,1,0:T(8,128)(2,1)S(1)}, bf16[4,128,128]{2,1,0:T(8,128)(2,1)S(1)}, bf16[4,128,128]{2,1,0:T(8,128)(2,1)S(1)}) custom-call(s32[1]{0:T(128)} %bitcast.turn_ref, s32[1]{0:T(128)} %bitcast.8.me_ref, bf16[64,8192]{1,0:T(8,128)(2,1)S(1)} %copy-done, ...), custom_call_target="tpu_custom_call" | custom-call | flops 2147483648 | bytes 16777216 | tf_op jit(solution)/shard_map/back_last/pallas_call | solution.py:261
  46.0 1.3 collective-permute-start.7
  47.6 1.4 %collective-permute-start.9 = (bf16[4,128,128]{2,1,0:T(8,128)(2,1)S(1)}, bf16[4,128,128]{2,1,0:T(8,128)(2,1)S(1)}, u32[]{:S(2)}, u32[]{:S(2)}) collective-permute-start(bf16[4,128,128]{2,1,0:T(8,128)(2,1)S(1)} %get-tuple-element.13), channel_id=1, source_target_pairs={{0,6},{2,4},{4,2},{6,0},{8,14},{10,12},{12,10},{14,8},{16,22},{18,... | collective-permute-start | bytes 393224 | tf_op jit(solution)/shard_map/ppermute | solution.py:357
  49.1 4.9 %attend.1 = (bf16[16,128,128]{2,1,0:T(8,128)(2,1)}, f32[4,1,512]{2,1,0:T(1,128)S(1)}) custom-call(bf16[16,3,128,128]{3,2,1,0:T(8,128)(2,1)S(1)} %all-to-all-done.qkv_ref), custom_call_target="tpu_custom_call" | custom-call | flops 1073741824 | bytes 2097152 | tf_op jit(solution)/shard_map/attend/pallas_call | solution.py:279
  54.0 5.8 %all-to-all-start.1 = ((bf16[16,128,128]{2,1,0:T(8,128)(2,1)}), bf16[16,128,128]{2,1,0:T(8,128)(2,1)S(1)}, u32[]{:S(2)}, u32[]{:S(2)}) async-start(bf16[16,128,128]{2,1,0:T(8,128)(2,1)} %get-tuple-element.8.att_ref), calls=%async_computation.1 | async-start | bytes 1048576 | tf_op jit(solution)/shard_map/all_to_all | solution.py:348
  59.8 0.3 collective-permute-start.10
  60.2 2.2 %collective-permute-start.11 = (bf16[4,128,128]{2,1,0:T(8,128)(2,1)S(1)}, bf16[4,128,128]{2,1,0:T(8,128)(2,1)S(1)}, u32[]{:S(2)}, u32[]{:S(2)}) collective-permute-start(bf16[4,128,128]{2,1,0:T(8,128)(2,1)S(1)} %pad_maximum_fusion.1), channel_id=1, source_target_pairs={{0,16},{2,18},{4,20},{6,22},{8,24},{10,26},{12,28},{14,30},{16,0},... | collective-permute-start | bytes 393224 | tf_op jit(solution)/shard_map/ppermute | solution.py:362
  62.4 0.3 collective-permute-start.12
  62.7 9.4 %collective-permute-done.10.refs_4_ = bf16[4,128,128]{2,1,0:T(8,128)(2,1)S(1)} collective-permute-done((bf16[4,128,128]{2,1,0:T(8,128)(2,1)S(1)}, bf16[4,128,128]{2,1,0:T(8,128)(2,1)S(1)}, u32[]{:S(2)}, u32[]{:S(2)}) %collective-permute-start.10) | collective-permute-done | bytes 131104 | tf_op jit(solution)/shard_map/ppermute | solution.py:362
  72.1 7.5 %collective-permute-done.11.refs_5_ = bf16[4,128,128]{2,1,0:T(8,128)(2,1)S(1)} collective-permute-done((bf16[4,128,128]{2,1,0:T(8,128)(2,1)S(1)}, bf16[4,128,128]{2,1,0:T(8,128)(2,1)S(1)}, u32[]{:S(2)}, u32[]{:S(2)}) %collective-permute-start.11) | collective-permute-done | bytes 131104 | tf_op jit(solution)/shard_map/ppermute | solution.py:362
  79.7 4.6 %collective-permute-done.12.refs_6_ = bf16[4,128,128]{2,1,0:T(8,128)(2,1)S(1)} collective-permute-done((bf16[4,128,128]{2,1,0:T(8,128)(2,1)S(1)}, bf16[4,128,128]{2,1,0:T(8,128)(2,1)S(1)}, u32[]{:S(2)}, u32[]{:S(2)}) %collective-permute-start.12) | collective-permute-done | bytes 131104 | tf_op jit(solution)/shard_map/ppermute | solution.py:362
  84.3 8.6 %attend_grad.1 = bf16[16,3,128,128]{3,2,1,0:T(8,128)(2,1)} custom-call(s32[1]{0:T(128)} %bitcast.8.me_ref, bf16[16,3,128,128]{3,2,1,0:T(8,128)(2,1)S(1)} %all-to-all-done.qkv_ref, bf16[16,128,128]{2,1,0:T(8,128)(2,1)} %get-tuple-element.8.att_ref, f32[4,1,512]{2,1,0:T(1,128)S(1)} %get-tuple-element.9.lse_ref, ...), custom_call_target="tpu_custom_call" | custom-call | flops 2684354560 | bytes 4194304 | tf_op jit(solution)/shard_map/attend_grad/pallas_call | solution.py:318
  92.9 4.8 %all-to-all-start.2 = ((bf16[16,3,128,128]{3,2,1,0:T(8,128)(2,1)}), bf16[16,3,128,128]{3,2,1,0:T(8,128)(2,1)S(1)}, u32[]{:S(2)}, u32[]{:S(2)}) async-start(bf16[16,3,128,128]{3,2,1,0:T(8,128)(2,1)} %attend_grad.1), calls=%async_computation.2 | async-start | bytes 3145728 | tf_op jit(solution)/shard_map/all_to_all | solution.py:348
  97.7 2.9 %fusion.22.refs_2_ = f32[128,1024]{1,0:T(8,128)S(1)} fusion(bf16[16,128,128]{2,1,0:T(8,128)(2,1)S(1)} %all-to-all-done.1, bf16[16,128,8192]{2,1,0:T(8,128)(2,1)} %bitcast.22), kind=kOutput, calls=%fused_computation.15 | convolution fusion | flops 536870912 | bytes 5242880 | tf_op jit(solution)/shard_map/hrd,hdm->rm/dot_general | solution.py:371
  100.6 1.3 collective-permute-start.1
  101.9 4.6 %fusion.16.refs_8_ = f32[128,2048]{1,0:T(8,128)S(1)} fusion(bf16[16,128,128]{2,1,0:T(8,128)(2,1)S(1)} %all-to-all-done.1, bf16[16,128,8192]{2,1,0:T(8,128)(2,1)} %bitcast.23), kind=kOutput, calls=%fused_computation.12 | convolution fusion | flops 1073741824 | bytes 9961472 | tf_op jit(solution)/shard_map/hrd,hdm->rm/dot_general | solution.py:371
  106.9 4.6 %fusion.13.refs_6_ = f32[128,2048]{1,0:T(8,128)S(1)} fusion(bf16[16,128,128]{2,1,0:T(8,128)(2,1)S(1)} %all-to-all-done.1, bf16[16,128,8192]{2,1,0:T(8,128)(2,1)} %bitcast.24), kind=kOutput, calls=%fused_computation.11 | convolution fusion | flops 1073741824 | bytes 9961472 | tf_op jit(solution)/shard_map/hrd,hdm->rm/dot_general | solution.py:371
  111.6 1.3 collective-permute-start.3
  112.9 4.6 %fusion.10.refs_4_ = f32[128,2048]{1,0:T(8,128)S(1)} fusion(bf16[16,128,128]{2,1,0:T(8,128)(2,1)S(1)} %all-to-all-done.1, bf16[16,128,8192]{2,1,0:T(8,128)(2,1)} %bitcast.25), kind=kOutput, calls=%fused_computation.10 | convolution fusion | flops 1073741824 | bytes 9961472 | tf_op jit(solution)/shard_map/hrd,hdm->rm/dot_general | solution.py:371
  117.9 2.9 %fusion.19.refs_0_ = f32[128,1024]{1,0:T(8,128)S(1)} fusion(bf16[16,128,128]{2,1,0:T(8,128)(2,1)S(1)} %all-to-all-done.1, bf16[16,128,8192]{2,1,0:T(8,128)(2,1)} %bitcast.26), kind=kOutput, calls=%fused_computation.14 | convolution fusion | flops 536870912 | bytes 5242880 | tf_op jit(solution)/shard_map/hrd,hdm->rm/dot_general | solution.py:371
  120.8 1.3 collective-permute-start
  122.1 5.5 %collective-permute-done.refs_1_ = bf16[64,1024]{1,0:T(8,128)(2,1)S(1)} collective-permute-done((bf16[64,1024]{1,0:T(8,128)(2,1)S(1)}, bf16[64,1024]{1,0:T(8,128)(2,1)S(1)}, u32[]{:S(2)}, u32[]{:S(2)}) %collective-permute-start) | collective-permute-done | bytes 131104 | tf_op jit(solution)/shard_map/ppermute | solution.py:378
  127.6 1.5 %finish.1 = f32[64,8192]{1,0:T(8,128)} custom-call(s32[1]{0:T(128)} %bitcast.turn_ref, f32[128,1024]{1,0:T(8,128)S(1)} %fusion.19.refs_0_, bf16[64,1024]{1,0:T(8,128)(2,1)S(1)} %collective-permute-done.refs_1_, f32[128,1024]{1,0:T(8,128)S(1)} %fusion.22.refs_2_, bf16[64,1024]{1,0:T(8,128)(2,1)S(1)} %collective-permute-done.1.refs_3_, ...), custom_call_target="tpu_custom_call" | custom-call | tf_op jit(solution)/shard_map/finish/pallas_call | solution.py:303
  129.1 4.8 %all-to-all-done.2.x_ref = bf16[16,3,128,128]{3,2,1,0:T(8,128)(2,1)S(1)} async-done(((bf16[16,3,128,128]{3,2,1,0:T(8,128)(2,1)}), bf16[16,3,128,128]{3,2,1,0:T(8,128)(2,1)S(1)}, u32[]{:S(2)}, u32[]{:S(2)}) %all-to-all-start.2) | async-done | bytes 1572896 | tf_op jit(solution)/shard_map/all_to_all | solution.py:348
  133.9 2.9 %join_heads.1 = f32[128,3,16,128]{3,2,1,0:T(8,128)} custom-call(bf16[16,3,128,128]{3,2,1,0:T(8,128)(2,1)S(1)} %all-to-all-done.2.x_ref), custom_call_target="tpu_custom_call" | custom-call | tf_op jit(solution)/shard_map/join_heads/pallas_call | solution.py:218
  (27 shorter events, 1.5 us)
Async XLA Ops:
  0.6 25.1 %copy-start = (bf16[64,8192]{1,0:T(8,128)(2,1)S(1)}, bf16[64,8192]{1,0:T(8,128)(2,1)}, u32[]{:S(2)}) copy-start(bf16[64,8192]{1,0:T(8,128)(2,1)} %own_ref.3) | copy-start | bytes 3145732
  3.7 45.4 %all-to-all-start = ((bf16[16,3,128,128]{3,2,1,0:T(8,128)(2,1)}), bf16[16,3,128,128]{3,2,1,0:T(8,128)(2,1)S(1)}, u32[]{:S(2)}, u32[]{:S(2)}) async-start(bf16[16,3,128,128]{3,2,1,0:T(8,128)(2,1)} %bitcast.27), calls=%async_computation | async-start | bytes 3145728 | tf_op jit(solution)/shard_map/all_to_all | solution.py:348
  12.5 13.3 %collective-permute-start.6 = (bf16[64,4096]{1,0:T(8,128)(2,1)}, bf16[64,4096]{1,0:T(8,128)(2,1)S(1)}, u32[]{:S(2)}, u32[]{:S(2)}) collective-permute-start(bf16[64,4096]{1,0:T(8,128)(2,1)} %get-tuple-element.14), channel_id=1, source_target_pairs={{0,1},{1,0},{2,3},{3,2},{4,5},{5,4},{6,7},{7,6},{8,9},{9,8},{10,11... | collective-permute-start | bytes 1572872 | tf_op jit(solution)/shard_map/ppermute | solution.py:353
  13.7 23.4 %collective-permute-start.5 = (bf16[64,4096]{1,0:T(8,128)(2,1)}, bf16[64,4096]{1,0:T(8,128)(2,1)}, u32[]{:S(2)}, u32[]{:S(2)}) collective-permute-start(bf16[64,4096]{1,0:T(8,128)(2,1)} %get-tuple-element.15), channel_id=1, source_target_pairs={{0,1},{1,0},{2,3},{3,2},{4,5},{5,4},{6,7},{7,6},{8,9},{9,8},{10,11... | collective-permute-start | bytes 1572872 | tf_op jit(solution)/shard_map/ppermute | solution.py:353
  46.0 3.0 %collective-permute-start.7 = (bf16[4,128,128]{2,1,0:T(8,128)(2,1)S(1)}, bf16[4,128,128]{2,1,0:T(8,128)(2,1)S(1)}, u32[]{:S(2)}, u32[]{:S(2)}) collective-permute-start(bf16[4,128,128]{2,1,0:T(8,128)(2,1)S(1)} %get-tuple-element.11), channel_id=1, source_target_pairs={{0,2},{2,0},{4,6},{6,4},{8,10},{10,8},{12,14},{14,12},{16,18},{18,... | collective-permute-start | bytes 393224 | tf_op jit(solution)/shard_map/ppermute | solution.py:357
  47.3 12.5 %collective-permute-start.8 = (bf16[4,128,128]{2,1,0:T(8,128)(2,1)S(1)}, bf16[4,128,128]{2,1,0:T(8,128)(2,1)S(1)}, u32[]{:S(2)}, u32[]{:S(2)}) collective-permute-start(bf16[4,128,128]{2,1,0:T(8,128)(2,1)S(1)} %get-tuple-element.12), channel_id=1, source_target_pairs={{0,4},{2,6},{4,0},{6,2},{8,12},{10,14},{12,8},{14,10},{16,20},{18,... | collective-permute-start | bytes 393224 | tf_op jit(solution)/shard_map/ppermute | solution.py:357
  47.6 12.2 %collective-permute-start.9 = (bf16[4,128,128]{2,1,0:T(8,128)(2,1)S(1)}, bf16[4,128,128]{2,1,0:T(8,128)(2,1)S(1)}, u32[]{:S(2)}, u32[]{:S(2)}) collective-permute-start(bf16[4,128,128]{2,1,0:T(8,128)(2,1)S(1)} %get-tuple-element.13), channel_id=1, source_target_pairs={{0,6},{2,4},{4,2},{6,0},{8,14},{10,12},{12,10},{14,8},{16,22},{18,... | collective-permute-start | bytes 393224 | tf_op jit(solution)/shard_map/ppermute | solution.py:357
  54.0 38.9 %all-to-all-start.1 = ((bf16[16,128,128]{2,1,0:T(8,128)(2,1)}), bf16[16,128,128]{2,1,0:T(8,128)(2,1)S(1)}, u32[]{:S(2)}, u32[]{:S(2)}) async-start(bf16[16,128,128]{2,1,0:T(8,128)(2,1)} %get-tuple-element.8.att_ref), calls=%async_computation.1 | async-start | bytes 1048576 | tf_op jit(solution)/shard_map/all_to_all | solution.py:348
  59.8 12.3 %collective-permute-start.10 = (bf16[4,128,128]{2,1,0:T(8,128)(2,1)S(1)}, bf16[4,128,128]{2,1,0:T(8,128)(2,1)S(1)}, u32[]{:S(2)}, u32[]{:S(2)}) collective-permute-start(bf16[4,128,128]{2,1,0:T(8,128)(2,1)S(1)} %pad_maximum_fusion), channel_id=1, source_target_pairs={{0,8},{2,10},{4,12},{6,14},{8,0},{10,2},{12,4},{14,6},{16,24},{18,... | collective-permute-start | bytes 393224 | tf_op jit(solution)/shard_map/ppermute | solution.py:362
  60.2 19.5 %collective-permute-start.11 = (bf16[4,128,128]{2,1,0:T(8,128)(2,1)S(1)}, bf16[4,128,128]{2,1,0:T(8,128)(2,1)S(1)}, u32[]{:S(2)}, u32[]{:S(2)}) collective-permute-start(bf16[4,128,128]{2,1,0:T(8,128)(2,1)S(1)} %pad_maximum_fusion.1), channel_id=1, source_target_pairs={{0,16},{2,18},{4,20},{6,22},{8,24},{10,26},{12,28},{14,30},{16,0},... | collective-permute-start | bytes 393224 | tf_op jit(solution)/shard_map/ppermute | solution.py:362
  62.4 21.9 %collective-permute-start.12 = (bf16[4,128,128]{2,1,0:T(8,128)(2,1)S(1)}, bf16[4,128,128]{2,1,0:T(8,128)(2,1)S(1)}, u32[]{:S(2)}, u32[]{:S(2)}) collective-permute-start(bf16[4,128,128]{2,1,0:T(8,128)(2,1)S(1)} %pad_maximum_fusion.2), channel_id=1, source_target_pairs={{0,24},{2,26},{4,28},{6,30},{8,16},{10,18},{12,20},{14,22},{16,8},... | collective-permute-start | bytes 393224 | tf_op jit(solution)/shard_map/ppermute | solution.py:362
  92.9 41.0 %all-to-all-start.2 = ((bf16[16,3,128,128]{3,2,1,0:T(8,128)(2,1)}), bf16[16,3,128,128]{3,2,1,0:T(8,128)(2,1)S(1)}, u32[]{:S(2)}, u32[]{:S(2)}) async-start(bf16[16,3,128,128]{3,2,1,0:T(8,128)(2,1)} %attend_grad.1), calls=%async_computation.2 | async-start | bytes 3145728 | tf_op jit(solution)/shard_map/all_to_all | solution.py:348
  100.6 21.5 %collective-permute-start.1 = (bf16[64,1024]{1,0:T(8,128)(2,1)S(1)}, bf16[64,1024]{1,0:T(8,128)(2,1)S(1)}, u32[]{:S(2)}, u32[]{:S(2)}) collective-permute-start(bf16[64,1024]{1,0:T(8,128)(2,1)S(1)} %dynamic-slice_convert_fusion.3), channel_id=1, source_target_pairs={{0,1},{1,0},{2,3},{3,2},{4,5},{5,4},{6,7},{7,6},{8,9},{9,8},{10,11... | collective-permute-start | bytes 393224 | tf_op jit(solution)/shard_map/ppermute | solution.py:378
  106.6 21.0 %collective-permute-start.4 = (bf16[64,2048]{1,0:T(8,128)(2,1)S(1)}, bf16[64,2048]{1,0:T(8,128)(2,1)S(1)}, u32[]{:S(2)}, u32[]{:S(2)}) collective-permute-start(bf16[64,2048]{1,0:T(8,128)(2,1)S(1)} %dynamic-slice_convert_fusion), channel_id=1, source_target_pairs={{0,1},{1,0},{2,3},{3,2},{4,5},{5,4},{6,7},{7,6},{8,9},{9,8},{10,11... | collective-permute-start | bytes 786440 | tf_op jit(solution)/shard_map/ppermute | solution.py:378
  111.6 16.0 %collective-permute-start.3 = (bf16[64,2048]{1,0:T(8,128)(2,1)S(1)}, bf16[64,2048]{1,0:T(8,128)(2,1)S(1)}, u32[]{:S(2)}, u32[]{:S(2)}) collective-permute-start(bf16[64,2048]{1,0:T(8,128)(2,1)S(1)} %dynamic-slice_convert_fusion.1), channel_id=1, source_target_pairs={{0,1},{1,0},{2,3},{3,2},{4,5},{5,4},{6,7},{7,6},{8,9},{9,8},{10,11... | collective-permute-start | bytes 786440 | tf_op jit(solution)/shard_map/ppermute | solution.py:378
  117.6 10.0 %collective-permute-start.2 = (bf16[64,2048]{1,0:T(8,128)(2,1)S(1)}, bf16[64,2048]{1,0:T(8,128)(2,1)S(1)}, u32[]{:S(2)}, u32[]{:S(2)}) collective-permute-start(bf16[64,2048]{1,0:T(8,128)(2,1)S(1)} %dynamic-slice_convert_fusion.2), channel_id=1, source_target_pairs={{0,1},{1,0},{2,3},{3,2},{4,5},{5,4},{6,7},{7,6},{8,9},{9,8},{10,11... | collective-permute-start | bytes 786440 | tf_op jit(solution)/shard_map/ppermute | solution.py:378
  120.8 6.8 %collective-permute-start = (bf16[64,1024]{1,0:T(8,128)(2,1)S(1)}, bf16[64,1024]{1,0:T(8,128)(2,1)S(1)}, u32[]{:S(2)}, u32[]{:S(2)}) collective-permute-start(bf16[64,1024]{1,0:T(8,128)(2,1)S(1)} %dynamic-slice_convert_fusion.4), channel_id=1, source_target_pairs={{0,1},{1,0},{2,3},{3,2},{4,5},{5,4},{6,7},{7,6},{8,9},{9,8},{10,11... | collective-permute-start | bytes 393224 | tf_op jit(solution)/shard_map/ppermute | solution.py:378

commit v10 on v9

--- a/solution.py
+++ b/solution.py
@@ -11,6 +11,7 @@
 
 HD = 128
 LOG2E = math.log2(math.e)
+BACK_PARTS = (4, 2, 2)
 MIX_PARTS = (1, 1, 2, 2, 2)
 MIB = 1024 * 1024
 
@@ -68,33 +69,36 @@
         x_buf[pl.ds(pl.multiple_of(place * half, half), half)] = x_ref[...]
 
 
-def back_first_kernel(turn_ref, own_ref, other_ref, w_ref, out_ref, x_buf):
+def back_term(turn_ref, own_ref, other_ref, w_ref, x_buf):
     @pl.when(pl.program_id(0) == 0)
     def _():
         stack_rows(turn_ref, own_ref, other_ref, x_buf)
 
-    out_ref[...] = dot_nt(w_ref[...], x_buf[...])
-
-
-def back_last_kernel(turn_ref, me_ref, own_ref, other_ref, w_ref, y_ref, *refs):
+    return dot_nt(w_ref[...], x_buf[...])
+
+
+def back_first_kernel(turn_ref, own_ref, other_ref, w_ref, out_ref, x_buf):
+    out_ref[...] = back_term(turn_ref, own_ref, other_ref, w_ref, x_buf)
+
+
+def back_next_kernel(turn_ref, own_ref, other_ref, w_ref, y_ref, out_ref, x_buf):
+    out_ref[...] = y_ref[...] + back_term(turn_ref, own_ref, other_ref, w_ref, x_buf)
+
+
+def back_last_kernel(turn_ref, own_ref, other_ref, w_ref, y_ref, me_ref, *refs):
     *out_refs, x_buf, chunks = refs
     step = pl.program_id(0)
     group = w_ref.shape[0] // HD
-
-    @pl.when(step == 0)
-    def _():
-        stack_rows(turn_ref, own_ref, other_ref, x_buf)
-
-    y = y_ref[...] + dot_nt(w_ref[...], x_buf[...])
+    y = y_ref[...] + back_term(turn_ref, own_ref, other_ref, w_ref, x_buf)
     for h in range(group):
         head = (step * group + h) ^ me_ref[0]
         chunks[head] = y[h * HD : (h + 1) * HD].T.astype(jnp.bfloat16)
 
     @pl.when(step == pl.num_programs(0) - 1)
     def _():
-        for e, ref in enumerate(out_refs):
-            for d in range(ref.shape[0]):
-                ref[d] = chunks[PLANE * d + e]
+        for d, ref in enumerate(out_refs):
+            for e in range(PLANE):
+                ref[e] = chunks[PLANE * d + e]
 
 
 def forward_kernel(step, qkv_ref, att_ref, lse_ref, v_t, s_buf):
@@ -143,11 +147,11 @@
 def backward_kernel(step, me_ref, qkv_ref, att_ref, lse_ref, *refs):
     parts, rest = refs[:-5], refs[-5:]
     out_ref, g_ref, k_t, dq_t, delta = rest
-    plane, others = parts[:PLANE], parts[PLANE:]
-    for e, ref in enumerate(plane):
-        g_ref[me_ref[0] ^ e] = ref[0]
-        for d, other in enumerate(others, 1):
-            g_ref[me_ref[0] ^ (PLANE * d + e)] = other[e]
+    outer, others = parts[: 1 - PLANE], parts[1 - PLANE :]
+    for d, ref in enumerate(outer):
+        g_ref[me_ref[0] ^ (PLANE * d)] = ref[0]
+        for e, other in enumerate(others, 1):
+            g_ref[me_ref[0] ^ (PLANE * d + e)] = other[d]
     chunks, _, unit, _ = qkv_ref.shape
     per = step // unit
     blocks = chunks // per
@@ -229,46 +233,52 @@
 
 
 def project_back(turn, me, own, other, weights):
-    half, width = own.shape
+    half, _ = own.shape
     deep = weights.shape[0]
+    heads = deep // HD
     group = 4 * HD
-    part = width // 2
-    cost = pl.CostEstimate(
-        flops=2 * half * width * deep, transcendentals=0, bytes_accessed=width * deep
-    )
-    params = pltpu.CompilerParams(vmem_limit_bytes=22 * MIB)
-
-    def rows(c):
-        return pl.BlockSpec((half, part), lambda b: (0, c))
-
-    def block(c):
-        return pl.BlockSpec((group, part), lambda b: (b, c))
-
     partial = pl.BlockSpec((group, 2 * half), lambda b: (b, 0))
-    x_buf = pltpu.VMEM((2 * half, part), jnp.bfloat16)
-    y = pl.pallas_call(
-        back_first_kernel,
-        grid=(deep // group,),
-        out_shape=jax.ShapeDtypeStruct((deep, 2 * half), jnp.float32),
-        in_specs=[in_smem(), rows(0), *in_vmem(1), block(0)],
-        out_specs=partial,
-        scratch_shapes=[x_buf],
-        compiler_params=params,
-        cost_estimate=cost,
-        name="back_first",
-    )(turn, own, other[0], weights)
-    heads = deep // HD
-    return pl.pallas_call(
-        back_last_kernel,
-        grid=(deep // group,),
-        out_shape=[jax.ShapeDtypeStruct((heads // PLANE, 2 * half, HD), jnp.bfloat16)] * PLANE,
-        in_specs=[in_smem(), in_smem(), rows(1), *in_vmem(1), block(1), partial],
-        out_specs=in_vmem(PLANE),
-        scratch_shapes=[x_buf, pltpu.VMEM((heads, 2 * half, HD), jnp.bfloat16)],
-        compiler_params=params,
-        cost_estimate=cost,
-        name="back_last",
-    )(turn, me, own, other[1], weights, y)
+    start = 0
+    y = None
+    for c, piece in enumerate(other):
+        part = piece.shape[1]
+        place = start // part
+        start += part
+        last = c == len(other) - 1
+        operands = [turn, own, piece, weights]
+        in_specs = [
+            in_smem(),
+            pl.BlockSpec((half, part), lambda b, place=place: (0, place)),
+            *in_vmem(1),
+            pl.BlockSpec((group, part), lambda b, place=place: (b, place)),
+        ]
+        scratch = [pltpu.VMEM((2 * half, part), jnp.bfloat16)]
+        if y is not None:
+            operands.append(y)
+            in_specs.append(partial)
+        if last:
+            operands.append(me)
+            in_specs.append(in_smem())
+            scratch.append(pltpu.VMEM((heads, 2 * half, HD), jnp.bfloat16))
+            shape = jax.ShapeDtypeStruct((PLANE, 2 * half, HD), jnp.bfloat16)
+            out_shape, out_specs = [shape] * (heads // PLANE), in_vmem(heads // PLANE)
+            kernel = back_last_kernel
+        else:
+            out_shape, out_specs = jax.ShapeDtypeStruct((deep, 2 * half), jnp.float32), partial
+            kernel = back_next_kernel if c else back_first_kernel
+        y = pl.pallas_call(
+            kernel,
+            grid=(deep // group,),
+            out_shape=out_shape,
+            in_specs=in_specs,
+            out_specs=out_specs,
+            scratch_shapes=scratch,
+            compiler_params=pltpu.CompilerParams(vmem_limit_bytes=22 * MIB),
+            cost_estimate=pl.CostEstimate(
+                flops=4 * half * part * deep, transcendentals=0, bytes_accessed=2 * part * deep
+            ),
+        )(*operands)
+    return y
 
 
 def attend(qkv, step):
@@ -310,7 +320,7 @@
     )(turn, *flat)
 
 
-def attend_grad(me, qkv, att, lse, plane, others, step):
+def attend_grad(me, qkv, att, lse, outer, others, step):
     chunks, _, unit, _ = qkv.shape
     length = chunks * unit
     blocks = length // step
@@ -318,7 +328,7 @@
     return pl.pallas_call(
         functools.partial(backward_kernel, step),
         out_shape=jax.ShapeDtypeStruct((chunks, 3, unit, HD), jnp.bfloat16),
-        in_specs=[in_smem(), *in_vmem(3 + len(plane) + len(others))],
+        in_specs=[in_smem(), *in_vmem(3 + len(outer) + len(others))],
         out_specs=in_vmem(1)[0],
         scratch_shapes=[
             pltpu.VMEM((chunks, unit, HD), jnp.bfloat16),
@@ -331,7 +341,7 @@
             flops=10 * area * HD, transcendentals=area, bytes_accessed=16 * length * HD
         ),
         name="attend_grad",
-    )(me, qkv, att, lse, *plane, *others)
+    )(me, qkv, att, lse, *outer, *others)
 
 
 def by_head(qkv, grad_out, attn_out):
@@ -348,21 +358,23 @@
         return lax.all_to_all(x, "ctx", 0, 0, tiled=True)
 
     other = []
-    for c in range(2):
-        cut = grad_out[:, c * (width // 2) : (c + 1) * (width // 2)]
-        other.append(lax.ppermute(cut, "tp", swap))
+    start = 0
+    for eighths in BACK_PARTS:
+        stop = start + eighths * (width // 8)
+        other.append(lax.ppermute(grad_out[:, start:stop], "tp", swap))
+        start = stop
     mine = spread(jnp.transpose(qkv, (1, 2, 0, 3)))
-    plane = list(project_back(turn.reshape(1), me, grad_out, other, attn_out))
+    outer = list(project_back(turn.reshape(1), me, grad_out, other, attn_out))
+    for d in range(1, len(outer)):
+        pairs = [(i, i ^ (PLANE * d)) for i in range(heads)]
+        outer[d] = lax.ppermute(outer[d], "ctx", pairs)
+    others = []
     for e in range(1, PLANE):
-        plane[e] = lax.ppermute(plane[e], "ctx", [(i, i ^ e) for i in range(heads)])
-    others = []
-    for d in range(1, heads // PLANE):
-        sent = jnp.stack([x[d] for x in plane])
-        pairs = [(i, i ^ (PLANE * d)) for i in range(heads)]
-        others.append(lax.ppermute(sent, "ctx", pairs))
+        sent = jnp.stack([x[e] for x in outer])
+        others.append(lax.ppermute(sent, "ctx", [(i, i ^ e) for i in range(heads)]))
     att, lse = attend(mine, step)
     local = spread(att)
-    grads = attend_grad(me, mine, att, lse, plane, others, step)
+    grads = attend_grad(me, mine, att, lse, outer, others, step)
     grads = spread(grads)
     pieces = []
     start = 0

time: 138 us -> 131 us (0.949)
  waiting for transfers between devices: 46.5 us -> 29.7 us
  starting transfers between devices: 28.9 us -> 34.7 us
  local copies, waits for them, and re-layouts: 5.51 us -> 8.14 us
  Pallas kernels: 35.3 us -> 36.8 us
    ppermute x8 -> x9, waiting for transfers between devices: 36.2 us -> 19.4 us  [the longest x3 9.51 us: by_head(): others.append(lax.ppermute(sent, 'ctx', [(i, i ^ e) for i in range(heads)]))]
    all_to_all x3, starting transfers between devices: 17.1 us -> 22.5 us  [spread(): return lax.all_to_all(x, 'ctx', 0, 0, tiled=True)]
    pallas_call x2 -> x3, Pallas kernels: 17.3 us -> 20 us  [project_back(): pl.pallas_call(kernel, grid=(deep // group,), out_shape=out_shape, in_spe...]
    slice x5 -> x6, local copies, waits for them, and re-layouts: 2.3 us -> 3.79 us  [the longest x2 3.75 us: by_head(): other.append(lax.ppermute(grad_out[:, start:stop], 'tp', swap))]
    unnamed x3 -> x5, local copies, waits for them, and re-layouts: 3.05 us -> 4.19 us
    ppermute x8 -> x9, starting transfers between devices: 7.34 us -> 7.73 us  [the longest x3 2.71 us: by_head(): outer[d] = lax.ppermute(outer[d], 'ctx', pairs)]
  transfers between devices with their start and end apart: 16 -> 17, of which waited for: 7 -> 6; matrix products, arithmetic and copies ran while one was open for 16% -> 18% of each run, Pallas kernels for 24% -> 26%
where the time goes in v10:
time: 131 us; the launch traced here: 130 us
  Pallas kernels  36.8 us (28%)
  starting transfers between devices  34.7 us (26%)
  waiting for transfers between devices  29.7 us (23%)
  matrix products  19.7 us (15%)
  local copies, waits for them, and re-layouts  8.14 us (6%)
    all_to_all x3, starting transfers between devices, spread(): return lax.all_to_all(x, 'ctx', 0, 0, tiled=True)  22.5 us
    pallas_call x3, Pallas kernels, project_back(): pl.pallas_call(kernel, grid=(deep // group,), out_shape=out_shape, in_spe...  20 us
    dot_general x5, matrix products, by_head(): jnp.einsum('hrd,hdm->rm', local, weights[:, :, start:stop], preferred_ele...  19.7 us
    ppermute x3, waiting for transfers between devices, by_head(): others.append(lax.ppermute(sent, 'ctx', [(i, i ^ e) for i in range(heads)]))  9.51 us
    ppermute x3, waiting for transfers between devices, by_head(): other.append(lax.ppermute(grad_out[:, start:stop], 'tp', swap))  8.74 us
    pallas_call x1, Pallas kernels, attend_grad(): pl.pallas_call(functools.partial(backward_kernel, step), out_shape=jax.Sh...  7.44 us
    ppermute x5, waiting for transfers between devices, by_head(): pieces.append((mixed, lax.ppermute(sent.astype(jnp.bfloat16), 'tp', swap)))  5.5 us
    pallas_call x1, Pallas kernels, attend(): pl.pallas_call(functools.partial(forward_kernel, step), out_shape=(jax.Sh...  4.94 us
  transfers between devices with their start and end apart: 17, of which 6 were waited for; matrix products, arithmetic and copies ran while one was open for 18% of the time, Pallas kernels for 26%

profile of v10, /device:TPU:13, one launch (start us, length us, event | category | flops | bytes accessed | tf_op | source)
XLA Modules:
  0.0 129.9 jit_solution(7564955185225266110)
XLA Ops:
  0.6 3.0 %copy.7 = bf16[128,16,3,128]{3,0,2,1:T(8,128)(2,1)} copy(bf16[128,16,3,128]{3,1,2,0:T(8,128)(2,1)} %param.3) | data formatting | bytes 3145728 | tf_op args[0]
  3.7 6.5 %all-to-all-start = ((bf16[16,3,128,128]{3,2,1,0:T(8,128)(2,1)}), bf16[16,3,128,128]{3,2,1,0:T(8,128)(2,1)S(1)}, u32[]{:S(2)}, u32[]{:S(2)}) async-start(bf16[16,3,128,128]{3,2,1,0:T(8,128)(2,1)} %bitcast.27), calls=%async_computation | async-start | bytes 3145728 | tf_op jit(solution)/shard_map/all_to_all | solution.py:358
  10.2 1.9 %slice.67 = bf16[64,4096]{1,0:T(8,128)(2,1)} slice(bf16[64,8192]{1,0:T(8,128)(2,1)} %own_ref.5), slice={[0:64], [0:4096]} | slice | bytes 1048576 | tf_op jit(solution)/shard_map/slice | solution.py:364
  12.1 1.2 collective-permute-start.7
  13.3 1.9 %fusion.25 = (bf16[64,2048]{1,0:T(8,128)(2,1)}, bf16[64,2048]{1,0:T(8,128)(2,1)}) fusion(bf16[64,8192]{1,0:T(8,128)(2,1)} %own_ref.5), kind=kLoop, calls=%fused_computation.24 | loop fusion | bytes 1048576 | tf_op jit(solution)/shard_map/slice | solution.py:364
  15.4 1.2 collective-permute-start.5
  16.6 8.7 %collective-permute-done.7.other_ref = bf16[64,4096]{1,0:T(8,128)(2,1)S(1)} collective-permute-done((bf16[64,4096]{1,0:T(8,128)(2,1)}, bf16[64,4096]{1,0:T(8,128)(2,1)S(1)}, u32[]{:S(2)}, u32[]{:S(2)}) %collective-permute-start.7) | collective-permute-done | bytes 524320 | tf_op jit(solution)/shard_map/ppermute | solution.py:364
  25.4 8.5 %shard_map.50.y_ref = f32[2048,128]{1,0:T(8,128)S(1)} custom-call(s32[1]{0:T(128)} %bitcast.turn_ref, bf16[64,8192]{1,0:T(8,128)(2,1)S(1)} %copy-done, bf16[64,4096]{1,0:T(8,128)(2,1)S(1)} %collective-permute-done.7.other_ref, bf16[2048,8192]{1,0:T(8,128)(2,1)} %w_ref.5), custom_call_target="tpu_custom_call" | custom-call | flops 2147483648 | bytes 16777216 | tf_op jit(solution)/shard_map/pallas_call | solution.py:269
  33.9 5.6 %shard_map.51.y_ref = f32[2048,128]{1,0:T(8,128)S(1)} custom-call(s32[1]{0:T(128)} %bitcast.turn_ref, bf16[64,8192]{1,0:T(8,128)(2,1)S(1)} %copy-done, bf16[64,2048]{1,0:T(8,128)(2,1)S(1)} %collective-permute-done.6.other_ref, bf16[2048,8192]{1,0:T(8,128)(2,1)} %w_ref.5, f32[2048,128]{1,0:T(8,128)S(1)} %shard_map.50.y_ref), custom_call_target="tpu_custom_call" | custom-call | flops 1073741824 | bytes 8388608 | tf_op jit(solution)/shard_map/pallas_call | solution.py:269
  39.5 5.9 %shard_map.52 = (bf16[4,128,128]{2,1,0:T(8,128)(2,1)S(1)}, bf16[4,128,128]{2,1,0:T(8,128)(2,1)S(1)}, bf16[4,128,128]{2,1,0:T(8,128)(2,1)S(1)}, bf16[4,128,128]{2,1,0:T(8,128)(2,1)S(1)}) custom-call(s32[1]{0:T(128)} %bitcast.turn_ref, bf16[64,8192]{1,0:T(8,128)(2,1)S(1)} %copy-done, bf16[64,2048]{1,0:T(8,128)(2,1)} %collective-permute-done.5.other_ref, ...), custom_call_target="tpu_custom_call" | custom-call | flops 1073741824 | bytes 8388608 | tf_op jit(solution)/shard_map/pallas_call | solution.py:269
  45.8 2.1 %collective-permute-start.9 = (bf16[4,128,128]{2,1,0:T(8,128)(2,1)S(1)}, bf16[4,128,128]{2,1,0:T(8,128)(2,1)S(1)}, u32[]{:S(2)}, u32[]{:S(2)}) collective-permute-start(bf16[4,128,128]{2,1,0:T(8,128)(2,1)S(1)} %get-tuple-element.12), channel_id=1, source_target_pairs={{0,16},{2,18},{4,20},{6,22},{8,24},{10,26},{12,28},{14,30},{16,0},... | collective-permute-start | bytes 393224 | tf_op jit(solution)/shard_map/ppermute | solution.py:370
  48.2 1.2 collective-permute-done.8.refs_1_
  49.4 4.9 %attend.1 = (bf16[16,128,128]{2,1,0:T(8,128)(2,1)}, f32[4,1,512]{2,1,0:T(1,128)S(1)}) custom-call(bf16[16,3,128,128]{3,2,1,0:T(8,128)(2,1)S(1)} %all-to-all-done.qkv_ref), custom_call_target="tpu_custom_call" | custom-call | flops 1073741824 | bytes 2097152 | tf_op jit(solution)/shard_map/attend/pallas_call | solution.py:289
  54.3 9.4 %all-to-all-start.1 = ((bf16[16,128,128]{2,1,0:T(8,128)(2,1)}), bf16[16,128,128]{2,1,0:T(8,128)(2,1)S(1)}, u32[]{:S(2)}, u32[]{:S(2)}) async-start(bf16[16,128,128]{2,1,0:T(8,128)(2,1)} %get-tuple-element.8.att_ref), calls=%async_computation.1 | async-start | bytes 1048576 | tf_op jit(solution)/shard_map/all_to_all | solution.py:358
  64.6 1.5 %collective-permute-start.13 = (bf16[4,128,128]{2,1,0:T(8,128)(2,1)S(1)}, bf16[4,128,128]{2,1,0:T(8,128)(2,1)S(1)}, u32[]{:S(2)}, u32[]{:S(2)}) collective-permute-start(bf16[4,128,128]{2,1,0:T(8,128)(2,1)S(1)} %pad_maximum_fusion.2), channel_id=1, source_target_pairs={{0,6},{2,4},{4,2},{6,0},{8,14},{10,12},{12,10},{14,8},{16,22},{18,... | collective-permute-start | bytes 393224 | tf_op jit(solution)/shard_map/ppermute | solution.py:374
  66.2 5.4 %collective-permute-done.12.refs_5_ = bf16[4,128,128]{2,1,0:T(8,128)(2,1)S(1)} collective-permute-done((bf16[4,128,128]{2,1,0:T(8,128)(2,1)S(1)}, bf16[4,128,128]{2,1,0:T(8,128)(2,1)S(1)}, u32[]{:S(2)}, u32[]{:S(2)}) %collective-permute-start.12) | collective-permute-done | bytes 131104 | tf_op jit(solution)/shard_map/ppermute | solution.py:374
  71.6 4.1 %collective-permute-done.13.refs_6_ = bf16[4,128,128]{2,1,0:T(8,128)(2,1)S(1)} collective-permute-done((bf16[4,128,128]{2,1,0:T(8,128)(2,1)S(1)}, bf16[4,128,128]{2,1,0:T(8,128)(2,1)S(1)}, u32[]{:S(2)}, u32[]{:S(2)}) %collective-permute-start.13) | collective-permute-done | bytes 131104 | tf_op jit(solution)/shard_map/ppermute | solution.py:374
  75.7 7.4 %attend_grad.1 = bf16[16,3,128,128]{3,2,1,0:T(8,128)(2,1)S(1)} custom-call(s32[1]{0:T(128)} %bitcast.8.me_ref, bf16[16,3,128,128]{3,2,1,0:T(8,128)(2,1)S(1)} %all-to-all-done.qkv_ref, bf16[16,128,128]{2,1,0:T(8,128)(2,1)} %get-tuple-element.8.att_ref, f32[4,1,512]{2,1,0:T(1,128)S(1)} %get-tuple-element.9.lse_ref, ...), custom_call_target="tpu_custom_call" | custom-call | flops 2684354560 | bytes 4194304 | tf_op jit(solution)/shard_map/attend_grad/pallas_call | solution.py:328
  83.1 1.1 copy-done.1
  84.3 6.6 %all-to-all-start.2 = ((bf16[16,3,128,128]{3,2,1,0:T(8,128)(2,1)}), bf16[16,3,128,128]{3,2,1,0:T(8,128)(2,1)S(1)}, u32[]{:S(2)}, u32[]{:S(2)}) async-start(bf16[16,3,128,128]{3,2,1,0:T(8,128)(2,1)} %copy-done.1), calls=%async_computation.2 | async-start | bytes 3145728 | tf_op jit(solution)/shard_map/all_to_all | solution.py:358
  90.8 2.9 %fusion.22.refs_2_ = f32[128,1024]{1,0:T(8,128)S(1)} fusion(bf16[16,128,128]{2,1,0:T(8,128)(2,1)S(1)} %all-to-all-done.1, bf16[16,128,8192]{2,1,0:T(8,128)(2,1)} %bitcast.22), kind=kOutput, calls=%fused_computation.15 | convolution fusion | flops 536870912 | bytes 5242880 | tf_op jit(solution)/shard_map/hrd,hdm->rm/dot_general | solution.py:383
  93.8 1.2 collective-permute-start.1
  95.0 4.6 %fusion.16.refs_8_ = f32[128,2048]{1,0:T(8,128)S(1)} fusion(bf16[16,128,128]{2,1,0:T(8,128)(2,1)S(1)} %all-to-all-done.1, bf16[16,128,8192]{2,1,0:T(8,128)(2,1)} %bitcast.23), kind=kOutput, calls=%fused_computation.12 | convolution fusion | flops 1073741824 | bytes 9961472 | tf_op jit(solution)/shard_map/hrd,hdm->rm/dot_general | solution.py:383
  100.1 4.6 %fusion.13.refs_6_ = f32[128,2048]{1,0:T(8,128)S(1)} fusion(bf16[16,128,128]{2,1,0:T(8,128)(2,1)S(1)} %all-to-all-done.1, bf16[16,128,8192]{2,1,0:T(8,128)(2,1)} %bitcast.24), kind=kOutput, calls=%fused_computation.11 | convolution fusion | flops 1073741824 | bytes 9961472 | tf_op jit(solution)/shard_map/hrd,hdm->rm/dot_general | solution.py:383
  104.7 1.2 collective-permute-start.3
  106.0 4.6 %fusion.10.refs_4_ = f32[128,2048]{1,0:T(8,128)S(1)} fusion(bf16[16,128,128]{2,1,0:T(8,128)(2,1)S(1)} %all-to-all-done.1, bf16[16,128,8192]{2,1,0:T(8,128)(2,1)} %bitcast.25), kind=kOutput, calls=%fused_computation.10 | convolution fusion | flops 1073741824 | bytes 9961472 | tf_op jit(solution)/shard_map/hrd,hdm->rm/dot_general | solution.py:383
  111.0 2.9 %fusion.19.refs_0_ = f32[128,1024]{1,0:T(8,128)S(1)} fusion(bf16[16,128,128]{2,1,0:T(8,128)(2,1)S(1)} %all-to-all-done.1, bf16[16,128,8192]{2,1,0:T(8,128)(2,1)} %bitcast.26), kind=kOutput, calls=%fused_computation.14 | convolution fusion | flops 536870912 | bytes 5242880 | tf_op jit(solution)/shard_map/hrd,hdm->rm/dot_general | solution.py:383
  114.0 1.2 collective-permute-start
  115.2 5.5 %collective-permute-done.refs_1_ = bf16[64,1024]{1,0:T(8,128)(2,1)S(1)} collective-permute-done((bf16[64,1024]{1,0:T(8,128)(2,1)S(1)}, bf16[64,1024]{1,0:T(8,128)(2,1)S(1)}, u32[]{:S(2)}, u32[]{:S(2)}) %collective-permute-start) | collective-permute-done | bytes 131104 | tf_op jit(solution)/shard_map/ppermute | solution.py:390
  120.7 1.5 %finish.1 = f32[64,8192]{1,0:T(8,128)} custom-call(s32[1]{0:T(128)} %bitcast.turn_ref, f32[128,1024]{1,0:T(8,128)S(1)} %fusion.19.refs_0_, bf16[64,1024]{1,0:T(8,128)(2,1)S(1)} %collective-permute-done.refs_1_, f32[128,1024]{1,0:T(8,128)S(1)} %fusion.22.refs_2_, bf16[64,1024]{1,0:T(8,128)(2,1)S(1)} %collective-permute-done.1.refs_3_, ...), custom_call_target="tpu_custom_call" | custom-call | tf_op jit(solution)/shard_map/finish/pallas_call | solution.py:313
  122.2 4.8 %all-to-all-done.2.x_ref = bf16[16,3,128,128]{3,2,1,0:T(8,128)(2,1)S(1)} async-done(((bf16[16,3,128,128]{3,2,1,0:T(8,128)(2,1)}), bf16[16,3,128,128]{3,2,1,0:T(8,128)(2,1)S(1)}, u32[]{:S(2)}, u32[]{:S(2)}) %all-to-all-start.2) | async-done | bytes 1572896 | tf_op jit(solution)/shard_map/all_to_all | solution.py:358
  127.0 2.9 %join_heads.1 = f32[128,3,16,128]{3,2,1,0:T(8,128)} custom-call(bf16[16,3,128,128]{3,2,1,0:T(8,128)(2,1)S(1)} %all-to-all-done.2.x_ref), custom_call_target="tpu_custom_call" | custom-call | tf_op jit(solution)/shard_map/join_heads/pallas_call | solution.py:222
  (33 shorter events, 2.7 us)
Async XLA Ops:
  0.6 24.8 %copy-start = (bf16[64,8192]{1,0:T(8,128)(2,1)S(1)}, bf16[64,8192]{1,0:T(8,128)(2,1)}, u32[]{:S(2)}) copy-start(bf16[64,8192]{1,0:T(8,128)(2,1)} %own_ref.5) | copy-start | bytes 3145732
  3.7 45.7 %all-to-all-start = ((bf16[16,3,128,128]{3,2,1,0:T(8,128)(2,1)}), bf16[16,3,128,128]{3,2,1,0:T(8,128)(2,1)S(1)}, u32[]{:S(2)}, u32[]{:S(2)}) async-start(bf16[16,3,128,128]{3,2,1,0:T(8,128)(2,1)} %bitcast.27), calls=%async_computation | async-start | bytes 3145728 | tf_op jit(solution)/shard_map/all_to_all | solution.py:358
  12.1 13.3 %collective-permute-start.7 = (bf16[64,4096]{1,0:T(8,128)(2,1)}, bf16[64,4096]{1,0:T(8,128)(2,1)S(1)}, u32[]{:S(2)}, u32[]{:S(2)}) collective-permute-start(bf16[64,4096]{1,0:T(8,128)(2,1)} %slice.67), channel_id=1, source_target_pairs={{0,1},{1,0},{2,3},{3,2},{4,5},{5,4},{6,7},{7,6},{8,9},{9,8},{10,11... | collective-permute-start | bytes 1572872 | tf_op jit(solution)/shard_map/ppermute | solution.py:364
  15.2 18.7 %collective-permute-start.6 = (bf16[64,2048]{1,0:T(8,128)(2,1)}, bf16[64,2048]{1,0:T(8,128)(2,1)S(1)}, u32[]{:S(2)}, u32[]{:S(2)}) collective-permute-start(bf16[64,2048]{1,0:T(8,128)(2,1)} %get-tuple-element.14), channel_id=1, source_target_pairs={{0,1},{1,0},{2,3},{3,2},{4,5},{5,4},{6,7},{7,6},{8,9},{9,8},{10,11... | collective-permute-start | bytes 786440 | tf_op jit(solution)/shard_map/ppermute | solution.py:364
  15.4 24.1 %collective-permute-start.5 = (bf16[64,2048]{1,0:T(8,128)(2,1)}, bf16[64,2048]{1,0:T(8,128)(2,1)}, u32[]{:S(2)}, u32[]{:S(2)}) collective-permute-start(bf16[64,2048]{1,0:T(8,128)(2,1)} %get-tuple-element.15), channel_id=1, source_target_pairs={{0,1},{1,0},{2,3},{3,2},{4,5},{5,4},{6,7},{7,6},{8,9},{9,8},{10,11... | collective-permute-start | bytes 786440 | tf_op jit(solution)/shard_map/ppermute | solution.py:364
  45.5 3.9 %collective-permute-start.8 = (bf16[4,128,128]{2,1,0:T(8,128)(2,1)S(1)}, bf16[4,128,128]{2,1,0:T(8,128)(2,1)S(1)}, u32[]{:S(2)}, u32[]{:S(2)}) collective-permute-start(bf16[4,128,128]{2,1,0:T(8,128)(2,1)S(1)} %get-tuple-element.11), channel_id=1, source_target_pairs={{0,8},{2,10},{4,12},{6,14},{8,0},{10,2},{12,4},{14,6},{16,24},{18,... | collective-permute-start | bytes 393224 | tf_op jit(solution)/shard_map/ppermute | solution.py:370
  45.8 17.9 %collective-permute-start.9 = (bf16[4,128,128]{2,1,0:T(8,128)(2,1)S(1)}, bf16[4,128,128]{2,1,0:T(8,128)(2,1)S(1)}, u32[]{:S(2)}, u32[]{:S(2)}) collective-permute-start(bf16[4,128,128]{2,1,0:T(8,128)(2,1)S(1)} %get-tuple-element.12), channel_id=1, source_target_pairs={{0,16},{2,18},{4,20},{6,22},{8,24},{10,26},{12,28},{14,30},{16,0},... | collective-permute-start | bytes 393224 | tf_op jit(solution)/shard_map/ppermute | solution.py:370
  47.9 15.8 %collective-permute-start.10 = (bf16[4,128,128]{2,1,0:T(8,128)(2,1)S(1)}, bf16[4,128,128]{2,1,0:T(8,128)(2,1)S(1)}, u32[]{:S(2)}, u32[]{:S(2)}) collective-permute-start(bf16[4,128,128]{2,1,0:T(8,128)(2,1)S(1)} %get-tuple-element.13), channel_id=1, source_target_pairs={{0,24},{2,26},{4,28},{6,30},{8,16},{10,18},{12,20},{14,22},{16,8},... | collective-permute-start | bytes 393224 | tf_op jit(solution)/shard_map/ppermute | solution.py:370
  54.3 30.0 %all-to-all-start.1 = ((bf16[16,128,128]{2,1,0:T(8,128)(2,1)}), bf16[16,128,128]{2,1,0:T(8,128)(2,1)S(1)}, u32[]{:S(2)}, u32[]{:S(2)}) async-start(bf16[16,128,128]{2,1,0:T(8,128)(2,1)} %get-tuple-element.8.att_ref), calls=%async_computation.1 | async-start | bytes 1048576 | tf_op jit(solution)/shard_map/all_to_all | solution.py:358
  63.8 2.4 %collective-permute-start.11 = (bf16[4,128,128]{2,1,0:T(8,128)(2,1)S(1)}, bf16[4,128,128]{2,1,0:T(8,128)(2,1)S(1)}, u32[]{:S(2)}, u32[]{:S(2)}) collective-permute-start(bf16[4,128,128]{2,1,0:T(8,128)(2,1)S(1)} %pad_maximum_fusion), channel_id=1, source_target_pairs={{0,2},{2,0},{4,6},{6,4},{8,10},{10,8},{12,14},{14,12},{16,18},{18,... | collective-permute-start | bytes 393224 | tf_op jit(solution)/shard_map/ppermute | solution.py:374
  64.3 7.3 %collective-permute-start.12 = (bf16[4,128,128]{2,1,0:T(8,128)(2,1)S(1)}, bf16[4,128,128]{2,1,0:T(8,128)(2,1)S(1)}, u32[]{:S(2)}, u32[]{:S(2)}) collective-permute-start(bf16[4,128,128]{2,1,0:T(8,128)(2,1)S(1)} %pad_maximum_fusion.1), channel_id=1, source_target_pairs={{0,4},{2,6},{4,0},{6,2},{8,12},{10,14},{12,8},{14,10},{16,20},{18,... | collective-permute-start | bytes 393224 | tf_op jit(solution)/shard_map/ppermute | solution.py:374
  64.6 11.0 %collective-permute-start.13 = (bf16[4,128,128]{2,1,0:T(8,128)(2,1)S(1)}, bf16[4,128,128]{2,1,0:T(8,128)(2,1)S(1)}, u32[]{:S(2)}, u32[]{:S(2)}) collective-permute-start(bf16[4,128,128]{2,1,0:T(8,128)(2,1)S(1)} %pad_maximum_fusion.2), channel_id=1, source_target_pairs={{0,6},{2,4},{4,2},{6,0},{8,14},{10,12},{12,10},{14,8},{16,22},{18,... | collective-permute-start | bytes 393224 | tf_op jit(solution)/shard_map/ppermute | solution.py:374
  83.1 1.1 copy-start.1
  84.3 42.8 %all-to-all-start.2 = ((bf16[16,3,128,128]{3,2,1,0:T(8,128)(2,1)}), bf16[16,3,128,128]{3,2,1,0:T(8,128)(2,1)S(1)}, u32[]{:S(2)}, u32[]{:S(2)}) async-start(bf16[16,3,128,128]{3,2,1,0:T(8,128)(2,1)} %copy-done.1), calls=%async_computation.2 | async-start | bytes 3145728 | tf_op jit(solution)/shard_map/all_to_all | solution.py:358
  93.8 21.4 %collective-permute-start.1 = (bf16[64,1024]{1,0:T(8,128)(2,1)S(1)}, bf16[64,1024]{1,0:T(8,128)(2,1)S(1)}, u32[]{:S(2)}, u32[]{:S(2)}) collective-permute-start(bf16[64,1024]{1,0:T(8,128)(2,1)S(1)} %dynamic-slice_convert_fusion.3), channel_id=1, source_target_pairs={{0,1},{1,0},{2,3},{3,2},{4,5},{5,4},{6,7},{7,6},{8,9},{9,8},{10,11... | collective-permute-start | bytes 393224 | tf_op jit(solution)/shard_map/ppermute | solution.py:390
  99.7 21.0 %collective-permute-start.4 = (bf16[64,2048]{1,0:T(8,128)(2,1)S(1)}, bf16[64,2048]{1,0:T(8,128)(2,1)S(1)}, u32[]{:S(2)}, u32[]{:S(2)}) collective-permute-start(bf16[64,2048]{1,0:T(8,128)(2,1)S(1)} %dynamic-slice_convert_fusion), channel_id=1, source_target_pairs={{0,1},{1,0},{2,3},{3,2},{4,5},{5,4},{6,7},{7,6},{8,9},{9,8},{10,11... | collective-permute-start | bytes 786440 | tf_op jit(solution)/shard_map/ppermute | solution.py:390
  104.7 16.0 %collective-permute-start.3 = (bf16[64,2048]{1,0:T(8,128)(2,1)S(1)}, bf16[64,2048]{1,0:T(8,128)(2,1)S(1)}, u32[]{:S(2)}, u32[]{:S(2)}) collective-permute-start(bf16[64,2048]{1,0:T(8,128)(2,1)S(1)} %dynamic-slice_convert_fusion.1), channel_id=1, source_target_pairs={{0,1},{1,0},{2,3},{3,2},{4,5},{5,4},{6,7},{7,6},{8,9},{9,8},{10,11... | collective-permute-start | bytes 786440 | tf_op jit(solution)/shard_map/ppermute | solution.py:390
  110.7 10.0 %collective-permute-start.2 = (bf16[64,2048]{1,0:T(8,128)(2,1)S(1)}, bf16[64,2048]{1,0:T(8,128)(2,1)S(1)}, u32[]{:S(2)}, u32[]{:S(2)}) collective-permute-start(bf16[64,2048]{1,0:T(8,128)(2,1)S(1)} %dynamic-slice_convert_fusion.2), channel_id=1, source_target_pairs={{0,1},{1,0},{2,3},{3,2},{4,5},{5,4},{6,7},{7,6},{8,9},{9,8},{10,11... | collective-permute-start | bytes 786440 | tf_op jit(solution)/shard_map/ppermute | solution.py:390
  114.0 6.7 %collective-permute-start = (bf16[64,1024]{1,0:T(8,128)(2,1)S(1)}, bf16[64,1024]{1,0:T(8,128)(2,1)S(1)}, u32[]{:S(2)}, u32[]{:S(2)}) collective-permute-start(bf16[64,1024]{1,0:T(8,128)(2,1)S(1)} %dynamic-slice_convert_fusion.4), channel_id=1, source_target_pairs={{0,1},{1,0},{2,3},{3,2},{4,5},{5,4},{6,7},{7,6},{8,9},{9,8},{10,11... | collective-permute-start | bytes 393224 | tf_op jit(solution)/shard_map/ppermute | solution.py:390

commit v11 on v9

--- a/solution.py
+++ b/solution.py
@@ -347,11 +347,11 @@
     def spread(x):
         return lax.all_to_all(x, "ctx", 0, 0, tiled=True)
 
-    other = []
-    for c in range(2):
-        cut = grad_out[:, c * (width // 2) : (c + 1) * (width // 2)]
-        other.append(lax.ppermute(cut, "tp", swap))
-    mine = spread(jnp.transpose(qkv, (1, 2, 0, 3)))
+    cut = width // 2
+    other = [lax.ppermute(grad_out[:, :cut], "tp", swap)]
+    by_heads, late = lax.optimization_barrier((jnp.transpose(qkv, (1, 2, 0, 3)), grad_out))
+    mine = spread(by_heads)
+    other.append(lax.ppermute(late[:, cut:], "tp", swap))
     plane = list(project_back(turn.reshape(1), me, grad_out, other, attn_out))
     for e in range(1, PLANE):
         plane[e] = lax.ppermute(plane[e], "ctx", [(i, i ^ e) for i in range(heads)])

time: 138 us -> 139 us (level)
  waiting for transfers between devices: 46.5 us -> 43.1 us
  local copies, waits for them, and re-layouts: 5.51 us -> 8.2 us
  other arithmetic: 0.06 us -> 1.59 us
    ppermute x2, waiting for transfers between devices: 14.7 us -> 12.8 us  [the longest x1 9.96 us: by_head(): other = [lax.ppermute(grad_out[:, :cut], 'tp', swap)]]
    another operation x3, other arithmetic: 0.06 us -> 1.59 us  [by_head(): sent = jnp.stack([x[d] for x in plane])]
    ppermute x3, waiting for transfers between devices: 21.6 us -> 20 us  [by_head(): others.append(lax.ppermute(sent, 'ctx', pairs))]
    slice x1 -> x2, local copies, waits for them, and re-layouts: 2.26 us -> 3.74 us  [the longest x1 1.87 us: by_head(): other = [lax.ppermute(grad_out[:, :cut], 'tp', swap)]]
  transfers between devices with their start and end apart: 16 -> 16, of which waited for: 7 -> 7; matrix products, arithmetic and copies ran while one was open for 16% -> 19% of each run, Pallas kernels for 24% -> 24%
where the time goes in v11:
time: 139 us; the launch traced here: 138 us
  waiting for transfers between devices  43.1 us (31%)
  Pallas kernels  35.3 us (25%)
  starting transfers between devices  28.9 us (21%)
  matrix products  19.7 us (14%)
  local copies, waits for them, and re-layouts  8.2 us (6%)
  other arithmetic  1.59 us (1%)
    ppermute x3, waiting for transfers between devices, by_head(): others.append(lax.ppermute(sent, 'ctx', pairs))  20 us
    dot_general x5, matrix products, by_head(): jnp.einsum('hrd,hdm->rm', local, weights[:, :, start:stop], preferred_ele...  19.7 us
    all_to_all x3, starting transfers between devices, spread(): return lax.all_to_all(x, 'ctx', 0, 0, tiled=True)  17.1 us
    ppermute x1, waiting for transfers between devices, by_head(): other = [lax.ppermute(grad_out[:, :cut], 'tp', swap)]  9.96 us
    pallas_call x1, Pallas kernels, project_back(): pl.pallas_call(back_last_kernel, grid=(deep // group,), out_shape=[jax.Sh...  8.86 us
    pallas_call x1, Pallas kernels, attend_grad(): pl.pallas_call(functools.partial(backward_kernel, step), out_shape=jax.Sh...  8.6 us
    pallas_call x1, Pallas kernels, project_back(): pl.pallas_call(back_first_kernel, grid=(deep // group,), out_shape=jax.Sh...  8.48 us
    ppermute x5, waiting for transfers between devices, by_head(): pieces.append((mixed, lax.ppermute(sent.astype(jnp.bfloat16), 'tp', swap)))  5.5 us
  transfers between devices with their start and end apart: 16, of which 7 were waited for; matrix products, arithmetic and copies ran while one was open for 19% of the time, Pallas kernels for 24%

profile of v11, /device:TPU:13, one launch (start us, length us, event | category | flops | bytes accessed | tf_op | source)
XLA Modules:
  0.0 137.6 jit_solution(17664476085814775501)
XLA Ops:
  0.6 3.0 %copy.7 = bf16[128,16,3,128]{3,0,2,1:T(8,128)(2,1)} copy(bf16[128,16,3,128]{3,1,2,0:T(8,128)(2,1)} %param.3) | data formatting | bytes 3145728 | tf_op args[0]
  3.7 6.5 %all-to-all-start = ((bf16[16,3,128,128]{3,2,1,0:T(8,128)(2,1)}), bf16[16,3,128,128]{3,2,1,0:T(8,128)(2,1)S(1)}, u32[]{:S(2)}, u32[]{:S(2)}) async-start(bf16[16,3,128,128]{3,2,1,0:T(8,128)(2,1)} %bitcast.27), calls=%async_computation | async-start | bytes 3145728 | tf_op jit(solution)/shard_map/all_to_all | solution.py:348
  10.2 1.9 %slice.63 = bf16[64,4096]{1,0:T(8,128)(2,1)} slice(bf16[64,8192]{1,0:T(8,128)(2,1)} %own_ref.3), slice={[0:64], [0:4096]} | slice | bytes 1048576 | tf_op jit(solution)/shard_map/slice | solution.py:351
  12.1 1.2 collective-permute-start.6
  13.3 1.9 %slice.62 = bf16[64,4096]{1,0:T(8,128)(2,1)} slice(bf16[64,8192]{1,0:T(8,128)(2,1)} %own_ref.3), slice={[0:64], [4096:8192]} | slice | bytes 1048576 | tf_op jit(solution)/shard_map/slice | solution.py:354
  15.4 10.0 %collective-permute-done.6.other_ref = bf16[64,4096]{1,0:T(8,128)(2,1)S(1)} collective-permute-done((bf16[64,4096]{1,0:T(8,128)(2,1)}, bf16[64,4096]{1,0:T(8,128)(2,1)S(1)}, u32[]{:S(2)}, u32[]{:S(2)}) %collective-permute-start.6) | collective-permute-done | bytes 524320 | tf_op jit(solution)/shard_map/ppermute | solution.py:351
  25.4 8.5 %back_first.1.y_ref = f32[2048,128]{1,0:T(8,128)S(1)} custom-call(s32[1]{0:T(128)} %bitcast.turn_ref, bf16[64,8192]{1,0:T(8,128)(2,1)S(1)} %copy-done, bf16[64,4096]{1,0:T(8,128)(2,1)S(1)} %collective-permute-done.6.other_ref, bf16[2048,8192]{1,0:T(8,128)(2,1)} %w_ref.3), custom_call_target="tpu_custom_call" | custom-call | flops 2147483648 | bytes 16777216 | tf_op jit(solution)/shard_map/back_first/pallas_call | solution.py:249
  33.9 2.8 %collective-permute-done.5.other_ref = bf16[64,4096]{1,0:T(8,128)(2,1)} collective-permute-done((bf16[64,4096]{1,0:T(8,128)(2,1)}, bf16[64,4096]{1,0:T(8,128)(2,1)}, u32[]{:S(2)}, u32[]{:S(2)}) %collective-permute-start.5) | collective-permute-done | bytes 524320 | tf_op jit(solution)/shard_map/ppermute | solution.py:354
  36.7 8.9 %back_last.1 = (bf16[4,128,128]{2,1,0:T(8,128)(2,1)S(1)}, bf16[4,128,128]{2,1,0:T(8,128)(2,1)S(1)}, bf16[4,128,128]{2,1,0:T(8,128)(2,1)S(1)}, bf16[4,128,128]{2,1,0:T(8,128)(2,1)S(1)}) custom-call(s32[1]{0:T(128)} %bitcast.turn_ref, s32[1]{0:T(128)} %bitcast.8.me_ref, bf16[64,8192]{1,0:T(8,128)(2,1)S(1)} %copy-done, ...), custom_call_target="tpu_custom_call" | custom-call | flops 2147483648 | bytes 16777216 | tf_op jit(solution)/shard_map/back_last/pallas_call | solution.py:261
  45.6 1.3 collective-permute-start.7
  47.2 1.4 %collective-permute-start.9 = (bf16[4,128,128]{2,1,0:T(8,128)(2,1)S(1)}, bf16[4,128,128]{2,1,0:T(8,128)(2,1)S(1)}, u32[]{:S(2)}, u32[]{:S(2)}) collective-permute-start(bf16[4,128,128]{2,1,0:T(8,128)(2,1)S(1)} %get-tuple-element.17), channel_id=1, source_target_pairs={{0,6},{2,4},{4,2},{6,0},{8,14},{10,12},{12,10},{14,8},{16,22},{18,... | collective-permute-start | bytes 393224 | tf_op jit(solution)/shard_map/ppermute | solution.py:357
  49.9 4.9 %attend.1 = (bf16[16,128,128]{2,1,0:T(8,128)(2,1)}, f32[4,1,512]{2,1,0:T(1,128)S(1)}) custom-call(bf16[16,3,128,128]{3,2,1,0:T(8,128)(2,1)S(1)} %all-to-all-done.qkv_ref), custom_call_target="tpu_custom_call" | custom-call | flops 1073741824 | bytes 2097152 | tf_op jit(solution)/shard_map/attend/pallas_call | solution.py:279
  54.8 5.8 %all-to-all-start.1 = ((bf16[16,128,128]{2,1,0:T(8,128)(2,1)}), bf16[16,128,128]{2,1,0:T(8,128)(2,1)S(1)}, u32[]{:S(2)}, u32[]{:S(2)}) async-start(bf16[16,128,128]{2,1,0:T(8,128)(2,1)} %get-tuple-element.11.att_ref), calls=%async_computation.1 | async-start | bytes 1048576 | tf_op jit(solution)/shard_map/all_to_all | solution.py:348
  60.6 0.8 pad_maximum_fusion
  62.5 2.2 %collective-permute-start.11 = (bf16[4,128,128]{2,1,0:T(8,128)(2,1)S(1)}, bf16[4,128,128]{2,1,0:T(8,128)(2,1)S(1)}, u32[]{:S(2)}, u32[]{:S(2)}) collective-permute-start(bf16[4,128,128]{2,1,0:T(8,128)(2,1)S(1)} %pad_maximum_fusion.1), channel_id=1, source_target_pairs={{0,16},{2,18},{4,20},{6,22},{8,24},{10,26},{12,28},{14,30},{16,0},... | collective-permute-start | bytes 393224 | tf_op jit(solution)/shard_map/ppermute | solution.py:362
  65.1 7.9 %collective-permute-done.10.refs_4_ = bf16[4,128,128]{2,1,0:T(8,128)(2,1)S(1)} collective-permute-done((bf16[4,128,128]{2,1,0:T(8,128)(2,1)S(1)}, bf16[4,128,128]{2,1,0:T(8,128)(2,1)S(1)}, u32[]{:S(2)}, u32[]{:S(2)}) %collective-permute-start.10) | collective-permute-done | bytes 131104 | tf_op jit(solution)/shard_map/ppermute | solution.py:362
  73.0 7.5 %collective-permute-done.11.refs_5_ = bf16[4,128,128]{2,1,0:T(8,128)(2,1)S(1)} collective-permute-done((bf16[4,128,128]{2,1,0:T(8,128)(2,1)S(1)}, bf16[4,128,128]{2,1,0:T(8,128)(2,1)S(1)}, u32[]{:S(2)}, u32[]{:S(2)}) %collective-permute-start.11) | collective-permute-done | bytes 131104 | tf_op jit(solution)/shard_map/ppermute | solution.py:362
  80.5 4.6 %collective-permute-done.12.refs_6_ = bf16[4,128,128]{2,1,0:T(8,128)(2,1)S(1)} collective-permute-done((bf16[4,128,128]{2,1,0:T(8,128)(2,1)S(1)}, bf16[4,128,128]{2,1,0:T(8,128)(2,1)S(1)}, u32[]{:S(2)}, u32[]{:S(2)}) %collective-permute-start.12) | collective-permute-done | bytes 131104 | tf_op jit(solution)/shard_map/ppermute | solution.py:362
  85.1 8.6 %attend_grad.1 = bf16[16,3,128,128]{3,2,1,0:T(8,128)(2,1)} custom-call(s32[1]{0:T(128)} %bitcast.8.me_ref, bf16[16,3,128,128]{3,2,1,0:T(8,128)(2,1)S(1)} %all-to-all-done.qkv_ref, bf16[16,128,128]{2,1,0:T(8,128)(2,1)} %get-tuple-element.11.att_ref, f32[4,1,512]{2,1,0:T(1,128)S(1)} %get-tuple-element.12.lse_ref, ...), custom_call_target="tpu_custom_call" | custom-call | flops 2684354560 | bytes 4194304 | tf_op jit(solution)/shard_map/attend_grad/pallas_call | solution.py:318
  93.7 4.8 %all-to-all-start.2 = ((bf16[16,3,128,128]{3,2,1,0:T(8,128)(2,1)}), bf16[16,3,128,128]{3,2,1,0:T(8,128)(2,1)S(1)}, u32[]{:S(2)}, u32[]{:S(2)}) async-start(bf16[16,3,128,128]{3,2,1,0:T(8,128)(2,1)} %attend_grad.1), calls=%async_computation.2 | async-start | bytes 3145728 | tf_op jit(solution)/shard_map/all_to_all | solution.py:348
  98.5 2.9 %fusion.22.refs_2_ = f32[128,1024]{1,0:T(8,128)S(1)} fusion(bf16[16,128,128]{2,1,0:T(8,128)(2,1)S(1)} %all-to-all-done.1, bf16[16,128,8192]{2,1,0:T(8,128)(2,1)} %bitcast.22), kind=kOutput, calls=%fused_computation.15 | convolution fusion | flops 536870912 | bytes 5242880 | tf_op jit(solution)/shard_map/hrd,hdm->rm/dot_general | solution.py:371
  101.4 1.3 collective-permute-start.1
  102.7 4.6 %fusion.16.refs_8_ = f32[128,2048]{1,0:T(8,128)S(1)} fusion(bf16[16,128,128]{2,1,0:T(8,128)(2,1)S(1)} %all-to-all-done.1, bf16[16,128,8192]{2,1,0:T(8,128)(2,1)} %bitcast.23), kind=kOutput, calls=%fused_computation.12 | convolution fusion | flops 1073741824 | bytes 9961472 | tf_op jit(solution)/shard_map/hrd,hdm->rm/dot_general | solution.py:371
  107.7 4.6 %fusion.13.refs_6_ = f32[128,2048]{1,0:T(8,128)S(1)} fusion(bf16[16,128,128]{2,1,0:T(8,128)(2,1)S(1)} %all-to-all-done.1, bf16[16,128,8192]{2,1,0:T(8,128)(2,1)} %bitcast.24), kind=kOutput, calls=%fused_computation.11 | convolution fusion | flops 1073741824 | bytes 9961472 | tf_op jit(solution)/shard_map/hrd,hdm->rm/dot_general | solution.py:371
  112.4 1.3 collective-permute-start.3
  113.7 4.6 %fusion.10.refs_4_ = f32[128,2048]{1,0:T(8,128)S(1)} fusion(bf16[16,128,128]{2,1,0:T(8,128)(2,1)S(1)} %all-to-all-done.1, bf16[16,128,8192]{2,1,0:T(8,128)(2,1)} %bitcast.25), kind=kOutput, calls=%fused_computation.10 | convolution fusion | flops 1073741824 | bytes 9961472 | tf_op jit(solution)/shard_map/hrd,hdm->rm/dot_general | solution.py:371
  118.7 2.9 %fusion.19.refs_0_ = f32[128,1024]{1,0:T(8,128)S(1)} fusion(bf16[16,128,128]{2,1,0:T(8,128)(2,1)S(1)} %all-to-all-done.1, bf16[16,128,8192]{2,1,0:T(8,128)(2,1)} %bitcast.26), kind=kOutput, calls=%fused_computation.14 | convolution fusion | flops 536870912 | bytes 5242880 | tf_op jit(solution)/shard_map/hrd,hdm->rm/dot_general | solution.py:371
  121.6 1.3 collective-permute-start
  122.9 5.5 %collective-permute-done.refs_1_ = bf16[64,1024]{1,0:T(8,128)(2,1)S(1)} collective-permute-done((bf16[64,1024]{1,0:T(8,128)(2,1)S(1)}, bf16[64,1024]{1,0:T(8,128)(2,1)S(1)}, u32[]{:S(2)}, u32[]{:S(2)}) %collective-permute-start) | collective-permute-done | bytes 131104 | tf_op jit(solution)/shard_map/ppermute | solution.py:378
  128.4 1.5 %finish.1 = f32[64,8192]{1,0:T(8,128)} custom-call(s32[1]{0:T(128)} %bitcast.turn_ref, f32[128,1024]{1,0:T(8,128)S(1)} %fusion.19.refs_0_, bf16[64,1024]{1,0:T(8,128)(2,1)S(1)} %collective-permute-done.refs_1_, f32[128,1024]{1,0:T(8,128)S(1)} %fusion.22.refs_2_, bf16[64,1024]{1,0:T(8,128)(2,1)S(1)} %collective-permute-done.1.refs_3_, ...), custom_call_target="tpu_custom_call" | custom-call | tf_op jit(solution)/shard_map/finish/pallas_call | solution.py:303
  129.9 4.8 %all-to-all-done.2.x_ref = bf16[16,3,128,128]{3,2,1,0:T(8,128)(2,1)S(1)} async-done(((bf16[16,3,128,128]{3,2,1,0:T(8,128)(2,1)}), bf16[16,3,128,128]{3,2,1,0:T(8,128)(2,1)S(1)}, u32[]{:S(2)}, u32[]{:S(2)}) %all-to-all-start.2) | async-done | bytes 1572896 | tf_op jit(solution)/shard_map/all_to_all | solution.py:348
  134.7 2.9 %join_heads.1 = f32[128,3,16,128]{3,2,1,0:T(8,128)} custom-call(bf16[16,3,128,128]{3,2,1,0:T(8,128)(2,1)S(1)} %all-to-all-done.2.x_ref), custom_call_target="tpu_custom_call" | custom-call | tf_op jit(solution)/shard_map/join_heads/pallas_call | solution.py:218
  (28 shorter events, 4.1 us)
Async XLA Ops:
  0.6 24.8 %copy-start = (bf16[64,8192]{1,0:T(8,128)(2,1)S(1)}, bf16[64,8192]{1,0:T(8,128)(2,1)}, u32[]{:S(2)}) copy-start(bf16[64,8192]{1,0:T(8,128)(2,1)} %own_ref.3) | copy-start | bytes 3145732
  3.7 46.2 %all-to-all-start = ((bf16[16,3,128,128]{3,2,1,0:T(8,128)(2,1)}), bf16[16,3,128,128]{3,2,1,0:T(8,128)(2,1)S(1)}, u32[]{:S(2)}, u32[]{:S(2)}) async-start(bf16[16,3,128,128]{3,2,1,0:T(8,128)(2,1)} %bitcast.27), calls=%async_computation | async-start | bytes 3145728 | tf_op jit(solution)/shard_map/all_to_all | solution.py:348
  12.1 13.3 %collective-permute-start.6 = (bf16[64,4096]{1,0:T(8,128)(2,1)}, bf16[64,4096]{1,0:T(8,128)(2,1)S(1)}, u32[]{:S(2)}, u32[]{:S(2)}) collective-permute-start(bf16[64,4096]{1,0:T(8,128)(2,1)} %slice.63), channel_id=1, source_target_pairs={{0,1},{1,0},{2,3},{3,2},{4,5},{5,4},{6,7},{7,6},{8,9},{9,8},{10,11... | collective-permute-start | bytes 1572872 | tf_op jit(solution)/shard_map/ppermute | solution.py:351
  15.2 21.6 %collective-permute-start.5 = (bf16[64,4096]{1,0:T(8,128)(2,1)}, bf16[64,4096]{1,0:T(8,128)(2,1)}, u32[]{:S(2)}, u32[]{:S(2)}) collective-permute-start(bf16[64,4096]{1,0:T(8,128)(2,1)} %slice.62), channel_id=1, source_target_pairs={{0,1},{1,0},{2,3},{3,2},{4,5},{5,4},{6,7},{7,6},{8,9},{9,8},{10,11... | collective-permute-start | bytes 1572872 | tf_op jit(solution)/shard_map/ppermute | solution.py:354
  45.6 3.6 %collective-permute-start.7 = (bf16[4,128,128]{2,1,0:T(8,128)(2,1)S(1)}, bf16[4,128,128]{2,1,0:T(8,128)(2,1)S(1)}, u32[]{:S(2)}, u32[]{:S(2)}) collective-permute-start(bf16[4,128,128]{2,1,0:T(8,128)(2,1)S(1)} %get-tuple-element.15), channel_id=1, source_target_pairs={{0,2},{2,0},{4,6},{6,4},{8,10},{10,8},{12,14},{14,12},{16,18},{18,... | collective-permute-start | bytes 393224 | tf_op jit(solution)/shard_map/ppermute | solution.py:357
  46.9 13.7 %collective-permute-start.8 = (bf16[4,128,128]{2,1,0:T(8,128)(2,1)S(1)}, bf16[4,128,128]{2,1,0:T(8,128)(2,1)S(1)}, u32[]{:S(2)}, u32[]{:S(2)}) collective-permute-start(bf16[4,128,128]{2,1,0:T(8,128)(2,1)S(1)} %get-tuple-element.16), channel_id=1, source_target_pairs={{0,4},{2,6},{4,0},{6,2},{8,12},{10,14},{12,8},{14,10},{16,20},{18,... | collective-permute-start | bytes 393224 | tf_op jit(solution)/shard_map/ppermute | solution.py:357
  47.2 13.4 %collective-permute-start.9 = (bf16[4,128,128]{2,1,0:T(8,128)(2,1)S(1)}, bf16[4,128,128]{2,1,0:T(8,128)(2,1)S(1)}, u32[]{:S(2)}, u32[]{:S(2)}) collective-permute-start(bf16[4,128,128]{2,1,0:T(8,128)(2,1)S(1)} %get-tuple-element.17), channel_id=1, source_target_pairs={{0,6},{2,4},{4,2},{6,0},{8,14},{10,12},{12,10},{14,8},{16,22},{18,... | collective-permute-start | bytes 393224 | tf_op jit(solution)/shard_map/ppermute | solution.py:357
  54.8 38.9 %all-to-all-start.1 = ((bf16[16,128,128]{2,1,0:T(8,128)(2,1)}), bf16[16,128,128]{2,1,0:T(8,128)(2,1)S(1)}, u32[]{:S(2)}, u32[]{:S(2)}) async-start(bf16[16,128,128]{2,1,0:T(8,128)(2,1)} %get-tuple-element.11.att_ref), calls=%async_computation.1 | async-start | bytes 1048576 | tf_op jit(solution)/shard_map/all_to_all | solution.py:348
  61.4 11.5 %collective-permute-start.10 = (bf16[4,128,128]{2,1,0:T(8,128)(2,1)S(1)}, bf16[4,128,128]{2,1,0:T(8,128)(2,1)S(1)}, u32[]{:S(2)}, u32[]{:S(2)}) collective-permute-start(bf16[4,128,128]{2,1,0:T(8,128)(2,1)S(1)} %pad_maximum_fusion), channel_id=1, source_target_pairs={{0,8},{2,10},{4,12},{6,14},{8,0},{10,2},{12,4},{14,6},{16,24},{18,... | collective-permute-start | bytes 393224 | tf_op jit(solution)/shard_map/ppermute | solution.py:362
  62.5 17.9 %collective-permute-start.11 = (bf16[4,128,128]{2,1,0:T(8,128)(2,1)S(1)}, bf16[4,128,128]{2,1,0:T(8,128)(2,1)S(1)}, u32[]{:S(2)}, u32[]{:S(2)}) collective-permute-start(bf16[4,128,128]{2,1,0:T(8,128)(2,1)S(1)} %pad_maximum_fusion.1), channel_id=1, source_target_pairs={{0,16},{2,18},{4,20},{6,22},{8,24},{10,26},{12,28},{14,30},{16,0},... | collective-permute-start | bytes 393224 | tf_op jit(solution)/shard_map/ppermute | solution.py:362
  64.7 20.4 %collective-permute-start.12 = (bf16[4,128,128]{2,1,0:T(8,128)(2,1)S(1)}, bf16[4,128,128]{2,1,0:T(8,128)(2,1)S(1)}, u32[]{:S(2)}, u32[]{:S(2)}) collective-permute-start(bf16[4,128,128]{2,1,0:T(8,128)(2,1)S(1)} %pad_maximum_fusion.2), channel_id=1, source_target_pairs={{0,24},{2,26},{4,28},{6,30},{8,16},{10,18},{12,20},{14,22},{16,8},... | collective-permute-start | bytes 393224 | tf_op jit(solution)/shard_map/ppermute | solution.py:362
  93.7 41.0 %all-to-all-start.2 = ((bf16[16,3,128,128]{3,2,1,0:T(8,128)(2,1)}), bf16[16,3,128,128]{3,2,1,0:T(8,128)(2,1)S(1)}, u32[]{:S(2)}, u32[]{:S(2)}) async-start(bf16[16,3,128,128]{3,2,1,0:T(8,128)(2,1)} %attend_grad.1), calls=%async_computation.2 | async-start | bytes 3145728 | tf_op jit(solution)/shard_map/all_to_all | solution.py:348
  101.4 21.5 %collective-permute-start.1 = (bf16[64,1024]{1,0:T(8,128)(2,1)S(1)}, bf16[64,1024]{1,0:T(8,128)(2,1)S(1)}, u32[]{:S(2)}, u32[]{:S(2)}) collective-permute-start(bf16[64,1024]{1,0:T(8,128)(2,1)S(1)} %dynamic-slice_convert_fusion.3), channel_id=1, source_target_pairs={{0,1},{1,0},{2,3},{3,2},{4,5},{5,4},{6,7},{7,6},{8,9},{9,8},{10,11... | collective-permute-start | bytes 393224 | tf_op jit(solution)/shard_map/ppermute | solution.py:378
  107.4 21.0 %collective-permute-start.4 = (bf16[64,2048]{1,0:T(8,128)(2,1)S(1)}, bf16[64,2048]{1,0:T(8,128)(2,1)S(1)}, u32[]{:S(2)}, u32[]{:S(2)}) collective-permute-start(bf16[64,2048]{1,0:T(8,128)(2,1)S(1)} %dynamic-slice_convert_fusion), channel_id=1, source_target_pairs={{0,1},{1,0},{2,3},{3,2},{4,5},{5,4},{6,7},{7,6},{8,9},{9,8},{10,11... | collective-permute-start | bytes 786440 | tf_op jit(solution)/shard_map/ppermute | solution.py:378
  112.4 16.0 %collective-permute-start.3 = (bf16[64,2048]{1,0:T(8,128)(2,1)S(1)}, bf16[64,2048]{1,0:T(8,128)(2,1)S(1)}, u32[]{:S(2)}, u32[]{:S(2)}) collective-permute-start(bf16[64,2048]{1,0:T(8,128)(2,1)S(1)} %dynamic-slice_convert_fusion.1), channel_id=1, source_target_pairs={{0,1},{1,0},{2,3},{3,2},{4,5},{5,4},{6,7},{7,6},{8,9},{9,8},{10,11... | collective-permute-start | bytes 786440 | tf_op jit(solution)/shard_map/ppermute | solution.py:378
  118.4 10.0 %collective-permute-start.2 = (bf16[64,2048]{1,0:T(8,128)(2,1)S(1)}, bf16[64,2048]{1,0:T(8,128)(2,1)S(1)}, u32[]{:S(2)}, u32[]{:S(2)}) collective-permute-start(bf16[64,2048]{1,0:T(8,128)(2,1)S(1)} %dynamic-slice_convert_fusion.2), channel_id=1, source_target_pairs={{0,1},{1,0},{2,3},{3,2},{4,5},{5,4},{6,7},{7,6},{8,9},{9,8},{10,11... | collective-permute-start | bytes 786440 | tf_op jit(solution)/shard_map/ppermute | solution.py:378
  121.6 6.8 %collective-permute-start = (bf16[64,1024]{1,0:T(8,128)(2,1)S(1)}, bf16[64,1024]{1,0:T(8,128)(2,1)S(1)}, u32[]{:S(2)}, u32[]{:S(2)}) collective-permute-start(bf16[64,1024]{1,0:T(8,128)(2,1)S(1)} %dynamic-slice_convert_fusion.4), channel_id=1, source_target_pairs={{0,1},{1,0},{2,3},{3,2},{4,5},{5,4},{6,7},{7,6},{8,9},{9,8},{10,11... | collective-permute-start | bytes 393224 | tf_op jit(solution)/shard_map/ppermute | solution.py:378
